TPU v7x, 32 devices: a whole 2x2x4 slice. The times are simulated.
32 devices in a mesh: ctx: 4 (over y, x), fsdp: 8 (over z, core).
Axes of the slice: x: 2, y: 2, z: 4, core: 2. Of those that a mesh axis runs over, the one named last changes fastest.
Arguments:
- tokens: bfloat16 [8, 1024, 2048], P('fsdp', 'ctx'), may hold values from -6 to 6
- dealing: int32 [8, 8], P('fsdp'), may hold values from 0 to 7, as said below
- first_gain: bfloat16 [2048], P('fsdp'), may hold values from 0.5 to 1.5
- query_weight: bfloat16 [2048, 2048], P('fsdp'), may hold values from -0.1875 to 0.1875
- key_weight: bfloat16 [2048, 256], P('fsdp'), may hold values from -0.1875 to 0.1875
- value_weight: bfloat16 [2048, 256], P('fsdp'), may hold values from -0.125 to 0.125
- output_weight: bfloat16 [2048, 2048], P('fsdp'), may hold values from -0.5 to 0.5
- second_gain: bfloat16 [2048], P('fsdp'), may hold values from 0.5 to 1.5
- gate_weight: bfloat16 [2048, 5632], P('fsdp'), may hold values from -0.125 to 0.125
- up_weight: bfloat16 [2048, 5632], P('fsdp'), may hold values from -0.125 to 0.125
- down_weight: bfloat16 [5632, 2048], P('fsdp'), may hold values from -0.15625 to 0.15625
- cotangent: bfloat16 [8, 1024, 2048], P('fsdp', 'ctx'), may hold values from -6 to 6
Outputs:
- block_output: bfloat16 [8, 1024, 2048], P('fsdp', 'ctx')
- input_grad: bfloat16 [8, 1024, 2048], P('fsdp', 'ctx')
- first_gain_grad: float32 [2048], P('fsdp')
- query_grad: float32 [2048, 2048], P('fsdp')
- key_grad: float32 [2048, 256], P('fsdp')
- value_grad: float32 [2048, 256], P('fsdp')
- output_grad: float32 [2048, 2048], P('fsdp')
- second_gain_grad: float32 [2048], P('fsdp')
- gate_grad: float32 [2048, 5632], P('fsdp')
- up_grad: float32 [2048, 5632], P('fsdp')
- down_grad: float32 [5632, 2048], P('fsdp')
Inputs may be any that keep to these rules, and one draw needn't show every extreme that they name: In each row of dealing every block number 0 to 7 appears once, and the two slots 2 c and 2 c + 1 of one device c of ctx hold two blocks whose numbers add up to 7.
All inputs are finite; a program needn't handle non-finite values.
Results may differ from a plain program's by a relative error of at most 0.024.
Values may be sent and summed in bfloat16 or wider, within the bound.
A program may use at most 576 MiB of HBM per device.

v0:
```python
import math

import jax
import jax.numpy as jnp
from jax import lax
from jax.sharding import PartitionSpec as P

D = 2048
FF = 5632
HEADS = 32
KV_HEADS = 4
HEAD_DIM = 64
KV_WIDTH = 256


epsilon = 1e-05


def rotary_tables(positions):
    frequency = jnp.exp(
        -math.log(10000.0) * jnp.arange(HEAD_DIM // 2).astype(jnp.float32) * (2.0 / HEAD_DIM)
    )
    angles = positions.astype(jnp.float32)[:, None] * frequency[None, :]
    return (jnp.cos(angles), jnp.sin(angles))


def rotate(matrix, cosine_table, sine_table):
    half_dim = HEAD_DIM // 2
    first_half = matrix[..., :half_dim]
    second_half = matrix[..., half_dim:]
    cosine_wide = cosine_table[:, None, :]
    sine_wide = sine_table[:, None, :]
    return jnp.concatenate(
        [
            first_half * cosine_wide - second_half * sine_wide,
            second_half * cosine_wide + first_half * sine_wide,
        ],
        axis=-1,
    )


def unrotate(matrix, cosine_table, sine_table):
    half_dim = HEAD_DIM // 2
    first_half = matrix[..., :half_dim]
    second_half = matrix[..., half_dim:]
    cosine_wide = cosine_table[:, None, :]
    sine_wide = sine_table[:, None, :]
    return jnp.concatenate(
        [
            first_half * cosine_wide + second_half * sine_wide,
            second_half * cosine_wide - first_half * sine_wide,
        ],
        axis=-1,
    )


def norm_parts(values):
    inverse = lax.rsqrt(jnp.mean(values * values, axis=-1, keepdims=True) + epsilon)
    return (values * inverse, inverse)


def norm_back(gradient, normed, inverse):
    return inverse * (gradient - normed * jnp.mean(gradient * normed, axis=-1, keepdims=True))


def times_transposed(left_side, right_side):
    return lax.dot_general(
        left_side, right_side, (((1,), (1,)), ((), ())), preferred_element_type=jnp.float32
    )


def masked_scores(head_queries, head_keys, allowed):
    scores = jnp.einsum(
        "qhd,kd->hqk", head_queries, head_keys, preferred_element_type=jnp.float32
    ) * (1.0 / math.sqrt(HEAD_DIM))
    return jnp.where(allowed[None], scores, -1e30)


def attend_forward(queries, keys_all, values_all, allowed):
    group_size = HEADS // KV_HEADS
    outputs = []
    log_totals = []
    for group_index in range(KV_HEADS):
        head_queries = queries[:, group_index * group_size : (group_index + 1) * group_size]
        scores = masked_scores(head_queries, keys_all[:, group_index], allowed)
        largest = jnp.max(scores, axis=-1, keepdims=True)
        exponent = jnp.exp(scores - largest)
        totals = jnp.sum(exponent, axis=-1, keepdims=True)
        weights = (exponent / totals).astype(jnp.bfloat16)
        outputs.append(
            jnp.einsum(
                "hqk,kd->qhd",
                weights,
                values_all[:, group_index],
                preferred_element_type=jnp.float32,
            )
        )
        log_totals.append(largest + jnp.log(totals))
    return (jnp.concatenate(outputs, axis=1), log_totals)


def attend_backward(queries, keys_all, values_all, allowed, log_totals, grad_attended):
    group_size = HEADS // KV_HEADS
    query_parts = []
    key_parts = []
    value_parts = []
    for group_index in range(KV_HEADS):
        head_queries = queries[:, group_index * group_size : (group_index + 1) * group_size]
        head_grads = grad_attended[:, group_index * group_size : (group_index + 1) * group_size]
        head_keys = keys_all[:, group_index]
        head_values = values_all[:, group_index]
        scores = masked_scores(head_queries, head_keys, allowed)
        weights = jnp.exp(scores - log_totals[group_index])
        grad_probs = jnp.einsum(
            "qhd,kd->hqk", head_grads, head_values, preferred_element_type=jnp.float32
        )
        row_dots = jnp.sum(weights * grad_probs, axis=-1, keepdims=True)
        grad_scores = (weights * (grad_probs - row_dots) * (1.0 / math.sqrt(HEAD_DIM))).astype(
            jnp.bfloat16
        )
        value_parts.append(
            jnp.einsum(
                "hqk,qhd->kd",
                weights.astype(jnp.bfloat16),
                head_grads,
                preferred_element_type=jnp.float32,
            )
        )
        query_parts.append(
            jnp.einsum("hqk,kd->qhd", grad_scores, head_keys, preferred_element_type=jnp.float32)
        )
        key_parts.append(
            jnp.einsum("hqk,qhd->kd", grad_scores, head_queries, preferred_element_type=jnp.float32)
        )
    return (
        jnp.concatenate(query_parts, axis=1),
        jnp.stack(key_parts, axis=1),
        jnp.stack(value_parts, axis=1),
    )


def column_term(source, gradient):
    return lax.dot_general(
        source, gradient, (((0,), (0,)), ((), ())), preferred_element_type=jnp.float32
    )


def stacked_term(sources, gradients):
    return jnp.concatenate(
        [column_term(source, gradient) for source, gradient in zip(sources, gradients)], axis=1
    )


def per_device(
    tokens,
    dealing,
    first_gain,
    query_weight,
    key_weight,
    value_weight,
    output_weight,
    second_gain,
    gate_weight,
    up_weight,
    down_weight,
    cotangent,
):
    shard_count = lax.axis_size("fsdp")
    ctx_index = lax.axis_index("ctx")
    shard_index = lax.axis_index("fsdp")
    row_count = tokens.shape[1]
    block_rows = row_count // 2
    offsets = jnp.arange(block_rows, dtype=jnp.int32)
    all_positions = (dealing[0][:, None] * block_rows + offsets[None, :]).reshape(-1)
    own_positions = lax.dynamic_slice_in_dim(all_positions, ctx_index * row_count, row_count)
    allowed = all_positions[None, :] <= own_positions[:, None]
    cosine_table, sine_table = rotary_tables(own_positions)
    inputs = tokens[0].astype(jnp.float32)
    gain_first, query_full, key_full, value_full, output_full = (
        lax.all_gather(first_gain, "fsdp", axis=0, tiled=True),
        lax.all_gather(query_weight, "fsdp", axis=0, tiled=True),
        lax.all_gather(key_weight, "fsdp", axis=0, tiled=True),
        lax.all_gather(value_weight, "fsdp", axis=0, tiled=True),
        lax.all_gather(output_weight, "fsdp", axis=0, tiled=True),
    )
    normed_first, inverse_first = norm_parts(inputs)
    first_input = (normed_first * gain_first.astype(jnp.float32)).astype(jnp.bfloat16)
    queries = jnp.dot(first_input, query_full, preferred_element_type=jnp.float32)
    own_keys = jnp.dot(first_input, key_full, preferred_element_type=jnp.float32)
    own_values = jnp.dot(first_input, value_full, preferred_element_type=jnp.float32).astype(
        jnp.bfloat16
    )
    query_rot = rotate(
        queries.reshape(row_count, HEADS, HEAD_DIM), cosine_table, sine_table
    ).astype(jnp.bfloat16)
    key_rot = (
        rotate(own_keys.reshape(row_count, KV_HEADS, HEAD_DIM), cosine_table, sine_table)
        .astype(jnp.bfloat16)
        .reshape(row_count, KV_WIDTH)
    )
    keys_all, values_all = (
        lax.all_gather(key_rot, "ctx", axis=0, tiled=True),
        lax.all_gather(own_values, "ctx", axis=0, tiled=True),
    )
    keys_all = keys_all.reshape(-1, KV_HEADS, HEAD_DIM)
    values_all = values_all.reshape(-1, KV_HEADS, HEAD_DIM)
    attended, log_totals = attend_forward(query_rot, keys_all, values_all, allowed)
    attended = attended.reshape(row_count, D).astype(jnp.bfloat16)
    residual_mid = inputs + jnp.dot(attended, output_full, preferred_element_type=jnp.float32)
    gain_second, gate_full, up_full, down_full = (
        lax.all_gather(second_gain, "fsdp", axis=0, tiled=True),
        lax.all_gather(gate_weight, "fsdp", axis=0, tiled=True),
        lax.all_gather(up_weight, "fsdp", axis=0, tiled=True),
        lax.all_gather(down_weight, "fsdp", axis=0, tiled=True),
    )
    normed_second, inverse_second = norm_parts(residual_mid)
    second_input = (normed_second * gain_second.astype(jnp.float32)).astype(jnp.bfloat16)
    gate_act = jnp.dot(second_input, gate_full, preferred_element_type=jnp.float32)
    upward = jnp.dot(second_input, up_full, preferred_element_type=jnp.float32)
    sigmoid_gate = jax.nn.sigmoid(gate_act)
    silu_gate = gate_act * sigmoid_gate
    hidden = (silu_gate * upward).astype(jnp.bfloat16)
    block_output = (
        residual_mid + jnp.dot(hidden, down_full, preferred_element_type=jnp.float32)
    ).astype(jnp.bfloat16)
    grad_out = cotangent[0]
    grad_hidden = times_transposed(grad_out, down_full)
    down_piece = lax.psum_scatter(
        column_term(hidden, grad_out).astype(jnp.bfloat16), "fsdp", scatter_dimension=0, tiled=True
    )
    grad_gate = (
        grad_hidden * upward * sigmoid_gate * (1.0 + gate_act * (1.0 - sigmoid_gate))
    ).astype(jnp.bfloat16)
    grad_up = (grad_hidden * silu_gate).astype(jnp.bfloat16)
    grad_second = times_transposed(grad_gate, gate_full) + times_transposed(grad_up, up_full)
    second_gain_part = jnp.sum(grad_second * normed_second, axis=0)
    grad_mid = grad_out.astype(jnp.float32) + norm_back(
        grad_second * gain_second.astype(jnp.float32), normed_second, inverse_second
    )
    grad_branch = grad_mid.astype(jnp.bfloat16)
    gain_first, query_full, key_full, value_full, output_full = (
        lax.all_gather(first_gain, "fsdp", axis=0, tiled=True),
        lax.all_gather(query_weight, "fsdp", axis=0, tiled=True),
        lax.all_gather(key_weight, "fsdp", axis=0, tiled=True),
        lax.all_gather(value_weight, "fsdp", axis=0, tiled=True),
        lax.all_gather(output_weight, "fsdp", axis=0, tiled=True),
    )
    grad_attended = times_transposed(grad_branch, output_full).astype(jnp.bfloat16)
    grad_query_rot, key_terms, value_terms = attend_backward(
        query_rot,
        keys_all,
        values_all,
        allowed,
        log_totals,
        grad_attended.reshape(row_count, HEADS, HEAD_DIM),
    )
    key_sums, value_sums = (
        lax.psum_scatter(
            key_terms.reshape(-1, KV_WIDTH).astype(jnp.bfloat16),
            "ctx",
            scatter_dimension=0,
            tiled=True,
        ).astype(jnp.float32),
        lax.psum_scatter(
            value_terms.reshape(-1, KV_WIDTH).astype(jnp.bfloat16),
            "ctx",
            scatter_dimension=0,
            tiled=True,
        ).astype(jnp.float32),
    )
    grad_query = (
        unrotate(grad_query_rot, cosine_table, sine_table)
        .reshape(row_count, D)
        .astype(jnp.bfloat16)
    )
    grad_key = (
        unrotate(key_sums.reshape(row_count, KV_HEADS, HEAD_DIM), cosine_table, sine_table)
        .reshape(row_count, KV_WIDTH)
        .astype(jnp.bfloat16)
    )
    grad_value = value_sums.astype(jnp.bfloat16)
    grad_first = (
        times_transposed(grad_query, query_full)
        + times_transposed(grad_key, key_full)
        + times_transposed(grad_value, value_full)
    )
    first_gain_part = jnp.sum(grad_first * normed_first, axis=0)
    grad_input = grad_mid + norm_back(
        grad_first * gain_first.astype(jnp.float32), normed_first, inverse_first
    )
    grad_qkv = jnp.concatenate([grad_query, grad_key, grad_value], axis=1)
    grad_gate_up = jnp.concatenate([grad_gate, grad_up], axis=1)
    gradients = (grad_qkv, grad_branch, grad_gate_up)
    sources = (first_input, attended, second_input)
    row_piece = lax.psum_scatter(
        stacked_term(sources, gradients).astype(jnp.bfloat16),
        "fsdp",
        scatter_dimension=0,
        tiled=True,
    )
    down_shard, row_shard = (
        lax.psum(down_piece, "ctx").astype(jnp.float32),
        lax.psum(row_piece, "ctx").astype(jnp.float32),
    )
    gain_totals = lax.psum(jnp.stack([first_gain_part, second_gain_part]), ("ctx", "fsdp"))
    gain_rows = D // shard_count
    gain_shard = lax.dynamic_slice_in_dim(gain_totals, shard_index * gain_rows, gain_rows, 1)
    key_begin = D
    value_begin = D + KV_WIDTH
    output_begin = D + 2 * KV_WIDTH
    gate_begin = 2 * D + 2 * KV_WIDTH
    up_begin = gate_begin + FF
    return (
        block_output[None],
        grad_input.astype(jnp.bfloat16)[None],
        gain_shard[0],
        row_shard[:, :key_begin],
        row_shard[:, key_begin:value_begin],
        row_shard[:, value_begin:output_begin],
        row_shard[:, output_begin:gate_begin],
        gain_shard[1],
        row_shard[:, gate_begin:up_begin],
        row_shard[:, up_begin:],
        down_shard,
    )


def solution(mesh):
    in_specs = (
        P("fsdp", "ctx", None),
        P("fsdp", None),
        P("fsdp"),
        P("fsdp", None),
        P("fsdp", None),
        P("fsdp", None),
        P("fsdp", None),
        P("fsdp"),
        P("fsdp", None),
        P("fsdp", None),
        P("fsdp", None),
        P("fsdp", "ctx", None),
    )
    out_specs = (
        P("fsdp", "ctx", None),
        P("fsdp", "ctx", None),
        P("fsdp"),
        P("fsdp", None),
        P("fsdp", None),
        P("fsdp", None),
        P("fsdp", None),
        P("fsdp"),
        P("fsdp", None),
        P("fsdp", None),
        P("fsdp", None),
    )
    return jax.shard_map(
        per_device, mesh=mesh, in_specs=in_specs, out_specs=out_specs, check_vma=False
    )
```

profile of v0, /device:TPU:0, one launch (start us, length us, event | category | flops | bytes accessed | tf_op | source)
XLA Modules:
  0.0 2122.7 jit_solution(3202706513948020430)
XLA Ops:
  12.0 13.5 all-gather.1
  59.9 14.3 all_gather.42
  74.2 66.8 %all-gather.14.cloned.1.call-done = bf16[2048,2048]{1,0:T(8,128)(2,1)} async-done(((bf16[256,2048]{1,0:T(8,128)(2,1)}), bf16[2048,2048]{1,0:T(8,128)(2,1)}) %all-gather.14.cloned.1.call-update) | async-done | bytes 8388624 | tf_op jit(solution)/shard_map/all_gather | solution.py:181
  185.9 37.3 %all-gather.16.cloned.1.call-done = bf16[2048,2048]{1,0:T(8,128)(2,1)} async-done(((bf16[256,2048]{1,0:T(8,128)(2,1)}), bf16[2048,2048]{1,0:T(8,128)(2,1)}) %all-gather.16.cloned.1.call-update) | async-done | bytes 8388624 | tf_op jit(solution)/shard_map/all_gather | solution.py:184
  230.9 195.0 %all-gather.20.cloned.1.call-done = bf16[2048,5632]{1,0:T(8,128)(2,1)} async-done(((bf16[256,5632]{1,0:T(8,128)(2,1)}), bf16[2048,5632]{1,0:T(8,128)(2,1)}) %all-gather.20.cloned.1.call-update) | async-done | bytes 23068688 | tf_op jit(solution)/shard_map/all_gather | solution.py:213
  425.9 15.0 fusion.202
  440.9 187.4 %all-gather.18.cloned.1.call-done = bf16[2048,5632]{1,0:T(8,128)(2,1)} async-done(((bf16[256,5632]{1,0:T(8,128)(2,1)}), bf16[2048,5632]{1,0:T(8,128)(2,1)}) %all-gather.18.cloned.1.call-update) | async-done | bytes 23068688 | tf_op jit(solution)/shard_map/all_gather | solution.py:212
  628.3 14.2 fusion.201
  642.5 188.3 %all-gather.22.cloned.1.call-done = bf16[5632,2048]{1,0:T(8,128)(2,1)} async-done(((bf16[704,2048]{1,0:T(8,128)(2,1)}), bf16[5632,2048]{1,0:T(8,128)(2,1)}) %all-gather.22.cloned.1.call-update) | async-done | bytes 23068688 | tf_op jit(solution)/shard_map/all_gather | solution.py:214
  830.8 25.6 %multiply_convert_fusion = (bf16[256,5632]{1,0:T(8,128)(2,1)}, bf16[256,5632]{1,0:T(8,128)(2,1)}, bf16[256,5632]{1,0:T(8,128)(2,1)}) fusion(f32[256,5632]{1,0:T(8,128)} %fusion.201, f32[256,5632]{1,0:T(8,128)} %fusion.202, bf16[5632,2048]{1,0:T(8,128)(2,1)} %all-gather.22.cloned.1.call-done, bf16[1,256,2048]{2,1,0:T(8,128)(2,1)S(1)} %copy-done.15), kind=kOutput, calls=%fused_computation.56 | convolution fusion | flops 5927206912 | bytes 44302336 | tf_op jit(solution)/shard_map/dot_general | solution.py:67
  869.0 13.9 multiply_reduce_fusion
  933.8 13.7 fusion.139
  947.5 14.8 fusion.136
  962.3 15.3 fusion.137
  1035.1 15.9 fusion.81
  1050.9 15.1 fusion.82
  1066.1 15.1 fusion.83
  1084.2 21.7 %convolution_convert_fusion = bf16[2048,11264]{1,0:T(8,128)(2,1)} fusion(bf16[256,2048]{1,0:T(8,128)(2,1)} %copy-done.17, bf16[256,5632]{1,0:T(8,128)(2,1)} %get-tuple-element.19, bf16[256,5632]{1,0:T(8,128)(2,1)} %get-tuple-element.20), kind=kOutput, calls=%fused_computation.5 | convolution fusion | flops 11845763072 | bytes 52953088 | tf_op jit(solution)/shard_map/dot_general | solution.py:143
  1114.0 44.0 %pad_maximum_fusion = bf16[2048,15872]{1,0:T(8,128)(2,1)} fusion(bf16[2048,11264]{1,0:T(8,128)(2,1)} %convolution_convert_fusion, bf16[2048,2048]{1,0:T(8,128)(2,1)} %copy.91, bf16[2048,2560]{1,0:T(8,128)(2,1)} %convolution_convert_fusion.2), kind=kLoop, calls=%fused_computation.4 | loop fusion | flops 195035136 | bytes 130023424 | tf_op jit(solution)/shard_map/concatenate | solution.py:149
  1158.0 102.1 %reduce-scatter.11.cloned.1.call-done = bf16[704,2048]{1,0:T(8,128)(2,1)} async-done(((bf16[5632,2048]{1,0:T(8,128)(2,1)}), bf16[704,2048]{1,0:T(8,128)(2,1)}) %reduce-scatter.11.cloned.1.call-update) | async-done | bytes 2883600 | tf_op jit(solution)/shard_map/reduce_scatter | solution.py:228
  1260.2 621.3 %reduce-scatter.9.cloned.1.call-done = bf16[256,15872]{1,0:T(8,128)(2,1)} async-done(((bf16[2048,15872]{1,0:T(8,128)(2,1)}), bf16[256,15872]{1,0:T(8,128)(2,1)}) %reduce-scatter.9.cloned.1.call-update) | async-done | bytes 8126480 | tf_op jit(solution)/shard_map/reduce_scatter | solution.py:295
  1887.8 13.4 fusion.64
  1904.0 38.8 %psum.21 = f32[2,2048]{1,0:T(2,128)S(1)} all-reduce(f32[2,2048]{1,0:T(2,128)S(1)} %pad_maximum_fusion.9), channel_id=1, replica_groups=mesh['ctx'=4,'fsdp'=8] {'ctx','fsdp'}, use_global_device_ids=true, to_apply=%region_20.21 | all-reduce | flops 4096 | bytes 32768 | tf_op jit(solution)/shard_map/psum | solution.py:305
  1946.7 153.0 %all-reduce.3.cloned.1.call-done = (bf16[256,15872]{1,0:T(8,128)(2,1)}, bf16[704,2048]{1,0:T(8,128)(2,1)}) async-done(((bf16[256,15872]{1,0:T(8,128)(2,1)}, bf16[704,2048]{1,0:T(8,128)(2,1)}), (bf16[256,15872]{1,0:T(8,128)(2,1)}, bf16[704,2048]{1,0:T(8,128)(2,1)})) %all-reduce.3.cloned.1.call-update) | async-done | bytes 11010064 | tf_op jit(solution)/shard_map/psum | solution.py:303
  (217 shorter events, 251.9 us)
Async XLA Ops:
  7.2 27.1 %copy-start.45 = (s32[1,8]{1,0:T(1,128)S(1)}, s32[1,8]{1,0:T(1,128)}, u32[]{:S(2)}) copy-start(s32[1,8]{1,0:T(1,128)} %param.13) | copy-start | bytes 100
  7.2 27.3 %copy-start.4 = (bf16[1,256,2048]{2,1,0:T(8,128)(2,1)S(1)}, bf16[1,256,2048]{2,1,0:T(8,128)(2,1)}, u32[]{:S(2)}) copy-start(bf16[1,256,2048]{2,1,0:T(8,128)(2,1)} %param.12) | copy-start | bytes 3145732
  7.2 28.0 %all-gather.10.cloned.1.call-start = ((), (), s32[]{:S(2)}) async-start(), calls=%async_computation.4 | async-start | bytes 1179648 | tf_op jit(solution)/shard_map/all_gather | solution.py:183
  8.0 49.9 %all-gather.12.cloned.1.call-start = ((), (), s32[]{:S(2)}) async-start(), calls=%async_computation.5 | async-start | bytes 1179648 | tf_op jit(solution)/shard_map/all_gather | solution.py:182
  8.7 132.4 %all-gather.14.cloned.1.call-start = ((), (), s32[]{:S(2)}) async-start(), calls=%async_computation.6 | async-start | bytes 9437184 | tf_op jit(solution)/shard_map/all_gather | solution.py:181
  9.4 213.7 %all-gather.16.cloned.1.call-start = ((), (), s32[]{:S(2)}) async-start(), calls=%async_computation.7 | async-start | bytes 9437184 | tf_op jit(solution)/shard_map/all_gather | solution.py:184
  10.0 415.9 %all-gather.20.cloned.1.call-start = ((), (), s32[]{:S(2)}) async-start(), calls=%async_computation.9 | async-start | bytes 25952256 | tf_op jit(solution)/shard_map/all_gather | solution.py:213
  10.6 617.7 %all-gather.18.cloned.1.call-start = ((), (), s32[]{:S(2)}) async-start(), calls=%async_computation.8 | async-start | bytes 25952256 | tf_op jit(solution)/shard_map/all_gather | solution.py:212
  11.2 819.7 %all-gather.22.cloned.1.call-start = ((), (), s32[]{:S(2)}) async-start(), calls=%async_computation.10 | async-start | bytes 25952256 | tf_op jit(solution)/shard_map/all_gather | solution.py:214
  11.9 1093.9 %reduce-scatter.5.cloned.1.call-start = ((), (), s32[]{:S(2)}) async-start(), calls=%async_computation.11 | async-start | bytes 655360 | tf_op jit(solution)/shard_map/reduce_scatter | solution.py:258
  34.3 119.4 %copy-start.33 = (f32[8,1,256]{2,1,0:T(1,128)}, f32[8,1,256]{2,1,0:T(1,128)S(1)}, u32[]{:S(2)}) copy-start(f32[8,1,256]{2,1,0:T(1,128)S(1)} %convert_element_type.184) | copy-start | bytes 24580
  34.8 118.9 %copy-start.40 = (f32[256]{0:T(256)}, f32[256]{0:T(256)S(1)}, u32[]{:S(2)}) copy-start(f32[256]{0:T(256)S(1)} %add_rsqrt_fusion.1) | copy-start | bytes 3076
  35.0 124.7 %copy-start.27 = (f32[256,32]{0,1:T(8,128)}, f32[256,32]{0,1:T(8,128)S(1)}, u32[]{:S(2)}) copy-start(f32[256,32]{0,1:T(8,128)S(1)} %get-tuple-element.38) | copy-start | bytes 98308
  35.0 124.7 %copy-start.29 = (f32[256,32]{0,1:T(8,128)}, f32[256,32]{0,1:T(8,128)S(1)}, u32[]{:S(2)}) copy-start(f32[256,32]{0,1:T(8,128)S(1)} %get-tuple-element.39) | copy-start | bytes 98308
  47.5 134.9 %copy-start.22 = (bf16[1024,256]{0,1:T(8,128)(2,1)}, bf16[1024,256]{0,1:T(8,128)(2,1)S(1)}, u32[]{:S(2)}) copy-start(bf16[1024,256]{0,1:T(8,128)(2,1)S(1)} %copy.71) | copy-start | bytes 1572868
  74.2 93.9 %copy-start.20 = (bf16[1024,256]{0,1:T(8,128)(2,1)}, bf16[1024,256]{0,1:T(8,128)(2,1)S(1)}, u32[]{:S(2)}) copy-start(bf16[1024,256]{0,1:T(8,128)(2,1)S(1)} %all_gather.42) | copy-start | bytes 1572868
  229.3 639.7 %copy-start.6 = (f32[256,2048]{1,0:T(8,128)}, f32[256,2048]{1,0:T(8,128)S(1)}, u32[]{:S(2)}) copy-start(f32[256,2048]{1,0:T(8,128)S(1)} %get-tuple-element.49) | copy-start | bytes 6291460
  230.9 195.0 %copy-start.17 = (bf16[256,2048]{1,0:T(8,128)(2,1)}, bf16[256,2048]{1,0:T(8,128)(2,1)S(1)}, u32[]{:S(2)}) copy-start(bf16[256,2048]{1,0:T(8,128)(2,1)S(1)} %multiply_convert_fusion.3) | copy-start | bytes 3145732
  440.9 390.0 %copy-start.15 = (bf16[1,256,2048]{2,1,0:T(8,128)(2,1)S(1)}, bf16[1,256,2048]{2,1,0:T(8,128)(2,1)}, u32[]{:S(2)}) copy-start(bf16[1,256,2048]{2,1,0:T(8,128)(2,1)} %param.23) | copy-start | bytes 3145732
  979.5 127.3 %reduce-scatter.7.cloned.1.call-start = ((), (), s32[]{:S(2)}) async-start(), calls=%async_computation.12 | async-start | bytes 655360 | tf_op jit(solution)/shard_map/reduce_scatter | solution.py:264
  990.2 270.0 %reduce-scatter.11.cloned.1.call-start = ((), (), s32[]{:S(2)}) async-start(), calls=%async_computation.14 | async-start | bytes 25952256 | tf_op jit(solution)/shard_map/reduce_scatter | solution.py:228
  1003.0 878.4 %reduce-scatter.9.cloned.1.call-start = ((), (), s32[]{:S(2)}) async-start(), calls=%async_computation.13 | async-start | bytes 73138176 | tf_op jit(solution)/shard_map/reduce_scatter | solution.py:295
  1084.2 22.7 %copy-start.41 = (f32[256]{0:T(256)S(1)}, f32[256]{0:T(256)}, u32[]{:S(2)}) copy-start(f32[256]{0:T(256)} %copy-done.40) | copy-start | bytes 3076
  1158.0 941.7 %all-reduce.3.cloned.1.call-start = ((), (), s32[]{:S(2)}) async-start(), calls=%async_computation.15 | async-start | bytes 22020096 | tf_op jit(solution)/shard_map/psum | solution.py:303
  (40 other events, 399.3 us)
Sparse Core Ops, SparseCore 0:
  9.7 24.8 all-gather.9
  36.1 21.6 all-gather.11
  59.4 81.6 all-gather.13
  142.6 80.5 all-gather.15
  224.7 201.1 all-gather.19
  427.4 200.8 all-gather.17
  629.9 200.8 all-gather.21
  979.6 22.9 reduce-scatter.4
  1005.7 24.7 reduce-scatter.6
  1032.7 227.3 reduce-scatter.10
  1262.6 618.8 reduce-scatter.8
  1885.0 214.5 all-reduce.2
where the time goes:
time: 2130 us; the launch traced here: 2120 us
  waiting for transfers between devices  1570 us (74%)
  matrix products  340 us (16%)
  blocking collectives  85.7 us (4%)
  other arithmetic  72 us (3%)
  local copies, waits for them, and re-layouts  43.4 us (2%)
    reduce_scatter x1, waiting for transfers between devices, per_device(): lax.psum_scatter(stacked_term(sources, gradients).astype(jnp.bfloat16), '...  621 us
    all_gather x1, waiting for transfers between devices, per_device(): lax.all_gather(up_weight, 'fsdp', axis=0, tiled=True)  195 us
    all_gather x1, waiting for transfers between devices, per_device(): lax.all_gather(down_weight, 'fsdp', axis=0, tiled=True)  188 us
    all_gather x1, waiting for transfers between devices, per_device(): lax.all_gather(gate_weight, 'fsdp', axis=0, tiled=True)  187 us
    psum x1, waiting for transfers between devices, per_device(): lax.psum(row_piece, 'ctx').astype(jnp.float32)  153 us
    reduce_scatter x1, waiting for transfers between devices, per_device(): lax.psum_scatter(column_term(hidden, grad_out).astype(jnp.bfloat16), 'fsd...  102 us
    dot_general x7, matrix products, times_transposed(): lax.dot_general(left_side, right_side, (((1,), (1,)), ((), ())), preferre...  67.8 us
    all_gather x1, waiting for transfers between devices, per_device(): lax.all_gather(query_weight, 'fsdp', axis=0, tiled=True)  66.8 us
  transfers between devices with their start and end apart: 12, of which 9 were waited for; matrix products, arithmetic and copies ran while one was open for 14% of the time, Pallas kernels for 0%

commit v1 on v0

v1 whole, which is shorter than its diff:
```python
import math

import jax
import jax.numpy as jnp
from jax import lax
from jax.sharding import PartitionSpec as P

D = 2048
FF = 5632
HEADS = 32
KV_HEADS = 4
HEAD_DIM = 64
KV_WIDTH = 256


epsilon = 1e-05


def rotary_tables(positions):
    frequency = jnp.exp(
        -math.log(10000.0) * jnp.arange(HEAD_DIM // 2).astype(jnp.float32) * (2.0 / HEAD_DIM)
    )
    angles = positions.astype(jnp.float32)[:, None] * frequency[None, :]
    return (jnp.cos(angles), jnp.sin(angles))


def rotate(matrix, cosine_table, sine_table):
    half_dim = HEAD_DIM // 2
    first_half = matrix[..., :half_dim]
    second_half = matrix[..., half_dim:]
    cosine_wide = cosine_table[:, None, :]
    sine_wide = sine_table[:, None, :]
    return jnp.concatenate(
        [
            first_half * cosine_wide - second_half * sine_wide,
            second_half * cosine_wide + first_half * sine_wide,
        ],
        axis=-1,
    )


def unrotate(matrix, cosine_table, sine_table):
    half_dim = HEAD_DIM // 2
    first_half = matrix[..., :half_dim]
    second_half = matrix[..., half_dim:]
    cosine_wide = cosine_table[:, None, :]
    sine_wide = sine_table[:, None, :]
    return jnp.concatenate(
        [
            first_half * cosine_wide + second_half * sine_wide,
            second_half * cosine_wide - first_half * sine_wide,
        ],
        axis=-1,
    )


def norm_parts(values):
    inverse = lax.rsqrt(jnp.mean(values * values, axis=-1, keepdims=True) + epsilon)
    return (values * inverse, inverse)


def norm_back(gradient, normed, inverse):
    return inverse * (gradient - normed * jnp.mean(gradient * normed, axis=-1, keepdims=True))


def times_transposed(left_side, right_side):
    return lax.dot_general(
        left_side, right_side, (((1,), (1,)), ((), ())), preferred_element_type=jnp.float32
    )


def take_columns(matrix, outer, parts, index):
    rows, columns = matrix.shape
    pieces = matrix.reshape(rows, outer, parts, columns // (outer * parts))
    return lax.dynamic_index_in_dim(pieces, index, axis=2, keepdims=False).reshape(rows, -1)


def take_rows(matrix, parts, index):
    count = matrix.shape[0] // parts
    return lax.dynamic_slice_in_dim(matrix, index * count, count, axis=0)


def put_columns(gathered, outer):
    parts, rows, columns = gathered.shape
    return (
        gathered.reshape(parts, rows, outer, columns // outer)
        .transpose(1, 2, 0, 3)
        .reshape(rows, parts * columns)
    )


def masked_scores(head_queries, head_keys, allowed):
    scores = jnp.einsum(
        "qhd,kd->hqk", head_queries, head_keys, preferred_element_type=jnp.float32
    ) * (1.0 / math.sqrt(HEAD_DIM))
    return jnp.where(allowed[None], scores, -1e30)


def attend_forward(queries, keys, values, allowed):
    outputs = []
    log_totals = []
    group_size = queries.shape[1] // keys.shape[1]
    for group_index in range(keys.shape[1]):
        head_queries = queries[:, group_index * group_size : (group_index + 1) * group_size]
        scores = masked_scores(head_queries, keys[:, group_index], allowed)
        largest = jnp.max(scores, axis=-1, keepdims=True)
        exponent = jnp.exp(scores - largest)
        totals = jnp.sum(exponent, axis=-1, keepdims=True)
        weights = (exponent / totals).astype(jnp.bfloat16)
        outputs.append(
            jnp.einsum(
                "hqk,kd->qhd", weights, values[:, group_index], preferred_element_type=jnp.float32
            )
        )
        log_totals.append(largest + jnp.log(totals))
    return (jnp.concatenate(outputs, axis=1), log_totals)


def attend_backward(queries, keys, values, allowed, log_totals, grad_attended):
    query_parts = []
    key_parts = []
    value_parts = []
    group_size = queries.shape[1] // keys.shape[1]
    for group_index in range(keys.shape[1]):
        head_queries = queries[:, group_index * group_size : (group_index + 1) * group_size]
        head_grads = grad_attended[:, group_index * group_size : (group_index + 1) * group_size]
        head_keys = keys[:, group_index]
        head_values = values[:, group_index]
        scores = masked_scores(head_queries, head_keys, allowed)
        weights = jnp.exp(scores - log_totals[group_index])
        grad_probs = jnp.einsum(
            "qhd,kd->hqk", head_grads, head_values, preferred_element_type=jnp.float32
        )
        row_dots = jnp.sum(weights * grad_probs, axis=-1, keepdims=True)
        grad_scores = (weights * (grad_probs - row_dots) * (1.0 / math.sqrt(HEAD_DIM))).astype(
            jnp.bfloat16
        )
        value_parts.append(
            jnp.einsum(
                "hqk,qhd->kd",
                weights.astype(jnp.bfloat16),
                head_grads,
                preferred_element_type=jnp.float32,
            )
        )
        query_parts.append(
            jnp.einsum("hqk,kd->qhd", grad_scores, head_keys, preferred_element_type=jnp.float32)
        )
        key_parts.append(
            jnp.einsum("hqk,qhd->kd", grad_scores, head_queries, preferred_element_type=jnp.float32)
        )
    return (
        jnp.concatenate(query_parts, axis=1),
        jnp.stack(key_parts, axis=1),
        jnp.stack(value_parts, axis=1),
    )


def column_term(source, gradient):
    return lax.dot_general(
        source, gradient, (((0,), (0,)), ((), ())), preferred_element_type=jnp.float32
    )


def product(left_side, right_side):
    return jnp.dot(left_side, right_side, preferred_element_type=jnp.float32)


def gather_shards(array):
    return lax.all_gather(array, "fsdp", axis=0, tiled=True)


def gather_rows(array):
    return lax.all_gather(array, "ctx", axis=0, tiled=True)


def scatter_rows(array):
    return lax.psum_scatter(
        array.astype(jnp.bfloat16), "ctx", scatter_dimension=0, tiled=True
    ).astype(jnp.float32)


def scatter_shards(array):
    return lax.psum_scatter(
        array.astype(jnp.bfloat16), "fsdp", scatter_dimension=0, tiled=True
    )


def per_device(
    tokens,
    dealing,
    first_gain,
    query_weight,
    key_weight,
    value_weight,
    output_weight,
    second_gain,
    gate_weight,
    up_weight,
    down_weight,
    cotangent,
):
    shard_count = lax.axis_size("fsdp")
    part_count = lax.axis_size("ctx")
    ctx_index = lax.axis_index("ctx")
    shard_index = lax.axis_index("fsdp")
    row_count = tokens.shape[1]
    block_rows = row_count // 2
    seq_rows = row_count * part_count
    own_heads = HEADS // part_count
    dealt_heads = (D // shard_count // part_count) % HEAD_DIM == 0
    offsets = jnp.arange(block_rows, dtype=jnp.int32)
    positions = (dealing[0][:, None] * block_rows + offsets[None, :]).reshape(-1)
    allowed = positions[None, :] <= positions[:, None]
    cosine_table, sine_table = rotary_tables(positions)
    inputs = tokens[0].astype(jnp.float32)

    gain_first = gather_shards(first_gain).astype(jnp.float32)
    gain_second = gather_shards(second_gain).astype(jnp.float32)
    key_value = gather_shards(jnp.concatenate([key_weight, value_weight], axis=1))
    if dealt_heads:
        query_part = gather_shards(take_columns(query_weight, shard_count, part_count, ctx_index))
        output_part = gather_shards(take_rows(output_weight, part_count, ctx_index))
    else:
        query_part = gather_shards(take_columns(query_weight, 1, part_count, ctx_index))
        output_part = take_rows(gather_shards(output_weight), part_count, ctx_index)
    gate_part = gather_shards(take_columns(gate_weight, shard_count, part_count, ctx_index))
    up_part = gather_shards(take_columns(up_weight, shard_count, part_count, ctx_index))
    down_part = gather_shards(take_rows(down_weight, part_count, ctx_index))

    normed_first, inverse_first = norm_parts(inputs)
    first_input = (normed_first * gain_first).astype(jnp.bfloat16)
    first_all = gather_rows(first_input)
    grad_out_all = gather_rows(cotangent[0])
    query_rot = rotate(
        product(first_all, query_part).reshape(seq_rows, own_heads, HEAD_DIM),
        cosine_table,
        sine_table,
    ).astype(jnp.bfloat16)
    key_value_rows = product(first_all, key_value)
    key_rot = rotate(
        key_value_rows[:, :KV_WIDTH].reshape(seq_rows, KV_HEADS, HEAD_DIM), cosine_table, sine_table
    ).astype(jnp.bfloat16)
    value_rows = (
        key_value_rows[:, KV_WIDTH:].astype(jnp.bfloat16).reshape(seq_rows, KV_HEADS, HEAD_DIM)
    )
    if not dealt_heads:
        kv_heads = max(1, KV_HEADS // part_count)
        kv_first = ctx_index * KV_HEADS // part_count
        key_rot = lax.dynamic_slice_in_dim(key_rot, kv_first, kv_heads, 1)
        value_rows = lax.dynamic_slice_in_dim(value_rows, kv_first, kv_heads, 1)
    attended, log_totals = attend_forward(query_rot, key_rot, value_rows, allowed)
    attended = attended.reshape(seq_rows, own_heads * HEAD_DIM).astype(jnp.bfloat16)
    residual_mid = inputs + scatter_rows(product(attended, output_part))

    normed_second, inverse_second = norm_parts(residual_mid)
    second_input = (normed_second * gain_second).astype(jnp.bfloat16)
    second_all = gather_rows(second_input)
    gate_act = product(second_all, gate_part)
    upward = product(second_all, up_part)
    sigmoid_gate = jax.nn.sigmoid(gate_act)
    silu_gate = gate_act * sigmoid_gate
    hidden = (silu_gate * upward).astype(jnp.bfloat16)
    block_output = (residual_mid + scatter_rows(product(hidden, down_part))).astype(jnp.bfloat16)

    grad_hidden = times_transposed(grad_out_all, down_part)
    down_piece = scatter_shards(column_term(hidden, grad_out_all))
    grad_gate = (
        grad_hidden * upward * sigmoid_gate * (1.0 + gate_act * (1.0 - sigmoid_gate))
    ).astype(jnp.bfloat16)
    grad_up = (grad_hidden * silu_gate).astype(jnp.bfloat16)
    grad_second = scatter_rows(
        times_transposed(grad_gate, gate_part) + times_transposed(grad_up, up_part)
    )
    gate_piece = scatter_shards(column_term(second_all, grad_gate))
    up_piece = scatter_shards(column_term(second_all, grad_up))
    second_gain_part = jnp.sum(grad_second * normed_second, axis=0)
    grad_mid = cotangent[0].astype(jnp.float32) + norm_back(
        grad_second * gain_second, normed_second, inverse_second
    )

    branch_all = gather_rows(grad_mid.astype(jnp.bfloat16))
    grad_attended = times_transposed(branch_all, output_part).astype(jnp.bfloat16)
    grad_query_rot, key_terms, value_terms = attend_backward(
        query_rot,
        key_rot,
        value_rows,
        allowed,
        log_totals,
        grad_attended.reshape(seq_rows, own_heads, HEAD_DIM),
    )
    grad_query = (
        unrotate(grad_query_rot, cosine_table, sine_table)
        .reshape(seq_rows, own_heads * HEAD_DIM)
        .astype(jnp.bfloat16)
    )
    grad_key = unrotate(key_terms, cosine_table, sine_table).astype(jnp.bfloat16)
    grad_value = value_terms.astype(jnp.bfloat16)
    if not dealt_heads:
        empty = jnp.zeros((seq_rows, KV_HEADS, HEAD_DIM), jnp.bfloat16)
        grad_key = lax.dynamic_update_slice_in_dim(empty, grad_key, kv_first, 1)
        grad_value = lax.dynamic_update_slice_in_dim(empty, grad_value, kv_first, 1)
    grad_key_value = jnp.concatenate(
        [grad_key.reshape(seq_rows, KV_WIDTH), grad_value.reshape(seq_rows, KV_WIDTH)], axis=1
    )
    grad_first = scatter_rows(
        times_transposed(grad_query, query_part) + times_transposed(grad_key_value, key_value)
    )
    first_gain_part = jnp.sum(grad_first * normed_first, axis=0)
    grad_input = grad_mid + norm_back(grad_first * gain_first, normed_first, inverse_first)

    query_piece = scatter_shards(column_term(first_all, grad_query))
    key_value_piece = scatter_shards(column_term(first_all, grad_key_value))
    output_term = column_term(attended, branch_all)
    if dealt_heads:
        output_shard = gather_rows(scatter_shards(output_term))
    else:
        spread = jnp.zeros((D, D), jnp.float32)
        spread = lax.dynamic_update_slice_in_dim(
            spread, output_term, ctx_index * output_term.shape[0], 0
        )
        output_shard = lax.psum(scatter_shards(spread), "ctx")

    def gather_columns(piece, outer):
        return put_columns(lax.all_gather(piece, "ctx", axis=0), outer).astype(jnp.float32)

    key_value_shard = lax.psum(key_value_piece, "ctx").astype(jnp.float32)
    gain_totals = lax.psum(jnp.stack([first_gain_part, second_gain_part]), ("ctx", "fsdp"))
    gain_rows = D // shard_count
    gain_shard = lax.dynamic_slice_in_dim(gain_totals, shard_index * gain_rows, gain_rows, 1)
    return (
        block_output[None],
        grad_input.astype(jnp.bfloat16)[None],
        gain_shard[0],
        gather_columns(query_piece, shard_count if dealt_heads else 1),
        key_value_shard[:, :KV_WIDTH],
        key_value_shard[:, KV_WIDTH:],
        output_shard.astype(jnp.float32),
        gain_shard[1],
        gather_columns(gate_piece, shard_count),
        gather_columns(up_piece, shard_count),
        gather_rows(down_piece).astype(jnp.float32),
    )


def solution(mesh):
    in_specs = (
        P("fsdp", "ctx", None),
        P("fsdp", None),
        P("fsdp"),
        P("fsdp", None),
        P("fsdp", None),
        P("fsdp", None),
        P("fsdp", None),
        P("fsdp"),
        P("fsdp", None),
        P("fsdp", None),
        P("fsdp", None),
        P("fsdp", "ctx", None),
    )
    out_specs = (
        P("fsdp", "ctx", None),
        P("fsdp", "ctx", None),
        P("fsdp"),
        P("fsdp", None),
        P("fsdp", None),
        P("fsdp", None),
        P("fsdp", None),
        P("fsdp"),
        P("fsdp", None),
        P("fsdp", None),
        P("fsdp", None),
    )
    return jax.shard_map(
        per_device, mesh=mesh, in_specs=in_specs, out_specs=out_specs, check_vma=False
    )
```

time: 2130 us -> 1340 us (0.63)
  waiting for transfers between devices: 1570 us -> 793 us
  local copies, waits for them, and re-layouts: 43.4 us -> 89.5 us
  other arithmetic: 72 us -> 46 us
  matrix products: 340 us -> 317 us
    reduce_scatter x4 -> x10, waiting for transfers between devices: 723 us -> 282 us  [the longest x4 151 us: scatter_rows(): lax.psum_scatter(array.astype(jnp.bfloat16), 'ctx', scatter_dimension=0,...]
    all_gather x7 -> x15, waiting for transfers between devices: 685 us -> 468 us  [the longest x6 205 us: gather_rows(): return lax.all_gather(array, 'ctx', axis=0, tiled=True)]
    psum x1, waiting for transfers between devices: 153 us -> 40.8 us  [per_device(): key_value_shard = lax.psum(key_value_piece, 'ctx').astype(jnp.float32)]
    convert_element_type x1 -> x9, local copies, waits for them, and re-layouts: 1.47 us -> 43.9 us  [gather_columns(): put_columns(lax.all_gather(piece, 'ctx', axis=0), outer).astype(jnp.float32)]
    concatenate x1, other arithmetic: 44 us -> 1.84 us  [per_device(): jnp.concatenate([key_weight, value_weight], axis=1)]
    unnamed x106 -> x120, local copies, waits for them, and re-layouts: 1.98 us -> 33.8 us
    all_gather x4 -> x2, blocking collectives: 46.9 us -> 25 us  [gather_shards(): return lax.all_gather(array, 'fsdp', axis=0, tiled=True)]
    dot_general x7 -> x6, matrix products: 67.8 us -> 47.7 us  [times_transposed(): lax.dot_general(left_side, right_side, (((1,), (1,)), ((), ())), preferre...]
  transfers between devices with their start and end apart: 12 -> 26, of which waited for: 9 -> 23; matrix products, arithmetic and copies ran while one was open for 14% -> 29% of each run, Pallas kernels for 0% -> 0%
where the time goes in v1:
time: 1340 us; the launch traced here: 1330 us
  waiting for transfers between devices  793 us (59%)
  matrix products  317 us (24%)
  local copies, waits for them, and re-layouts  89.5 us (7%)
  blocking collectives  64.9 us (5%)
  other arithmetic  46 us (3%)
  between operations  15.4 us (1%)
    all_gather x6, waiting for transfers between devices, gather_rows(): return lax.all_gather(array, 'ctx', axis=0, tiled=True)  205 us
    all_gather x6, waiting for transfers between devices, gather_shards(): return lax.all_gather(array, 'fsdp', axis=0, tiled=True)  196 us
    reduce_scatter x4, waiting for transfers between devices, scatter_rows(): lax.psum_scatter(array.astype(jnp.bfloat16), 'ctx', scatter_dimension=0,...  151 us
    reduce_scatter x6, waiting for transfers between devices, scatter_shards(): lax.psum_scatter(array.astype(jnp.bfloat16), 'fsdp', scatter_dimension=0,...  131 us
    all_gather x3, waiting for transfers between devices, gather_columns(): lax.all_gather(piece, 'ctx', axis=0)  67.3 us
    dot_general x4, matrix products, attend_backward(): jnp.einsum('hqk,kd->qhd', grad_scores, head_keys, preferred_element_type=...  63.8 us
    dot_general x4, matrix products, attend_backward(): jnp.einsum('hqk,qhd->kd', grad_scores, head_queries, preferred_element_ty...  55.3 us
    dot_general x6, matrix products, product(): return jnp.dot(left_side, right_side, preferred_element_type=jnp.float32)  51.6 us
  transfers between devices with their start and end apart: 26, of which 23 were waited for; matrix products, arithmetic and copies ran while one was open for 29% of the time, Pallas kernels for 0%

profile of v1, /device:TPU:0, one launch (start us, length us, event | category | flops | bytes accessed | tf_op | source)
XLA Modules:
  0.0 1327.1 jit_solution(12939767906932782241)
XLA Ops:
  42.0 54.6 %all-gather.22.cloned.1.call-done = bf16[1024,2048]{1,0:T(8,128)(2,1)} async-done(((bf16[256,2048]{1,0:T(8,128)(2,1)}), bf16[1024,2048]{1,0:T(8,128)(2,1)}) %all-gather.22.cloned.1.call-update) | async-done | bytes 4194320 | tf_op jit(solution)/shard_map/all_gather | solution.py:174
  103.8 26.0 %all-gather.26.cloned.1.call-done = bf16[2048,512]{0,1:T(8,128)(2,1)} async-done(((bf16[256,512]{0,1:T(8,128)(2,1)}), bf16[2048,512]{0,1:T(8,128)(2,1)}) %all-gather.26.cloned.1.call-update) | async-done | bytes 2097168 | tf_op jit(solution)/shard_map/all_gather | solution.py:170
  186.1 33.5 %reduce-scatter.11.cloned.1.call-done = bf16[256,2048]{1,0:T(8,128)(2,1)} async-done(((bf16[1024,2048]{1,0:T(8,128)(2,1)}), bf16[256,2048]{1,0:T(8,128)(2,1)}) %reduce-scatter.11.cloned.1.call-update) | async-done | bytes 1048592 | tf_op jit(solution)/shard_map/reduce_scatter | solution.py:178
  233.0 49.6 %all-gather.34.cloned.1.call-done = bf16[2048,1408]{0,1:T(8,128)(2,1)} async-done(((bf16[256,1408]{0,1:T(8,128)(2,1)}), bf16[2048,1408]{0,1:T(8,128)(2,1)}) %all-gather.34.cloned.1.call-update) | async-done | bytes 5767184 | tf_op jit(solution)/shard_map/all_gather | solution.py:170
  282.6 53.5 %all-gather.30.cloned.1.call-done = bf16[1024,2048]{1,0:T(8,128)(2,1)} async-done(((bf16[256,2048]{1,0:T(8,128)(2,1)}), bf16[1024,2048]{1,0:T(8,128)(2,1)}) %all-gather.30.cloned.1.call-update) | async-done | bytes 4194320 | tf_op jit(solution)/shard_map/all_gather | solution.py:174
  347.8 51.4 %all-gather.32.cloned.1.call-done = bf16[2048,1408]{0,1:T(8,128)(2,1)} async-done(((bf16[256,1408]{0,1:T(8,128)(2,1)}), bf16[2048,1408]{0,1:T(8,128)(2,1)}) %all-gather.32.cloned.1.call-update) | async-done | bytes 5767184 | tf_op jit(solution)/shard_map/all_gather | solution.py:170
  410.9 41.2 %all-gather.44.cloned.1.call-done = bf16[1,1024,2048]{2,1,0:T(8,128)(2,1)} async-done(((bf16[1,256,2048]{2,1,0:T(8,128)(2,1)}), bf16[1,1024,2048]{2,1,0:T(8,128)(2,1)}) %all-gather.44.cloned.1.call-update) | async-done | bytes 4194320 | tf_op jit(solution)/shard_map/all_gather | solution.py:174
  452.1 62.6 %all-gather.36.cloned.1.call-done = bf16[1408,2048]{1,0:T(8,128)(2,1)} async-done(((bf16[176,2048]{1,0:T(8,128)(2,1)}), bf16[1408,2048]{1,0:T(8,128)(2,1)}) %all-gather.36.cloned.1.call-update) | async-done | bytes 5767184 | tf_op jit(solution)/shard_map/all_gather | solution.py:170
  514.7 16.0 %fusion.27 = (bf16[1024,1408]{1,0:T(8,128)(2,1)S(1)}, bf16[1024,1408]{1,0:T(8,128)(2,1)S(1)}, bf16[1024,1408]{1,0:T(8,128)(2,1)}) fusion(f32[1024,1408]{1,0:T(8,128)} %fusion.195, f32[1024,1408]{1,0:T(8,128)} %fusion.196, bf16[1408,2048]{1,0:T(8,128)(2,1)} %all-gather.36.cloned.1.call-done, bf16[1,1024,2048]{2,1,0:T(8,128)(2,1)} %all-gather.44.cloned.1.call-done), kind=kOutput, calls=%fused_computation.58 | convolution fusion | flops 5927206912 | bytes 30146560 | tf_op jit(solution)/shard_map/dot_general | solution.py:67
  548.8 51.5 %reduce-scatter.15.cloned.1.call-done = bf16[256,2048]{1,0:T(8,128)(2,1)} async-done(((bf16[1024,2048]{1,0:T(8,128)(2,1)}), bf16[256,2048]{1,0:T(8,128)(2,1)}) %reduce-scatter.15.cloned.1.call-update) | async-done | bytes 1048592 | tf_op jit(solution)/shard_map/reduce_scatter | solution.py:178
  643.3 16.2 %all-gather.38.cloned.1.call-done = bf16[1024,2048]{1,0:T(8,128)(2,1)} async-done(((bf16[256,2048]{1,0:T(8,128)(2,1)}), bf16[1024,2048]{1,0:T(8,128)(2,1)}) %all-gather.38.cloned.1.call-update) | async-done | bytes 4194320 | tf_op jit(solution)/shard_map/all_gather | solution.py:174
  792.7 16.3 %fusion.82 = f32[1024,2,64]{0,2,1:T(8,128)} fusion(f32[1024,1024,2]{1,0,2:T(8,128)} %fusion.146, f32[2,1024,1024]{1,2,0:T(8,128)} %copy-done.3, f32[2,1024]{1,0:T(2,128)S(1)} %log_add_fusion.3, bf16[1024,4,32]{0,2,1:T(8,128)(2,1)S(1)} %copy-done.17, bf16[1024,4,32]{0,2,1:T(8,128)(2,1)S(1)} %copy-done.19), kind=kOutput, calls=%fused_computation.134 | convolution fusion | flops 283380736 | bytes 34619392 | tf_op jit(solution)/shard_map/hqk,kd->qhd/dot_general | solution.py:147
  838.8 20.4 %reduce-scatter.29.cloned.1.call-done = bf16[176,2048]{1,0:T(8,128)(2,1)} async-done(((bf16[1408,2048]{1,0:T(8,128)(2,1)}), bf16[176,2048]{1,0:T(8,128)(2,1)}) %reduce-scatter.29.cloned.1.call-update) | async-done | bytes 720912 | tf_op jit(solution)/shard_map/reduce_scatter | solution.py:184
  859.3 36.8 %reduce-scatter.21.cloned.1.call-done = bf16[256,512]{1,0:T(8,128)(2,1)} async-done(((bf16[2048,512]{1,0:T(8,128)(2,1)}), bf16[256,512]{1,0:T(8,128)(2,1)}) %reduce-scatter.21.cloned.1.call-update) | async-done | bytes 262160 | tf_op jit(solution)/shard_map/reduce_scatter | solution.py:184
  896.2 37.1 %reduce-scatter.19.cloned.1.call-done = bf16[256,512]{1,0:T(8,128)(2,1)} async-done(((bf16[2048,512]{1,0:T(8,128)(2,1)}), bf16[256,512]{1,0:T(8,128)(2,1)}) %reduce-scatter.19.cloned.1.call-update) | async-done | bytes 262160 | tf_op jit(solution)/shard_map/reduce_scatter | solution.py:184
  933.4 36.4 %reduce-scatter.23.cloned.1.call-done = bf16[64,2048]{1,0:T(8,128)(2,1)} async-done(((bf16[512,2048]{1,0:T(8,128)(2,1)}), bf16[64,2048]{1,0:T(8,128)(2,1)}) %reduce-scatter.23.cloned.1.call-update) | async-done | bytes 262160 | tf_op jit(solution)/shard_map/reduce_scatter | solution.py:184
  989.8 22.4 %all-gather.50.cloned.1.call-done = bf16[1024,1408]{1,0:T(8,128)(2,1)} async-done(((bf16[256,1408]{1,0:T(8,128)(2,1)}), bf16[1024,1408]{1,0:T(8,128)(2,1)}) %all-gather.50.cloned.1.call-update) | async-done | bytes 2883600 | tf_op jit(solution)/shard_map/all_gather | solution.py:325
  1037.5 18.1 %all-gather.48.cloned.1.call-done = bf16[1024,1408]{1,0:T(8,128)(2,1)} async-done(((bf16[256,1408]{1,0:T(8,128)(2,1)}), bf16[1024,1408]{1,0:T(8,128)(2,1)}) %all-gather.48.cloned.1.call-update) | async-done | bytes 2883600 | tf_op jit(solution)/shard_map/all_gather | solution.py:325
  1081.1 18.3 %all-gather.42.cloned.1.call-done = bf16[704,2048]{1,0:T(8,128)(2,1)} async-done(((bf16[176,2048]{1,0:T(8,128)(2,1)}), bf16[704,2048]{1,0:T(8,128)(2,1)}) %all-gather.42.cloned.1.call-update) | async-done | bytes 2883600 | tf_op jit(solution)/shard_map/all_gather | solution.py:174
  1104.5 40.8 %all-reduce.2.cloned.1.call-done = bf16[256,512]{1,0:T(8,128)(2,1)} async-done(((bf16[256,512]{1,0:T(8,128)(2,1)}), bf16[256,512]{1,0:T(8,128)(2,1)}) %all-reduce.2.cloned.1.call-update) | async-done | bytes 262160 | tf_op jit(solution)/shard_map/psum | solution.py:327
  1147.0 26.9 %all-gather.46.cloned.1.call-done = bf16[1024,512]{1,0:T(8,128)(2,1)} async-done(((bf16[256,512]{1,0:T(8,128)(2,1)}), bf16[1024,512]{1,0:T(8,128)(2,1)}) %all-gather.46.cloned.1.call-update) | async-done | bytes 1048592 | tf_op jit(solution)/shard_map/all_gather | solution.py:325
  1181.2 21.2 %all-gather.40.cloned.1.call-done = bf16[256,2048]{1,0:T(8,128)(2,1)} async-done(((bf16[64,2048]{1,0:T(8,128)(2,1)}), bf16[256,2048]{1,0:T(8,128)(2,1)}) %all-gather.40.cloned.1.call-update) | async-done | bytes 1048592 | tf_op jit(solution)/shard_map/all_gather | solution.py:174
  1205.3 53.0 %reduce-scatter.17.cloned.1.call-done = bf16[256,2048]{1,0:T(8,128)(2,1)} async-done(((bf16[1024,2048]{1,0:T(8,128)(2,1)}), bf16[256,2048]{1,0:T(8,128)(2,1)}) %reduce-scatter.17.cloned.1.call-update) | async-done | bytes 1048592 | tf_op jit(solution)/shard_map/reduce_scatter | solution.py:178
  1260.8 39.9 %psum.14 = f32[2,2048]{1,0:T(2,128)S(1)} all-reduce(f32[2,2048]{1,0:T(2,128)S(1)} %pad_maximum_fusion.12), channel_id=1, replica_groups=mesh['ctx'=4,'fsdp'=8] {'ctx','fsdp'}, use_global_device_ids=true, to_apply=%region_22.23 | all-reduce | flops 4096 | bytes 32768 | tf_op jit(solution)/shard_map/psum | solution.py:328
  (282 shorter events, 468.3 us)
Async XLA Ops:
  27.9 101.8 %all-gather.26.cloned.1.call-start = ((), (), s32[]{:S(2)}) async-start(), calls=%async_computation.12 | async-start | bytes 2359296 | tf_op jit(solution)/shard_map/all_gather | solution.py:170
  31.9 129.3 %all-gather.28.cloned.1.call-start = ((), (), s32[]{:S(2)}) async-start(), calls=%async_computation.13 | async-start | bytes 2359296 | tf_op jit(solution)/shard_map/all_gather | solution.py:170
  33.7 186.0 %reduce-scatter.11.cloned.1.call-start = ((), (), s32[]{:S(2)}) async-start(), calls=%async_computation.14 | async-start | bytes 5242880 | tf_op jit(solution)/shard_map/reduce_scatter | solution.py:178
  167.7 114.8 %all-gather.34.cloned.1.call-start = ((), (), s32[]{:S(2)}) async-start(), calls=%async_computation.17 | async-start | bytes 6488064 | tf_op jit(solution)/shard_map/all_gather | solution.py:170
  174.4 161.6 %all-gather.30.cloned.1.call-start = ((), (), s32[]{:S(2)}) async-start(), calls=%async_computation.15 | async-start | bytes 5242880 | tf_op jit(solution)/shard_map/all_gather | solution.py:174
  224.5 174.7 %all-gather.32.cloned.1.call-start = ((), (), s32[]{:S(2)}) async-start(), calls=%async_computation.16 | async-start | bytes 6488064 | tf_op jit(solution)/shard_map/all_gather | solution.py:170
  231.2 220.9 %all-gather.44.cloned.1.call-start = ((), (), s32[]{:S(2)}) async-start(), calls=%async_computation.32 | async-start | bytes 5242880 | tf_op jit(solution)/shard_map/all_gather | solution.py:174
  231.9 282.8 %all-gather.36.cloned.1.call-start = ((), (), s32[]{:S(2)}) async-start(), calls=%async_computation.18 | async-start | bytes 6488064 | tf_op jit(solution)/shard_map/all_gather | solution.py:170
  233.0 367.3 %reduce-scatter.15.cloned.1.call-start = ((), (), s32[]{:S(2)}) async-start(), calls=%async_computation.20 | async-start | bytes 5242880 | tf_op jit(solution)/shard_map/reduce_scatter | solution.py:178
  548.7 110.8 %all-gather.38.cloned.1.call-start = ((), (), s32[]{:S(2)}) async-start(), calls=%async_computation.21 | async-start | bytes 5242880 | tf_op jit(solution)/shard_map/all_gather | solution.py:174
  606.6 230.9 %reduce-scatter.27.cloned.1.call-start = ((), (), s32[]{:S(2)}) async-start(), calls=%async_computation.29 | async-start | bytes 6488064 | tf_op jit(solution)/shard_map/reduce_scatter | solution.py:184
  617.7 220.6 %reduce-scatter.25.cloned.1.call-start = ((), (), s32[]{:S(2)}) async-start(), calls=%async_computation.28 | async-start | bytes 6488064 | tf_op jit(solution)/shard_map/reduce_scatter | solution.py:184
  630.7 228.5 %reduce-scatter.29.cloned.1.call-start = ((), (), s32[]{:S(2)}) async-start(), calls=%async_computation.30 | async-start | bytes 6488064 | tf_op jit(solution)/shard_map/reduce_scatter | solution.py:184
  643.2 252.9 %reduce-scatter.21.cloned.1.call-start = ((), (), s32[]{:S(2)}) async-start(), calls=%async_computation.24 | async-start | bytes 2359296 | tf_op jit(solution)/shard_map/reduce_scatter | solution.py:184
  760.6 172.7 %reduce-scatter.19.cloned.1.call-start = ((), (), s32[]{:S(2)}) async-start(), calls=%async_computation.23 | async-start | bytes 2359296 | tf_op jit(solution)/shard_map/reduce_scatter | solution.py:184
  831.5 138.3 %reduce-scatter.23.cloned.1.call-start = ((), (), s32[]{:S(2)}) async-start(), calls=%async_computation.26 | async-start | bytes 2359296 | tf_op jit(solution)/shard_map/reduce_scatter | solution.py:184
  837.5 174.7 %all-gather.50.cloned.1.call-start = ((), (), s32[]{:S(2)}) async-start(), calls=%async_computation.35 | async-start | bytes 3604480 | tf_op jit(solution)/shard_map/all_gather | solution.py:325
  838.2 217.4 %all-gather.48.cloned.1.call-start = ((), (), s32[]{:S(2)}) async-start(), calls=%async_computation.34 | async-start | bytes 3604480 | tf_op jit(solution)/shard_map/all_gather | solution.py:325
  838.8 260.5 %all-gather.42.cloned.1.call-start = ((), (), s32[]{:S(2)}) async-start(), calls=%async_computation.31 | async-start | bytes 3604480 | tf_op jit(solution)/shard_map/all_gather | solution.py:174
  859.3 286.0 %all-reduce.2.cloned.1.call-start = ((), (), s32[]{:S(2)}) async-start(), calls=%async_computation.25 | async-start | bytes 524288 | tf_op jit(solution)/shard_map/psum | solution.py:327
  896.2 277.7 %all-gather.46.cloned.1.call-start = ((), (), s32[]{:S(2)}) async-start(), calls=%async_computation.33 | async-start | bytes 1310720 | tf_op jit(solution)/shard_map/all_gather | solution.py:325
  933.3 269.1 %all-gather.40.cloned.1.call-start = ((), (), s32[]{:S(2)}) async-start(), calls=%async_computation.27 | async-start | bytes 1310720 | tf_op jit(solution)/shard_map/all_gather | solution.py:174
  969.8 288.6 %reduce-scatter.17.cloned.1.call-start = ((), (), s32[]{:S(2)}) async-start(), calls=%async_computation.22 | async-start | bytes 5242880 | tf_op jit(solution)/shard_map/reduce_scatter | solution.py:178
  978.5 335.8 %reduce-scatter.13.cloned.1.call-start = ((), (), s32[]{:S(2)}) async-start(), calls=%async_computation.19 | async-start | bytes 5242880 | tf_op jit(solution)/shard_map/reduce_scatter | solution.py:178
  (58 other events, 2588.4 us)
Sparse Core Ops, SparseCore 0:
  10.2 31.7 all-gather.23
  44.5 52.1 all-gather.21
  98.9 30.8 all-gather.25
  131.8 28.1 all-gather.27
  167.9 51.7 reduce-scatter.10
  221.7 60.8 all-gather.33
  285.2 50.8 all-gather.29
  338.3 60.8 all-gather.31
  401.2 50.8 all-gather.43
  454.3 60.4 all-gather.35
  548.9 51.3 reduce-scatter.14
  606.8 52.6 all-gather.37
  662.4 64.8 reduce-scatter.26
  730.0 63.2 reduce-scatter.24
  796.0 63.2 reduce-scatter.28
  862.0 34.1 reduce-scatter.20
  898.8 34.4 reduce-scatter.18
  935.5 34.2 reduce-scatter.22
  971.6 40.4 all-gather.49
  1013.8 41.7 all-gather.47
  1057.5 41.7 all-gather.41
  1102.3 42.9 all-reduce.1
  1205.6 52.6 reduce-scatter.16
  1261.2 53.0 reduce-scatter.12
  (2 shorter events, 53.1 us)

commit v2 on v1

v2 whole, which is shorter than its diff:
```python
import functools
import math

import jax
import jax.numpy as jnp
from jax import lax
from jax.experimental import pallas as pl
from jax.experimental.pallas import tpu as pltpu
from jax.sharding import PartitionSpec as P

D = 2048
FF = 5632
HEADS = 32
KV_HEADS = 4
HEAD_DIM = 64
KV_WIDTH = 256


epsilon = 1e-05


MESH = pl.DeviceIdType.MESH
VMEM = pl.BlockSpec(memory_space=pltpu.VMEM)
SMEM = pl.BlockSpec(memory_space=pltpu.SMEM)
HBM = pl.BlockSpec(memory_space=pl.ANY)
LANES = 128
PAIR = LANES // HEAD_DIM
QUERY_ROWS = 256


def shape(dims, kind=jnp.bfloat16):
    return jax.ShapeDtypeStruct(dims, kind)


def norm_parts(values):
    inverse = lax.rsqrt(jnp.mean(values * values, axis=-1, keepdims=True) + epsilon)
    return (values * inverse, inverse)


def norm_back(gradient, normed, inverse):
    return inverse * (gradient - normed * jnp.mean(gradient * normed, axis=-1, keepdims=True))


def product(left_side, right_side):
    return jnp.dot(left_side, right_side, preferred_element_type=jnp.float32)


def times_transposed(left_side, right_side):
    return lax.dot_general(
        left_side, right_side, (((1,), (1,)), ((), ())), preferred_element_type=jnp.float32
    )


def column_term(source, gradient):
    return lax.dot_general(
        source, gradient, (((0,), (0,)), ((), ())), preferred_element_type=jnp.float32
    )


def meet(count):
    me = lax.axis_index("ctx")
    barrier = pltpu.get_barrier_semaphore()
    for step in range(1, count):
        pl.semaphore_signal(
            barrier, inc=1, device_id={"ctx": lax.rem(me + step, count)}, device_id_type=MESH
        )
    pl.semaphore_wait(barrier, count - 1)


def send_rows(count, piece, source, target, sems):
    local_sem, send_sem, recv_sem = sems
    me = lax.axis_index("ctx")
    copies = []
    for step in range(1, count):
        copies.append(
            pltpu.make_async_remote_copy(
                src_ref=source,
                dst_ref=target,
                send_sem=send_sem.at[step - 1, piece],
                recv_sem=recv_sem.at[step - 1, piece],
                device_id={"ctx": lax.rem(me + step, count)},
                device_id_type=MESH,
            )
        )
    copies.append(pltpu.make_async_copy(source, target, local_sem.at[piece]))
    for copy in copies:
        copy.start()
    return copies


def send_sems(count, pieces):
    return [
        pltpu.SemaphoreType.DMA((pieces,)),
        pltpu.SemaphoreType.DMA((count - 1, pieces)),
        pltpu.SemaphoreType.DMA((count - 1, pieces)),
    ]


def scatter_products(count, pairs, send_buf, recv_buf, total, send_sem, recv_sem):
    me = lax.axis_index("ctx")
    rows, width = total.shape
    tile = 512

    def block(owner, store):
        start = pl.multiple_of(owner * rows, rows)

        def column(index, carry):
            columns = pl.ds(pl.multiple_of(index * tile, tile), tile)
            value = None
            for left, right, transposed in pairs:
                piece = left[pl.ds(start, rows), :]
                if transposed:
                    term = times_transposed(piece, right[columns, :])
                else:
                    term = product(piece, right[:, columns])
                value = term if value is None else value + term
            store(columns, value)
            return carry

        lax.fori_loop(0, width // tile, column, 0)

    copies = []
    for step in range(1, count):
        owner = lax.rem(me + step, count)

        def store_sent(columns, value, step=step):
            send_buf[step - 1, :, columns] = value.astype(send_buf.dtype)

        block(owner, store_sent)
        copy = pltpu.make_async_remote_copy(
            src_ref=send_buf.at[step - 1],
            dst_ref=recv_buf.at[step - 1],
            send_sem=send_sem.at[step - 1],
            recv_sem=recv_sem.at[step - 1],
            device_id={"ctx": owner},
            device_id_type=MESH,
        )
        copy.start()
        copies.append(copy)

    def store_own(columns, value):
        total[:, columns] = value

    block(me, store_own)
    return copies


def scatter_scratch(count, rows, width):
    return [
        pltpu.VMEM((count - 1, rows, width), jnp.bfloat16),
        pltpu.VMEM((count - 1, rows, width), jnp.bfloat16),
        pltpu.VMEM((rows, width), jnp.float32),
        pltpu.SemaphoreType.DMA((count - 1,)),
        pltpu.SemaphoreType.DMA((count - 1,)),
    ]


def received(count, recv_buf, total, rows):
    value = total[rows, :]
    for step in range(count - 1):
        value = value + recv_buf[step, rows, :].astype(jnp.float32)
    return value


STRIP = 32
PIECES = 2


def for_strips(first, rows, body):
    def strip(index, carry):
        body(pl.ds(pl.multiple_of(first + index * STRIP, STRIP), STRIP))
        return carry

    lax.fori_loop(0, rows // STRIP, strip, 0)


def call_plane(body, count, ident, outs, out_specs, in_specs, scratch, cost, megabytes, args):
    return pl.pallas_call(
        functools.partial(body, count),
        out_shape=outs,
        in_specs=in_specs,
        out_specs=out_specs,
        scratch_shapes=scratch,
        compiler_params=pltpu.CompilerParams(
            collective_id=ident, has_side_effects=True, vmem_limit_bytes=megabytes << 20
        ),
        cost_estimate=pl.CostEstimate(flops=cost, bytes_accessed=cost // 300, transcendentals=0),
    )(*args)


def start_body(
    count, tokens, gain, grad_out, first_all, grad_out_all, own, *sems
):
    me = lax.axis_index("ctx")
    rows = tokens.shape[0]
    size = rows // PIECES
    meet(count)
    copies = []
    for piece in range(PIECES):

        def strip(where):
            values = tokens[where, :].astype(jnp.float32)
            normed, _ = norm_parts(values)
            own[where, :] = (normed * gain[...]).astype(jnp.bfloat16)

        for_strips(piece * size, size, strip)
        place = pl.ds(pl.multiple_of(me * rows + piece * size, size), size)
        part = pl.ds(piece * size, size)
        copies += send_rows(count, piece, own.at[part], first_all.at[place], sems)
    for piece in range(PIECES):
        place = pl.ds(pl.multiple_of(me * rows + piece * size, size), size)
        part = pl.ds(piece * size, size)
        copies += send_rows(
            count, PIECES + piece, grad_out.at[part], grad_out_all.at[place], sems
        )
    for copy in copies:
        copy.wait()


def start_gather(count, ident, tokens, gain, grad_out):
    rows, width = tokens.shape
    gathered = shape((count * rows, width))
    return call_plane(
        start_body,
        count,
        ident,
        (gathered, gathered),
        (HBM, HBM),
        [VMEM] * 3,
        [pltpu.VMEM((rows, width), jnp.bfloat16)] + send_sems(count, 2 * PIECES),
        10**11 * 5,
        32,
        (tokens, gain, grad_out),
    )


def middle_body(
    count,
    attended,
    weight,
    tokens,
    gain,
    residual,
    second_all,
    own,
    send_buf,
    recv_buf,
    total,
    send_sem,
    recv_sem,
    *sems,
):
    me = lax.axis_index("ctx")
    rows = tokens.shape[0]
    size = rows // PIECES
    meet(count)
    copies = scatter_products(
        count, [(attended, weight, False)], send_buf, recv_buf, total, send_sem, recv_sem
    )
    for copy in copies:
        copy.wait()
    copies = []
    for piece in range(PIECES):

        def strip(where):
            values = tokens[where, :].astype(jnp.float32) + received(count, recv_buf, total, where)
            residual[where, :] = values
            normed, _ = norm_parts(values)
            own[where, :] = (normed * gain[...]).astype(jnp.bfloat16)

        for_strips(piece * size, size, strip)
        place = pl.ds(pl.multiple_of(me * rows + piece * size, size), size)
        copies += send_rows(
            count, piece, own.at[pl.ds(piece * size, size)], second_all.at[place], sems
        )
    for copy in copies:
        copy.wait()


def middle_gather(count, ident, attended, weight, tokens, gain):
    rows, width = tokens.shape
    return call_plane(
        middle_body,
        count,
        ident,
        (shape((rows, width), jnp.float32), shape((count * rows, width))),
        (VMEM, HBM),
        [VMEM] * 4,
        [pltpu.VMEM((rows, width), jnp.bfloat16)]
        + scatter_scratch(count, rows, width)
        + send_sems(count, PIECES),
        10**11,
        48,
        (attended, weight, tokens, gain),
    )


def output_body(
    count, hidden, weight, residual, output, send_buf, recv_buf, total, send_sem, recv_sem
):
    meet(count)
    copies = scatter_products(
        count, [(hidden, weight, False)], send_buf, recv_buf, total, send_sem, recv_sem
    )
    for copy in copies:
        copy.wait()

    def strip(where):
        values = residual[where, :] + received(count, recv_buf, total, where)
        output[where, :] = values.astype(jnp.bfloat16)

    for_strips(0, output.shape[0], strip)


def output_scatter(count, ident, hidden, weight, residual):
    rows, width = residual.shape
    return call_plane(
        output_body,
        count,
        ident,
        shape((rows, width)),
        VMEM,
        [VMEM] * 3,
        scatter_scratch(count, rows, width),
        10**11,
        48,
        (hidden, weight, residual),
    )


def middle_back_body(
    count,
    grad_gate,
    gate_weight,
    grad_up,
    up_weight,
    residual,
    gain,
    grad_out,
    grad_mid,
    gain_part,
    branch_all,
    own,
    send_buf,
    recv_buf,
    total,
    send_sem,
    recv_sem,
    *sems,
):
    me = lax.axis_index("ctx")
    rows = residual.shape[0]
    size = rows // PIECES
    meet(count)
    copies = scatter_products(
        count,
        [(grad_gate, gate_weight, True), (grad_up, up_weight, True)],
        send_buf,
        recv_buf,
        total,
        send_sem,
        recv_sem,
    )
    gain_part[...] = jnp.zeros_like(gain_part)
    for copy in copies:
        copy.wait()
    copies = []
    for piece in range(PIECES):

        def strip(where):
            gradient = received(count, recv_buf, total, where)
            normed, inverse = norm_parts(residual[where, :])
            gain_part[...] += jnp.sum(gradient * normed, axis=0, keepdims=True)
            values = grad_out[where, :].astype(jnp.float32) + norm_back(
                gradient * gain[...], normed, inverse
            )
            grad_mid[where, :] = values
            own[where, :] = values.astype(jnp.bfloat16)

        for_strips(piece * size, size, strip)
        place = pl.ds(pl.multiple_of(me * rows + piece * size, size), size)
        copies += send_rows(
            count, piece, own.at[pl.ds(piece * size, size)], branch_all.at[place], sems
        )
    for copy in copies:
        copy.wait()


def middle_back(
    count, ident, grad_gate, gate_weight, grad_up, up_weight, residual, gain, grad_out
):
    rows, width = residual.shape
    return call_plane(
        middle_back_body,
        count,
        ident,
        (
            shape((rows, width), jnp.float32),
            shape((1, width), jnp.float32),
            shape((count * rows, width)),
        ),
        (VMEM, VMEM, HBM),
        [VMEM] * 7,
        [pltpu.VMEM((rows, width), jnp.bfloat16)]
        + scatter_scratch(count, rows, width)
        + send_sems(count, PIECES),
        10**11,
        56,
        (grad_gate, gate_weight, grad_up, up_weight, residual, gain, grad_out),
    )


def input_back_body(
    count,
    grad_query,
    query_weight,
    grad_key_value,
    key_value_weight,
    tokens,
    gain,
    grad_mid,
    grad_input,
    gain_part,
    send_buf,
    recv_buf,
    total,
    send_sem,
    recv_sem,
):
    meet(count)
    copies = scatter_products(
        count,
        [(grad_query, query_weight, True), (grad_key_value, key_value_weight, True)],
        send_buf,
        recv_buf,
        total,
        send_sem,
        recv_sem,
    )
    gain_part[...] = jnp.zeros_like(gain_part)
    for copy in copies:
        copy.wait()

    def strip(where):
        gradient = received(count, recv_buf, total, where)
        normed, inverse = norm_parts(tokens[where, :].astype(jnp.float32))
        gain_part[...] += jnp.sum(gradient * normed, axis=0, keepdims=True)
        values = grad_mid[where, :] + norm_back(gradient * gain[...], normed, inverse)
        grad_input[where, :] = values.astype(jnp.bfloat16)

    for_strips(0, grad_input.shape[0], strip)


def input_back(
    count, ident, grad_query, query_weight, grad_key_value, key_value_weight, tokens, gain, grad_mid
):
    rows, width = tokens.shape
    return call_plane(
        input_back_body,
        count,
        ident,
        (shape((rows, width)), shape((1, width), jnp.float32)),
        (VMEM, VMEM),
        [VMEM] * 7,
        scatter_scratch(count, rows, width),
        10**11,
        48,
        (grad_query, query_weight, grad_key_value, key_value_weight, tokens, gain, grad_mid),
    )


def rotary_tables(length):
    frequency = jnp.exp(
        -math.log(10000.0) * jnp.arange(HEAD_DIM // 2).astype(jnp.float32) * (2.0 / HEAD_DIM)
    )
    angles = jnp.arange(length).astype(jnp.float32)[:, None] * frequency[None, :]
    cosine, sine = (jnp.cos(angles), jnp.sin(angles))
    return (
        jnp.concatenate([cosine] * (2 * PAIR), axis=1),
        jnp.concatenate([-sine, sine] * PAIR, axis=1),
    )


def low_lanes(dims, size):
    return lax.rem(lax.broadcasted_iota(jnp.int32, dims, len(dims) - 1), 2 * size) < size


def turn(values, cosine, sine):
    half = HEAD_DIM // 2
    swapped = jnp.where(
        low_lanes(values.shape, half),
        pltpu.roll(values, LANES - half, 1),
        pltpu.roll(values, half, 1),
    )
    return values * cosine + swapped * sine


def two_heads(values):
    low = low_lanes(values.shape, HEAD_DIM)
    zero = jnp.zeros_like(values)
    return jnp.concatenate([jnp.where(low, values, zero), jnp.where(low, zero, values)], axis=0)


def pick_heads(values):
    rows = values.shape[1] // PAIR
    return jnp.concatenate(
        [values[:HEAD_DIM, :rows], values[HEAD_DIM:, rows:]], axis=0
    )


def later_key(dims):
    key = lax.broadcasted_iota(jnp.int32, dims, 0)
    query = lax.rem(lax.broadcasted_iota(jnp.int32, dims, 1), QUERY_ROWS)
    return key > query


def block_rows_at(order, block, rows):
    return pl.ds(pl.multiple_of(order[block] * rows, rows), rows)


def rows_in_order(order, source, index, rows):
    per = QUERY_ROWS // rows
    return jnp.concatenate(
        [source[block_rows_at(order, index * per + i, rows), :] for i in range(per)], axis=0
    )


def attend_body(
    block_rows,
    order,
    first_all,
    query_weight,
    key_value_weight,
    cosine,
    sine,
    attended,
    queries,
    keys,
    values,
    log_totals,
    values_across,
):
    length, width = queries.shape
    kv_heads = keys.shape[0]
    pairs = width // LANES
    blocks = length // QUERY_ROWS

    def project(index, carry):
        place = pl.ds(pl.multiple_of(index * QUERY_ROWS, QUERY_ROWS), QUERY_ROWS)
        rows = rows_in_order(order, first_all, index, block_rows)
        cos_rows, sin_rows = (cosine[place, :], sine[place, :])
        projected = product(rows, query_weight[...])
        for pair in range(pairs):
            lanes = slice(pair * LANES, (pair + 1) * LANES)
            turned = turn(projected[:, lanes], cos_rows, sin_rows).astype(jnp.bfloat16)
            queries[place, lanes] = turned * jnp.asarray(1.0 / math.sqrt(HEAD_DIM), jnp.bfloat16)
        projected = product(rows, key_value_weight[...])
        for head in range(2 * kv_heads):
            tile = projected[:, head // PAIR * LANES : (head // PAIR + 1) * LANES]
            if head < kv_heads:
                tile = turn(tile, cos_rows, sin_rows)
            low = low_lanes(tile.shape, HEAD_DIM)
            moved = pltpu.roll(tile, HEAD_DIM, 1)
            both = jnp.where(low, tile, moved) if head % PAIR == 0 else jnp.where(low, moved, tile)
            if head < kv_heads:
                keys[head, place, :] = both.astype(jnp.bfloat16)
            else:
                values[head - kv_heads, place, :] = both.astype(jnp.bfloat16)
                values_across[head - kv_heads, :, place] = both.T.astype(jnp.bfloat16)
        return carry

    lax.fori_loop(0, blocks, project, 0)

    def attend(pair, carry):
        kv_head = pair // (pairs // kv_heads)
        lanes = pl.ds(pl.multiple_of(pair * LANES, LANES), LANES)
        for index in range(blocks):
            seen = (index + 1) * QUERY_ROWS
            rows = two_heads(queries[index * QUERY_ROWS : seen, lanes])
            scores = times_transposed(keys[kv_head, :seen, :], rows)
            own = scores[seen - QUERY_ROWS :]
            own = jnp.where(later_key(own.shape), -1e30, own)
            if index:
                scores = jnp.concatenate([scores[: seen - QUERY_ROWS], own], axis=0)
            else:
                scores = own
            largest = jnp.max(scores, axis=0, keepdims=True)
            exponent = jnp.exp(scores - largest)
            totals = jnp.sum(exponent, axis=0, keepdims=True)
            mixed = product(values_across[kv_head, :, :seen], exponent.astype(jnp.bfloat16))
            log_totals[pl.ds(pair * blocks + index, 1), :] = largest + jnp.log(totals)
            mixed = pick_heads(mixed / totals).T.astype(jnp.bfloat16)
            per = QUERY_ROWS // block_rows
            for i in range(per):
                attended[block_rows_at(order, index * per + i, block_rows), lanes] = mixed[
                    i * block_rows : (i + 1) * block_rows
                ]
        return carry

    lax.fori_loop(0, pairs, attend, 0)


def attend_forward(block_rows, kv_heads, order, first_all, query_weight, key_value_weight, tables):
    length, _ = first_all.shape
    width = query_weight.shape[1]
    blocks = length // QUERY_ROWS
    wide = shape((kv_heads, length, LANES))
    return pl.pallas_call(
        functools.partial(attend_body, block_rows),
        out_shape=(
            shape((length, width)),
            shape((length, width)),
            wide,
            wide,
            shape((width // LANES * blocks, PAIR * QUERY_ROWS), jnp.float32),
        ),
        in_specs=[SMEM] + [VMEM] * 5,
        out_specs=(VMEM,) * 5,
        scratch_shapes=[pltpu.VMEM((kv_heads, LANES, length), jnp.bfloat16)],
        compiler_params=pltpu.CompilerParams(vmem_limit_bytes=48 << 20),
        cost_estimate=pl.CostEstimate(
            flops=3 * 10**10, bytes_accessed=10**7, transcendentals=10**7
        ),
    )(order, first_all, query_weight, key_value_weight, *tables)


def attend_back_body(
    block_rows,
    order,
    branch_all,
    output_weight,
    queries,
    keys,
    values,
    attended,
    log_totals,
    cosine,
    sine,
    grad_query,
    grad_key_value,
    grads,
    row_dots,
    keys_across,
    key_sums,
    value_sums,
):
    length, width = queries.shape
    kv_heads = keys.shape[0]
    pairs = width // LANES
    blocks = length // QUERY_ROWS
    per = QUERY_ROWS // block_rows

    def project(index, carry):
        place = pl.ds(pl.multiple_of(index * QUERY_ROWS, QUERY_ROWS), QUERY_ROWS)
        rows = rows_in_order(order, branch_all, index, block_rows)
        low = times_transposed(rows, output_weight[...]).astype(jnp.bfloat16)
        grads[place, :] = low
        dots = low.astype(jnp.float32) * rows_in_order(order, attended, index, block_rows).astype(
            jnp.float32
        )
        for pair in range(pairs):
            across = dots[:, pair * LANES : (pair + 1) * LANES].T
            sums = [
                jnp.sum(across[i * HEAD_DIM : (i + 1) * HEAD_DIM], axis=0, keepdims=True)
                for i in range(PAIR)
            ]
            row_dots[pl.ds(pair * blocks + index, 1), :] = jnp.concatenate(sums, axis=1)
        for head in range(kv_heads):
            keys_across[head, :, place] = keys[head, place, :].T
        return carry

    lax.fori_loop(0, blocks, project, 0)

    group = pairs // kv_heads

    def attend(kv_head, carry):
        key_sums[kv_head] = jnp.zeros(key_sums.shape[1:], jnp.float32)
        value_sums[kv_head] = jnp.zeros(value_sums.shape[1:], jnp.float32)
        for member in range(group):
            pair = kv_head * group + member
            lanes = pl.ds(pl.multiple_of(pair * LANES, LANES), LANES)
            for index in range(blocks):
                seen = (index + 1) * QUERY_ROWS
                place = slice(index * QUERY_ROWS, seen)
                rows = two_heads(queries[place, lanes])
                grad_rows = two_heads(grads[place, lanes])
                row = pl.ds(pair * blocks + index, 1)
                scores = times_transposed(keys[kv_head, :seen, :], rows)
                weights = jnp.exp(scores - log_totals[row, :])
                own = weights[seen - QUERY_ROWS :]
                own = jnp.where(later_key(own.shape), 0.0, own)
                if index:
                    weights = jnp.concatenate([weights[: seen - QUERY_ROWS], own], axis=0)
                else:
                    weights = own
                grad_probs = times_transposed(values[kv_head, :seen, :], grad_rows)
                grad_scores = (weights * (grad_probs - row_dots[row, :])).astype(jnp.bfloat16)
                value_sums[kv_head, :seen, :] += product(weights.astype(jnp.bfloat16), grad_rows)
                key_sums[kv_head, :seen, :] += product(grad_scores, rows)
                turned = product(keys_across[kv_head, :, :seen], grad_scores)
                turned = pick_heads(turned).T * (1.0 / math.sqrt(HEAD_DIM))
                turned = turn(turned, cosine[place, :], -sine[place, :]).astype(jnp.bfloat16)
                for i in range(per):
                    grad_query[block_rows_at(order, index * per + i, block_rows), lanes] = turned[
                        i * block_rows : (i + 1) * block_rows
                    ]
        return carry

    lax.fori_loop(0, kv_heads, attend, 0)

    def finish(block, carry):
        place = pl.ds(pl.multiple_of(block * block_rows, block_rows), block_rows)
        target = block_rows_at(order, block, block_rows)

        def head_sum(head):
            if head < kv_heads:
                tile = key_sums[head, place, :]
            else:
                tile = value_sums[head - kv_heads, place, :]
            tile = tile + pltpu.roll(tile, HEAD_DIM, 1)
            if head < kv_heads:
                tile = turn(tile, cosine[place, :], -sine[place, :])
            return tile

        for tile in range(2 * kv_heads // PAIR):
            first, second = (head_sum(tile * PAIR), head_sum(tile * PAIR + 1))
            joined = jnp.where(low_lanes(first.shape, HEAD_DIM), first, second)
            grad_key_value[target, tile * LANES : (tile + 1) * LANES] = joined.astype(jnp.bfloat16)
        return carry

    lax.fori_loop(0, length // block_rows, finish, 0)


def attend_backward(
    block_rows, order, branch_all, output_weight, queries, keys, values, attended, log_totals, tables
):
    length, width = queries.shape
    kv_heads = keys.shape[0]
    return pl.pallas_call(
        functools.partial(attend_back_body, block_rows),
        out_shape=(shape((length, width)), shape((length, 2 * kv_heads * HEAD_DIM))),
        in_specs=[SMEM] + [VMEM] * 9,
        out_specs=(VMEM, VMEM),
        scratch_shapes=[
            pltpu.VMEM((length, width), jnp.bfloat16),
            pltpu.VMEM(log_totals.shape, jnp.float32),
            pltpu.VMEM((kv_heads, LANES, length), jnp.bfloat16),
            pltpu.VMEM((kv_heads, length, LANES), jnp.float32),
            pltpu.VMEM((kv_heads, length, LANES), jnp.float32),
        ],
        compiler_params=pltpu.CompilerParams(vmem_limit_bytes=56 << 20),
        cost_estimate=pl.CostEstimate(
            flops=6 * 10**10, bytes_accessed=10**7, transcendentals=10**7
        ),
    )(
        order,
        branch_all,
        output_weight,
        queries,
        keys,
        values,
        attended,
        log_totals,
        *tables,
    )


def take_columns(matrix, outer, parts, index):
    rows, columns = matrix.shape
    pieces = matrix.reshape(rows, outer, parts, columns // (outer * parts))
    return lax.dynamic_index_in_dim(pieces, index, axis=2, keepdims=False).reshape(rows, -1)


def take_rows(matrix, parts, index):
    count = matrix.shape[0] // parts
    return lax.dynamic_slice_in_dim(matrix, index * count, count, axis=0)


def put_columns(gathered, outer):
    parts, rows, columns = gathered.shape
    return (
        gathered.reshape(parts, rows, outer, columns // outer)
        .transpose(1, 2, 0, 3)
        .reshape(rows, parts * columns)
    )


def gather_shards(array):
    return lax.all_gather(array, "fsdp", axis=0, tiled=True)


def scatter_shards(array):
    return lax.psum_scatter(
        array.astype(jnp.bfloat16), "fsdp", scatter_dimension=0, tiled=True
    )


def per_device(
    tokens,
    dealing,
    first_gain,
    query_weight,
    key_weight,
    value_weight,
    output_weight,
    second_gain,
    gate_weight,
    up_weight,
    down_weight,
    cotangent,
):
    shard_count = lax.axis_size("fsdp")
    part_count = lax.axis_size("ctx")
    ctx_index = lax.axis_index("ctx")
    shard_index = lax.axis_index("fsdp")
    row_count = tokens.shape[1]
    block_rows = row_count // 2
    seq_rows = row_count * part_count
    own_heads = HEADS // part_count
    dealt_heads = (D // shard_count // part_count) % HEAD_DIM == 0
    kv_heads = KV_HEADS if dealt_heads else max(1, KV_HEADS // part_count)
    kv_first = 0 if dealt_heads else ctx_index * KV_HEADS // part_count
    blocks = jnp.arange(2 * part_count, dtype=jnp.int32)
    order = jnp.sum(
        jnp.where(dealing[0][None, :] == blocks[:, None], blocks[None, :], 0), axis=1
    ).astype(jnp.int32)
    tables = rotary_tables(seq_rows)

    gains = gather_shards(jnp.stack([first_gain, second_gain], axis=1)).astype(jnp.float32)
    gain_first, gain_second = (gains[:, 0][None], gains[:, 1][None])
    key_value = jnp.concatenate([key_weight, value_weight], axis=1)
    if dealt_heads:
        query_part = gather_shards(
            jnp.concatenate(
                [take_columns(query_weight, shard_count, part_count, ctx_index), key_value], axis=1
            )
        )
        query_part, key_value = (query_part[:, : D // part_count], query_part[:, D // part_count :])
        output_part = gather_shards(take_rows(output_weight, part_count, ctx_index))
    else:
        query_part = gather_shards(take_columns(query_weight, 1, part_count, ctx_index))
        output_part = take_rows(gather_shards(output_weight), part_count, ctx_index)
        key_value = gather_shards(key_value).reshape(D, 2, KV_HEADS, HEAD_DIM)
        key_value = lax.dynamic_slice_in_dim(key_value, kv_first, kv_heads, 2).reshape(D, -1)
    gate_part = gather_shards(take_columns(gate_weight, shard_count, part_count, ctx_index))
    up_part = gather_shards(take_columns(up_weight, shard_count, part_count, ctx_index))
    down_part = gather_shards(take_rows(down_weight, part_count, ctx_index))

    first_all, grad_out_all = start_gather(part_count, 1, tokens[0], gain_first, cotangent[0])
    attended, query_rot, key_rot, value_rows, log_totals = attend_forward(
        block_rows, kv_heads, order, first_all, query_part, key_value, tables
    )
    residual_mid, second_all = middle_gather(
        part_count, 2, attended, output_part, tokens[0], gain_second
    )

    gate_act = product(second_all, gate_part)
    upward = product(second_all, up_part)
    sigmoid_gate = jax.nn.sigmoid(gate_act)
    silu_gate = gate_act * sigmoid_gate
    hidden = (silu_gate * upward).astype(jnp.bfloat16)
    grad_hidden = times_transposed(grad_out_all, down_part)
    down_piece = scatter_shards(column_term(hidden, grad_out_all))
    grad_gate = (
        grad_hidden * upward * sigmoid_gate * (1.0 + gate_act * (1.0 - sigmoid_gate))
    ).astype(jnp.bfloat16)
    grad_up = (grad_hidden * silu_gate).astype(jnp.bfloat16)
    grad_mid, second_gain_part, branch_all = middle_back(
        part_count, 3, grad_gate, gate_part, grad_up, up_part, residual_mid, gain_second, cotangent[0]
    )
    gate_piece = scatter_shards(column_term(second_all, grad_gate))
    up_piece = scatter_shards(column_term(second_all, grad_up))
    block_output = output_scatter(part_count, 4, hidden, down_part, residual_mid)

    grad_query, grad_key_value = attend_backward(
        block_rows,
        order,
        branch_all,
        output_part,
        query_rot,
        key_rot,
        value_rows,
        attended,
        log_totals,
        tables,
    )
    grad_input, first_gain_part = input_back(
        part_count,
        5,
        grad_query,
        query_part,
        grad_key_value,
        key_value,
        tokens[0],
        gain_first,
        grad_mid,
    )

    query_piece = scatter_shards(column_term(first_all, grad_query))
    key_value_piece = scatter_shards(column_term(first_all, grad_key_value))
    output_term = column_term(attended, branch_all)

    def gather_columns(piece, outer):
        return put_columns(lax.all_gather(piece, "ctx", axis=0), outer).astype(jnp.float32)

    if dealt_heads:
        output_shard = lax.all_gather(scatter_shards(output_term), "ctx", axis=0, tiled=True)
        key_value_shard = lax.psum(key_value_piece, "ctx").astype(jnp.float32)
    else:
        spread = jnp.zeros((D, D), jnp.float32)
        spread = lax.dynamic_update_slice_in_dim(
            spread, output_term, ctx_index * output_term.shape[0], 0
        )
        output_shard = lax.psum(scatter_shards(spread), "ctx")
        wide = jnp.zeros((D // shard_count, 2, KV_HEADS, HEAD_DIM), jnp.bfloat16)
        wide = lax.dynamic_update_slice_in_dim(
            wide, key_value_piece.reshape(-1, 2, kv_heads, HEAD_DIM), kv_first, 2
        )
        key_value_shard = lax.psum(wide.reshape(-1, 2 * KV_WIDTH), "ctx").astype(jnp.float32)
    gain_totals = lax.psum(
        jnp.concatenate([first_gain_part, second_gain_part], axis=0), ("ctx", "fsdp")
    )
    gain_rows = D // shard_count
    gain_shard = lax.dynamic_slice_in_dim(gain_totals, shard_index * gain_rows, gain_rows, 1)
    return (
        block_output[None],
        grad_input[None],
        gain_shard[0],
        gather_columns(query_piece, shard_count if dealt_heads else 1),
        key_value_shard[:, :KV_WIDTH],
        key_value_shard[:, KV_WIDTH:],
        output_shard.astype(jnp.float32),
        gain_shard[1],
        gather_columns(gate_piece, shard_count),
        gather_columns(up_piece, shard_count),
        lax.all_gather(down_piece, "ctx", axis=0, tiled=True).astype(jnp.float32),
    )


def solution(mesh):
    in_specs = (
        P("fsdp", "ctx", None),
        P("fsdp", None),
        P("fsdp"),
        P("fsdp", None),
        P("fsdp", None),
        P("fsdp", None),
        P("fsdp", None),
        P("fsdp"),
        P("fsdp", None),
        P("fsdp", None),
        P("fsdp", None),
        P("fsdp", "ctx", None),
    )
    out_specs = (
        P("fsdp", "ctx", None),
        P("fsdp", "ctx", None),
        P("fsdp"),
        P("fsdp", None),
        P("fsdp", None),
        P("fsdp", None),
        P("fsdp", None),
        P("fsdp"),
        P("fsdp", None),
        P("fsdp", None),
        P("fsdp", None),
    )
    return jax.shard_map(
        per_device, mesh=mesh, in_specs=in_specs, out_specs=out_specs, check_vma=False
    )
```

time: 1340 us -> 1050 us (0.78)
  waiting for transfers between devices: 793 us -> 300 us
  Pallas kernels: 0 us -> 460 us
  matrix products: 317 us -> 90.2 us
  other arithmetic: 46 us -> 14.1 us
  local copies, waits for them, and re-layouts: 89.5 us -> 107 us
    pallas_call x0 -> x7, Pallas kernels: none -> 460 us  [the longest x5 413 us: call_plane(): pl.pallas_call(functools.partial(body, count), out_shape=outs, in_specs=i...]
    all_gather x6 -> x5, waiting for transfers between devices: 196 us -> 0.03 us  [gather_shards(): return lax.all_gather(array, 'fsdp', axis=0, tiled=True)]
    dot_general x24 -> x0, matrix products: 171 us -> none  [the longest x4 63.8 us: attend_backward(): jnp.einsum('hqk,kd->qhd', grad_scores, head_keys, preferred_element_type=...]
    all_gather x6 -> x2, waiting for transfers between devices: 205 us -> 35.8 us  [the longest x1 18.3 us: per_device(): lax.all_gather(down_piece, 'ctx', axis=0, tiled=True).astype(jnp.float32)]
    reduce_scatter x4 -> x0, waiting for transfers between devices: 151 us -> none  [scatter_rows(): lax.psum_scatter(array.astype(jnp.bfloat16), 'ctx', scatter_dimension=0,...]
    reduce_scatter x6, waiting for transfers between devices: 131 us -> 204 us  [scatter_shards(): lax.psum_scatter(array.astype(jnp.bfloat16), 'fsdp', scatter_dimension=0,...]
    psum x1, waiting for transfers between devices: 40.8 us -> 0.01 us  [per_device(): key_value_shard = lax.psum(key_value_piece, 'ctx').astype(jnp.float32)]
    dot_general x6 -> x1, matrix products: 47.7 us -> 17.1 us  [times_transposed(): lax.dot_general(left_side, right_side, (((1,), (1,)), ((), ())), preferre...]
  transfers between devices with their start and end apart: 26 -> 17, of which waited for: 23 -> 9; matrix products, arithmetic and copies ran while one was open for 29% -> 15% of each run, Pallas kernels for 0% -> 31%
where the time goes in v2:
time: 1050 us; the launch traced here: 1040 us
  Pallas kernels  460 us (44%)
  waiting for transfers between devices  300 us (29%)
  local copies, waits for them, and re-layouts  107 us (10%)
  matrix products  90.2 us (9%)
  blocking collectives  55.2 us (5%)
  between operations  14.6 us (1%)
  other arithmetic  14.1 us (1%)
    pallas_call x5, Pallas kernels, call_plane(): pl.pallas_call(functools.partial(body, count), out_shape=outs, in_specs=i...  413 us
    reduce_scatter x6, waiting for transfers between devices, scatter_shards(): lax.psum_scatter(array.astype(jnp.bfloat16), 'fsdp', scatter_dimension=0,...  204 us
    all_gather x3, waiting for transfers between devices, gather_columns(): lax.all_gather(piece, 'ctx', axis=0)  59.1 us
    dot_general x6, matrix products, column_term(): lax.dot_general(source, gradient, (((0,), (0,)), ((), ())), preferred_ele...  49.8 us
    unnamed x80, local copies, waits for them, and re-layouts  45.1 us
    convert_element_type x9, local copies, waits for them, and re-layouts, gather_columns(): put_columns(lax.all_gather(piece, 'ctx', axis=0), outer).astype(jnp.float32)  43.9 us
    psum x1, blocking collectives, per_device(): lax.psum(jnp.concatenate([first_gain_part, second_gain_part], axis=0), ('...  41.4 us
    pallas_call x1, Pallas kernels, attend_backward(): pl.pallas_call(functools.partial(attend_back_body, block_rows), out_shape...  26.9 us
  transfers between devices with their start and end apart: 17, of which 9 were waited for; matrix products, arithmetic and copies ran while one was open for 15% of the time, Pallas kernels for 31%

profile of v2, /device:TPU:0, one launch (start us, length us, event | category | flops | bytes accessed | tf_op | source)
XLA Modules:
  0.0 1041.6 jit_solution(17934113780086439465)
XLA Ops:
  32.1 13.8 %all_gather.42 = bf16[2048,2]{0,1:T(2,128)(2,1)S(1)} all-gather(bf16[256,2]{0,1:T(2,128)(2,1)S(1)} %pad_maximum_fusion.4), channel_id=1, replica_groups=mesh['ctx'=4,'fsdp'=8] {'fsdp'}, dimensions={0}, use_global_device_ids=true | all-gather | bytes 9216 | tf_op jit(solution)/shard_map/all_gather | solution.py:789
  51.6 94.7 %shard_map.203 = (bf16[1024,2048]{1,0:T(8,128)(2,1)S(1)}, bf16[1024,2048]{1,0:T(8,128)(2,1)S(1)}) custom-call(bf16[256,2048]{1,0:T(8,128)(2,1)S(1)} %bitcast.51, f32[1,2048]{1,0:T(1,128)S(1)} %get-tuple-element.86.gain, bf16[256,2048]{1,0:T(8,128)(2,1)S(1)} %bitcast.50), custom_call_target="tpu_custom_call" | custom-call | flops 499999997952 | bytes 1666666624 | tf_op jit(solution)/shard_map/pallas_call | solution.py:178
  155.6 20.1 %shard_map.204 = (bf16[1024,512]{1,0:T(8,128)(2,1)S(1)}, bf16[1024,512]{1,0:T(8,128)(2,1)S(1)}, bf16[4,1024,128]{2,1,0:T(8,128)(2,1)S(1)}, bf16[4,1024,128]{2,1,0:T(8,128)(2,1)S(1)}, f32[16,512]{1,0:T(8,128)S(1)}) custom-call(s32[8]{0:T(128)S(1)} %select_reduce_fusion.order, bf16[1024,2048]{1,0:T(8,128)(2,1)} %copy-done.17, ...), custom_call_target="tpu_custom_call" | custom-call | flops 30000001024 | bytes 10000000 | tf_op jit(solution)/shard_map/pallas_call | solution.py:608
  179.3 99.3 %shard_map.205 = (f32[256,2048]{1,0:T(8,128)S(1)}, bf16[1024,2048]{1,0:T(8,128)(2,1)}) custom-call(bf16[1024,512]{1,0:T(8,128)(2,1)S(1)} %get-tuple-element.28.attended, bf16[512,2048]{1,0:T(8,128)(2,1)} %all-gather.16.cloned.1.call-done.weight.output_weight, bf16[256,2048]{1,0:T(8,128)(2,1)S(1)} %bitcast.52, f32[1,2048]{1,0:T(1,128)S(1)} %get-tuple-element.85.gain), custom_call_target="tpu_custom_call" | custom-call | flops 99999997952 | bytes 333333344 | tf_op jit(solution)/shard_map/pallas_call | solution.py:178
  279.9 11.7 %fusion.5 = f32[1024,1408]{1,0:T(8,128)} fusion(bf16[1024,2048]{1,0:T(8,128)(2,1)} %get-tuple-element.29, bf16[2048,1408]{1,0:T(8,128)(2,1)} %all-gather.18.cloned.1.call-done.gate_weight), kind=kOutput, calls=%fused_computation.34 | convolution fusion | flops 5905580032 | bytes 15728640 | tf_op jit(solution)/shard_map/dot_general | solution.py:45
  291.5 11.7 %fusion.6 = f32[1024,1408]{1,0:T(8,128)} fusion(bf16[1024,2048]{1,0:T(8,128)(2,1)} %get-tuple-element.29, bf16[2048,1408]{1,0:T(8,128)(2,1)} %all-gather.20.cloned.1.call-done.up_weight), kind=kOutput, calls=%fused_computation.35 | convolution fusion | flops 5905580032 | bytes 15728640 | tf_op jit(solution)/shard_map/dot_general | solution.py:45
  303.2 17.1 %multiply_convert_fusion = (bf16[1024,1408]{1,0:T(8,128)(2,1)}, bf16[1024,1408]{1,0:T(8,128)(2,1)}, bf16[1024,1408]{1,0:T(8,128)(2,1)}) fusion(f32[1024,1408]{1,0:T(8,128)} %fusion.5, f32[1024,1408]{1,0:T(8,128)} %fusion.6, bf16[1024,2048]{1,0:T(8,128)(2,1)} %copy-done.19, bf16[1408,2048]{1,0:T(8,128)(2,1)} %all-gather.22.cloned.1.call-done.weight), kind=kOutput, calls=%fused_computation.3 | convolution fusion | flops 5927206912 | bytes 30146560 | tf_op jit(solution)/shard_map/dot_general | solution.py:49
  320.3 111.6 %shard_map.207 = (f32[256,2048]{1,0:T(8,128)}, f32[1,2048]{1,0:T(1,128)}, bf16[1024,2048]{1,0:T(8,128)(2,1)}) custom-call(bf16[1024,1408]{1,0:T(8,128)(2,1)} %get-tuple-element.77.grad_gate, bf16[2048,1408]{1,0:T(8,128)(2,1)} %all-gather.18.cloned.1.call-done.gate_weight, bf16[1024,1408]{1,0:T(8,128)(2,1)} %get-tuple-element.76.grad_up, ...), custom_call_target="tpu_custom_call" | custom-call | flops 99999997952 | bytes 333333344 | tf_op jit(solution)/shard_map/pallas_call | solution.py:178
  431.9 26.9 %shard_map.208 = (bf16[1024,512]{1,0:T(8,128)(2,1)}, bf16[1024,512]{1,0:T(8,128)(2,1)}) custom-call(s32[8]{0:T(128)} %copy-done.14, bf16[1024,2048]{1,0:T(8,128)(2,1)} %get-tuple-element.32.branch_all, bf16[512,2048]{1,0:T(8,128)(2,1)} %all-gather.16.cloned.1.call-done.weight.output_weight, bf16[1024,512]{1,0:T(8,128)(2,1)} %copy-done.23, ...), custom_call_target="tpu_custom_call" | custom-call | flops 60000002048 | bytes 10000000 | tf_op jit(solution)/shard_map/pallas_call | solution.py:739
  476.1 11.0 %convolution_convert_fusion.2 = bf16[2048,1408]{1,0:T(8,128)(2,1)} fusion(bf16[1024,2048]{1,0:T(8,128)(2,1)} %get-tuple-element.29, bf16[1024,1408]{1,0:T(8,128)(2,1)} %get-tuple-element.77.grad_gate), kind=kOutput, calls=%fused_computation.2 | convolution fusion | flops 5908463616 | bytes 12845056 | tf_op jit(solution)/shard_map/dot_general | solution.py:55
  487.3 11.3 %convolution_convert_fusion.1 = bf16[2048,1408]{1,0:T(8,128)(2,1)} fusion(bf16[1024,2048]{1,0:T(8,128)(2,1)} %get-tuple-element.29, bf16[1024,1408]{1,0:T(8,128)(2,1)} %get-tuple-element.76.grad_up), kind=kOutput, calls=%fused_computation.1 | convolution fusion | flops 5908463616 | bytes 12845056 | tf_op jit(solution)/shard_map/dot_general | solution.py:55
  498.6 10.4 %convolution_convert_fusion = bf16[1408,2048]{1,0:T(8,128)(2,1)} fusion(bf16[1024,1408]{1,0:T(8,128)(2,1)} %get-tuple-element.78.hidden, bf16[1024,2048]{1,0:T(8,128)(2,1)} %copy-done.19), kind=kOutput, calls=%fused_computation | convolution fusion | flops 5908463616 | bytes 12845056 | tf_op jit(solution)/shard_map/dot_general | solution.py:55
  509.7 24.1 %reduce-scatter.7.cloned.1.call-done = bf16[256,512]{1,0:T(8,128)(2,1)} async-done(((bf16[2048,512]{1,0:T(8,128)(2,1)}), bf16[256,512]{1,0:T(8,128)(2,1)}) %reduce-scatter.7.cloned.1.call-update) | async-done | bytes 262160 | tf_op jit(solution)/shard_map/reduce_scatter | solution.py:793
  533.8 36.7 %reduce-scatter.11.cloned.1.call-done = bf16[64,2048]{1,0:T(8,128)(2,1)} async-done(((bf16[512,2048]{1,0:T(8,128)(2,1)}), bf16[64,2048]{1,0:T(8,128)(2,1)}) %reduce-scatter.11.cloned.1.call-update) | async-done | bytes 262160 | tf_op jit(solution)/shard_map/reduce_scatter | solution.py:793
  570.6 66.4 %reduce-scatter.13.cloned.1.call-done = bf16[256,1408]{1,0:T(8,128)(2,1)} async-done(((bf16[2048,1408]{1,0:T(8,128)(2,1)}), bf16[256,1408]{1,0:T(8,128)(2,1)}) %reduce-scatter.13.cloned.1.call-update) | async-done | bytes 720912 | tf_op jit(solution)/shard_map/reduce_scatter | solution.py:793
  637.0 65.9 %reduce-scatter.15.cloned.1.call-done = bf16[256,1408]{1,0:T(8,128)(2,1)} async-done(((bf16[2048,1408]{1,0:T(8,128)(2,1)}), bf16[256,1408]{1,0:T(8,128)(2,1)}) %reduce-scatter.15.cloned.1.call-update) | async-done | bytes 720912 | tf_op jit(solution)/shard_map/reduce_scatter | solution.py:793
  704.2 53.1 %shard_map.209 = (bf16[256,2048]{1,0:T(8,128)(2,1)S(1)}, f32[1,2048]{1,0:T(1,128)S(1)}) custom-call(bf16[1024,512]{1,0:T(8,128)(2,1)S(1)} %copy-done.21, bf16[2048,512]{1,0:T(8,128)(2,1)} %get-tuple-element.80.query_weight, bf16[1024,512]{1,0:T(8,128)(2,1)S(1)} %copy-done.22, bf16[2048,512]{1,0:T(8,128)(2,1)} %get-tuple-element.79.key_value_weight, ...), custom_call_target="tpu_custom_call" | custom-call | flops 99999997952 | bytes 333333344 | tf_op jit(solution)/shard_map/pallas_call | solution.py:178
  758.3 10.7 %reduce-scatter.17.cloned.1.call-done = bf16[176,2048]{1,0:T(8,128)(2,1)} async-done(((bf16[1408,2048]{1,0:T(8,128)(2,1)}), bf16[176,2048]{1,0:T(8,128)(2,1)}) %reduce-scatter.17.cloned.1.call-update) | async-done | bytes 720912 | tf_op jit(solution)/shard_map/reduce_scatter | solution.py:793
  772.5 54.4 %shard_map.206 = bf16[256,2048]{1,0:T(8,128)(2,1)S(1)} custom-call(bf16[1024,1408]{1,0:T(8,128)(2,1)S(1)} %copy-done.20, bf16[1408,2048]{1,0:T(8,128)(2,1)} %all-gather.22.cloned.1.call-done.weight, f32[256,2048]{1,0:T(8,128)S(1)} %copy-done.27), custom_call_target="tpu_custom_call" | custom-call | flops 99999997952 | bytes 333333344 | tf_op jit(solution)/shard_map/pallas_call | solution.py:178
  827.9 41.4 %psum.14 = f32[2,2048]{1,0:T(2,128)S(1)} all-reduce(f32[2,2048]{1,0:T(2,128)S(1)} %pad_maximum_fusion.3), channel_id=1, replica_groups=mesh['ctx'=4,'fsdp'=8] {'ctx','fsdp'}, use_global_device_ids=true, to_apply=%region_1.2 | all-reduce | flops 4096 | bytes 32768 | tf_op jit(solution)/shard_map/psum | solution.py:920
  879.1 17.5 %all-gather.24.cloned.1.call-done = bf16[256,2048]{1,0:T(8,128)(2,1)} async-done(((bf16[64,2048]{1,0:T(8,128)(2,1)}), bf16[256,2048]{1,0:T(8,128)(2,1)}) %all-gather.24.cloned.1.call-update) | async-done | bytes 1048592 | tf_op jit(solution)/shard_map/all_gather | solution.py:907
  899.4 40.9 %all-gather.30.cloned.1.call-done = bf16[1024,1408]{1,0:T(8,128)(2,1)} async-done(((bf16[256,1408]{1,0:T(8,128)(2,1)}), bf16[1024,1408]{1,0:T(8,128)(2,1)}) %all-gather.30.cloned.1.call-update) | async-done | bytes 2883600 | tf_op jit(solution)/shard_map/all_gather | solution.py:904
  965.7 18.3 %all-gather.32.cloned.1.call-done = bf16[1024,1408]{1,0:T(8,128)(2,1)} async-done(((bf16[256,1408]{1,0:T(8,128)(2,1)}), bf16[1024,1408]{1,0:T(8,128)(2,1)}) %all-gather.32.cloned.1.call-update) | async-done | bytes 2883600 | tf_op jit(solution)/shard_map/all_gather | solution.py:904
  1009.4 18.3 %all-gather.26.cloned.1.call-done = bf16[704,2048]{1,0:T(8,128)(2,1)} async-done(((bf16[176,2048]{1,0:T(8,128)(2,1)}), bf16[704,2048]{1,0:T(8,128)(2,1)}) %all-gather.26.cloned.1.call-update) | async-done | bytes 2883600 | tf_op jit(solution)/shard_map/all_gather | solution.py:936
  (158 shorter events, 139.8 us)
Async XLA Ops:
  7.2 143.5 %all-gather.14.cloned.1.call-start = ((), (), s32[]{:S(2)}) async-start(), calls=%async_computation.6 | async-start | bytes 4718592 | tf_op jit(solution)/shard_map/all_gather | solution.py:789
  12.6 166.6 %all-gather.16.cloned.1.call-start = ((), (), s32[]{:S(2)}) async-start(), calls=%async_computation.7 | async-start | bytes 2359296 | tf_op jit(solution)/shard_map/all_gather | solution.py:789
  14.4 265.5 %all-gather.18.cloned.1.call-start = ((), (), s32[]{:S(2)}) async-start(), calls=%async_computation.8 | async-start | bytes 6488064 | tf_op jit(solution)/shard_map/all_gather | solution.py:789
  28.5 263.0 %all-gather.20.cloned.1.call-start = ((), (), s32[]{:S(2)}) async-start(), calls=%async_computation.9 | async-start | bytes 6488064 | tf_op jit(solution)/shard_map/all_gather | solution.py:789
  30.8 272.4 %all-gather.22.cloned.1.call-start = ((), (), s32[]{:S(2)}) async-start(), calls=%async_computation.10 | async-start | bytes 6488064 | tf_op jit(solution)/shard_map/all_gather | solution.py:789
  31.9 477.3 %reduce-scatter.9.cloned.1.call-start = ((), (), s32[]{:S(2)}) async-start(), calls=%async_computation.12 | async-start | bytes 2359296 | tf_op jit(solution)/shard_map/reduce_scatter | solution.py:793
  32.1 123.5 %copy-start.14 = (s32[8]{0:T(128)}, s32[8]{0:T(128)S(1)}, u32[]{:S(2)}) copy-start(s32[8]{0:T(128)S(1)} %select_reduce_fusion.order) | copy-start | bytes 100
  45.9 100.4 %copy-start.8 = (f32[1,2048]{1,0:T(1,128)}, f32[1,2048]{1,0:T(1,128)S(1)}, u32[]{:S(2)}) copy-start(f32[1,2048]{1,0:T(1,128)S(1)} %get-tuple-element.86.gain) | copy-start | bytes 24580
  45.9 133.3 %copy-start.10 = (f32[1,2048]{1,0:T(1,128)}, f32[1,2048]{1,0:T(1,128)S(1)}, u32[]{:S(2)}) copy-start(f32[1,2048]{1,0:T(1,128)S(1)} %get-tuple-element.85.gain) | copy-start | bytes 24580
  51.6 98.1 %copy-start.30 = (f32[1024,32]{1,0:T(8,128)S(1)}, f32[1024,32]{1,0:T(8,128)}, u32[]{:S(2)}) copy-start(f32[1024,32]{1,0:T(8,128)} %get-tuple-element.88) | copy-start | bytes 393220
  51.6 98.1 %copy-start.31 = (f32[1024,32]{1,0:T(8,128)S(1)}, f32[1024,32]{1,0:T(8,128)}, u32[]{:S(2)}) copy-start(f32[1024,32]{1,0:T(8,128)} %get-tuple-element.89) | copy-start | bytes 393220
  179.3 99.3 %copy-start.15 = (bf16[1024,512]{1,0:T(8,128)(2,1)}, bf16[1024,512]{1,0:T(8,128)(2,1)S(1)}, u32[]{:S(2)}) copy-start(bf16[1024,512]{1,0:T(8,128)(2,1)S(1)} %get-tuple-element.28.attended) | copy-start | bytes 3145732
  463.9 69.9 %reduce-scatter.7.cloned.1.call-start = ((), (), s32[]{:S(2)}) async-start(), calls=%async_computation.11 | async-start | bytes 2359296 | tf_op jit(solution)/shard_map/reduce_scatter | solution.py:793
  470.1 100.5 %reduce-scatter.11.cloned.1.call-start = ((), (), s32[]{:S(2)}) async-start(), calls=%async_computation.14 | async-start | bytes 2359296 | tf_op jit(solution)/shard_map/reduce_scatter | solution.py:793
  476.1 160.8 %reduce-scatter.13.cloned.1.call-start = ((), (), s32[]{:S(2)}) async-start(), calls=%async_computation.16 | async-start | bytes 6488064 | tf_op jit(solution)/shard_map/reduce_scatter | solution.py:793
  487.2 215.7 %reduce-scatter.15.cloned.1.call-start = ((), (), s32[]{:S(2)}) async-start(), calls=%async_computation.17 | async-start | bytes 6488064 | tf_op jit(solution)/shard_map/reduce_scatter | solution.py:793
  498.5 270.5 %reduce-scatter.17.cloned.1.call-start = ((), (), s32[]{:S(2)}) async-start(), calls=%async_computation.18 | async-start | bytes 6488064 | tf_op jit(solution)/shard_map/reduce_scatter | solution.py:793
  509.0 194.0 %copy-start.9 = (f32[1,2048]{1,0:T(1,128)S(1)}, f32[1,2048]{1,0:T(1,128)}, u32[]{:S(2)}) copy-start(f32[1,2048]{1,0:T(1,128)} %copy-done.8) | copy-start | bytes 24580
  509.1 360.9 %all-reduce.2.cloned.1.call-start = ((), (), s32[]{:S(2)}) async-start(), calls=%async_computation.13 | async-start | bytes 524288 | tf_op jit(solution)/shard_map/psum | solution.py:908
  509.6 362.1 %all-gather.28.cloned.1.call-start = ((), (), s32[]{:S(2)}) async-start(), calls=%async_computation.20 | async-start | bytes 1310720 | tf_op jit(solution)/shard_map/all_gather | solution.py:904
  533.8 362.8 %all-gather.24.cloned.1.call-start = ((), (), s32[]{:S(2)}) async-start(), calls=%async_computation.15 | async-start | bytes 1310720 | tf_op jit(solution)/shard_map/all_gather | solution.py:907
  570.5 369.7 %all-gather.30.cloned.1.call-start = ((), (), s32[]{:S(2)}) async-start(), calls=%async_computation.21 | async-start | bytes 3604480 | tf_op jit(solution)/shard_map/all_gather | solution.py:904
  637.0 347.0 %all-gather.32.cloned.1.call-start = ((), (), s32[]{:S(2)}) async-start(), calls=%async_computation.22 | async-start | bytes 3604480 | tf_op jit(solution)/shard_map/all_gather | solution.py:904
  702.9 324.7 %all-gather.26.cloned.1.call-start = ((), (), s32[]{:S(2)}) async-start(), calls=%async_computation.19 | async-start | bytes 3604480 | tf_op jit(solution)/shard_map/all_gather | solution.py:936
  (29 other events, 312.5 us)
Sparse Core Ops, SparseCore 0:
  12.8 49.8 all-gather.13
  64.8 27.8 all-gather.15
  94.9 59.9 all-gather.17
  157.0 59.0 all-gather.19
  217.6 59.0 all-gather.21
  464.0 32.9 reduce-scatter.8
  499.3 34.4 reduce-scatter.6
  536.0 34.4 reduce-scatter.10
  573.4 63.4 reduce-scatter.12
  639.7 63.2 reduce-scatter.14
  705.8 63.2 reduce-scatter.16
  771.8 66.9 all-reduce.1
  840.8 26.9 all-gather.27
  869.6 26.9 all-gather.23
  898.4 41.7 all-gather.29
  942.1 41.7 all-gather.31
  985.8 41.7 all-gather.25

commit v3 on v2

v3 whole, which is shorter than its diff:
```python
import functools
import math

import jax
import jax.numpy as jnp
from jax import lax
from jax.experimental import pallas as pl
from jax.experimental.pallas import tpu as pltpu
from jax.sharding import PartitionSpec as P

D = 2048
FF = 5632
HEADS = 32
KV_HEADS = 4
HEAD_DIM = 64
KV_WIDTH = 256


epsilon = 1e-05


MESH = pl.DeviceIdType.MESH
VMEM = pl.BlockSpec(memory_space=pltpu.VMEM)
SMEM = pl.BlockSpec(memory_space=pltpu.SMEM)
HBM = pl.BlockSpec(memory_space=pl.ANY)
LANES = 128
PAIR = LANES // HEAD_DIM
QUERY_ROWS = 256


def shape(dims, kind=jnp.bfloat16):
    return jax.ShapeDtypeStruct(dims, kind)


def norm_parts(values):
    inverse = lax.rsqrt(jnp.mean(values * values, axis=-1, keepdims=True) + epsilon)
    return (values * inverse, inverse)


def norm_back(gradient, normed, inverse):
    return inverse * (gradient - normed * jnp.mean(gradient * normed, axis=-1, keepdims=True))


def product(left_side, right_side):
    return jnp.dot(left_side, right_side, preferred_element_type=jnp.float32)


def times_transposed(left_side, right_side):
    return lax.dot_general(
        left_side, right_side, (((1,), (1,)), ((), ())), preferred_element_type=jnp.float32
    )


def column_term(source, gradient):
    return lax.dot_general(
        source, gradient, (((0,), (0,)), ((), ())), preferred_element_type=jnp.float32
    )


STRIP = 32
PIECES = 4


def plane_places():
    me = lax.axis_index("ctx")
    return (me, me + 1 - 2 * lax.rem(me, 2), lax.rem(me + 2, 4), 3 - me)


def signal(barrier, **place):
    pl.semaphore_signal(barrier, inc=1, device_id=place, device_id_type=MESH)


def meet(count, shards=1):
    me = lax.axis_index("ctx")
    barrier = pltpu.get_barrier_semaphore()
    for step in range(1, count):
        signal(barrier, ctx=lax.rem(me + step, count))
    for step in range(1, shards):
        signal(barrier, fsdp=lax.rem(lax.axis_index("fsdp") + step, shards))
    pl.semaphore_wait(barrier, count - 1 + shards - 1)


def remote(source, target, send_sem, recv_sem, **place):
    copy = pltpu.make_async_remote_copy(
        src_ref=source,
        dst_ref=target,
        send_sem=send_sem,
        recv_sem=recv_sem,
        device_id=place,
        device_id_type=MESH,
    )
    copy.start()
    return copy


def gather_sems(count):
    sends = 3 if count == 4 else count - 1
    return [
        pltpu.SemaphoreType.DMA((PIECES,)),
        pltpu.SemaphoreType.DMA((sends, PIECES)),
        pltpu.SemaphoreType.DMA((sends, PIECES)),
    ]


class RowGather:
    def __init__(self, count, own, out, sems):
        self.count, self.own, self.out = (count, own, out)
        self.local_sem, self.send_sem, self.recv_sem = sems
        self.size = own.shape[0] // PIECES
        self.copies = [[] for _ in range(PIECES)]

    def place(self, owner, piece):
        start = owner * self.own.shape[0] + piece * self.size
        return self.out.at[pl.ds(pl.multiple_of(start, self.size), self.size)]

    def send(self, piece):
        me = lax.axis_index("ctx")
        source = self.own.at[pl.ds(piece * self.size, self.size)]
        target = self.place(me, piece)
        if self.count == 4:
            _, across, along, _ = plane_places()
            peers = (across, along)
        else:
            peers = [lax.rem(me + step, self.count) for step in range(1, self.count)]
        for index, peer in enumerate(peers):
            self.copies[piece].append(
                remote(
                    source,
                    target,
                    self.send_sem.at[index, piece],
                    self.recv_sem.at[index, piece],
                    ctx=peer,
                )
            )
        local = pltpu.make_async_copy(source, target, self.local_sem.at[piece])
        local.start()
        self.copies[piece].append(local)

    def finish(self):
        if self.count != 4:
            for copies in self.copies:
                for copy in copies:
                    copy.wait()
            return
        _, across, along, _ = plane_places()
        relays = []
        for piece in (0, PIECES // 2, 1, PIECES // 2 + 1):
            first = piece < PIECES // 2
            came, left = (0, 1) if first else (1, 0)
            owner, peer = (across, along) if first else (along, across)
            self.copies[piece][came].wait_recv()
            block = self.place(owner, piece)
            relays.append(
                remote(
                    block, block, self.send_sem.at[2, piece], self.recv_sem.at[2, piece], ctx=peer
                )
            )
        for piece in range(PIECES):
            to_across, to_along, local = self.copies[piece]
            (to_along if piece < PIECES // 2 else to_across).wait_recv()
            to_across.wait_send()
            to_along.wait_send()
            local.wait()
        for relay in relays:
            relay.wait()


def product_blocks(count, pairs, rows, width):
    tile = 512

    def block(owner, store):
        start = pl.multiple_of(owner * rows, rows)

        def column(index, carry):
            columns = pl.ds(pl.multiple_of(index * tile, tile), tile)
            value = None
            for left, right, transposed in pairs:
                piece = left[pl.ds(start, rows), :]
                if transposed:
                    term = times_transposed(piece, right[columns, : piece.shape[1]])
                else:
                    term = product(piece, right[:, columns])
                value = term if value is None else value + term
            store(columns, value)
            return carry

        lax.fori_loop(0, width // tile, column, 0)

    return block


def scatter_products(count, pairs, send_buf, recv_buf, kept, total, send_sem, recv_sem):
    rows, width = total.shape
    half = rows // 2
    block = product_blocks(count, pairs, rows, width)
    me = lax.axis_index("ctx")

    def store_own(columns, value):
        total[:, columns] = value

    def send(slot, part, sem, peer):
        return remote(
            send_buf.at[slot, part],
            recv_buf.at[slot, part],
            send_sem.at[sem],
            recv_sem.at[sem],
            ctx=peer,
        )

    if count != 4:
        copies = []
        for step in range(1, count):
            owner = lax.rem(me + step, count)

            def store_sent(columns, value, step=step):
                send_buf[step - 1, :, columns] = value.astype(send_buf.dtype)

            block(owner, store_sent)
            copies.append(send(step - 1, pl.ds(0, rows), step - 1, owner))
        block(me, store_own)
        for copy in copies:
            copy.wait()
        return
    _, across, along, corner = plane_places()
    low, high = (pl.ds(0, half), pl.ds(half, half))

    def store_corner(columns, value):
        send_buf[0, :, columns] = value.astype(send_buf.dtype)

    def store_across(columns, value):
        send_buf[1, low, columns] = value[:half].astype(send_buf.dtype)
        kept[high, columns] = value[half:]

    def store_along(columns, value):
        send_buf[1, high, columns] = value[half:].astype(send_buf.dtype)
        kept[low, columns] = value[:half]

    block(corner, store_corner)
    relay_low = send(0, low, 0, across)
    relay_high = send(0, high, 1, along)
    block(across, store_across)
    direct_low = send(1, low, 2, across)
    block(along, store_along)
    direct_high = send(1, high, 3, along)
    block(me, store_own)

    def add(where):
        value = kept[where, :] + recv_buf[0, where, :].astype(jnp.float32)
        send_buf[2, where, :] = value.astype(send_buf.dtype)

    relay_low.wait_recv()
    for_strips(0, half, add)
    final_low = send(2, low, 4, along)
    relay_high.wait_recv()
    for_strips(half, half, add)
    final_high = send(2, high, 5, across)
    relay_low.wait_send()
    relay_high.wait_send()
    direct_low.wait()
    direct_high.wait()
    final_low.wait()
    final_high.wait()


def scatter_scratch(count, rows, width):
    slots = 3 if count == 4 else count - 1
    sems = 6 if count == 4 else count - 1
    return [
        pltpu.VMEM((slots, rows, width), jnp.bfloat16),
        pltpu.VMEM((slots, rows, width), jnp.bfloat16),
        pltpu.VMEM((rows, width) if count == 4 else (8, LANES), jnp.float32),
        pltpu.VMEM((rows, width), jnp.float32),
        pltpu.SemaphoreType.DMA((sems,)),
        pltpu.SemaphoreType.DMA((sems,)),
    ]


def received(count, recv_buf, total, rows):
    value = total[rows, :]
    for slot in (1, 2) if count == 4 else range(count - 1):
        value = value + recv_buf[slot, rows, :].astype(jnp.float32)
    return value


def for_strips(first, rows, body):
    def strip(index, carry):
        body(pl.ds(pl.multiple_of(first + index * STRIP, STRIP), STRIP))
        return carry

    lax.fori_loop(0, rows // STRIP, strip, 0)


def call_plane(body, ident, outs, out_specs, in_specs, scratch, flops, megabytes, args):
    return pl.pallas_call(
        body,
        out_shape=outs,
        in_specs=in_specs,
        out_specs=out_specs,
        scratch_shapes=scratch,
        compiler_params=pltpu.CompilerParams(
            collective_id=ident, has_side_effects=True, vmem_limit_bytes=megabytes << 20
        ),
        cost_estimate=pl.CostEstimate(
            flops=flops, bytes_accessed=flops // 300, transcendentals=0
        ),
    )(*args)


def start_body(count, shards, tokens, gains, tokens_all, gains_all, *sems):
    meet(count, shards)
    gain_local, gain_send, gain_recv = sems[:3]
    me = lax.axis_index("fsdp")
    copies = []
    for step in range(1, shards):
        copies.append(
            remote(
                gains,
                gains_all.at[me],
                gain_send.at[step - 1],
                gain_recv.at[step - 1],
                fsdp=lax.rem(me + step, shards),
            )
        )
    local = pltpu.make_async_copy(gains, gains_all.at[me], gain_local)
    local.start()
    first = RowGather(count, tokens, tokens_all, sems[3:6])
    order = (0, PIECES // 2, 1, PIECES // 2 + 1)
    for piece in order:
        first.send(piece)
    first.finish()
    local.wait()
    for copy in copies:
        copy.wait()


def start_gather(count, shards, ident, tokens, gains):
    rows, width = tokens.shape
    gathered = shape((count * rows, width))
    return call_plane(
        functools.partial(start_body, count, shards),
        ident,
        (gathered, shape((shards,) + gains.shape)),
        (HBM, HBM),
        [HBM] * 2,
        [
            pltpu.SemaphoreType.DMA,
            pltpu.SemaphoreType.DMA((shards - 1,)),
            pltpu.SemaphoreType.DMA((shards - 1,)),
        ]
        + gather_sems(count),
        4 * 10**10,
        4,
        (tokens, gains),
    )


def strips_and_send(gather, strip):
    size = gather.size
    for piece in range(PIECES):
        for_strips(piece * size, size, strip)
        gather.send(piece)
    gather.finish()


def middle_body(
    count, attended, weight, tokens, gain, residual, second_all, own, send_buf, recv_buf, kept, total,
    send_sem, recv_sem, *sems
):
    meet(count)
    scatter_products(
        count, [(attended, weight, False)], send_buf, recv_buf, kept, total, send_sem, recv_sem
    )

    def strip(where):
        values = tokens[where, :].astype(jnp.float32) + received(count, recv_buf, total, where)
        residual[where, :] = values
        normed, _ = norm_parts(values)
        own[where, :] = (normed * gain[...]).astype(jnp.bfloat16)

    strips_and_send(RowGather(count, own, second_all, sems), strip)


def middle_gather(count, ident, attended, weight, tokens, gain):
    rows, width = tokens.shape
    return call_plane(
        functools.partial(middle_body, count),
        ident,
        (shape((rows, width), jnp.float32), shape((count * rows, width))),
        (VMEM, HBM),
        [VMEM] * 4,
        [pltpu.VMEM((rows, width), jnp.bfloat16)]
        + scatter_scratch(count, rows, width)
        + gather_sems(count),
        6 * 10**10,
        40,
        (attended, weight, tokens, gain),
    )


def middle_back_body(
    count, grad_gate_up, gate_up_weight, residual, gain, grad_out, grad_mid, gain_part,
    branch_all, own, send_buf, recv_buf, kept, total, send_sem, recv_sem, *sems
):
    meet(count)
    scatter_products(
        count,
        [(grad_gate_up, gate_up_weight, True)],
        send_buf,
        recv_buf,
        kept,
        total,
        send_sem,
        recv_sem,
    )
    gain_part[...] = jnp.zeros_like(gain_part)

    def strip(where):
        gradient = received(count, recv_buf, total, where)
        normed, inverse = norm_parts(residual[where, :])
        gain_part[...] += jnp.sum(gradient * normed, axis=0, keepdims=True)
        values = grad_out[where, :].astype(jnp.float32) + norm_back(
            gradient * gain[...], normed, inverse
        )
        grad_mid[where, :] = values
        own[where, :] = values.astype(jnp.bfloat16)

    strips_and_send(RowGather(count, own, branch_all, sems), strip)


def column_halves(array):
    rows, width = array.shape
    if width // 2 % LANES:
        return ((array[:, : width // 2], array[:, width // 2 :]), (VMEM, VMEM))
    specs = [pl.BlockSpec((rows, width // 2), lambda *index, side=side: (0, side)) for side in (0, 1)]
    return ((array, array), specs)


def middle_back(count, ident, grad_gate_up, gate_up_weight, residual, gain, grad_out):
    rows, width = residual.shape
    return call_plane(
        functools.partial(middle_back_body, count),
        ident,
        (
            shape((rows, width), jnp.float32),
            shape((1, width), jnp.float32),
            shape((count * rows, width)),
        ),
        (VMEM, VMEM, HBM),
        [VMEM] * 5,
        [pltpu.VMEM((rows, width), jnp.bfloat16)]
        + scatter_scratch(count, rows, width)
        + gather_sems(count),
        6 * 10**10,
        52,
        (grad_gate_up, gate_up_weight, residual, gain, grad_out),
    )


def input_back_body(
    count, shards, grad_packed, weight, tokens, gain, grad_mid, second_part, grad_input, gain_sums, gain_part, parts, part_recv, sums, sums_recv, send_buf,
    recv_buf, kept, total, send_sem, recv_sem, part_send_sem, part_recv_sem, sums_send_sem,
    sums_recv_sem
):
    meet(count, shards)
    scatter_products(
        count,
        [(grad_packed, weight, True)],
        send_buf,
        recv_buf,
        kept,
        total,
        send_sem,
        recv_sem,
    )
    gain_part[...] = jnp.zeros_like(gain_part)

    def strip(where):
        gradient = received(count, recv_buf, total, where)
        normed, inverse = norm_parts(tokens[where, :].astype(jnp.float32))
        gain_part[...] += jnp.sum(gradient * normed, axis=0, keepdims=True)
        values = grad_mid[where, :] + norm_back(gradient * gain[...], normed, inverse)
        grad_input[where, :] = values.astype(jnp.bfloat16)

    for_strips(0, grad_input.shape[0], strip)
    me = lax.axis_index("fsdp")
    span = parts.shape[2]
    for shard in range(shards):
        lanes = slice(shard * span, (shard + 1) * span)
        parts[shard, 0:1, :] = gain_part[:, lanes]
        parts[shard, 1:2, :] = second_part[:, lanes]
    copies = []
    for step in range(1, shards):
        peer = lax.rem(me + step, shards)
        copies.append(
            remote(
                parts.at[peer],
                part_recv.at[step - 1],
                part_send_sem.at[step - 1],
                part_recv_sem.at[step - 1],
                fsdp=peer,
            )
        )
    for copy in copies:
        copy.wait()
    value = parts[me]
    for step in range(1, shards):
        value = value + part_recv[step - 1]
    sums[...] = value
    copies = []
    for step in range(1, count):
        copies.append(
            remote(
                sums,
                sums_recv.at[step - 1],
                sums_send_sem.at[step - 1],
                sums_recv_sem.at[step - 1],
                ctx=lax.rem(lax.axis_index("ctx") + step, count),
            )
        )
    for copy in copies:
        copy.wait()
    for step in range(1, count):
        value = value + sums_recv[step - 1]
    gain_sums[...] = value


def input_back(
    count, shards, ident, grad_packed, weight, tokens, gain, grad_mid, second_part
):
    rows, width = tokens.shape
    span = width // shards
    return call_plane(
        functools.partial(input_back_body, count, shards),
        ident,
        (shape((rows, width)), shape((2, span), jnp.float32)),
        (VMEM, VMEM),
        [VMEM] * 6,
        [
            pltpu.VMEM((1, width), jnp.float32),
            pltpu.VMEM((shards, 2, span), jnp.float32),
            pltpu.VMEM((shards - 1, 2, span), jnp.float32),
            pltpu.VMEM((2, span), jnp.float32),
            pltpu.VMEM((count - 1, 2, span), jnp.float32),
        ]
        + scatter_scratch(count, rows, width)
        + [
            pltpu.SemaphoreType.DMA((shards - 1,)),
            pltpu.SemaphoreType.DMA((shards - 1,)),
            pltpu.SemaphoreType.DMA((count - 1,)),
            pltpu.SemaphoreType.DMA((count - 1,)),
        ],
        5 * 10**10,
        40,
        (grad_packed, weight, tokens, gain, grad_mid, second_part),
    )


def swap(array, along):
    pairs = [(i, (i + 2) % 4) if along else (i, i + 1 - 2 * (i % 2)) for i in range(4)]
    return lax.ppermute(array, "ctx", pairs)


def plane_gather(array):
    if lax.axis_size("ctx") != 4:
        return lax.all_gather(array, "ctx", axis=0)
    half = array.shape[0] // 2
    across, along = (swap(array, False), swap(array, True))
    low, high = (swap(across[:half], True), swap(along[half:], False))
    return (array, across, along, low, high)


def take_half(partial, owner, side):
    rows = partial.shape[0] // lax.axis_size("ctx")
    half = rows // 2
    return lax.dynamic_slice_in_dim(partial, owner * rows + side * half, half, 0)


def plane_relay(partial):
    if lax.axis_size("ctx") != 4:
        return (partial,)
    me, across, along, corner = plane_places()
    take = functools.partial(take_half, partial)
    low = swap(jnp.stack([take(corner, 0), take(across, 0)]), False)
    high = swap(jnp.stack([take(corner, 1), take(along, 1)]), True)
    return (low, high)


def add_parts(first, second):
    return first.astype(jnp.float32) + second.astype(jnp.float32)


def plane_last(partial, relayed):
    if lax.axis_size("ctx") != 4:
        return (lax.psum_scatter(relayed[0], "ctx", scatter_dimension=0, tiled=True),)
    me, across, along, corner = plane_places()
    take = functools.partial(take_half, partial)
    low, high = relayed
    last_low = swap(add_parts(take(along, 0), low[0]).astype(jnp.bfloat16), True)
    last_high = swap(add_parts(take(across, 1), high[0]).astype(jnp.bfloat16), False)
    return (last_low, last_high)


def plane_scatter(partial, relayed, last):
    if lax.axis_size("ctx") != 4:
        return last[0].astype(jnp.float32)
    me = lax.axis_index("ctx")
    return jnp.concatenate(
        [
            add_parts(take_half(partial, me, side), relayed[side][1])
            + last[side].astype(jnp.float32)
            for side in (0, 1)
        ],
        axis=0,
    )


def hidden_body(rows, gate_weight, up_weight, gate_up, hidden):
    width = hidden.shape[1]
    gate = product(rows[...], gate_weight[...])
    gate_up[:, :width] = gate
    upward = product(rows[...], up_weight[...])
    gate_up[:, width:] = upward
    hidden[...] = (gate * jax.nn.sigmoid(gate) * upward).astype(jnp.bfloat16)


def hidden_forward(second_all, gate_up_weight):
    length, depth = second_all.shape
    width = gate_up_weight.shape[1] // 2
    (gate_weight, up_weight), specs = column_halves(gate_up_weight)
    step = QUERY_ROWS
    return pl.pallas_call(
        hidden_body,
        grid=(length // step,),
        out_shape=(shape((length, 2 * width), jnp.float32), shape((length, width))),
        in_specs=[pl.BlockSpec((step, depth), lambda i: (i, 0))] + list(specs),
        out_specs=(
            pl.BlockSpec((step, 2 * width), lambda i: (i, 0)),
            pl.BlockSpec((step, width), lambda i: (i, 0)),
        ),
        compiler_params=pltpu.CompilerParams(vmem_limit_bytes=52 << 20),
        cost_estimate=pl.CostEstimate(
            flops=4 * length * depth * width, bytes_accessed=3 * 10**7, transcendentals=10**6
        ),
    )(second_all, gate_weight, up_weight)


def hidden_back_body(grad_rows, down_weight, gate_up, grad_gate_up):
    width = down_weight.shape[0]
    grad_hidden = times_transposed(grad_rows[...], down_weight[...])
    gate, upward = (gate_up[:, :width], gate_up[:, width:])
    sigmoid_gate = jax.nn.sigmoid(gate)
    silu_gate = gate * sigmoid_gate
    grad_gate = grad_hidden * upward * sigmoid_gate * (1.0 + gate * (1.0 - sigmoid_gate))
    grad_gate_up[:, :width] = grad_gate.astype(jnp.bfloat16)
    grad_gate_up[:, width:] = (grad_hidden * silu_gate).astype(jnp.bfloat16)


def hidden_backward(grad_out_all, down_weight, gate_up):
    length, depth = grad_out_all.shape
    width = down_weight.shape[0]
    step = QUERY_ROWS
    return pl.pallas_call(
        hidden_back_body,
        grid=(length // step,),
        out_shape=shape((length, 2 * width)),
        in_specs=[
            pl.BlockSpec((step, depth), lambda i: (i, 0)),
            pl.BlockSpec((width, depth), lambda i: (0, 0)),
            pl.BlockSpec((step, 2 * width), lambda i: (i, 0)),
        ],
        out_specs=pl.BlockSpec((step, 2 * width), lambda i: (i, 0)),
        compiler_params=pltpu.CompilerParams(vmem_limit_bytes=48 << 20),
        cost_estimate=pl.CostEstimate(
            flops=2 * length * depth * width, bytes_accessed=3 * 10**7, transcendentals=10**6
        ),
    )(grad_out_all, down_weight, gate_up)


def attention_grads_body(inputs, grad_packed, attended, branch_all, packed):
    width = grad_packed.shape[1]
    packed[:, :width] = product(inputs[...].T, grad_packed[...]).astype(jnp.bfloat16)
    rows = HEAD_DIM
    heads = attended[...].T
    upper = lax.rem(pl.program_id(0), PAIR) == 1
    heads = jnp.where(upper, heads[rows:], heads[:rows])
    out = product(heads, branch_all[...]).astype(jnp.bfloat16)
    part = out.shape[1] // (packed.shape[0] // rows)
    for index in range(packed.shape[0] // rows):
        packed[index * rows : (index + 1) * rows, width:] = out[
            :, index * part : (index + 1) * part
        ]


def attention_grads(shards, first_all, grad_packed, attended, branch_all):
    length, depth = first_all.shape
    span = depth // shards
    width = grad_packed.shape[1] + attended.shape[1]
    return pl.pallas_call(
        attention_grads_body,
        grid=(shards,),
        out_shape=shape((depth, width)),
        in_specs=[
            pl.BlockSpec((length, span), lambda i: (0, i)),
            pl.BlockSpec(grad_packed.shape, lambda i: (0, 0)),
            pl.BlockSpec((length, LANES), lambda i: (0, i // PAIR)),
            pl.BlockSpec(branch_all.shape, lambda i: (0, 0)),
        ],
        out_specs=pl.BlockSpec((span, width), lambda i: (i, 0)),
        compiler_params=pltpu.CompilerParams(vmem_limit_bytes=48 << 20),
        cost_estimate=pl.CostEstimate(
            flops=2 * length * depth * width, bytes_accessed=2 * 10**7, transcendentals=0
        ),
    )(first_all, grad_packed, attended, branch_all)


def sort_parts(parts, sorted_parts, corner_low):
    me, across, along, corner = plane_places()
    own, from_across, from_along, low, high = parts
    sorted_parts[me] = own[...]
    sorted_parts[across] = from_across[...]
    sorted_parts[along] = from_along[...]

    @pl.when(corner_low)
    def _():
        sorted_parts[corner] = low[...]

    @pl.when(jnp.logical_not(corner_low))
    def _():
        sorted_parts[corner] = high[...]


def place_hidden_body(shards, *refs):
    parts, (gate, up, sorted_parts) = (refs[:5], refs[5:])
    steps = pl.num_programs(0)
    sort_parts(parts, sorted_parts, pl.program_id(0) < steps // 2)
    count = sorted_parts.shape[0]
    width = sorted_parts.shape[2] // 2
    span = width // shards
    for target, offset in ((gate, 0), (up, width)):
        values = [
            sorted_parts[part, :, offset : offset + width].astype(jnp.float32)
            for part in range(count)
        ]
        target[...] = jnp.concatenate(
            [
                values[part][:, shard * span : (shard + 1) * span]
                for shard in range(shards)
                for part in range(count)
            ],
            axis=1,
        )


def place_hidden(shards, parts):
    rows, width = parts[0].shape
    step = 32
    half = rows // step // 2
    outs = shape((rows, 2 * width), jnp.float32)
    whole = pl.BlockSpec((step, width), lambda i: (i, 0))
    low = pl.BlockSpec((step, width), lambda i: (jnp.minimum(i, half - 1), 0))
    high = pl.BlockSpec((step, width), lambda i: (jnp.maximum(i - half, 0), 0))
    result = pl.BlockSpec((step, 2 * width), lambda i: (i, 0))
    return pl.pallas_call(
        functools.partial(place_hidden_body, shards),
        grid=(rows // step,),
        out_shape=(outs, outs),
        in_specs=[whole, whole, whole, low, high],
        out_specs=(result, result),
        scratch_shapes=[pltpu.VMEM((4, step, width), jnp.bfloat16)],
        cost_estimate=pl.CostEstimate(flops=0, bytes_accessed=2 * 10**7, transcendentals=0),
        compiler_params=pltpu.CompilerParams(vmem_limit_bytes=24 << 20),
    )(*parts)


def place_rows_body(own, from_across, from_along, low, high, out):
    me, across, along, corner = plane_places()
    rows = own.shape[0]

    def put(owner, offset, ref):
        size = ref.shape[0]
        start = pl.multiple_of(owner * rows + offset, 8)
        out[pl.ds(start, size), :] = ref[...].astype(out.dtype)

    put(me, 0, own)
    put(across, 0, from_across)
    put(along, 0, from_along)
    put(corner, 0, low)
    put(corner, rows // 2, high)


def place_rows(parts, kind):
    rows, width = parts[0].shape
    return pl.pallas_call(
        place_rows_body,
        out_shape=shape((4 * rows, width), kind),
        in_specs=[VMEM] * 5,
        out_specs=VMEM,
        cost_estimate=pl.CostEstimate(flops=0, bytes_accessed=10**7, transcendentals=0),
        compiler_params=pltpu.CompilerParams(vmem_limit_bytes=24 << 20),
    )(*parts)


def place_attention_body(shards, own, from_across, from_along, low, high, query, key, value, output, sorted_parts):
    me, across, along, corner = plane_places()
    rows = own.shape[0]
    sorted_parts[me] = own[...]
    sorted_parts[across] = from_across[...]
    sorted_parts[along] = from_along[...]
    sorted_parts[corner, : rows // 2] = low[...]
    sorted_parts[corner, rows // 2 :] = high[...]
    count = sorted_parts.shape[0]
    width = query.shape[1] // count
    span = width // shards
    values = [sorted_parts[part, :, :width].astype(jnp.float32) for part in range(count)]
    query[...] = jnp.concatenate(
        [
            values[part][:, shard * span : (shard + 1) * span]
            for shard in range(shards)
            for part in range(count)
        ],
        axis=1,
    )
    sums = None
    for part in range(count):
        term = sorted_parts[part, :, width : width + 2 * KV_WIDTH].astype(jnp.float32)
        sums = term if sums is None else sums + term
    key[...] = sums[:, :KV_WIDTH]
    value[...] = sums[:, KV_WIDTH:]
    height = rows // count
    for part in range(count):
        for index in range(count):
            tile = sorted_parts[part, index * height : (index + 1) * height, width + 2 * KV_WIDTH :]
            output[part * height : (part + 1) * height, index * width : (index + 1) * width] = (
                tile.astype(jnp.float32)
            )


def place_attention(shards, parts):
    rows, width = parts[0].shape
    wide = shape((rows, D), jnp.float32)
    narrow = shape((rows, KV_WIDTH), jnp.float32)
    return pl.pallas_call(
        functools.partial(place_attention_body, shards),
        out_shape=(wide, narrow, narrow, wide),
        in_specs=[VMEM] * 5,
        out_specs=(VMEM,) * 4,
        scratch_shapes=[pltpu.VMEM((4, rows, width), jnp.bfloat16)],
        cost_estimate=pl.CostEstimate(flops=0, bytes_accessed=10**7, transcendentals=0),
        compiler_params=pltpu.CompilerParams(vmem_limit_bytes=32 << 20),
    )(*parts)


def rotary_tables(length):
    frequency = jnp.exp(
        -math.log(10000.0) * jnp.arange(HEAD_DIM // 2).astype(jnp.float32) * (2.0 / HEAD_DIM)
    )
    angles = jnp.arange(length).astype(jnp.float32)[:, None] * frequency[None, :]
    cosine, sine = (jnp.cos(angles), jnp.sin(angles))
    return (
        jnp.concatenate([cosine] * (2 * PAIR), axis=1),
        jnp.concatenate([-sine, sine] * PAIR, axis=1),
    )


def low_lanes(dims, size):
    return lax.rem(lax.broadcasted_iota(jnp.int32, dims, len(dims) - 1), 2 * size) < size


def turn(values, cosine, sine):
    half = HEAD_DIM // 2
    swapped = jnp.where(
        low_lanes(values.shape, half),
        pltpu.roll(values, LANES - half, 1),
        pltpu.roll(values, half, 1),
    )
    return values * cosine + swapped * sine


def two_heads(values):
    low = low_lanes(values.shape, HEAD_DIM)
    zero = jnp.zeros_like(values)
    return jnp.concatenate([jnp.where(low, values, zero), jnp.where(low, zero, values)], axis=0)


def pick_heads(values):
    rows = values.shape[1] // PAIR
    return jnp.concatenate(
        [values[:HEAD_DIM, :rows], values[HEAD_DIM:, rows:]], axis=0
    )


def later_key(dims):
    key = lax.broadcasted_iota(jnp.int32, dims, 0)
    query = lax.rem(lax.broadcasted_iota(jnp.int32, dims, 1), QUERY_ROWS)
    return key > query


def block_rows_at(order, block, rows):
    return pl.ds(pl.multiple_of(order[block] * rows, rows), rows)


def rows_in_order(order, source, index, rows):
    per = QUERY_ROWS // rows
    return jnp.concatenate(
        [source[block_rows_at(order, index * per + i, rows), :] for i in range(per)], axis=0
    )


def attend_body(
    block_rows,
    order,
    tokens_all,
    gain,
    weight,
    cosine,
    sine,
    attended,
    queries,
    keys,
    values,
    log_totals,
    first_all,
    values_across,
):
    length, width = queries.shape
    kv_heads = keys.shape[0]
    pairs = width // LANES
    blocks = length // QUERY_ROWS

    def project(index, carry):
        place = pl.ds(pl.multiple_of(index * QUERY_ROWS, QUERY_ROWS), QUERY_ROWS)
        normed, _ = norm_parts(
            rows_in_order(order, tokens_all, index, block_rows).astype(jnp.float32)
        )
        rows = (normed * gain[...]).astype(jnp.bfloat16)
        for i in range(QUERY_ROWS // block_rows):
            first_all[block_rows_at(order, index * (QUERY_ROWS // block_rows) + i, block_rows), :] = (
                rows[i * block_rows : (i + 1) * block_rows]
            )
        cos_rows, sin_rows = (cosine[place, :], sine[place, :])
        projected = product(rows, weight[:, :width])
        for pair in range(pairs):
            lanes = slice(pair * LANES, (pair + 1) * LANES)
            turned = turn(projected[:, lanes], cos_rows, sin_rows).astype(jnp.bfloat16)
            queries[place, lanes] = turned * jnp.asarray(1.0 / math.sqrt(HEAD_DIM), jnp.bfloat16)
        projected = product(rows, weight[:, width : width + 2 * kv_heads * HEAD_DIM])
        for head in range(2 * kv_heads):
            tile = projected[:, head // PAIR * LANES : (head // PAIR + 1) * LANES]
            if head < kv_heads:
                tile = turn(tile, cos_rows, sin_rows)
            low = low_lanes(tile.shape, HEAD_DIM)
            moved = pltpu.roll(tile, HEAD_DIM, 1)
            both = jnp.where(low, tile, moved) if head % PAIR == 0 else jnp.where(low, moved, tile)
            if head < kv_heads:
                keys[head, place, :] = both.astype(jnp.bfloat16)
            else:
                values[head - kv_heads, place, :] = both.astype(jnp.bfloat16)
                values_across[head - kv_heads, :, place] = both.T.astype(jnp.bfloat16)
        return carry

    lax.fori_loop(0, blocks, project, 0)

    def attend(pair, carry):
        kv_head = pair // (pairs // kv_heads)
        lanes = pl.ds(pl.multiple_of(pair * LANES, LANES), LANES)
        for index in range(blocks):
            seen = (index + 1) * QUERY_ROWS
            rows = two_heads(queries[index * QUERY_ROWS : seen, lanes])
            scores = times_transposed(keys[kv_head, :seen, :], rows)
            own = scores[seen - QUERY_ROWS :]
            own = jnp.where(later_key(own.shape), -1e30, own)
            if index:
                scores = jnp.concatenate([scores[: seen - QUERY_ROWS], own], axis=0)
            else:
                scores = own
            largest = jnp.max(scores, axis=0, keepdims=True)
            exponent = jnp.exp(scores - largest)
            totals = jnp.sum(exponent, axis=0, keepdims=True)
            mixed = product(values_across[kv_head, :, :seen], exponent.astype(jnp.bfloat16))
            log_totals[pl.ds(pair * blocks + index, 1), :] = largest + jnp.log(totals)
            mixed = pick_heads(mixed / totals).T.astype(jnp.bfloat16)
            per = QUERY_ROWS // block_rows
            for i in range(per):
                attended[block_rows_at(order, index * per + i, block_rows), lanes] = mixed[
                    i * block_rows : (i + 1) * block_rows
                ]
        return carry

    lax.fori_loop(0, pairs, attend, 0)


def attend_forward(block_rows, width, kv_heads, order, tokens_all, gain, weight, tables):
    length, _ = tokens_all.shape
    blocks = length // QUERY_ROWS
    wide = shape((kv_heads, length, LANES))
    return pl.pallas_call(
        functools.partial(attend_body, block_rows),
        out_shape=(
            shape((length, width)),
            shape((length, width)),
            wide,
            wide,
            shape((width // LANES * blocks, PAIR * QUERY_ROWS), jnp.float32),
            shape(tokens_all.shape),
        ),
        in_specs=[SMEM] + [VMEM] * 5,
        out_specs=(VMEM,) * 6,
        scratch_shapes=[pltpu.VMEM((kv_heads, LANES, length), jnp.bfloat16)],
        compiler_params=pltpu.CompilerParams(vmem_limit_bytes=48 << 20),
        cost_estimate=pl.CostEstimate(
            flops=3 * 10**10, bytes_accessed=10**7, transcendentals=10**7
        ),
    )(order, tokens_all, gain, weight, *tables)


def attend_back_body(
    block_rows,
    order,
    branch_all,
    output_weight,
    queries,
    keys,
    values,
    attended,
    log_totals,
    cosine,
    sine,
    grad_packed,
    grads,
    row_dots,
    keys_across,
    key_sums,
    value_sums,
):
    length, width = queries.shape
    kv_heads = keys.shape[0]
    pairs = width // LANES
    blocks = length // QUERY_ROWS
    per = QUERY_ROWS // block_rows

    def project(index, carry):
        place = pl.ds(pl.multiple_of(index * QUERY_ROWS, QUERY_ROWS), QUERY_ROWS)
        rows = rows_in_order(order, branch_all, index, block_rows)
        low = times_transposed(rows, output_weight[...]).astype(jnp.bfloat16)
        grads[place, :] = low
        dots = low.astype(jnp.float32) * rows_in_order(order, attended, index, block_rows).astype(
            jnp.float32
        )
        for pair in range(pairs):
            across = dots[:, pair * LANES : (pair + 1) * LANES].T
            sums = [
                jnp.sum(across[i * HEAD_DIM : (i + 1) * HEAD_DIM], axis=0, keepdims=True)
                for i in range(PAIR)
            ]
            row_dots[pl.ds(pair * blocks + index, 1), :] = jnp.concatenate(sums, axis=1)
        for head in range(kv_heads):
            keys_across[head, :, place] = keys[head, place, :].T
        return carry

    lax.fori_loop(0, blocks, project, 0)

    group = pairs // kv_heads

    def attend(kv_head, carry):
        key_sums[kv_head] = jnp.zeros(key_sums.shape[1:], jnp.float32)
        value_sums[kv_head] = jnp.zeros(value_sums.shape[1:], jnp.float32)
        for member in range(group):
            pair = kv_head * group + member
            lanes = pl.ds(pl.multiple_of(pair * LANES, LANES), LANES)
            for index in range(blocks):
                seen = (index + 1) * QUERY_ROWS
                place = slice(index * QUERY_ROWS, seen)
                rows = two_heads(queries[place, lanes])
                grad_rows = two_heads(grads[place, lanes])
                row = pl.ds(pair * blocks + index, 1)
                scores = times_transposed(keys[kv_head, :seen, :], rows)
                weights = jnp.exp(scores - log_totals[row, :])
                own = weights[seen - QUERY_ROWS :]
                own = jnp.where(later_key(own.shape), 0.0, own)
                if index:
                    weights = jnp.concatenate([weights[: seen - QUERY_ROWS], own], axis=0)
                else:
                    weights = own
                grad_probs = times_transposed(values[kv_head, :seen, :], grad_rows)
                grad_scores = (weights * (grad_probs - row_dots[row, :])).astype(jnp.bfloat16)
                value_sums[kv_head, :seen, :] += product(weights.astype(jnp.bfloat16), grad_rows)
                key_sums[kv_head, :seen, :] += product(grad_scores, rows)
                turned = product(keys_across[kv_head, :, :seen], grad_scores)
                turned = pick_heads(turned).T * (1.0 / math.sqrt(HEAD_DIM))
                turned = turn(turned, cosine[place, :], -sine[place, :]).astype(jnp.bfloat16)
                for i in range(per):
                    grad_packed[block_rows_at(order, index * per + i, block_rows), lanes] = turned[
                        i * block_rows : (i + 1) * block_rows
                    ]
        return carry

    lax.fori_loop(0, kv_heads, attend, 0)

    def finish(block, carry):
        place = pl.ds(pl.multiple_of(block * block_rows, block_rows), block_rows)
        target = block_rows_at(order, block, block_rows)

        def head_sum(head):
            if head < kv_heads:
                tile = key_sums[head, place, :]
            else:
                tile = value_sums[head - kv_heads, place, :]
            tile = tile + pltpu.roll(tile, HEAD_DIM, 1)
            if head < kv_heads:
                tile = turn(tile, cosine[place, :], -sine[place, :])
            return tile

        for tile in range(2 * kv_heads // PAIR):
            first, second = (head_sum(tile * PAIR), head_sum(tile * PAIR + 1))
            joined = jnp.where(low_lanes(first.shape, HEAD_DIM), first, second)
            start = width + tile * LANES
            grad_packed[target, start : start + LANES] = joined.astype(jnp.bfloat16)
        return carry

    lax.fori_loop(0, length // block_rows, finish, 0)


def attend_backward(
    block_rows, order, branch_all, output_weight, queries, keys, values, attended, log_totals, tables
):
    length, width = queries.shape
    kv_heads = keys.shape[0]
    return pl.pallas_call(
        functools.partial(attend_back_body, block_rows),
        out_shape=shape((length, width + 2 * kv_heads * HEAD_DIM)),
        in_specs=[SMEM] + [VMEM] * 9,
        out_specs=VMEM,
        scratch_shapes=[
            pltpu.VMEM((length, width), jnp.bfloat16),
            pltpu.VMEM(log_totals.shape, jnp.float32),
            pltpu.VMEM((kv_heads, LANES, length), jnp.bfloat16),
            pltpu.VMEM((kv_heads, length, LANES), jnp.float32),
            pltpu.VMEM((kv_heads, length, LANES), jnp.float32),
        ],
        compiler_params=pltpu.CompilerParams(vmem_limit_bytes=56 << 20),
        cost_estimate=pl.CostEstimate(
            flops=6 * 10**10, bytes_accessed=10**7, transcendentals=10**7
        ),
    )(
        order,
        branch_all,
        output_weight,
        queries,
        keys,
        values,
        attended,
        log_totals,
        *tables,
    )


def for_part(body):
    me = lax.axis_index("ctx")
    for part in range(4):

        @pl.when(me == part)
        def _(part=part):
            body(part)


def strided_columns(array, shards, part):
    span = array.shape[1] // (4 * shards)
    values = array[...].astype(jnp.float32)
    starts = [(shard * 4 + part) * span for shard in range(shards)]
    return jnp.concatenate([values[:, i : i + span] for i in starts], axis=1).astype(array.dtype)


def pack_hidden_body(shards, gate, up, packed):
    def body(part):
        width = packed.shape[1] // 2
        packed[:, :width] = strided_columns(gate, shards, part)
        packed[:, width:] = strided_columns(up, shards, part)

    for_part(body)


def pack_hidden(shards, gate, up):
    rows, width = gate.shape
    step = 64
    block = pl.BlockSpec((step, width), lambda i: (i, 0))
    return pl.pallas_call(
        functools.partial(pack_hidden_body, shards),
        grid=(rows // step,),
        out_shape=shape((rows, width // 2)),
        in_specs=[block, block],
        out_specs=pl.BlockSpec((step, width // 2), lambda i: (i, 0)),
        cost_estimate=pl.CostEstimate(flops=0, bytes_accessed=10**7, transcendentals=0),
        compiler_params=pltpu.CompilerParams(vmem_limit_bytes=24 << 20),
    )(gate, up)


def pack_attention_body(shards, query, key, value, output, packed):
    def body(part):
        width = query.shape[1] // 4
        rows = output.shape[0] // 4
        packed[:, :width] = strided_columns(query, shards, part)
        packed[:, width : width + KV_WIDTH] = key[...]
        packed[:, width + KV_WIDTH : width + 2 * KV_WIDTH] = value[...]
        for index in range(4):
            packed[index * rows : (index + 1) * rows, width + 2 * KV_WIDTH :] = output[
                part * rows : (part + 1) * rows, index * width : (index + 1) * width
            ]

    for_part(body)


def pack_attention(shards, query, key, value, output):
    rows, width = query.shape
    return pl.pallas_call(
        functools.partial(pack_attention_body, shards),
        out_shape=shape((rows, width // 2 + 2 * KV_WIDTH)),
        in_specs=[VMEM] * 4,
        out_specs=VMEM,
        cost_estimate=pl.CostEstimate(flops=0, bytes_accessed=10**7, transcendentals=0),
        compiler_params=pltpu.CompilerParams(vmem_limit_bytes=24 << 20),
    )(query, key, value, output)


def take_columns(matrix, outer, parts, index):
    rows, columns = matrix.shape
    pieces = matrix.reshape(rows, outer, parts, columns // (outer * parts))
    return lax.dynamic_index_in_dim(pieces, index, axis=2, keepdims=False).reshape(rows, -1)


def take_rows(matrix, parts, index):
    count = matrix.shape[0] // parts
    return lax.dynamic_slice_in_dim(matrix, index * count, count, axis=0)


def put_columns(gathered, outer):
    parts, rows, columns = gathered.shape
    return (
        gathered.reshape(parts, rows, outer, columns // outer)
        .transpose(1, 2, 0, 3)
        .reshape(rows, parts * columns)
    )


def gather_shards(array):
    return lax.all_gather(array, "fsdp", axis=0, tiled=True)


def scatter_shards(array):
    return lax.psum_scatter(
        array.astype(jnp.bfloat16), "fsdp", scatter_dimension=0, tiled=True
    )


def per_device(
    tokens,
    dealing,
    first_gain,
    query_weight,
    key_weight,
    value_weight,
    output_weight,
    second_gain,
    gate_weight,
    up_weight,
    down_weight,
    cotangent,
):
    shard_count = lax.axis_size("fsdp")
    part_count = lax.axis_size("ctx")
    ctx_index = lax.axis_index("ctx")
    row_count = tokens.shape[1]
    block_rows = row_count // 2
    seq_rows = row_count * part_count
    part_width = D // part_count
    dealt_heads = D // shard_count // part_count == HEAD_DIM and part_count == 4
    kv_heads = KV_HEADS if dealt_heads else max(1, KV_HEADS // part_count)
    kv_first = 0 if dealt_heads else ctx_index * KV_HEADS // part_count
    blocks = jnp.arange(2 * part_count, dtype=jnp.int32)
    order = jnp.sum(
        jnp.where(dealing[0][None, :] == blocks[:, None], blocks[None, :], 0), axis=1
    ).astype(jnp.int32)
    tables = rotary_tables(seq_rows)

    tie = lax.optimization_barrier
    gains = jnp.stack([first_gain, second_gain])
    key_value = jnp.concatenate([key_weight, value_weight], axis=1)
    if dealt_heads:
        height = D // shard_count // part_count
        packed = gather_shards(
            pack_attention(shard_count, query_weight, key_weight, value_weight, output_weight)
        )
        tokens_all, gains_all = start_gather(part_count, shard_count, 1, tokens[0], gains)
        tokens_all, gate_weight, up_weight, grad_out = tie(
            (tokens_all, gate_weight, up_weight, cotangent[0])
        )
        gate_up_part = gather_shards(pack_hidden(shard_count, gate_weight, up_weight))
        grad_out_parts = plane_gather(grad_out)
        output_part = (
            packed[:, part_width + 2 * KV_WIDTH :]
            .reshape(shard_count, part_count, height, part_width)
            .transpose(0, 2, 1, 3)
            .reshape(part_width, D)
        )
    else:
        tokens_all, gains_all = start_gather(part_count, shard_count, 1, tokens[0], gains)
        grad_out_all = lax.all_gather(cotangent[0], "ctx", axis=0, tiled=True)
        query_part = gather_shards(take_columns(query_weight, 1, part_count, ctx_index))
        output_part = take_rows(gather_shards(output_weight), part_count, ctx_index)
        key_value = gather_shards(key_value).reshape(D, 2, KV_HEADS, HEAD_DIM)
        key_value = lax.dynamic_slice_in_dim(key_value, kv_first, kv_heads, 2).reshape(D, -1)
        packed = jnp.concatenate([query_part, key_value], axis=1)
        gate_up_part = gather_shards(
            jnp.concatenate(
                [
                    take_columns(gate_weight, shard_count, part_count, ctx_index),
                    take_columns(up_weight, shard_count, part_count, ctx_index),
                ],
                axis=1,
            )
        )
    down_part = gather_shards(take_rows(down_weight, part_count, ctx_index))

    gains = gains_all.transpose(1, 0, 2).reshape(2, D).astype(jnp.float32)
    gain_first, gain_second = (gains[0:1], gains[1:2])
    attended, query_rot, key_rot, value_rows, log_totals, first_all = attend_forward(
        block_rows, part_width, kv_heads, order, tokens_all, gain_first, packed, tables
    )
    if dealt_heads:
        attended, *grad_out_corner = tie((attended, *grad_out_parts[3:]))
        grad_out_parts = (*grad_out_parts[:3], *grad_out_corner)
    residual_mid, second_all = middle_gather(
        part_count, 2, attended, output_part, tokens[0], gain_second
    )
    if dealt_heads:
        second_all, *grad_out_parts = tie((second_all, *grad_out_parts))
        grad_out_all = place_rows(grad_out_parts, jnp.bfloat16)

    gate_up, hidden = hidden_forward(second_all, gate_up_part)
    down_term = column_term(hidden, grad_out_all).astype(jnp.bfloat16)
    down_part, down_term = tie((down_part, down_term))
    down_piece = scatter_shards(down_term)
    output_partial = product(hidden, down_part).astype(jnp.bfloat16)
    relayed = plane_relay(output_partial)
    grad_out_all, output_partial = tie((grad_out_all, output_partial))
    grad_gate_up = hidden_backward(grad_out_all, down_part, gate_up)
    gate_up_term = column_term(second_all, grad_gate_up).astype(jnp.bfloat16)
    grad_gate_up, gate_up_term, *relayed = tie((grad_gate_up, gate_up_term, *relayed))
    gate_up_piece = scatter_shards(gate_up_term)
    last = plane_last(output_partial, relayed)
    grad_mid, second_gain_part, branch_all = middle_back(
        part_count, 3, grad_gate_up, gate_up_part, residual_mid, gain_second, cotangent[0]
    )
    branch_all, down_piece, *last = tie((branch_all, down_piece, *last))
    block_output = (residual_mid + plane_scatter(output_partial, relayed, last)).astype(
        jnp.bfloat16
    )
    if dealt_heads:
        down_parts = plane_gather(down_piece)

    grad_packed = attend_backward(
        block_rows,
        order,
        branch_all,
        output_part,
        query_rot,
        key_rot,
        value_rows,
        attended,
        log_totals,
        tables,
    )
    if dealt_heads:
        packed_term = attention_grads(shard_count, first_all, grad_packed, attended, branch_all)
        grad_packed, packed_term, *down_parts = tie((grad_packed, packed_term, *down_parts))
        packed_piece = scatter_shards(packed_term)
    grad_input, gain_shard = input_back(
        part_count,
        shard_count,
        4,
        grad_packed,
        packed,
        tokens[0],
        gain_first,
        grad_mid,
        second_gain_part,
    )
    if dealt_heads:
        grad_input, packed_piece = tie((grad_input, packed_piece))
        gate_shard, up_shard = place_hidden(shard_count, plane_gather(gate_up_piece))
        down_shard = place_rows(down_parts, jnp.float32)
        query_shard, key_shard, value_shard, output_shard = place_attention(
            shard_count, plane_gather(packed_piece)
        )
    else:

        def gather_columns(piece, outer):
            return put_columns(lax.all_gather(piece, "ctx", axis=0), outer).astype(jnp.float32)

        width = FF // part_count
        gate_shard = gather_columns(gate_up_piece[:, :width], shard_count)
        up_shard = gather_columns(gate_up_piece[:, width:], shard_count)
        down_shard = lax.all_gather(down_piece, "ctx", axis=0, tiled=True).astype(jnp.float32)
        grad_query, grad_key_value = (grad_packed[:, :part_width], grad_packed[:, part_width:])
        query_piece = scatter_shards(column_term(first_all, grad_query))
        query_shard = gather_columns(query_piece, 1)
        key_value_piece = scatter_shards(column_term(first_all, grad_key_value))
        output_term = column_term(attended, branch_all)
        spread = jnp.zeros((D, D), jnp.float32)
        spread = lax.dynamic_update_slice_in_dim(
            spread, output_term, ctx_index * output_term.shape[0], 0
        )
        output_shard = lax.psum(scatter_shards(spread), "ctx").astype(jnp.float32)
        wide = jnp.zeros((D // shard_count, 2, KV_HEADS, HEAD_DIM), jnp.bfloat16)
        wide = lax.dynamic_update_slice_in_dim(
            wide, key_value_piece.reshape(-1, 2, kv_heads, HEAD_DIM), kv_first, 2
        )
        key_value_shard = lax.psum(wide.reshape(-1, 2 * KV_WIDTH), "ctx").astype(jnp.float32)
        key_shard, value_shard = (key_value_shard[:, :KV_WIDTH], key_value_shard[:, KV_WIDTH:])
    return (
        block_output[None],
        grad_input[None],
        gain_shard[0],
        query_shard,
        key_shard,
        value_shard,
        output_shard,
        gain_shard[1],
        gate_shard,
        up_shard,
        down_shard,
    )


def solution(mesh):
    in_specs = (
        P("fsdp", "ctx", None),
        P("fsdp", None),
        P("fsdp"),
        P("fsdp", None),
        P("fsdp", None),
        P("fsdp", None),
        P("fsdp", None),
        P("fsdp"),
        P("fsdp", None),
        P("fsdp", None),
        P("fsdp", None),
        P("fsdp", "ctx", None),
    )
    out_specs = (
        P("fsdp", "ctx", None),
        P("fsdp", "ctx", None),
        P("fsdp"),
        P("fsdp", None),
        P("fsdp", None),
        P("fsdp", None),
        P("fsdp", None),
        P("fsdp"),
        P("fsdp", None),
        P("fsdp", None),
        P("fsdp", None),
    )
    return jax.shard_map(
        per_device, mesh=mesh, in_specs=in_specs, out_specs=out_specs, check_vma=False
    )
```

time: 1050 us -> 577 us (0.55)
  waiting for transfers between devices: 300 us -> 56.3 us
  Pallas kernels: 460 us -> 385 us
  local copies, waits for them, and re-layouts: 107 us -> 46.2 us
  blocking collectives: 55.2 us -> 0 us
  matrix products: 90.2 us -> 36.8 us
  starting transfers between devices: 0.69 us -> 23.1 us
    reduce_scatter x6 -> x3, waiting for transfers between devices: 204 us -> 0.36 us  [scatter_shards(): lax.psum_scatter(array.astype(jnp.bfloat16), 'fsdp', scatter_dimension=0,...]
    all_gather x5 -> x0, waiting for transfers between devices: 94.9 us -> none  [the longest x3 59.1 us: gather_columns(): lax.all_gather(piece, 'ctx', axis=0)]
    pallas_call x5 -> x13, Pallas kernels: 413 us -> 333 us  [the longest x4 265 us: call_plane(): pl.pallas_call(body, out_shape=outs, in_specs=in_specs, out_specs=out_spe...]
    convert_element_type x9 -> x0, local copies, waits for them, and re-layouts: 43.9 us -> none  [gather_columns(): put_columns(lax.all_gather(piece, 'ctx', axis=0), outer).astype(jnp.float32)]
    psum x1 -> x0, blocking collectives: 41.4 us -> none  [per_device(): lax.psum(jnp.concatenate([first_gain_part, second_gain_part], axis=0), ('...]
    ppermute x0 -> x20, waiting for transfers between devices: none -> 38.9 us  [swap(): return lax.ppermute(array, 'ctx', pairs)]
    ppermute x0 -> x20, starting transfers between devices: none -> 22.8 us  [swap(): return lax.ppermute(array, 'ctx', pairs)]
    dot_general x6 -> x2, matrix products: 49.8 us -> 27.3 us  [column_term(): lax.dot_general(source, gradient, (((0,), (0,)), ((), ())), preferred_ele...]
  transfers between devices with their start and end apart: 17 -> 26, of which waited for: 9 -> 6; matrix products, arithmetic and copies ran while one was open for 15% -> 11% of each run, Pallas kernels for 31% -> 67%
where the time goes in v3:
time: 577 us; the launch traced here: 572 us
  Pallas kernels  385 us (67%)
  waiting for transfers between devices  56.3 us (10%)
  local copies, waits for them, and re-layouts  46.2 us (8%)
  matrix products  36.8 us (6%)
  starting transfers between devices  23.1 us (4%)
  between operations  14.9 us (3%)
  other arithmetic  9.85 us (2%)
    pallas_call x4, Pallas kernels, call_plane(): pl.pallas_call(body, out_shape=outs, in_specs=in_specs, out_specs=out_spe...  265 us
    ppermute x20, waiting for transfers between devices, swap(): return lax.ppermute(array, 'ctx', pairs)  38.9 us
    unnamed x108, local copies, waits for them, and re-layouts  30.4 us
    dot_general x2, matrix products, column_term(): lax.dot_general(source, gradient, (((0,), (0,)), ((), ())), preferred_ele...  27.3 us
    pallas_call x1, Pallas kernels, attend_backward(): pl.pallas_call(functools.partial(attend_back_body, block_rows), out_shape...  27.2 us
    pallas_call x1, Pallas kernels, attend_forward(): pl.pallas_call(functools.partial(attend_body, block_rows), out_shape=(sha...  23.9 us
    ppermute x20, starting transfers between devices, swap(): return lax.ppermute(array, 'ctx', pairs)  22.8 us
    pallas_call x1, Pallas kernels, hidden_forward(): pl.pallas_call(hidden_body, grid=(length // step,), out_shape=(shape((len...  20.5 us
  transfers between devices with their start and end apart: 26, of which 6 were waited for; matrix products, arithmetic and copies ran while one was open for 11% of the time, Pallas kernels for 67%

profile of v3, /device:TPU:0, one launch (start us, length us, event | category | flops | bytes accessed | tf_op | source)
XLA Modules:
  0.0 571.7 jit_solution(16647315498971906768)
XLA Ops:
  15.3 41.7 %shard_map.203 = (bf16[1024,2048]{1,0:T(8,128)(2,1)S(1)}, bf16[8,2,256]{2,1,0:T(2,128)(2,1)S(1)}) custom-call(bf16[256,2048]{1,0:T(8,128)(2,1)S(1)} %bitcast.56, bf16[2,256]{1,0:T(2,128)(2,1)S(1)} %pad_maximum_fusion.4.gains), custom_call_target="tpu_custom_call" | custom-call | flops 40000000000 | bytes 133333336 | tf_op jit(solution)/shard_map/pallas_call | solution.py:294
  57.0 2.0 copy-done.44
  67.2 19.1 %collective-permute-done.2.from_along = bf16[256,2048]{1,0:T(8,128)(2,1)} collective-permute-done((bf16[256,2048]{1,0:T(8,128)(2,1)}, bf16[256,2048]{1,0:T(8,128)(2,1)}, u32[]{:S(2)}, u32[]{:S(2)}) %collective-permute-start.2) | collective-permute-done | bytes 1048608 | tf_op jit(solution)/shard_map/ppermute | solution.py:560
  92.1 23.9 %shard_map.205 = (bf16[1024,512]{1,0:T(8,128)(2,1)S(1)}, bf16[1024,512]{1,0:T(8,128)(2,1)S(1)}, bf16[4,1024,128]{2,1,0:T(8,128)(2,1)S(1)}, bf16[4,1024,128]{2,1,...) custom-call(s32[8]{0:T(128)S(1)} %select_reduce_fusion.order, bf16[1024,2048]{1,0:T(8,128)(2,1)} %copy-done.44, ...), custom_call_target="tpu_custom_call" | custom-call | flops 30000001024 | bytes 10000000 | tf_op jit(solution)/shard_map/pallas_call | solution.py:996
  118.1 2.4 slice-done
  122.8 72.0 %shard_map.206 = (f32[256,2048]{1,0:T(8,128)S(1)}, bf16[1024,2048]{1,0:T(8,128)(2,1)S(1)}) custom-call(bf16[1024,512]{1,0:T(8,128)(2,1)S(1)} %get-tuple-element.73.attended, bf16[512,2048]{1,0:T(8,128)(2,1)S(1)} %bitcast.44, bf16[256,2048]{1,0:T(8,128)(2,1)S(1)} %bitcast.57, f32[1,2048]{1,0:T(1,128)S(1)} %bitcast.54), custom_call_target="tpu_custom_call" | custom-call | flops 60000002048 | bytes 200000000 | tf_op jit(solution)/shard_map/pallas_call | solution.py:294
  198.1 2.2 shard_map.207.grad_rows
  202.3 20.5 %shard_map.209 = (f32[1024,2816]{1,0:T(8,128)}, bf16[1024,1408]{1,0:T(8,128)(2,1)}) custom-call(bf16[1024,2048]{1,0:T(8,128)(2,1)} %copy-done.42, bf16[2048,2816]{1,0:T(8,128)(2,1)} %all-gather.6.cloned.1.call-done.gate_weight.up_weight.gate_up_weight, bf16[2048,2816]{1,0:T(8,128)(2,1)} %all-gather.6.cloned.1.call-done.gate_weight.up_weight.gate_up_weight), custom_call_target="tpu_custom_call" | custom-call | flops 11811160064 | bytes 30000000 | tf_op jit(solution)/shard_map/pallas_call | solution.py:631
  222.8 10.0 %convolution_convert_fusion.1 = bf16[1408,2048]{1,0:T(8,128)(2,1)} fusion(bf16[1024,1408]{1,0:T(8,128)(2,1)} %get-tuple-element.86, bf16[1024,2048]{1,0:T(8,128)(2,1)S(1)} %copy-done.3), kind=kOutput, calls=%fused_computation.1 | convolution fusion | flops 5908463616 | bytes 12845056 | tf_op jit(solution)/shard_map/dot_general | solution.py:55
  232.8 16.9 %all-gather.8.cloned.1.call-done.down_weight = bf16[1408,2048]{1,0:T(8,128)(2,1)} async-done(((bf16[176,2048]{1,0:T(8,128)(2,1)}), bf16[1408,2048]{1,0:T(8,128)(2,1)}) %all-gather.8.cloned.1.call-update) | async-done | bytes 5767184 | tf_op jit(solution)/shard_map/all_gather | solution.py:1245
  249.8 9.6 %convolution_convert_fusion.2 = bf16[1024,2048]{1,0:T(8,128)(2,1)S(1)} fusion(bf16[1024,1408]{1,0:T(8,128)(2,1)} %get-tuple-element.86, bf16[1408,2048]{1,0:T(8,128)(2,1)} %all-gather.8.cloned.1.call-done.down_weight), kind=kOutput, calls=%fused_computation.2 | convolution fusion | flops 5907677184 | bytes 12845056 | tf_op jit(solution)/shard_map/dot_general | solution.py:45
  263.8 13.6 %shard_map.210.grad_gate_up = bf16[1024,2816]{1,0:T(8,128)(2,1)} custom-call(bf16[1024,2048]{1,0:T(8,128)(2,1)S(1)} %copy-done.4, bf16[1408,2048]{1,0:T(8,128)(2,1)} %all-gather.8.cloned.1.call-done.down_weight, f32[1024,2816]{1,0:T(8,128)} %get-tuple-element.90.gate_up), custom_call_target="tpu_custom_call" | custom-call | flops 5905580032 | bytes 30000000 | tf_op jit(solution)/shard_map/pallas_call | solution.py:662
  277.4 17.2 %convolution_convert_fusion = bf16[2048,2816]{1,0:T(8,128)(2,1)} fusion(bf16[1024,2048]{1,0:T(8,128)(2,1)S(1)} %copy-done.43, bf16[1024,2816]{1,0:T(8,128)(2,1)} %shard_map.210.grad_gate_up), kind=kOutput, calls=%fused_computation | convolution fusion | flops 11816927232 | bytes 21495808 | tf_op jit(solution)/shard_map/dot_general | solution.py:55
  299.4 84.1 %shard_map.211 = (f32[256,2048]{1,0:T(8,128)}, f32[1,2048]{1,0:T(1,128)S(1)}, bf16[1024,2048]{1,0:T(8,128)(2,1)}) custom-call(bf16[1024,2816]{1,0:T(8,128)(2,1)} %shard_map.210.grad_gate_up, bf16[2048,2816]{1,0:T(8,128)(2,1)} %all-gather.6.cloned.1.call-done.gate_weight.up_weight.gate_up_weight, f32[256,2048]{1,0:T(8,128)} %copy-done.9, ...), custom_call_target="tpu_custom_call" | custom-call | flops 60000002048 | bytes 200000000 | tf_op jit(solution)/shard_map/pallas_call | solution.py:294
  386.3 27.2 %shard_map.212.grad_packed = bf16[1024,1024]{1,0:T(8,128)(2,1)} custom-call(s32[8]{0:T(128)} %copy-done.37, bf16[1024,2048]{1,0:T(8,128)(2,1)} %get-tuple-element.98.branch_all, bf16[512,2048]{1,0:T(8,128)(2,1)} %bitcast.45, bf16[1024,512]{1,0:T(8,128)(2,1)} %copy-done.45, bf16[4,1024,128]{2,1,0:T(8,128)(2,1)} %copy-done.46, ...), custom_call_target="tpu_custom_call" | custom-call | flops 60000002048 | bytes 10000000 | tf_op jit(solution)/shard_map/pallas_call | solution.py:1128
  420.3 15.1 %shard_map.213 = bf16[2048,1536]{1,0:T(8,128)(2,1)} custom-call(bf16[1024,2048]{1,0:T(8,128)(2,1)} %get-tuple-element.103.inputs, bf16[1024,1024]{1,0:T(8,128)(2,1)S(1)} %copy-done.38, bf16[1024,512]{1,0:T(8,128)(2,1)S(1)} %copy-done.41, bf16[1024,2048]{1,0:T(8,128)(2,1)} %get-tuple-element.98.branch_all), custom_call_target="tpu_custom_call" | custom-call | flops 6442450944 | bytes 20000000 | tf_op jit(solution)/shard_map/pallas_call | solution.py:698
  438.8 2.8 copy-done.27
  444.7 67.7 %shard_map.214 = (bf16[256,2048]{1,0:T(8,128)(2,1)S(1)}, f32[2,256]{1,0:T(2,128)S(1)}) custom-call(bf16[1024,1024]{1,0:T(8,128)(2,1)S(1)} %copy-done.39, bf16[2048,1536]{1,0:T(8,128)(2,1)S(1)} %copy-done.27, bf16[256,2048]{1,0:T(8,128)(2,1)S(1)} %bitcast.58, f32[1,2048]{1,0:T(1,128)S(1)} %bitcast.53, f32[256,2048]{1,0:T(8,128)S(1)} %copy-done.48, ...), custom_call_target="tpu_custom_call" | custom-call | flops 49999998976 | bytes 166666672 | tf_op jit(solution)/shard_map/pallas_call | solution.py:294
  515.4 2.5 fusion.5
  522.4 11.6 %collective-permute-done.13.from_along = bf16[256,1536]{1,0:T(8,128)(2,1)S(1)} collective-permute-done((bf16[256,1536]{1,0:T(8,128)(2,1)}, bf16[256,1536]{1,0:T(8,128)(2,1)S(1)}, u32[]{:S(2)}, u32[]{:S(2)}) %collective-permute-start.13) | collective-permute-done | bytes 786464 | tf_op jit(solution)/shard_map/ppermute | solution.py:560
  539.4 2.9 shard_map.217
  542.9 8.1 %collective-permute-done.19.refs_4_ = bf16[128,2816]{1,0:T(8,128)(2,1)S(1)} collective-permute-done((bf16[128,2816]{1,0:T(8,128)(2,1)S(1)}, bf16[128,2816]{1,0:T(8,128)(2,1)S(1)}, u32[]{:S(2)}, u32[]{:S(2)}) %collective-permute-start.19) | collective-permute-done | bytes 720928 | tf_op jit(solution)/shard_map/ppermute | solution.py:560
  551.0 8.7 %shard_map.216 = (f32[256,5632]{1,0:T(8,128)}, f32[256,5632]{1,0:T(8,128)}) custom-call(bf16[256,2816]{1,0:T(8,128)(2,1)S(1)} %copy-done.18, bf16[256,2816]{1,0:T(8,128)(2,1)} %collective-permute-done.16.refs_1_, bf16[256,2816]{1,0:T(8,128)(2,1)} %collective-permute-done.17.refs_2_, bf16[128,2816]{1,0:T(8,128)(2,1)S(1)} %collective-permute-done.18.refs_3_, ...), custom_call_target="tpu_custom_call" | custom-call | bytes 20000000 | tf_op jit(solution)/shard_map/pallas_call | solution.py:763
  559.7 4.0 shard_map.215
  (189 shorter events, 71.1 us)
Async XLA Ops:
  7.2 84.9 %all-gather.4.cloned.1.call-start = ((), (), s32[]{:S(2)}) async-start(), calls=%async_computation.3 | async-start | bytes 7077888 | tf_op jit(solution)/shard_map/all_gather | solution.py:1245
  12.7 189.6 %all-gather.6.cloned.1.call-start = ((), (), s32[]{:S(2)}) async-start(), calls=%async_computation.4 | async-start | bytes 12976128 | tf_op jit(solution)/shard_map/all_gather | solution.py:1245
  61.1 188.6 %all-gather.8.cloned.1.call-start = ((), (), s32[]{:S(2)}) async-start(), calls=%async_computation.5 | async-start | bytes 6488064 | tf_op jit(solution)/shard_map/all_gather | solution.py:1245
  61.1 25.2 %collective-permute-start.2 = (bf16[256,2048]{1,0:T(8,128)(2,1)}, bf16[256,2048]{1,0:T(8,128)(2,1)}, u32[]{:S(2)}, u32[]{:S(2)}) collective-permute-start(bf16[256,2048]{1,0:T(8,128)(2,1)} %bitcast.47), channel_id=1, source_target_pairs={{0,16},{8,24},{16,0},{24,8},{1,17},{9,25},{17,1},{25,9},{2,18},{10... | collective-permute-start | bytes 3145736 | tf_op jit(solution)/shard_map/ppermute | solution.py:560
  62.8 27.0 %collective-permute-start = (bf16[256,2048]{1,0:T(8,128)(2,1)}, bf16[256,2048]{1,0:T(8,128)(2,1)}, u32[]{:S(2)}, u32[]{:S(2)}) collective-permute-start(bf16[256,2048]{1,0:T(8,128)(2,1)} %bitcast.48), channel_id=1, source_target_pairs={{0,8},{8,0},{16,24},{24,16},{1,9},{9,1},{17,25},{25,17},{2,10},{10... | collective-permute-start | bytes 3145736 | tf_op jit(solution)/shard_map/ppermute | solution.py:560
  64.2 320.1 %reduce-scatter.4.cloned.1.call-start = ((), (), s32[]{:S(2)}) async-start(), calls=%async_computation.6 | async-start | bytes 6488064 | tf_op jit(solution)/shard_map/reduce_scatter | solution.py:1249
  88.2 34.6 %collective-permute-start.3 = (bf16[128,2048]{1,0:T(8,128)(2,1)}, bf16[128,2048]{1,0:T(8,128)(2,1)}, u32[]{:S(2)}, u32[]{:S(2)}) collective-permute-start(bf16[128,2048]{1,0:T(8,128)(2,1)} %slice.78), channel_id=1, source_target_pairs={{0,8},{8,0},{16,24},{24,16},{1,9},{9,1},{17,25},{25,17},{2,10},{10... | collective-permute-start | bytes 1572872 | tf_op jit(solution)/shard_map/ppermute | solution.py:560
  91.7 31.0 %collective-permute-start.1 = (bf16[128,2048]{1,0:T(8,128)(2,1)}, bf16[128,2048]{1,0:T(8,128)(2,1)}, u32[]{:S(2)}, u32[]{:S(2)}) collective-permute-start(bf16[128,2048]{1,0:T(8,128)(2,1)} %slice.77), channel_id=1, source_target_pairs={{0,16},{8,24},{16,0},{24,8},{1,17},{9,25},{17,1},{25,9},{2,18},{10... | collective-permute-start | bytes 1572872 | tf_op jit(solution)/shard_map/ppermute | solution.py:560
  249.7 186.2 %reduce-scatter.8.cloned.1.call-start = ((), (), s32[]{:S(2)}) async-start(), calls=%async_computation.8 | async-start | bytes 12976128 | tf_op jit(solution)/shard_map/reduce_scatter | solution.py:1249
  260.7 34.0 %collective-permute-start.4 = (bf16[2,128,2048]{2,1,0:T(8,128)(2,1)}, bf16[2,128,2048]{2,1,0:T(8,128)(2,1)}, u32[]{:S(2)}, u32[]{:S(2)}) collective-permute-start(bf16[2,128,2048]{2,1,0:T(8,128)(2,1)} %pad_maximum_fusion), channel_id=1, source_target_pairs={{0,8},{8,0},{16,24},{24,16},{1,9},{9,1},{17,25},{25,17},{2,10},{10... | collective-permute-start | bytes 3145736 | tf_op jit(solution)/shard_map/ppermute | solution.py:560
  262.3 32.4 %collective-permute-start.5 = (bf16[2,128,2048]{2,1,0:T(8,128)(2,1)S(1)}, bf16[2,128,2048]{2,1,0:T(8,128)(2,1)}, u32[]{:S(2)}, u32[]{:S(2)}) collective-permute-start(bf16[2,128,2048]{2,1,0:T(8,128)(2,1)S(1)} %pad_maximum_fusion.1), channel_id=1, source_target_pairs={{0,16},{8,24},{16,0},{24,8},{1,17},{9,25},{17,1},{25,9},{2,18},{10... | collective-permute-start | bytes 3145736 | tf_op jit(solution)/shard_map/ppermute | solution.py:560
  294.7 218.7 %reduce-scatter.6.cloned.1.call-start = ((), (), s32[]{:S(2)}) async-start(), calls=%async_computation.7 | async-start | bytes 7077888 | tf_op jit(solution)/shard_map/reduce_scatter | solution.py:1249
  296.8 86.7 %collective-permute-start.7 = (bf16[128,2048]{1,0:T(8,128)(2,1)S(1)}, bf16[128,2048]{1,0:T(8,128)(2,1)S(1)}, u32[]{:S(2)}, u32[]{:S(2)}) collective-permute-start(bf16[128,2048]{1,0:T(8,128)(2,1)S(1)} %get-tuple-element.127), channel_id=1, source_target_pairs={{0,8},{8,0},{16,24},{24,16},{1,9},{9,1},{17,25},{25,17},{2,10},{10... | collective-permute-start | bytes 1572872 | tf_op jit(solution)/shard_map/ppermute | solution.py:560
  298.0 86.3 %collective-permute-start.6 = (bf16[128,2048]{1,0:T(8,128)(2,1)S(1)}, bf16[128,2048]{1,0:T(8,128)(2,1)}, u32[]{:S(2)}, u32[]{:S(2)}) collective-permute-start(bf16[128,2048]{1,0:T(8,128)(2,1)S(1)} %get-tuple-element.128), channel_id=1, source_target_pairs={{0,16},{8,24},{16,0},{24,8},{1,17},{9,25},{17,1},{25,9},{2,18},{10... | collective-permute-start | bytes 1572872 | tf_op jit(solution)/shard_map/ppermute | solution.py:560
  384.3 29.2 %collective-permute-start.9 = (bf16[176,2048]{1,0:T(8,128)(2,1)}, bf16[176,2048]{1,0:T(8,128)(2,1)S(1)}, u32[]{:S(2)}, u32[]{:S(2)}) collective-permute-start(bf16[176,2048]{1,0:T(8,128)(2,1)} %reduce-scatter.4.cloned.1.call-done.own), channel_id=1, source_target_pairs={{0,16},{8,24},{16,0},{24,8},{1,17},{9,25},{17,1},{25,9},{2,18},{10... | collective-permute-start | bytes 2162696 | tf_op jit(solution)/shard_map/ppermute | solution.py:560
  384.9 30.8 %collective-permute-start.8 = (bf16[176,2048]{1,0:T(8,128)(2,1)}, bf16[176,2048]{1,0:T(8,128)(2,1)S(1)}, u32[]{:S(2)}, u32[]{:S(2)}) collective-permute-start(bf16[176,2048]{1,0:T(8,128)(2,1)} %reduce-scatter.4.cloned.1.call-done.own), channel_id=1, source_target_pairs={{0,8},{8,0},{16,24},{24,16},{1,9},{9,1},{17,25},{25,17},{2,10},{10... | collective-permute-start | bytes 2162696 | tf_op jit(solution)/shard_map/ppermute | solution.py:560
  435.9 82.0 %collective-permute-start.17 = (bf16[256,2816]{1,0:T(8,128)(2,1)}, bf16[256,2816]{1,0:T(8,128)(2,1)}, u32[]{:S(2)}, u32[]{:S(2)}) collective-permute-start(bf16[256,2816]{1,0:T(8,128)(2,1)} %reduce-scatter.8.cloned.1.call-done.refs_0_), channel_id=1, source_target_pairs={{0,16},{8,24},{16,0},{24,8},{1,17},{9,25},{17,1},{25,9},{2,18},{10... | collective-permute-start | bytes 4325384 | tf_op jit(solution)/shard_map/ppermute | solution.py:560
  437.3 83.3 %collective-permute-start.16 = (bf16[256,2816]{1,0:T(8,128)(2,1)}, bf16[256,2816]{1,0:T(8,128)(2,1)}, u32[]{:S(2)}, u32[]{:S(2)}) collective-permute-start(bf16[256,2816]{1,0:T(8,128)(2,1)} %reduce-scatter.8.cloned.1.call-done.refs_0_), channel_id=1, source_target_pairs={{0,8},{8,0},{16,24},{24,16},{1,9},{9,1},{17,25},{25,17},{2,10},{10... | collective-permute-start | bytes 4325384 | tf_op jit(solution)/shard_map/ppermute | solution.py:560
  513.4 20.7 %collective-permute-start.13 = (bf16[256,1536]{1,0:T(8,128)(2,1)}, bf16[256,1536]{1,0:T(8,128)(2,1)S(1)}, u32[]{:S(2)}, u32[]{:S(2)}) collective-permute-start(bf16[256,1536]{1,0:T(8,128)(2,1)} %reduce-scatter.6.cloned.1.call-done.own), channel_id=1, source_target_pairs={{0,16},{8,24},{16,0},{24,8},{1,17},{9,25},{17,1},{25,9},{2,18},{10... | collective-permute-start | bytes 2359304 | tf_op jit(solution)/shard_map/ppermute | solution.py:560
  514.8 20.8 %collective-permute-start.12 = (bf16[256,1536]{1,0:T(8,128)(2,1)}, bf16[256,1536]{1,0:T(8,128)(2,1)}, u32[]{:S(2)}, u32[]{:S(2)}) collective-permute-start(bf16[256,1536]{1,0:T(8,128)(2,1)} %reduce-scatter.6.cloned.1.call-done.own), channel_id=1, source_target_pairs={{0,8},{8,0},{16,24},{24,16},{1,9},{9,1},{17,25},{25,17},{2,10},{10... | collective-permute-start | bytes 2359304 | tf_op jit(solution)/shard_map/ppermute | solution.py:560
  519.1 31.8 %collective-permute-start.19 = (bf16[128,2816]{1,0:T(8,128)(2,1)S(1)}, bf16[128,2816]{1,0:T(8,128)(2,1)S(1)}, u32[]{:S(2)}, u32[]{:S(2)}) collective-permute-start(bf16[128,2816]{1,0:T(8,128)(2,1)S(1)} %slice.86), channel_id=1, source_target_pairs={{0,8},{8,0},{16,24},{24,16},{1,9},{9,1},{17,25},{25,17},{2,10},{10... | collective-permute-start | bytes 2162696 | tf_op jit(solution)/shard_map/ppermute | solution.py:560
  521.8 29.2 %collective-permute-start.18 = (bf16[128,2816]{1,0:T(8,128)(2,1)S(1)}, bf16[128,2816]{1,0:T(8,128)(2,1)S(1)}, u32[]{:S(2)}, u32[]{:S(2)}) collective-permute-start(bf16[128,2816]{1,0:T(8,128)(2,1)S(1)} %slice.85), channel_id=1, source_target_pairs={{0,16},{8,24},{16,0},{24,8},{1,17},{9,25},{17,1},{25,9},{2,18},{10... | collective-permute-start | bytes 2162696 | tf_op jit(solution)/shard_map/ppermute | solution.py:560
  535.0 24.7 %collective-permute-start.15 = (bf16[128,1536]{1,0:T(8,128)(2,1)S(1)}, bf16[128,1536]{1,0:T(8,128)(2,1)S(1)}, u32[]{:S(2)}, u32[]{:S(2)}) collective-permute-start(bf16[128,1536]{1,0:T(8,128)(2,1)S(1)} %slice.84), channel_id=1, source_target_pairs={{0,8},{8,0},{16,24},{24,16},{1,9},{9,1},{17,25},{25,17},{2,10},{10... | collective-permute-start | bytes 1179656 | tf_op jit(solution)/shard_map/ppermute | solution.py:560
  536.6 23.1 %collective-permute-start.14 = (bf16[128,1536]{1,0:T(8,128)(2,1)S(1)}, bf16[128,1536]{1,0:T(8,128)(2,1)S(1)}, u32[]{:S(2)}, u32[]{:S(2)}) collective-permute-start(bf16[128,1536]{1,0:T(8,128)(2,1)S(1)} %slice.83), channel_id=1, source_target_pairs={{0,16},{8,24},{16,0},{24,8},{1,17},{9,25},{17,1},{25,9},{2,18},{10... | collective-permute-start | bytes 1179656 | tf_op jit(solution)/shard_map/ppermute | solution.py:560
  (56 other events, 808.3 us)
Sparse Core Ops, SparseCore 0:
  12.8 67.4 all-gather.3
  82.5 106.7 all-gather.5
  190.9 58.7 all-gather.7
  252.4 63.5 reduce-scatter.3
  318.2 117.6 reduce-scatter.7
  438.1 68.1 reduce-scatter.5

commit v4 on v3

--- a/solution.py
+++ b/solution.py
@@ -22,10 +22,11 @@
 MESH = pl.DeviceIdType.MESH
 VMEM = pl.BlockSpec(memory_space=pltpu.VMEM)
 SMEM = pl.BlockSpec(memory_space=pltpu.SMEM)
-HBM = pl.BlockSpec(memory_space=pl.ANY)
+HBM = pl.BlockSpec(memory_space=pltpu.HBM)
 LANES = 128
 PAIR = LANES // HEAD_DIM
 QUERY_ROWS = 256
+VMEM_MEGABYTES = 60
 
 
 def shape(dims, kind=jnp.bfloat16):
@@ -108,6 +109,7 @@
         self.local_sem, self.send_sem, self.recv_sem = sems
         self.size = own.shape[0] // PIECES
         self.copies = [[] for _ in range(PIECES)]
+        self.relays = []
 
     def place(self, owner, piece):
         start = owner * self.own.shape[0] + piece * self.size
@@ -137,14 +139,15 @@
         self.copies[piece].append(local)
 
     def finish(self):
+        self.relay()
+        self.drain()
+
+    def relay(self, pieces=(0, PIECES // 2, 1, PIECES // 2 + 1)):
+        relays = self.relays
         if self.count != 4:
-            for copies in self.copies:
-                for copy in copies:
-                    copy.wait()
             return
         _, across, along, _ = plane_places()
-        relays = []
-        for piece in (0, PIECES // 2, 1, PIECES // 2 + 1):
+        for piece in pieces:
             first = piece < PIECES // 2
             came, left = (0, 1) if first else (1, 0)
             owner, peer = (across, along) if first else (along, across)
@@ -155,123 +158,303 @@
                     block, block, self.send_sem.at[2, piece], self.recv_sem.at[2, piece], ctx=peer
                 )
             )
+
+    def drain(self):
+        if self.count != 4:
+            for copies in self.copies:
+                for copy in copies:
+                    copy.wait()
+            return
         for piece in range(PIECES):
             to_across, to_along, local = self.copies[piece]
             (to_along if piece < PIECES // 2 else to_across).wait_recv()
             to_across.wait_send()
             to_along.wait_send()
             local.wait()
-        for relay in relays:
+        for relay in self.relays:
             relay.wait()
 
 
-def product_blocks(count, pairs, rows, width):
-    tile = 512
-
-    def block(owner, store):
-        start = pl.multiple_of(owner * rows, rows)
-
-        def column(index, carry):
-            columns = pl.ds(pl.multiple_of(index * tile, tile), tile)
-            value = None
-            for left, right, transposed in pairs:
-                piece = left[pl.ds(start, rows), :]
-                if transposed:
-                    term = times_transposed(piece, right[columns, : piece.shape[1]])
-                else:
-                    term = product(piece, right[:, columns])
-                value = term if value is None else value + term
-            store(columns, value)
+CHUNKS = 2
+
+
+def line_sems(shards):
+    hops = shards // 2 - 1
+    return [
+        pltpu.SemaphoreType.DMA,
+        pltpu.SemaphoreType.DMA((2 * hops, CHUNKS)),
+        pltpu.SemaphoreType.DMA((2 * hops, CHUNKS)),
+        pltpu.SemaphoreType.DMA((2 * hops + 1, CHUNKS)),
+        pltpu.SemaphoreType.DMA((2 * hops + 1, CHUNKS)),
+    ]
+
+
+class LineGather:
+    def __init__(self, shards, own, out, sems):
+        self.own, self.out = (own, out)
+        self.local_sem, self.send_sem, self.recv_sem, self.core_send, self.core_recv = sems
+        self.me = lax.axis_index("fsdp")
+        self.hops = shards // 2 - 1
+        self.chip = self.me // 2
+        self.twin = self.me + 1 - 2 * lax.rem(self.me, 2)
+        self.size = own.shape[0] // CHUNKS
+
+    def block(self, owner, chunk):
+        start = owner * self.own.shape[0] + chunk * self.size
+        return self.out.at[pl.ds(pl.multiple_of(start, self.size), self.size)]
+
+    def copy(self, distance, way, chunk, sems, index, peer):
+        owner = self.me - 2 * (1 - 2 * way) * distance
+        target = self.block(owner, chunk)
+        part = pl.ds(chunk * self.size, self.size)
+        send_sem, recv_sem = sems
+        return pltpu.make_async_remote_copy(
+            src_ref=self.own.at[part] if distance == 0 else target,
+            dst_ref=target,
+            send_sem=send_sem.at[index, chunk],
+            recv_sem=recv_sem.at[index, chunk],
+            device_id={"fsdp": peer},
+            device_id_type=MESH,
+        )
+
+    def hop(self, way, distance, chunk):
+        sems = (self.send_sem, self.recv_sem)
+        peer = self.me + 2 * (1 - 2 * way)
+        return self.copy(distance, way, chunk, sems, way * self.hops + distance, peer)
+
+    def cross(self, way, distance, chunk):
+        index = distance if way == 0 else self.hops + distance
+        sems = (self.core_send, self.core_recv)
+        return self.copy(distance, way, chunk, sems, index, self.twin)
+
+    def can_send(self, way):
+        return self.chip < self.hops if way == 0 else self.chip > 0
+
+    def behind(self, way, distance):
+        return self.chip >= distance if way == 0 else self.chip + distance <= self.hops
+
+    def local(self):
+        rows = self.own.shape[0]
+        target = self.out.at[pl.ds(pl.multiple_of(self.me * rows, rows), rows)]
+        return pltpu.make_async_copy(self.own, target, self.local_sem)
+
+    def start(self):
+        for chunk in range(CHUNKS):
+            for way in (0, 1):
+                pl.when(self.can_send(way))(
+                    lambda way=way, chunk=chunk: self.hop(way, 0, chunk).start()
+                )
+        for chunk in range(CHUNKS):
+            self.cross(0, 0, chunk).start()
+        self.local().start()
+
+    def step(self, distance, chunk):
+        for way in (0, 1):
+
+            @pl.when(self.behind(way, distance))
+            def _(way=way):
+                self.hop(way, distance - 1, chunk).wait_recv()
+                if distance < self.hops:
+                    pl.when(self.can_send(way))(lambda: self.hop(way, distance, chunk).start())
+                self.cross(way, distance, chunk).start()
+
+    def drain(self):
+        for chunk in range(CHUNKS):
+            for way in (0, 1):
+                for distance in range(self.hops):
+                    here = jnp.logical_and(self.can_send(way), self.behind(way, distance))
+                    pl.when(here)(
+                        lambda way=way, d=distance, chunk=chunk: self.hop(way, d, chunk).wait_send()
+                    )
+                for distance in range(1, self.hops + 1):
+                    pl.when(self.behind(way, distance))(
+                        lambda way=way, d=distance, chunk=chunk: self.cross(way, d, chunk).wait()
+                    )
+            self.cross(0, 0, chunk).wait()
+        self.local().wait()
+
+
+TILE = 512
+
+
+def begin(source, target, sem):
+    copy = pltpu.make_async_copy(source, target, sem)
+    copy.start()
+    return copy
+
+
+class Scatter:
+    def __init__(self, count, left, right, transposed, refs):
+        self.count, self.transposed = (count, transposed)
+        self.left_buf, self.right_buf, self.load_sem, *refs = refs
+        self.send_buf, self.recv_buf, self.kept, self.total, self.send_sem, self.recv_sem = refs
+        self.rows, self.width = self.total.shape
+        self.tiles = self.width // TILE
+        self.loads = {}
+        owners = self.owners()
+        depth = self.left_buf.shape[1]
+        self.load_left(left, owners[0], 0)
+        for tile in range(self.tiles):
+            columns = pl.ds(tile * TILE, TILE)
+            if transposed:
+                place = (columns, pl.ds(0, depth))
+                source, target = (right.at[place], self.right_buf.at[columns])
+            else:
+                source, target = (right.at[:, columns], self.right_buf.at[:, columns])
+            self.loads["tile", tile] = begin(source, target, self.load_sem.at[count + tile])
+        for index in range(1, count):
+            self.load_left(left, owners[index], index)
+
+    def owners(self):
+        me = lax.axis_index("ctx")
+        if self.count != 4:
+            return [lax.rem(me + step, self.count) for step in range(1, self.count)] + [me]
+        _, across, along, corner = plane_places()
+        return [corner, across, along, me]
+
+    def block_rows(self, owner):
+        return pl.ds(pl.multiple_of(owner * self.rows, self.rows), self.rows)
+
+    def load_left(self, left, owner, index):
+        rows = self.block_rows(owner)
+        self.loads["left", index] = begin(
+            left.at[rows], self.left_buf.at[rows], self.load_sem.at[index]
+        )
+
+    def tile(self, owner, columns):
+        piece = self.left_buf[self.block_rows(owner), :]
+        if self.transposed:
+            return times_transposed(piece, self.right_buf[columns, :])
+        return product(piece, self.right_buf[:, columns])
+
+    def block(self, index, store):
+        owner = self.owners()[index]
+        self.loads["left", index].wait()
+
+        def column(tile, carry):
+            columns = pl.ds(pl.multiple_of(tile * TILE, TILE), TILE)
+            store(columns, self.tile(owner, columns))
             return carry
 
-        lax.fori_loop(0, width // tile, column, 0)
-
-    return block
-
-
-def scatter_products(count, pairs, send_buf, recv_buf, kept, total, send_sem, recv_sem):
-    rows, width = total.shape
-    half = rows // 2
-    block = product_blocks(count, pairs, rows, width)
-    me = lax.axis_index("ctx")
-
-    def store_own(columns, value):
-        total[:, columns] = value
-
-    def send(slot, part, sem, peer):
+        lax.fori_loop(0, self.tiles, column, 0)
+
+    def send(self, slot, part, columns, sem, peer):
         return remote(
-            send_buf.at[slot, part],
-            recv_buf.at[slot, part],
-            send_sem.at[sem],
-            recv_sem.at[sem],
+            self.send_buf.at[slot, part, columns],
+            self.recv_buf.at[slot, part, columns],
+            self.send_sem.at[sem],
+            self.recv_sem.at[sem],
             ctx=peer,
         )
 
-    if count != 4:
+    def store_own(self, columns, value):
+        self.total[:, columns] = value
+
+    def run(self):
+        if self.count == 4:
+            self.run_relayed()
+        else:
+            self.run_direct()
+
+    def run_direct(self):
+        for tile in range(self.tiles):
+            self.loads["tile", tile].wait()
         copies = []
-        for step in range(1, count):
-            owner = lax.rem(me + step, count)
-
-            def store_sent(columns, value, step=step):
-                send_buf[step - 1, :, columns] = value.astype(send_buf.dtype)
-
-            block(owner, store_sent)
-            copies.append(send(step - 1, pl.ds(0, rows), step - 1, owner))
-        block(me, store_own)
-        for copy in copies:
+        everything = (pl.ds(0, self.rows), pl.ds(0, self.width))
+        for index, owner in enumerate(self.owners()[:-1]):
+
+            def store_sent(columns, value, index=index):
+                self.send_buf[index, :, columns] = value.astype(self.send_buf.dtype)
+
+            self.block(index, store_sent)
+            copies.append(self.send(index, *everything, index, owner))
+        self.block(self.count - 1, self.store_own)
+        self.relays, self.copies = ([], copies)
+
+    def run_relayed(self):
+        corner, across, along, me = self.owners()
+        send_buf, kept, tiles = (self.send_buf, self.kept, self.tiles)
+        half = self.rows // 2
+        low, high = (pl.ds(0, half), pl.ds(half, half))
+        whole = pl.ds(0, self.width)
+        relays = []
+        self.loads["left", 0].wait()
+        for tile in range(tiles):
+            columns = pl.ds(tile * TILE, TILE)
+            self.loads["tile", tile].wait()
+            send_buf[0, :, columns] = self.tile(corner, columns).astype(send_buf.dtype)
+            relays.append(
+                (
+                    self.send(0, low, columns, tile, across),
+                    self.send(0, high, columns, tiles + tile, along),
+                )
+            )
+
+        def store_across(columns, value):
+            send_buf[1, low, columns] = value[:half].astype(send_buf.dtype)
+            kept[high, columns] = value[half:]
+
+        def store_along(columns, value):
+            send_buf[1, high, columns] = value[half:].astype(send_buf.dtype)
+            kept[low, columns] = value[:half]
+
+        self.block(1, store_across)
+        copies = [self.send(1, low, whole, 4 * tiles, across)]
+        self.block(2, store_along)
+        copies.append(self.send(1, high, whole, 4 * tiles + 1, along))
+        self.block(3, self.store_own)
+        for tile in range(tiles):
+            columns = pl.ds(tile * TILE, TILE)
+            for side, peer in ((0, along), (1, across)):
+                relays[tile][side].wait_recv()
+                part = (low, high)[side]
+
+                def add(where, columns=columns):
+                    value = kept[where, columns] + self.recv_buf[0, where, columns].astype(
+                        jnp.float32
+                    )
+                    send_buf[2, where, columns] = value.astype(send_buf.dtype)
+
+                for_strips(side * half, half, add)
+                sem = (2 + side) * tiles + tile
+                copies.append(self.send(2, part, columns, sem, peer))
+        self.relays, self.copies = (relays, copies)
+
+    def finish(self):
+        for pair in self.relays:
+            for copy in pair:
+                copy.wait_send()
+        for copy in self.copies:
             copy.wait()
-        return
-    _, across, along, corner = plane_places()
-    low, high = (pl.ds(0, half), pl.ds(half, half))
-
-    def store_corner(columns, value):
-        send_buf[0, :, columns] = value.astype(send_buf.dtype)
-
-    def store_across(columns, value):
-        send_buf[1, low, columns] = value[:half].astype(send_buf.dtype)
-        kept[high, columns] = value[half:]
-
-    def store_along(columns, value):
-        send_buf[1, high, columns] = value[half:].astype(send_buf.dtype)
-        kept[low, columns] = value[:half]
-
-    block(corner, store_corner)
-    relay_low = send(0, low, 0, across)
-    relay_high = send(0, high, 1, along)
-    block(across, store_across)
-    direct_low = send(1, low, 2, across)
-    block(along, store_along)
-    direct_high = send(1, high, 3, along)
-    block(me, store_own)
-
-    def add(where):
-        value = kept[where, :] + recv_buf[0, where, :].astype(jnp.float32)
-        send_buf[2, where, :] = value.astype(send_buf.dtype)
-
-    relay_low.wait_recv()
-    for_strips(0, half, add)
-    final_low = send(2, low, 4, along)
-    relay_high.wait_recv()
-    for_strips(half, half, add)
-    final_high = send(2, high, 5, across)
-    relay_low.wait_send()
-    relay_high.wait_send()
-    direct_low.wait()
-    direct_high.wait()
-    final_low.wait()
-    final_high.wait()
-
-
-def scatter_scratch(count, rows, width):
+
+
+def scatter_scratch(count, rows, width, left, right, transposed, depth):
     slots = 3 if count == 4 else count - 1
-    sems = 6 if count == 4 else count - 1
+    sems = 4 * (width // TILE) + 2 if count == 4 else count - 1
     return [
+        pltpu.VMEM(left.shape, jnp.bfloat16),
+        pltpu.VMEM((width, depth) if transposed else (depth, width), jnp.bfloat16),
+        pltpu.SemaphoreType.DMA((count + width // TILE,)),
         pltpu.VMEM((slots, rows, width), jnp.bfloat16),
         pltpu.VMEM((slots, rows, width), jnp.bfloat16),
         pltpu.VMEM((rows, width) if count == 4 else (8, LANES), jnp.float32),
         pltpu.VMEM((rows, width), jnp.float32),
         pltpu.SemaphoreType.DMA((sems,)),
         pltpu.SemaphoreType.DMA((sems,)),
+    ]
+
+
+SCATTER_REFS = 9
+
+
+def side_loads(sources, refs):
+    *targets, sem = refs
+    return [begin(source, target, sem.at[i]) for i, (source, target) in enumerate(zip(sources, targets))]
+
+
+def side_scratch(*arrays):
+    return [pltpu.VMEM(a.shape, a.dtype) for a in arrays] + [
+        pltpu.SemaphoreType.DMA((len(arrays),))
     ]
 
 
@@ -306,10 +489,93 @@
     )(*args)
 
 
-def start_body(count, shards, tokens, gains, tokens_all, gains_all, *sems):
+def for_part(body):
+    me = lax.axis_index("ctx")
+    for part in range(4):
+
+        @pl.when(me == part)
+        def _(part=part):
+            body(part)
+
+
+def strided_columns(values, shards, part):
+    span = values.shape[1] // (4 * shards)
+    starts = [(shard * 4 + part) * span for shard in range(shards)]
+    wide = values.astype(jnp.float32)
+    return jnp.concatenate([wide[:, i : i + span] for i in starts], axis=1).astype(values.dtype)
+
+
+def pack_attention(shards, query, key, value, output, packed):
+    def body(part):
+        width = query.shape[1] // 4
+        rows = output.shape[0] // 4
+        packed[:, :width] = strided_columns(query[...], shards, part)
+        packed[:, width : width + KV_WIDTH] = key[...]
+        packed[:, width + KV_WIDTH : width + 2 * KV_WIDTH] = value[...]
+        for index in range(4):
+            packed[index * rows : (index + 1) * rows, width + 2 * KV_WIDTH :] = output[
+                part * rows : (part + 1) * rows, index * width : (index + 1) * width
+            ]
+
+    for_part(body)
+
+
+def pack_hidden(shards, gate, up, packed):
+    def body(part):
+        width = packed.shape[1] // 2
+
+        def strip(where):
+            packed[where, :width] = strided_columns(gate[where, :], shards, part)
+            packed[where, width:] = strided_columns(up[where, :], shards, part)
+
+        for_strips(0, packed.shape[0], strip)
+
+    for_part(body)
+
+
+def write_tables(cosine, sine):
+    half = HEAD_DIM // 2
+
+    def strip(where):
+        dims = (STRIP, LANES)
+        lane = lax.broadcasted_iota(jnp.int32, dims, 1)
+        place = lax.broadcasted_iota(jnp.int32, dims, 0) + where.start
+        index = lax.rem(lane, half).astype(jnp.float32)
+        frequency = jnp.exp(-math.log(10000.0) * index * (2.0 / HEAD_DIM))
+        angles = place.astype(jnp.float32) * frequency
+        cosine[where, :] = jnp.cos(angles)
+        sine[where, :] = jnp.where(low_lanes(dims, half), -jnp.sin(angles), jnp.sin(angles))
+
+    for_strips(0, cosine.shape[0], strip)
+
+
+def start_body(count, shards, tokens, first_gain, second_gain, *refs):
+    if count == 4:
+        weights, refs = (refs[:6], refs[6:])
+    tokens_all, gain_first, gain_second, cosine, sine, *refs = refs
+    if count == 4:
+        weights_all, packed_hidden, *refs = refs
+    gains, gains_all, gain_send, gain_recv, *refs = refs
     meet(count, shards)
-    gain_local, gain_send, gain_recv = sems[:3]
+    first = RowGather(count, tokens, tokens_all, refs[:3])
+    half = PIECES // 2
+    first.send(0)
+    first.send(half)
+    if count == 4:
+        packed, gate, up, load_sem, *line_refs = refs[3:]
+        loads = [
+            pltpu.make_async_copy(weights[4 + i], target, load_sem.at[i])
+            for i, target in enumerate((gate, up))
+        ]
+        for load in loads:
+            load.start()
+        pack_attention(shards, *weights[:4], packed)
+        line = LineGather(shards, packed, weights_all, line_refs)
+        line.start()
     me = lax.axis_index("fsdp")
+    gains[0:1, :] = first_gain[...]
+    gains[1:2, :] = second_gain[...]
+    gains_all[me] = gains[...]
     copies = []
     for step in range(1, shards):
         copies.append(
@@ -321,36 +587,75 @@
                 fsdp=lax.rem(me + step, shards),
             )
         )
-    local = pltpu.make_async_copy(gains, gains_all.at[me], gain_local)
-    local.start()
-    first = RowGather(count, tokens, tokens_all, sems[3:6])
-    order = (0, PIECES // 2, 1, PIECES // 2 + 1)
-    for piece in order:
-        first.send(piece)
-    first.finish()
-    local.wait()
+    if count != 4:
+        write_tables(cosine, sine)
+        first.send(1)
+        first.send(half + 1)
+        first.finish()
+    else:
+        steps = [(d, c) for d in range(1, line.hops + 1) for c in range(CHUNKS)]
+        line.step(*steps[0])
+        first.relay((0, half))
+        first.send(1)
+        first.send(half + 1)
+        write_tables(cosine, sine)
+        for step in steps[1:3]:
+            line.step(*step)
+        for load in loads:
+            load.wait()
+        pack_hidden(shards, gate, up, packed_hidden)
+        first.relay((1, half + 1))
+        for step in steps[3:-1]:
+            line.step(*step)
+        first.drain()
     for copy in copies:
         copy.wait()
-
-
-def start_gather(count, shards, ident, tokens, gains):
+    span = gains.shape[1]
+    for shard in range(shards):
+        lanes = slice(shard * span, (shard + 1) * span)
+        gain_first[:, lanes] = gains_all[shard, 0:1, :].astype(jnp.float32)
+        gain_second[:, lanes] = gains_all[shard, 1:2, :].astype(jnp.float32)
+    if count == 4:
+        line.step(*steps[-1])
+        line.drain()
+
+
+def start_gather(count, shards, ident, tokens, first_gain, second_gain, *weights):
     rows, width = tokens.shape
-    gathered = shape((count * rows, width))
+    span = first_gain.shape[1]
+    wide = shape((1, width), jnp.float32)
+    table = shape((count * rows, LANES), jnp.float32)
+    outs = [shape((count * rows, width)), wide, wide, table, table]
+    out_specs = [HBM] + [VMEM] * 4
+    in_specs = [HBM, VMEM, VMEM]
+    scratch = [
+        pltpu.VMEM((2, span), jnp.bfloat16),
+        pltpu.VMEM((shards, 2, span), jnp.bfloat16),
+        pltpu.SemaphoreType.DMA((shards - 1,)),
+        pltpu.SemaphoreType.DMA((shards - 1,)),
+    ] + gather_sems(count)
+    if weights:
+        height = weights[0].shape[0]
+        packed = width // 2 + 2 * KV_WIDTH
+        outs += [shape((shards * height, packed)), shape((height, FF // 2))]
+        out_specs += [HBM, VMEM]
+        in_specs += [VMEM] * 4 + [HBM] * 2
+        scratch += [
+            pltpu.VMEM((height, packed), jnp.bfloat16),
+            pltpu.VMEM((height, FF), jnp.bfloat16),
+            pltpu.VMEM((height, FF), jnp.bfloat16),
+            pltpu.SemaphoreType.DMA((2,)),
+        ] + line_sems(shards)
     return call_plane(
         functools.partial(start_body, count, shards),
         ident,
-        (gathered, shape((shards,) + gains.shape)),
-        (HBM, HBM),
-        [HBM] * 2,
-        [
-            pltpu.SemaphoreType.DMA,
-            pltpu.SemaphoreType.DMA((shards - 1,)),
-            pltpu.SemaphoreType.DMA((shards - 1,)),
-        ]
-        + gather_sems(count),
-        4 * 10**10,
-        4,
-        (tokens, gains),
+        tuple(outs),
+        tuple(out_specs),
+        in_specs,
+        scratch,
+        5 * 10**10,
+        VMEM_MEGABYTES,
+        (tokens, first_gain, second_gain, *weights),
     )
 
 
@@ -362,22 +667,25 @@
     gather.finish()
 
 
-def middle_body(
-    count, attended, weight, tokens, gain, residual, second_all, own, send_buf, recv_buf, kept, total,
-    send_sem, recv_sem, *sems
-):
+def middle_body(count, attended, weight, tokens, gain, residual, second_all, own, *refs):
+    scatter = Scatter(count, attended, weight, False, refs[:SCATTER_REFS])
+    side = refs[SCATTER_REFS : SCATTER_REFS + 2]
+    loads = side_loads([tokens], side)
     meet(count)
-    scatter_products(
-        count, [(attended, weight, False)], send_buf, recv_buf, kept, total, send_sem, recv_sem
-    )
+    scatter.run()
+    scatter.finish()
+    for load in loads:
+        load.wait()
 
     def strip(where):
-        values = tokens[where, :].astype(jnp.float32) + received(count, recv_buf, total, where)
+        values = side[0][where, :].astype(jnp.float32) + received(
+            count, scatter.recv_buf, scatter.total, where
+        )
         residual[where, :] = values
         normed, _ = norm_parts(values)
         own[where, :] = (normed * gain[...]).astype(jnp.bfloat16)
 
-    strips_and_send(RowGather(count, own, second_all, sems), strip)
+    strips_and_send(RowGather(count, own, second_all, refs[SCATTER_REFS + 2 :]), strip)
 
 
 def middle_gather(count, ident, attended, weight, tokens, gain):
@@ -387,44 +695,42 @@
         ident,
         (shape((rows, width), jnp.float32), shape((count * rows, width))),
         (VMEM, HBM),
-        [VMEM] * 4,
+        [HBM] * 3 + [VMEM],
         [pltpu.VMEM((rows, width), jnp.bfloat16)]
-        + scatter_scratch(count, rows, width)
+        + scatter_scratch(count, rows, width, attended, weight, False, attended.shape[1])
+        + side_scratch(tokens)
         + gather_sems(count),
         6 * 10**10,
-        40,
+        VMEM_MEGABYTES,
         (attended, weight, tokens, gain),
     )
 
 
 def middle_back_body(
-    count, grad_gate_up, gate_up_weight, residual, gain, grad_out, grad_mid, gain_part,
-    branch_all, own, send_buf, recv_buf, kept, total, send_sem, recv_sem, *sems
+    count, grad_gate_up, gate_up_weight, residual, grad_out, gain, grad_mid, gain_part, branch_all, own,
+    *refs
 ):
+    scatter = Scatter(count, grad_gate_up, gate_up_weight, True, refs[:SCATTER_REFS])
+    side = refs[SCATTER_REFS : SCATTER_REFS + 3]
+    loads = side_loads([residual, grad_out], side)
     meet(count)
-    scatter_products(
-        count,
-        [(grad_gate_up, gate_up_weight, True)],
-        send_buf,
-        recv_buf,
-        kept,
-        total,
-        send_sem,
-        recv_sem,
-    )
+    scatter.run()
+    scatter.finish()
     gain_part[...] = jnp.zeros_like(gain_part)
+    for load in loads:
+        load.wait()
 
     def strip(where):
-        gradient = received(count, recv_buf, total, where)
-        normed, inverse = norm_parts(residual[where, :])
+        gradient = received(count, scatter.recv_buf, scatter.total, where)
+        normed, inverse = norm_parts(side[0][where, :])
         gain_part[...] += jnp.sum(gradient * normed, axis=0, keepdims=True)
-        values = grad_out[where, :].astype(jnp.float32) + norm_back(
+        values = side[1][where, :].astype(jnp.float32) + norm_back(
             gradient * gain[...], normed, inverse
         )
         grad_mid[where, :] = values
         own[where, :] = values.astype(jnp.bfloat16)
 
-    strips_and_send(RowGather(count, own, branch_all, sems), strip)
+    strips_and_send(RowGather(count, own, branch_all, refs[SCATTER_REFS + 3 :]), strip)
 
 
 def column_halves(array):
@@ -446,42 +752,46 @@
             shape((count * rows, width)),
         ),
         (VMEM, VMEM, HBM),
-        [VMEM] * 5,
+        [HBM] * 4 + [VMEM],
         [pltpu.VMEM((rows, width), jnp.bfloat16)]
-        + scatter_scratch(count, rows, width)
+        + scatter_scratch(
+            count, rows, width, grad_gate_up, gate_up_weight, True, grad_gate_up.shape[1]
+        )
+        + side_scratch(residual, grad_out)
         + gather_sems(count),
         6 * 10**10,
-        52,
-        (grad_gate_up, gate_up_weight, residual, gain, grad_out),
+        VMEM_MEGABYTES,
+        (grad_gate_up, gate_up_weight, residual, grad_out, gain),
     )
 
 
 def input_back_body(
-    count, shards, grad_packed, weight, tokens, gain, grad_mid, second_part, grad_input, gain_sums, gain_part, parts, part_recv, sums, sums_recv, send_buf,
-    recv_buf, kept, total, send_sem, recv_sem, part_send_sem, part_recv_sem, sums_send_sem,
-    sums_recv_sem
+    count, shards, grad_packed, weight, tokens, grad_mid, piece, gain, second_part, grad_input, gain_sums,
+    piece_all, gain_part, parts, part_recv, sums, sums_recv, part_send_sem, part_recv_sem, sums_send_sem,
+    sums_recv_sem, *refs
 ):
+    scatter = Scatter(count, grad_packed, weight, True, refs[:SCATTER_REFS])
+    side = refs[SCATTER_REFS : SCATTER_REFS + 3]
+    loads = side_loads([tokens, grad_mid], side)
+    gather = RowGather(count, piece, piece_all, refs[SCATTER_REFS + 3 :])
     meet(count, shards)
-    scatter_products(
-        count,
-        [(grad_packed, weight, True)],
-        send_buf,
-        recv_buf,
-        kept,
-        total,
-        send_sem,
-        recv_sem,
-    )
+    scatter.run()
+    for part in range(PIECES):
+        gather.send(part)
+    scatter.finish()
     gain_part[...] = jnp.zeros_like(gain_part)
+    for load in loads:
+        load.wait()
 
     def strip(where):
-        gradient = received(count, recv_buf, total, where)
-        normed, inverse = norm_parts(tokens[where, :].astype(jnp.float32))
+        gradient = received(count, scatter.recv_buf, scatter.total, where)
+        normed, inverse = norm_parts(side[0][where, :].astype(jnp.float32))
         gain_part[...] += jnp.sum(gradient * normed, axis=0, keepdims=True)
-        values = grad_mid[where, :] + norm_back(gradient * gain[...], normed, inverse)
+        values = side[1][where, :] + norm_back(gradient * gain[...], normed, inverse)
         grad_input[where, :] = values.astype(jnp.bfloat16)
 
     for_strips(0, grad_input.shape[0], strip)
+    gather.relay()
     me = lax.axis_index("fsdp")
     span = parts.shape[2]
     for shard in range(shards):
@@ -522,36 +832,41 @@
     for step in range(1, count):
         value = value + sums_recv[step - 1]
     gain_sums[...] = value
+    gather.drain()
 
 
 def input_back(
-    count, shards, ident, grad_packed, weight, tokens, gain, grad_mid, second_part
+    count, shards, ident, grad_packed, weight, tokens, gain, grad_mid, second_part, piece
 ):
     rows, width = tokens.shape
     span = width // shards
     return call_plane(
         functools.partial(input_back_body, count, shards),
         ident,
-        (shape((rows, width)), shape((2, span), jnp.float32)),
-        (VMEM, VMEM),
-        [VMEM] * 6,
+        (
+            shape((rows, width)),
+            shape((2, span), jnp.float32),
+            shape((count * piece.shape[0], piece.shape[1])),
+        ),
+        (VMEM, VMEM, HBM),
+        [HBM] * 5 + [VMEM] * 2,
         [
             pltpu.VMEM((1, width), jnp.float32),
             pltpu.VMEM((shards, 2, span), jnp.float32),
             pltpu.VMEM((shards - 1, 2, span), jnp.float32),
             pltpu.VMEM((2, span), jnp.float32),
             pltpu.VMEM((count - 1, 2, span), jnp.float32),
-        ]
-        + scatter_scratch(count, rows, width)
-        + [
             pltpu.SemaphoreType.DMA((shards - 1,)),
             pltpu.SemaphoreType.DMA((shards - 1,)),
             pltpu.SemaphoreType.DMA((count - 1,)),
             pltpu.SemaphoreType.DMA((count - 1,)),
-        ],
+        ]
+        + scatter_scratch(count, rows, width, grad_packed, weight, True, grad_packed.shape[1])
+        + side_scratch(tokens, grad_mid)
+        + gather_sems(count),
         5 * 10**10,
-        40,
-        (grad_packed, weight, tokens, gain, grad_mid, second_part),
+        VMEM_MEGABYTES,
+        (grad_packed, weight, tokens, grad_mid, piece, gain, second_part),
     )
 
 
@@ -560,13 +875,18 @@
     return lax.ppermute(array, "ctx", pairs)
 
 
+def plane_near(array):
+    return (array, swap(array, False), swap(array, True))
+
+
+def plane_far(near):
+    _, across, along = near
+    half = across.shape[0] // 2
+    return (*near, swap(across[:half], True), swap(along[half:], False))
+
+
 def plane_gather(array):
-    if lax.axis_size("ctx") != 4:
-        return lax.all_gather(array, "ctx", axis=0)
-    half = array.shape[0] // 2
-    across, along = (swap(array, False), swap(array, True))
-    low, high = (swap(across[:half], True), swap(along[half:], False))
-    return (array, across, along, low, high)
+    return plane_far(plane_near(array))
 
 
 def take_half(partial, owner, side):
@@ -614,13 +934,16 @@
     )
 
 
-def hidden_body(rows, gate_weight, up_weight, gate_up, hidden):
+def hidden_body(rows, gate_weight, up_weight, gate_up, hidden, rows_across, hidden_across):
     width = hidden.shape[1]
+    rows_across[...] = rows[...].T
     gate = product(rows[...], gate_weight[...])
     gate_up[:, :width] = gate
     upward = product(rows[...], up_weight[...])
     gate_up[:, width:] = upward
-    hidden[...] = (gate * jax.nn.sigmoid(gate) * upward).astype(jnp.bfloat16)
+    low = (gate * jax.nn.sigmoid(gate) * upward).astype(jnp.bfloat16)
+    hidden[...] = low
+    hidden_across[...] = low.T
 
 
 def hidden_forward(second_all, gate_up_weight):
@@ -631,21 +954,29 @@
     return pl.pallas_call(
         hidden_body,
         grid=(length // step,),
-        out_shape=(shape((length, 2 * width), jnp.float32), shape((length, width))),
+        out_shape=(
+            shape((length, 2 * width), jnp.float32),
+            shape((length, width)),
+            shape((depth, length)),
+            shape((width, length)),
+        ),
         in_specs=[pl.BlockSpec((step, depth), lambda i: (i, 0))] + list(specs),
         out_specs=(
             pl.BlockSpec((step, 2 * width), lambda i: (i, 0)),
             pl.BlockSpec((step, width), lambda i: (i, 0)),
+            pl.BlockSpec((depth, step), lambda i: (0, i)),
+            pl.BlockSpec((width, step), lambda i: (0, i)),
         ),
-        compiler_params=pltpu.CompilerParams(vmem_limit_bytes=52 << 20),
+        compiler_params=pltpu.CompilerParams(vmem_limit_bytes=VMEM_MEGABYTES << 20),
         cost_estimate=pl.CostEstimate(
             flops=4 * length * depth * width, bytes_accessed=3 * 10**7, transcendentals=10**6
         ),
     )(second_all, gate_weight, up_weight)
 
 
-def hidden_back_body(grad_rows, down_weight, gate_up, grad_gate_up):
+def hidden_back_body(grad_rows, down_weight, gate_up, hidden, grad_gate_up, partial):
     width = down_weight.shape[0]
+    partial[...] = product(hidden[...], down_weight[...]).astype(jnp.bfloat16)
     grad_hidden = times_transposed(grad_rows[...], down_weight[...])
     gate, upward = (gate_up[:, :width], gate_up[:, width:])
     sigmoid_gate = jax.nn.sigmoid(gate)
@@ -655,62 +986,218 @@
     grad_gate_up[:, width:] = (grad_hidden * silu_gate).astype(jnp.bfloat16)
 
 
-def hidden_backward(grad_out_all, down_weight, gate_up):
+def hidden_backward(grad_out_all, down_weight, gate_up, hidden):
     length, depth = grad_out_all.shape
     width = down_weight.shape[0]
     step = QUERY_ROWS
     return pl.pallas_call(
         hidden_back_body,
         grid=(length // step,),
-        out_shape=shape((length, 2 * width)),
+        out_shape=(shape((length, 2 * width)), shape((length, depth))),
         in_specs=[
             pl.BlockSpec((step, depth), lambda i: (i, 0)),
             pl.BlockSpec((width, depth), lambda i: (0, 0)),
             pl.BlockSpec((step, 2 * width), lambda i: (i, 0)),
+            pl.BlockSpec((step, width), lambda i: (i, 0)),
         ],
-        out_specs=pl.BlockSpec((step, 2 * width), lambda i: (i, 0)),
-        compiler_params=pltpu.CompilerParams(vmem_limit_bytes=48 << 20),
+        out_specs=(
+            pl.BlockSpec((step, 2 * width), lambda i: (i, 0)),
+            pl.BlockSpec((step, depth), lambda i: (i, 0)),
+        ),
+        compiler_params=pltpu.CompilerParams(vmem_limit_bytes=VMEM_MEGABYTES << 20),
         cost_estimate=pl.CostEstimate(
-            flops=2 * length * depth * width, bytes_accessed=3 * 10**7, transcendentals=10**6
+            flops=4 * length * depth * width, bytes_accessed=3 * 10**7, transcendentals=10**6
         ),
-    )(grad_out_all, down_weight, gate_up)
-
-
-def attention_grads_body(inputs, grad_packed, attended, branch_all, packed):
-    width = grad_packed.shape[1]
-    packed[:, :width] = product(inputs[...].T, grad_packed[...]).astype(jnp.bfloat16)
-    rows = HEAD_DIM
-    heads = attended[...].T
-    upper = lax.rem(pl.program_id(0), PAIR) == 1
-    heads = jnp.where(upper, heads[rows:], heads[:rows])
-    out = product(heads, branch_all[...]).astype(jnp.bfloat16)
-    part = out.shape[1] // (packed.shape[0] // rows)
-    for index in range(packed.shape[0] // rows):
-        packed[index * rows : (index + 1) * rows, width:] = out[
-            :, index * part : (index + 1) * part
-        ]
-
-
-def attention_grads(shards, first_all, grad_packed, attended, branch_all):
-    length, depth = first_all.shape
-    span = depth // shards
-    width = grad_packed.shape[1] + attended.shape[1]
-    return pl.pallas_call(
-        attention_grads_body,
-        grid=(shards,),
-        out_shape=shape((depth, width)),
-        in_specs=[
-            pl.BlockSpec((length, span), lambda i: (0, i)),
-            pl.BlockSpec(grad_packed.shape, lambda i: (0, 0)),
-            pl.BlockSpec((length, LANES), lambda i: (0, i // PAIR)),
-            pl.BlockSpec(branch_all.shape, lambda i: (0, 0)),
+    )(grad_out_all, down_weight, gate_up, hidden)
+
+
+def meet_twin():
+    me = lax.axis_index("fsdp")
+    barrier = pltpu.get_barrier_semaphore()
+    signal(barrier, fsdp=me + 1 - 2 * lax.rem(me, 2))
+    pl.semaphore_wait(barrier, 1)
+
+
+def shard_rows(array, shards, core):
+    span = array.shape[0] // shards
+    starts = [pl.multiple_of((2 * i + core) * span, 16) for i in range(shards // 2)]
+    return jnp.concatenate([array[pl.ds(start, span), :] for start in starts], axis=0)
+
+
+GRAD_TILE = 256
+
+
+class CoreSum:
+    def __init__(self, send_buf, recv_buf, send_sem, recv_sem):
+        self.send_buf, self.recv_buf = (send_buf, recv_buf)
+        self.send_sem, self.recv_sem = (send_sem, recv_sem)
+
+    def copy(self, tile):
+        me = lax.axis_index("fsdp")
+        columns = pl.ds(pl.multiple_of(tile * GRAD_TILE, GRAD_TILE), GRAD_TILE)
+        return pltpu.make_async_remote_copy(
+            src_ref=self.send_buf.at[:, columns],
+            dst_ref=self.recv_buf.at[:, columns],
+            send_sem=self.send_sem.at[tile],
+            recv_sem=self.recv_sem.at[tile],
+            device_id={"fsdp": me + 1 - 2 * lax.rem(me, 2)},
+            device_id_type=MESH,
+        )
+
+
+def column_tile(tile):
+    return pl.ds(pl.multiple_of(tile * GRAD_TILE, GRAD_TILE), GRAD_TILE)
+
+
+def core_grads_body(shards, across, gradient, *refs):
+    *outs, half, send_buf, recv_buf, send_sem, recv_sem = refs
+    core = lax.rem(lax.axis_index("fsdp"), 2)
+    tiles = gradient.shape[1] // GRAD_TILE
+    sums = CoreSum(send_buf, recv_buf, send_sem, recv_sem)
+    half[...] = shard_rows(across, shards, 1 - core)
+    meet_twin()
+
+    def send(tile, carry):
+        columns = column_tile(tile)
+        send_buf[:, columns] = product(half[...], gradient[:, columns]).astype(jnp.bfloat16)
+        sums.copy(tile).start()
+        return carry
+
+    lax.fori_loop(0, tiles, send, 0)
+    half[...] = shard_rows(across, shards, core)
+
+    def total(tile):
+        columns = column_tile(tile)
+        value = product(half[...], gradient[:, columns])
+        sums.copy(tile).wait()
+        return (value + recv_buf[:, columns].astype(jnp.float32)).astype(jnp.bfloat16)
+
+    done = 0
+    first = 0
+    for out in outs:
+        width = out.shape[1]
+        whole = (first + width) // GRAD_TILE
+
+        def keep(tile, carry, out=out, first=first):
+            start = pl.multiple_of(tile * GRAD_TILE - first, LANES)
+            out[:, pl.ds(start, GRAD_TILE)] = total(tile)
+            return carry
+
+        lax.fori_loop(done // GRAD_TILE, whole, keep, 0)
+        done = whole * GRAD_TILE
+        rest = first + width - done
+        if rest and out is not outs[-1]:
+            value = total(whole)
+            out[:, width - rest :] = value[:, :rest]
+            following = outs[outs.index(out) + 1]
+            following[:, : GRAD_TILE - rest] = value[:, rest:]
+            done += GRAD_TILE
+        first += width
+
+
+def core_grads(shards, ident, source, gradient, parts=1):
+    depth, length = source.shape
+    width = gradient.shape[1]
+    tiles = width // GRAD_TILE
+    return call_plane(
+        functools.partial(core_grads_body, shards),
+        ident,
+        (shape((depth // 2, width // parts)),) * parts,
+        (VMEM,) * parts,
+        [VMEM] * 2,
+        [
+            pltpu.VMEM((depth // 2, length), jnp.bfloat16),
+            pltpu.VMEM((depth // 2, width), jnp.bfloat16),
+            pltpu.VMEM((depth // 2, width), jnp.bfloat16),
+            pltpu.SemaphoreType.DMA((tiles,)),
+            pltpu.SemaphoreType.DMA((tiles,)),
         ],
-        out_specs=pl.BlockSpec((span, width), lambda i: (i, 0)),
-        compiler_params=pltpu.CompilerParams(vmem_limit_bytes=48 << 20),
-        cost_estimate=pl.CostEstimate(
-            flops=2 * length * depth * width, bytes_accessed=2 * 10**7, transcendentals=0
-        ),
-    )(first_all, grad_packed, attended, branch_all)
+        2 * length * depth * width,
+        VMEM_MEGABYTES,
+        (source, gradient),
+    )
+
+
+def attention_grads_body(
+    shards, across, gradient, heads, branch_all, out, half, outs, send_buf, recv_buf, send_sem, recv_sem
+):
+    core = lax.rem(lax.axis_index("fsdp"), 2)
+    width = gradient.shape[1]
+    tiles = width // GRAD_TILE
+    total = out.shape[1] // GRAD_TILE
+    part = out.shape[1] - width
+    span = out.shape[0] // (shards // 2)
+    height = HEAD_DIM
+    sums = CoreSum(send_buf, recv_buf, send_sem, recv_sem)
+    meet_twin()
+
+    def heads_product(index, carry):
+        columns = pl.ds(pl.multiple_of(index * 512, 512), 512)
+        outs[:, columns] = product(heads[...], branch_all[:, columns])
+        return carry
+
+    lax.fori_loop(0, branch_all.shape[1] // 512, heads_product, 0)
+
+    def pieces(side):
+        for chip in range(shards // 2):
+            rows = pl.ds(pl.multiple_of((2 * chip + side) * height, height), height)
+            for index in range(span // height):
+                start = chip * span + index * height
+                yield slice(start, start + height), outs[rows, index * part : (index + 1) * part]
+
+    for rows, value in pieces(1 - core):
+        send_buf[rows, width:] = value.astype(jnp.bfloat16)
+    for tile in range(tiles, total):
+        sums.copy(tile).start()
+    half[...] = shard_rows(across, shards, 1 - core)
+
+    def send(tile, carry):
+        columns = column_tile(tile)
+        send_buf[:, columns] = product(half[...], gradient[:, columns]).astype(jnp.bfloat16)
+        sums.copy(tile).start()
+        return carry
+
+    lax.fori_loop(0, tiles, send, 0)
+    half[...] = shard_rows(across, shards, core)
+
+    def keep(tile, carry):
+        columns = column_tile(tile)
+        value = product(half[...], gradient[:, columns])
+        sums.copy(tile).wait()
+        out[:, columns] = (value + recv_buf[:, columns].astype(jnp.float32)).astype(jnp.bfloat16)
+        return carry
+
+    lax.fori_loop(0, tiles, keep, 0)
+    for tile in range(tiles, total):
+        sums.copy(tile).wait()
+    for rows, value in pieces(core):
+        value = value + recv_buf[rows, width:].astype(jnp.float32)
+        out[rows, width:] = value.astype(jnp.bfloat16)
+
+
+def attention_grads(shards, ident, first_across, grad_packed, heads_across, branch_all):
+    depth, length = first_across.shape
+    heads = heads_across.shape[0]
+    width = grad_packed.shape[1] + heads
+    tiles = width // GRAD_TILE
+    return call_plane(
+        functools.partial(attention_grads_body, shards),
+        ident,
+        shape((depth // 2, width)),
+        VMEM,
+        [VMEM] * 4,
+        [
+            pltpu.VMEM((depth // 2, length), jnp.bfloat16),
+            pltpu.VMEM((heads, branch_all.shape[1]), jnp.float32),
+            pltpu.VMEM((depth // 2, width), jnp.bfloat16),
+            pltpu.VMEM((depth // 2, width), jnp.bfloat16),
+            pltpu.SemaphoreType.DMA((tiles,)),
+            pltpu.SemaphoreType.DMA((tiles,)),
+        ],
+        2 * length * depth * width,
+        VMEM_MEGABYTES,
+        (first_across, grad_packed, heads_across, branch_all),
+    )
 
 
 def sort_parts(parts, sorted_parts, corner_low):
@@ -729,46 +1216,60 @@
         sorted_parts[corner] = high[...]
 
 
+def interleaved(values, shards):
+    span = values[0].shape[1] // shards
+    return jnp.concatenate(
+        [v[:, shard * span : (shard + 1) * span] for shard in range(shards) for v in values], axis=1
+    )
+
+
+def place_sorted_body(shards, *refs):
+    *parts, target = refs
+    target[...] = interleaved([part[...].astype(jnp.float32) for part in parts], shards)
+
+
+def place_sorted(shards, array):
+    rows, width = (array.shape[0] // 4, array.shape[1])
+    step = 64
+    steps = rows // step
+    return pl.pallas_call(
+        functools.partial(place_sorted_body, shards),
+        grid=(steps,),
+        out_shape=shape((rows, 4 * width), jnp.float32),
+        in_specs=[
+            pl.BlockSpec((step, width), lambda i, part=part: (part * steps + i, 0))
+            for part in range(4)
+        ],
+        out_specs=pl.BlockSpec((step, 4 * width), lambda i: (i, 0)),
+        cost_estimate=pl.CostEstimate(flops=0, bytes_accessed=10**7, transcendentals=0),
+        compiler_params=pltpu.CompilerParams(vmem_limit_bytes=VMEM_MEGABYTES << 20),
+    )(array, array, array, array)
+
+
 def place_hidden_body(shards, *refs):
-    parts, (gate, up, sorted_parts) = (refs[:5], refs[5:])
+    parts, (target, sorted_parts) = (refs[:5], refs[5:])
     steps = pl.num_programs(0)
     sort_parts(parts, sorted_parts, pl.program_id(0) < steps // 2)
-    count = sorted_parts.shape[0]
-    width = sorted_parts.shape[2] // 2
-    span = width // shards
-    for target, offset in ((gate, 0), (up, width)):
-        values = [
-            sorted_parts[part, :, offset : offset + width].astype(jnp.float32)
-            for part in range(count)
-        ]
-        target[...] = jnp.concatenate(
-            [
-                values[part][:, shard * span : (shard + 1) * span]
-                for shard in range(shards)
-                for part in range(count)
-            ],
-            axis=1,
-        )
+    values = [sorted_parts[part].astype(jnp.float32) for part in range(sorted_parts.shape[0])]
+    target[...] = interleaved(values, shards)
 
 
 def place_hidden(shards, parts):
     rows, width = parts[0].shape
-    step = 32
+    step = 64
     half = rows // step // 2
-    outs = shape((rows, 2 * width), jnp.float32)
     whole = pl.BlockSpec((step, width), lambda i: (i, 0))
     low = pl.BlockSpec((step, width), lambda i: (jnp.minimum(i, half - 1), 0))
     high = pl.BlockSpec((step, width), lambda i: (jnp.maximum(i - half, 0), 0))
-    result = pl.BlockSpec((step, 2 * width), lambda i: (i, 0))
     return pl.pallas_call(
         functools.partial(place_hidden_body, shards),
         grid=(rows // step,),
-        out_shape=(outs, outs),
+        out_shape=shape((rows, 4 * width), jnp.float32),
         in_specs=[whole, whole, whole, low, high],
-        out_specs=(result, result),
+        out_specs=pl.BlockSpec((step, 4 * width), lambda i: (i, 0)),
         scratch_shapes=[pltpu.VMEM((4, step, width), jnp.bfloat16)],
-        cost_estimate=pl.CostEstimate(flops=0, bytes_accessed=2 * 10**7, transcendentals=0),
-        compiler_params=pltpu.CompilerParams(vmem_limit_bytes=24 << 20),
+        cost_estimate=pl.CostEstimate(flops=0, bytes_accessed=10**7, transcendentals=0),
+        compiler_params=pltpu.CompilerParams(vmem_limit_bytes=VMEM_MEGABYTES << 20),
     )(*parts)
 
 
@@ -796,7 +1297,7 @@
         in_specs=[VMEM] * 5,
         out_specs=VMEM,
         cost_estimate=pl.CostEstimate(flops=0, bytes_accessed=10**7, transcendentals=0),
-        compiler_params=pltpu.CompilerParams(vmem_limit_bytes=24 << 20),
+        compiler_params=pltpu.CompilerParams(vmem_limit_bytes=VMEM_MEGABYTES << 20),
     )(*parts)
 
 
@@ -846,20 +1347,8 @@
         out_specs=(VMEM,) * 4,
         scratch_shapes=[pltpu.VMEM((4, rows, width), jnp.bfloat16)],
         cost_estimate=pl.CostEstimate(flops=0, bytes_accessed=10**7, transcendentals=0),
-        compiler_params=pltpu.CompilerParams(vmem_limit_bytes=32 << 20),
+        compiler_params=pltpu.CompilerParams(vmem_limit_bytes=VMEM_MEGABYTES << 20),
     )(*parts)
-
-
-def rotary_tables(length):
-    frequency = jnp.exp(
-        -math.log(10000.0) * jnp.arange(HEAD_DIM // 2).astype(jnp.float32) * (2.0 / HEAD_DIM)
-    )
-    angles = jnp.arange(length).astype(jnp.float32)[:, None] * frequency[None, :]
-    cosine, sine = (jnp.cos(angles), jnp.sin(angles))
-    return (
-        jnp.concatenate([cosine] * (2 * PAIR), axis=1),
-        jnp.concatenate([-sine, sine] * PAIR, axis=1),
-    )
 
 
 def low_lanes(dims, size):
@@ -906,9 +1395,28 @@
     )
 
 
+def slots(dealing, order):
+    for slot in range(dealing.shape[1]):
+        order[dealing[0, slot]] = slot
+
+
+def unpack_output(weight, output_part):
+    width = output_part.shape[0]
+    if weight.shape[1] <= width + 2 * KV_WIDTH:
+        return
+    parts = output_part.shape[1] // width
+    shards = width // HEAD_DIM
+    for shard in range(shards):
+        for part in range(parts):
+            start = (shard * parts + part) * HEAD_DIM
+            output_part[
+                shard * HEAD_DIM : (shard + 1) * HEAD_DIM, part * width : (part + 1) * width
+            ] = weight[start : start + HEAD_DIM, weight.shape[1] - width :]
+
+
 def attend_body(
     block_rows,
-    order,
+    dealing,
     tokens_all,
     gain,
     weight,
@@ -919,9 +1427,14 @@
     keys,
     values,
     log_totals,
-    first_all,
+    first_across,
+    heads_across,
+    output_part,
     values_across,
+    order,
 ):
+    slots(dealing, order)
+    unpack_output(weight, output_part)
     length, width = queries.shape
     kv_heads = keys.shape[0]
     pairs = width // LANES
@@ -933,10 +1446,11 @@
             rows_in_order(order, tokens_all, index, block_rows).astype(jnp.float32)
         )
         rows = (normed * gain[...]).astype(jnp.bfloat16)
+        turned_rows = rows.T
         for i in range(QUERY_ROWS // block_rows):
-            first_all[block_rows_at(order, index * (QUERY_ROWS // block_rows) + i, block_rows), :] = (
-                rows[i * block_rows : (i + 1) * block_rows]
-            )
+            first_across[
+                :, block_rows_at(order, index * (QUERY_ROWS // block_rows) + i, block_rows)
+            ] = turned_rows[:, i * block_rows : (i + 1) * block_rows]
         cos_rows, sin_rows = (cosine[place, :], sine[place, :])
         projected = product(rows, weight[:, :width])
         for pair in range(pairs):
@@ -978,7 +1492,12 @@
             totals = jnp.sum(exponent, axis=0, keepdims=True)
             mixed = product(values_across[kv_head, :, :seen], exponent.astype(jnp.bfloat16))
             log_totals[pl.ds(pair * blocks + index, 1), :] = largest + jnp.log(totals)
-            mixed = pick_heads(mixed / totals).T.astype(jnp.bfloat16)
+            across = pick_heads(mixed / totals).astype(jnp.bfloat16)
+            for i in range(QUERY_ROWS // block_rows):
+                heads_across[
+                    lanes, block_rows_at(order, index * (QUERY_ROWS // block_rows) + i, block_rows)
+                ] = across[:, i * block_rows : (i + 1) * block_rows]
+            mixed = across.T
             per = QUERY_ROWS // block_rows
             for i in range(per):
                 attended[block_rows_at(order, index * per + i, block_rows), lanes] = mixed[
@@ -989,7 +1508,7 @@
     lax.fori_loop(0, pairs, attend, 0)
 
 
-def attend_forward(block_rows, width, kv_heads, order, tokens_all, gain, weight, tables):
+def attend_forward(block_rows, width, kv_heads, dealing, tokens_all, gain, weight, tables):
     length, _ = tokens_all.shape
     blocks = length // QUERY_ROWS
     wide = shape((kv_heads, length, LANES))
@@ -1001,21 +1520,26 @@
             wide,
             wide,
             shape((width // LANES * blocks, PAIR * QUERY_ROWS), jnp.float32),
-            shape(tokens_all.shape),
+            shape(tokens_all.shape[::-1]),
+            shape((width, length)),
+            shape((width, tokens_all.shape[1])),
         ),
         in_specs=[SMEM] + [VMEM] * 5,
-        out_specs=(VMEM,) * 6,
-        scratch_shapes=[pltpu.VMEM((kv_heads, LANES, length), jnp.bfloat16)],
-        compiler_params=pltpu.CompilerParams(vmem_limit_bytes=48 << 20),
+        out_specs=(VMEM,) * 8,
+        scratch_shapes=[
+            pltpu.VMEM((kv_heads, LANES, length), jnp.bfloat16),
+            pltpu.SMEM((length // block_rows,), jnp.int32),
+        ],
+        compiler_params=pltpu.CompilerParams(vmem_limit_bytes=VMEM_MEGABYTES << 20),
         cost_estimate=pl.CostEstimate(
             flops=3 * 10**10, bytes_accessed=10**7, transcendentals=10**7
         ),
-    )(order, tokens_all, gain, weight, *tables)
+    )(dealing, tokens_all, gain, weight, *tables)
 
 
 def attend_back_body(
     block_rows,
-    order,
+    dealing,
     branch_all,
     output_weight,
     queries,
@@ -1031,7 +1555,9 @@
     keys_across,
     key_sums,
     value_sums,
+    order,
 ):
+    slots(dealing, order)
     length, width = queries.shape
     kv_heads = keys.shape[0]
     pairs = width // LANES
@@ -1121,7 +1647,7 @@
 
 
 def attend_backward(
-    block_rows, order, branch_all, output_weight, queries, keys, values, attended, log_totals, tables
+    block_rows, dealing, branch_all, output_weight, queries, keys, values, attended, log_totals, tables
 ):
     length, width = queries.shape
     kv_heads = keys.shape[0]
@@ -1136,13 +1662,14 @@
             pltpu.VMEM((kv_heads, LANES, length), jnp.bfloat16),
             pltpu.VMEM((kv_heads, length, LANES), jnp.float32),
             pltpu.VMEM((kv_heads, length, LANES), jnp.float32),
+            pltpu.SMEM((length // block_rows,), jnp.int32),
         ],
-        compiler_params=pltpu.CompilerParams(vmem_limit_bytes=56 << 20),
+        compiler_params=pltpu.CompilerParams(vmem_limit_bytes=VMEM_MEGABYTES << 20),
         cost_estimate=pl.CostEstimate(
             flops=6 * 10**10, bytes_accessed=10**7, transcendentals=10**7
         ),
     )(
-        order,
+        dealing,
         branch_all,
         output_weight,
         queries,
@@ -1154,73 +1681,6 @@
     )
 
 
-def for_part(body):
-    me = lax.axis_index("ctx")
-    for part in range(4):
-
-        @pl.when(me == part)
-        def _(part=part):
-            body(part)
-
-
-def strided_columns(array, shards, part):
-    span = array.shape[1] // (4 * shards)
-    values = array[...].astype(jnp.float32)
-    starts = [(shard * 4 + part) * span for shard in range(shards)]
-    return jnp.concatenate([values[:, i : i + span] for i in starts], axis=1).astype(array.dtype)
-
-
-def pack_hidden_body(shards, gate, up, packed):
-    def body(part):
-        width = packed.shape[1] // 2
-        packed[:, :width] = strided_columns(gate, shards, part)
-        packed[:, width:] = strided_columns(up, shards, part)
-
-    for_part(body)
-
-
-def pack_hidden(shards, gate, up):
-    rows, width = gate.shape
-    step = 64
-    block = pl.BlockSpec((step, width), lambda i: (i, 0))
-    return pl.pallas_call(
-        functools.partial(pack_hidden_body, shards),
-        grid=(rows // step,),
-        out_shape=shape((rows, width // 2)),
-        in_specs=[block, block],
-        out_specs=pl.BlockSpec((step, width // 2), lambda i: (i, 0)),
-        cost_estimate=pl.CostEstimate(flops=0, bytes_accessed=10**7, transcendentals=0),
-        compiler_params=pltpu.CompilerParams(vmem_limit_bytes=24 << 20),
-    )(gate, up)
-
-
-def pack_attention_body(shards, query, key, value, output, packed):
-    def body(part):
-        width = query.shape[1] // 4
-        rows = output.shape[0] // 4
-        packed[:, :width] = strided_columns(query, shards, part)
-        packed[:, width : width + KV_WIDTH] = key[...]
-        packed[:, width + KV_WIDTH : width + 2 * KV_WIDTH] = value[...]
-        for index in range(4):
-            packed[index * rows : (index + 1) * rows, width + 2 * KV_WIDTH :] = output[
-                part * rows : (part + 1) * rows, index * width : (index + 1) * width
-            ]
-
-    for_part(body)
-
-
-def pack_attention(shards, query, key, value, output):
-    rows, width = query.shape
-    return pl.pallas_call(
-        functools.partial(pack_attention_body, shards),
-        out_shape=shape((rows, width // 2 + 2 * KV_WIDTH)),
-        in_specs=[VMEM] * 4,
-        out_specs=VMEM,
-        cost_estimate=pl.CostEstimate(flops=0, bytes_accessed=10**7, transcendentals=0),
-        compiler_params=pltpu.CompilerParams(vmem_limit_bytes=24 << 20),
-    )(query, key, value, output)
-
-
 def take_columns(matrix, outer, parts, index):
     rows, columns = matrix.shape
     pieces = matrix.reshape(rows, outer, parts, columns // (outer * parts))
@@ -1245,9 +1705,15 @@
     return lax.all_gather(array, "fsdp", axis=0, tiled=True)
 
 
-def scatter_shards(array):
+def scatter_shards(array, by_core=False):
+    shards = lax.axis_size("fsdp")
+    groups = [list(range(core, shards, 2)) for core in range(2)] if by_core else None
     return lax.psum_scatter(
-        array.astype(jnp.bfloat16), "fsdp", scatter_dimension=0, tiled=True
+        array.astype(jnp.bfloat16),
+        "fsdp",
+        scatter_dimension=0,
+        tiled=True,
+        axis_index_groups=groups,
     )
 
 
@@ -1275,38 +1741,23 @@
     dealt_heads = D // shard_count // part_count == HEAD_DIM and part_count == 4
     kv_heads = KV_HEADS if dealt_heads else max(1, KV_HEADS // part_count)
     kv_first = 0 if dealt_heads else ctx_index * KV_HEADS // part_count
-    blocks = jnp.arange(2 * part_count, dtype=jnp.int32)
-    order = jnp.sum(
-        jnp.where(dealing[0][None, :] == blocks[:, None], blocks[None, :], 0), axis=1
-    ).astype(jnp.int32)
-    tables = rotary_tables(seq_rows)
-
     tie = lax.optimization_barrier
-    gains = jnp.stack([first_gain, second_gain])
-    key_value = jnp.concatenate([key_weight, value_weight], axis=1)
+    start = functools.partial(
+        start_gather, part_count, shard_count, 1, tokens[0], first_gain[None], second_gain[None]
+    )
     if dealt_heads:
-        height = D // shard_count // part_count
-        packed = gather_shards(
-            pack_attention(shard_count, query_weight, key_weight, value_weight, output_weight)
+        tokens_all, gain_first, gain_second, cosine, sine, packed, packed_hidden = start(
+            query_weight, key_weight, value_weight, output_weight, gate_weight, up_weight
         )
-        tokens_all, gains_all = start_gather(part_count, shard_count, 1, tokens[0], gains)
-        tokens_all, gate_weight, up_weight, grad_out = tie(
-            (tokens_all, gate_weight, up_weight, cotangent[0])
-        )
-        gate_up_part = gather_shards(pack_hidden(shard_count, gate_weight, up_weight))
-        grad_out_parts = plane_gather(grad_out)
-        output_part = (
-            packed[:, part_width + 2 * KV_WIDTH :]
-            .reshape(shard_count, part_count, height, part_width)
-            .transpose(0, 2, 1, 3)
-            .reshape(part_width, D)
-        )
+        packed, packed_hidden = tie((packed, packed_hidden))
+        gate_up_part = gather_shards(packed_hidden)
     else:
-        tokens_all, gains_all = start_gather(part_count, shard_count, 1, tokens[0], gains)
+        tokens_all, gain_first, gain_second, cosine, sine = start()
         grad_out_all = lax.all_gather(cotangent[0], "ctx", axis=0, tiled=True)
         query_part = gather_shards(take_columns(query_weight, 1, part_count, ctx_index))
         output_part = take_rows(gather_shards(output_weight), part_count, ctx_index)
-        key_value = gather_shards(key_value).reshape(D, 2, KV_HEADS, HEAD_DIM)
+        key_value = gather_shards(jnp.concatenate([key_weight, value_weight], axis=1))
+        key_value = key_value.reshape(D, 2, KV_HEADS, HEAD_DIM)
         key_value = lax.dynamic_slice_in_dim(key_value, kv_first, kv_heads, 2).reshape(D, -1)
         packed = jnp.concatenate([query_part, key_value], axis=1)
         gate_up_part = gather_shards(
@@ -1318,48 +1769,57 @@
                 axis=1,
             )
         )
+    tables = (cosine, sine)
     down_part = gather_shards(take_rows(down_weight, part_count, ctx_index))
 
-    gains = gains_all.transpose(1, 0, 2).reshape(2, D).astype(jnp.float32)
-    gain_first, gain_second = (gains[0:1], gains[1:2])
-    attended, query_rot, key_rot, value_rows, log_totals, first_all = attend_forward(
-        block_rows, part_width, kv_heads, order, tokens_all, gain_first, packed, tables
-    )
+    forward = attend_forward(
+        block_rows, part_width, kv_heads, dealing, tokens_all, gain_first, packed, tables
+    )
+    attended, query_rot, key_rot, value_rows, log_totals, first_across, heads_across = forward[:7]
     if dealt_heads:
-        attended, *grad_out_corner = tie((attended, *grad_out_parts[3:]))
-        grad_out_parts = (*grad_out_parts[:3], *grad_out_corner)
+        output_part = forward[7]
     residual_mid, second_all = middle_gather(
         part_count, 2, attended, output_part, tokens[0], gain_second
     )
     if dealt_heads:
-        second_all, *grad_out_parts = tie((second_all, *grad_out_parts))
-        grad_out_all = place_rows(grad_out_parts, jnp.bfloat16)
-
-    gate_up, hidden = hidden_forward(second_all, gate_up_part)
-    down_term = column_term(hidden, grad_out_all).astype(jnp.bfloat16)
+        second_all, grad_out = tie((second_all, cotangent[0]))
+        near = plane_near(grad_out)
+
+    gate_up, hidden, second_across, hidden_across = hidden_forward(second_all, gate_up_part)
+    if dealt_heads:
+        hidden_across, *near = tie((hidden_across, *near))
+        grad_out_all = place_rows(plane_far(near), jnp.bfloat16)
+        (down_term,) = core_grads(shard_count, 5, hidden_across, grad_out_all)
+    else:
+        down_term = column_term(hidden, grad_out_all)
     down_part, down_term = tie((down_part, down_term))
-    down_piece = scatter_shards(down_term)
-    output_partial = product(hidden, down_part).astype(jnp.bfloat16)
+    down_piece = scatter_shards(down_term, dealt_heads)
+    grad_gate_up, output_partial = hidden_backward(grad_out_all, down_part, gate_up, hidden)
     relayed = plane_relay(output_partial)
-    grad_out_all, output_partial = tie((grad_out_all, output_partial))
-    grad_gate_up = hidden_backward(grad_out_all, down_part, gate_up)
-    gate_up_term = column_term(second_all, grad_gate_up).astype(jnp.bfloat16)
-    grad_gate_up, gate_up_term, *relayed = tie((grad_gate_up, gate_up_term, *relayed))
-    gate_up_piece = scatter_shards(gate_up_term)
+    if dealt_heads:
+        terms = core_grads(shard_count, 6, second_across, grad_gate_up, 2)
+    else:
+        gate_up_term = column_term(second_all, grad_gate_up).astype(jnp.bfloat16)
+        terms = (gate_up_term[:, : FF // part_count], gate_up_term[:, FF // part_count :])
+    grad_gate_up, *tied = tie((grad_gate_up, *terms, *relayed))
+    terms, relayed = (tied[:2], tied[2:])
+    gate_piece = scatter_shards(terms[0], dealt_heads)
+    up_piece = scatter_shards(terms[1], dealt_heads)
     last = plane_last(output_partial, relayed)
     grad_mid, second_gain_part, branch_all = middle_back(
         part_count, 3, grad_gate_up, gate_up_part, residual_mid, gain_second, cotangent[0]
     )
-    branch_all, down_piece, *last = tie((branch_all, down_piece, *last))
+    branch_all, down_piece, gate_piece, *last = tie((branch_all, down_piece, gate_piece, *last))
     block_output = (residual_mid + plane_scatter(output_partial, relayed, last)).astype(
         jnp.bfloat16
     )
     if dealt_heads:
         down_parts = plane_gather(down_piece)
+        gate_parts = plane_gather(gate_piece)
 
     grad_packed = attend_backward(
         block_rows,
-        order,
+        dealing,
         branch_all,
         output_part,
         query_rot,
@@ -1370,10 +1830,13 @@
         tables,
     )
     if dealt_heads:
-        packed_term = attention_grads(shard_count, first_all, grad_packed, attended, branch_all)
-        grad_packed, packed_term, *down_parts = tie((grad_packed, packed_term, *down_parts))
-        packed_piece = scatter_shards(packed_term)
-    grad_input, gain_shard = input_back(
+        packed_term = attention_grads(
+            shard_count, 7, first_across, grad_packed, heads_across, branch_all
+        )
+        grad_packed, packed_term, *parts = tie((grad_packed, packed_term, *down_parts, *gate_parts))
+        down_parts, gate_parts = (parts[:5], parts[5:])
+        packed_piece = scatter_shards(packed_term, True)
+    grad_input, gain_shard, up_all = input_back(
         part_count,
         shard_count,
         4,
@@ -1383,10 +1846,12 @@
         gain_first,
         grad_mid,
         second_gain_part,
+        up_piece,
     )
     if dealt_heads:
         grad_input, packed_piece = tie((grad_input, packed_piece))
-        gate_shard, up_shard = place_hidden(shard_count, plane_gather(gate_up_piece))
+        gate_shard = place_hidden(shard_count, gate_parts)
+        up_shard = place_sorted(shard_count, up_all)
         down_shard = place_rows(down_parts, jnp.float32)
         query_shard, key_shard, value_shard, output_shard = place_attention(
             shard_count, plane_gather(packed_piece)
@@ -1396,14 +1861,15 @@
         def gather_columns(piece, outer):
             return put_columns(lax.all_gather(piece, "ctx", axis=0), outer).astype(jnp.float32)
 
-        width = FF // part_count
-        gate_shard = gather_columns(gate_up_piece[:, :width], shard_count)
-        up_shard = gather_columns(gate_up_piece[:, width:], shard_count)
+        gate_shard = gather_columns(gate_piece, shard_count)
+        up_shard = put_columns(
+            up_all.reshape(part_count, -1, FF // part_count), shard_count
+        ).astype(jnp.float32)
         down_shard = lax.all_gather(down_piece, "ctx", axis=0, tiled=True).astype(jnp.float32)
         grad_query, grad_key_value = (grad_packed[:, :part_width], grad_packed[:, part_width:])
-        query_piece = scatter_shards(column_term(first_all, grad_query))
+        query_piece = scatter_shards(product(first_across, grad_query))
         query_shard = gather_columns(query_piece, 1)
-        key_value_piece = scatter_shards(column_term(first_all, grad_key_value))
+        key_value_piece = scatter_shards(product(first_across, grad_key_value))
         output_term = column_term(attended, branch_all)
         spread = jnp.zeros((D, D), jnp.float32)
         spread = lax.dynamic_update_slice_in_dim(

time: 577 us -> 556 us (0.964)
  Pallas kernels: 385 us -> 465 us
  matrix products: 36.8 us -> 0 us
  local copies, waits for them, and re-layouts: 46.2 us -> 13.7 us
  waiting for transfers between devices: 56.3 us -> 31.7 us
    pallas_call x4 -> x7, Pallas kernels: 265 us -> 344 us  [call_plane(): pl.pallas_call(body, out_shape=outs, in_specs=in_specs, out_specs=out_spe...]
    dot_general x3 -> x0, matrix products: 36.8 us -> none  [the longest x2 27.3 us: column_term(): lax.dot_general(source, gradient, (((0,), (0,)), ((), ())), preferred_ele...]
    unnamed x108 -> x31, local copies, waits for them, and re-layouts: 30.4 us -> 1.83 us
    all_gather x3 -> x2, waiting for transfers between devices: 16.9 us -> 3.53 us  [gather_shards(): return lax.all_gather(array, 'fsdp', axis=0, tiled=True)]
    ppermute x20, waiting for transfers between devices: 38.9 us -> 28 us  [swap(): return lax.ppermute(array, 'ctx', pairs)]
    pallas_call x4 -> x2, Pallas kernels: 29.7 us -> 26.3 us  [the longest x1 20.8 us: hidden_backward(): pl.pallas_call(hidden_back_body, grid=(length // step,), out_shape=(shape...]
  transfers between devices with their start and end apart: 26 -> 26, of which waited for: 6 -> 7; matrix products, arithmetic and copies ran while one was open for 11% -> 3% of each run, Pallas kernels for 67% -> 72%
where the time goes in v4:
time: 556 us; the launch traced here: 553 us
  Pallas kernels  465 us (84%)
  waiting for transfers between devices  31.7 us (6%)
  starting transfers between devices  22.6 us (4%)
  between operations  14.7 us (3%)
  local copies, waits for them, and re-layouts  13.7 us (2%)
  other arithmetic  5.83 us (1%)
    pallas_call x7, Pallas kernels, call_plane(): pl.pallas_call(body, out_shape=outs, in_specs=in_specs, out_specs=out_spe...  344 us
    ppermute x20, waiting for transfers between devices, swap(): return lax.ppermute(array, 'ctx', pairs)  28 us
    pallas_call x1, Pallas kernels, attend_backward(): pl.pallas_call(functools.partial(attend_back_body, block_rows), out_shape...  27.1 us
    pallas_call x1, Pallas kernels, attend_forward(): pl.pallas_call(functools.partial(attend_body, block_rows), out_shape=(sha...  26.6 us
    ppermute x20, starting transfers between devices, swap(): return lax.ppermute(array, 'ctx', pairs)  21.6 us
    pallas_call x1, Pallas kernels, hidden_forward(): pl.pallas_call(hidden_body, grid=(length // step,), out_shape=(shape((len...  21.1 us
    pallas_call x1, Pallas kernels, hidden_backward(): pl.pallas_call(hidden_back_body, grid=(length // step,), out_shape=(shape...  20.8 us
  transfers between devices with their start and end apart: 26, of which 7 were waited for; matrix products, arithmetic and copies ran while one was open for 3% of the time, Pallas kernels for 72%

profile of v4, /device:TPU:0, one launch (start us, length us, event | category | flops | bytes accessed | tf_op | source)
XLA Modules:
  0.0 553.1 jit_solution(8117620826669999115)
XLA Ops:
  9.8 63.3 %shard_map.203 = (bf16[1024,2048]{1,0:T(8,128)(2,1)}, f32[1,2048]{1,0:T(1,128)}, f32[1,2048]{1,0:T(1,128)}, f32[1024,128]{1,0:T(8,128)}, f32[1024,128]{1,0:T(8,1...) custom-call(bf16[256,2048]{1,0:T(8,128)(2,1)} %bitcast.30, bf16[1,256]{1,0:T(2,128)(2,1)} %broadcast_in_dim.12.first_gain, ...), custom_call_target="tpu_custom_call" | custom-call | flops 49999998976 | bytes 166666672 | tf_op jit(solution)/shard_map/pallas_call | solution.py:477
  74.8 26.6 %shard_map.204 = (bf16[1024,512]{1,0:T(8,128)(2,1)}, bf16[1024,512]{1,0:T(8,128)(2,1)}, bf16[4,1024,128]{2,1,0:T(8,128)(2,1)}, bf16[4,1024,128]{2,1,0:T(8,128)(2...) custom-call(s32[1,8]{1,0:T(1,128)} %dealing.3, ...), custom_call_target="tpu_custom_call" | custom-call | flops 30000001024 | bytes 10000000 | tf_op jit(solution)/shard_map/pallas_call | solution.py:1515
  101.4 76.9 %shard_map.205 = (f32[256,2048]{1,0:T(8,128)}, bf16[1024,2048]{1,0:T(8,128)(2,1)}) custom-call(bf16[1024,512]{1,0:T(8,128)(2,1)} %get-tuple-element.87.attended, bf16[512,2048]{1,0:T(8,128)(2,1)} %get-tuple-element.88.weight.output_weight, bf16[256,2048]{1,0:T(8,128)(2,1)} %bitcast.31, f32[1,2048]{1,0:T(1,128)} %get-tuple-element.89.gain), custom_call_target="tpu_custom_call" | custom-call | flops 60000002048 | bytes 200000000 | tf_op jit(solution)/shard_map/pallas_call | solution.py:477
  180.5 21.1 %shard_map.206 = (f32[1024,2816]{1,0:T(8,128)}, bf16[1024,1408]{1,0:T(8,128)(2,1)}, bf16[2048,1024]{1,0:T(8,128)(2,1)}, bf16[1408,1024]{1,0:T(8,128)(2,1)}) custom-call(bf16[1024,2048]{1,0:T(8,128)(2,1)} %get-tuple-element.92.rows, bf16[2048,2816]{1,0:T(8,128)(2,1)} %all-gather.3.cloned.1.call-done.gate_weight.up_weight.gate_up_weight, ...), custom_call_target="tpu_custom_call" | custom-call | flops 11811160064 | bytes 30000000 | tf_op jit(solution)/shard_map/pallas_call | solution.py:954
  203.1 1.7 collective-permute-start.2
  205.3 10.6 %collective-permute-done.2.low = bf16[128,2048]{1,0:T(8,128)(2,1)S(1)} collective-permute-done((bf16[128,2048]{1,0:T(8,128)(2,1)S(1)}, bf16[128,2048]{1,0:T(8,128)(2,1)S(1)}, u32[]{:S(2)}, u32[]{:S(2)}) %collective-permute-start.2) | collective-permute-done | bytes 524320 | tf_op jit(solution)/shard_map/ppermute | solution.py:875
  218.0 4.5 shard_map.207.gradient.grad_rows
  222.4 15.1 %shard_map.208 = bf16[704,2048]{1,0:T(8,128)(2,1)} custom-call(bf16[1408,1024]{1,0:T(8,128)(2,1)} %get-tuple-element.99.across, bf16[1024,2048]{1,0:T(8,128)(2,1)} %shard_map.207.gradient.grad_rows), custom_call_target="tpu_custom_call" | custom-call | flops 5905580032 | bytes 19685266 | tf_op jit(solution)/shard_map/pallas_call | solution.py:477
  237.6 3.4 all-gather.5.cloned.1.call-done.down_weight
  241.2 20.8 %shard_map.209 = (bf16[1024,2816]{1,0:T(8,128)(2,1)}, bf16[1024,2048]{1,0:T(8,128)(2,1)}) custom-call(bf16[1024,2048]{1,0:T(8,128)(2,1)} %shard_map.207.gradient.grad_rows, bf16[1408,2048]{1,0:T(8,128)(2,1)} %all-gather.5.cloned.1.call-done.down_weight, f32[1024,2816]{1,0:T(8,128)} %get-tuple-element.101.gate_up, bf16[1024,1408]{1,0:T(8,128)(2,1)} %get-tuple-element.102.hidden), custom_call_target="tpu_custom_call" | custom-call | flops 11811160064 | bytes 30000000 | tf_op jit(solution)/shard_map/pallas_call | solution.py:993
  262.0 1.8 dynamic-slice_bitcast_fusion.1
  267.0 23.8 %shard_map.210 = (bf16[1024,1408]{1,0:T(8,128)(2,1)}, bf16[1024,1408]{1,0:T(8,128)(2,1)}) custom-call(bf16[2048,1024]{1,0:T(8,128)(2,1)} %get-tuple-element.105.across, bf16[1024,2816]{1,0:T(8,128)(2,1)} %get-tuple-element.109.gradient.grad_gate_up), custom_call_target="tpu_custom_call" | custom-call | flops 11811160064 | bytes 39370532 | tf_op jit(solution)/shard_map/pallas_call | solution.py:477
  291.0 2.0 fusion.3
  294.9 84.6 %shard_map.211 = (f32[256,2048]{1,0:T(8,128)}, f32[1,2048]{1,0:T(1,128)}, bf16[1024,2048]{1,0:T(8,128)(2,1)}) custom-call(bf16[1024,2816]{1,0:T(8,128)(2,1)} %get-tuple-element.109.gradient.grad_gate_up, bf16[2048,2816]{1,0:T(8,128)(2,1)} %all-gather.3.cloned.1.call-done.gate_weight.up_weight.gate_up_weight, f32[256,2048]{1,0:T(8,128)} %get-tuple-element.90.residual, ...), custom_call_target="tpu_custom_call" | custom-call | flops 60000002048 | bytes 200000000 | tf_op jit(solution)/shard_map/pallas_call | solution.py:477
  383.8 27.1 %shard_map.212.gradient.grad_packed = bf16[1024,1024]{1,0:T(8,128)(2,1)} custom-call(s32[1,8]{1,0:T(1,128)} %dealing.3, bf16[1024,2048]{1,0:T(8,128)(2,1)} %get-tuple-element.116.branch_all, bf16[512,2048]{1,0:T(8,128)(2,1)} %get-tuple-element.88.weight.output_weight, bf16[1024,512]{1,0:T(8,128)(2,1)} %get-tuple-element.117.queries, ...), custom_call_target="tpu_custom_call" | custom-call | flops 60000002048 | bytes 10000000 | tf_op jit(solution)/shard_map/pallas_call | solution.py:1654
  418.2 16.1 %shard_map.213 = bf16[1024,1536]{1,0:T(8,128)(2,1)} custom-call(bf16[2048,1024]{1,0:T(8,128)(2,1)} %get-tuple-element.121.across, bf16[1024,1024]{1,0:T(8,128)(2,1)} %shard_map.212.gradient.grad_packed, bf16[512,1024]{1,0:T(8,128)(2,1)} %get-tuple-element.122.heads, bf16[1024,2048]{1,0:T(8,128)(2,1)} %get-tuple-element.116.branch_all), custom_call_target="tpu_custom_call" | custom-call | flops 6442450944 | bytes 21474836 | tf_op jit(solution)/shard_map/pallas_call | solution.py:477
  434.4 64.2 %shard_map.214 = (bf16[256,2048]{1,0:T(8,128)(2,1)}, f32[2,256]{1,0:T(2,128)}, bf16[1024,1408]{1,0:T(8,128)(2,1)}) custom-call(bf16[1024,1024]{1,0:T(8,128)(2,1)} %shard_map.212.gradient.grad_packed, bf16[2048,1536]{1,0:T(8,128)(2,1)} %get-tuple-element.84.weight, bf16[256,2048]{1,0:T(8,128)(2,1)} %bitcast.32, f32[256,2048]{1,0:T(8,128)} %get-tuple-element.126.grad_mid, ...), custom_call_target="tpu_custom_call" | custom-call | flops 49999998976 | bytes 166666672 | tf_op jit(solution)/shard_map/pallas_call | solution.py:477
  500.8 2.3 fusion.5
  503.1 14.7 %collective-permute-done.16.from_across = bf16[256,1536]{1,0:T(8,128)(2,1)S(1)} collective-permute-done((bf16[256,1536]{1,0:T(8,128)(2,1)}, bf16[256,1536]{1,0:T(8,128)(2,1)S(1)}, u32[]{:S(2)}, u32[]{:S(2)}) %collective-permute-start.16) | collective-permute-done | bytes 786464 | tf_op jit(solution)/shard_map/ppermute | solution.py:875
  519.7 1.8 slice.61
  523.9 5.5 shard_map.217
  529.4 5.6 %shard_map.216 = f32[256,5632]{1,0:T(8,128)} custom-call(bf16[256,1408]{1,0:T(8,128)(2,1)} %reduce-scatter.7.cloned.1.call-done.refs_0_, bf16[256,1408]{1,0:T(8,128)(2,1)} %copy-done.8, bf16[256,1408]{1,0:T(8,128)(2,1)} %copy-done.9, bf16[128,1408]{1,0:T(8,128)(2,1)} %collective-permute-done.14.refs_3_, bf16[128,1408]{1,0:T(8,128)(2,1)} %collective-permute-done.15.refs_4_), custom_call_target="tpu_custom_call" | custom-call | bytes 10000000 | tf_op jit(solution)/shard_map/pallas_call | solution.py:1264
  535.0 4.8 shard_map.218
  540.3 4.7 shard_map.215
  (99 shorter events, 35.5 us)
Async XLA Ops:
  7.2 173.3 %all-gather.3.cloned.1.call-start = ((), (), s32[]{:S(2)}) async-start(), calls=%async_computation.4 | async-start | bytes 12976128 | tf_op jit(solution)/shard_map/all_gather | solution.py:1705
  73.2 167.8 %all-gather.5.cloned.1.call-start = ((), (), s32[]{:S(2)}) async-start(), calls=%async_computation.5 | async-start | bytes 6488064 | tf_op jit(solution)/shard_map/all_gather | solution.py:1705
  74.2 305.4 %reduce-scatter.5.cloned.1.call-start = ((), (), s32[]{:S(2)}) async-start(), calls=%async_computation.6 | async-start | bytes 3604480 | tf_op jit(solution)/shard_map/reduce_scatter | solution.py:1711
  178.3 24.7 %collective-permute-start = (bf16[256,2048]{1,0:T(8,128)(2,1)}, bf16[256,2048]{1,0:T(8,128)(2,1)S(1)}, u32[]{:S(2)}, u32[]{:S(2)}) collective-permute-start(bf16[256,2048]{1,0:T(8,128)(2,1)} %bitcast.1.own.grad_out), channel_id=1, source_target_pairs={{0,8},{8,0},{16,24},{24,16},{1,9},{9,1},{17,25},{25,17},{2,10},{10... | collective-permute-start | bytes 3145736 | tf_op jit(solution)/shard_map/ppermute | solution.py:875
  178.8 24.3 %collective-permute-start.1 = (bf16[256,2048]{1,0:T(8,128)(2,1)}, bf16[256,2048]{1,0:T(8,128)(2,1)S(1)}, u32[]{:S(2)}, u32[]{:S(2)}) collective-permute-start(bf16[256,2048]{1,0:T(8,128)(2,1)} %bitcast.1.own.grad_out), channel_id=1, source_target_pairs={{0,16},{8,24},{16,0},{24,8},{1,17},{9,25},{17,1},{25,9},{2,18},{10... | collective-permute-start | bytes 3145736 | tf_op jit(solution)/shard_map/ppermute | solution.py:875
  241.0 138.7 %reduce-scatter.7.cloned.1.call-start = ((), (), s32[]{:S(2)}) async-start(), calls=%async_computation.7 | async-start | bytes 3604480 | tf_op jit(solution)/shard_map/reduce_scatter | solution.py:1711
  263.9 27.0 %collective-permute-start.4 = (bf16[2,128,2048]{2,1,0:T(8,128)(2,1)S(1)}, bf16[2,128,2048]{2,1,0:T(8,128)(2,1)}, u32[]{:S(2)}, u32[]{:S(2)}) collective-permute-start(bf16[2,128,2048]{2,1,0:T(8,128)(2,1)S(1)} %pad_maximum_fusion), channel_id=1, source_target_pairs={{0,8},{8,0},{16,24},{24,16},{1,9},{9,1},{17,25},{25,17},{2,10},{10... | collective-permute-start | bytes 3145736 | tf_op jit(solution)/shard_map/ppermute | solution.py:875
  265.5 25.4 %collective-permute-start.5 = (bf16[2,128,2048]{2,1,0:T(8,128)(2,1)S(1)}, bf16[2,128,2048]{2,1,0:T(8,128)(2,1)S(1)}, u32[]{:S(2)}, u32[]{:S(2)}) collective-permute-start(bf16[2,128,2048]{2,1,0:T(8,128)(2,1)S(1)} %pad_maximum_fusion.1), channel_id=1, source_target_pairs={{0,16},{8,24},{16,0},{24,8},{1,17},{9,25},{17,1},{25,9},{2,18},{10... | collective-permute-start | bytes 3145736 | tf_op jit(solution)/shard_map/ppermute | solution.py:875
  290.9 143.5 %reduce-scatter.9.cloned.1.call-start = ((), (), s32[]{:S(2)}) async-start(), calls=%async_computation.8 | async-start | bytes 3604480 | tf_op jit(solution)/shard_map/reduce_scatter | solution.py:1711
  293.0 86.6 %collective-permute-start.6 = (bf16[128,2048]{1,0:T(8,128)(2,1)S(1)}, bf16[128,2048]{1,0:T(8,128)(2,1)S(1)}, u32[]{:S(2)}, u32[]{:S(2)}) collective-permute-start(bf16[128,2048]{1,0:T(8,128)(2,1)S(1)} %get-tuple-element.152), channel_id=1, source_target_pairs={{0,16},{8,24},{16,0},{24,8},{1,17},{9,25},{17,1},{25,9},{2,18},{10... | collective-permute-start | bytes 1572872 | tf_op jit(solution)/shard_map/ppermute | solution.py:875
  294.3 85.3 %collective-permute-start.7 = (bf16[128,2048]{1,0:T(8,128)(2,1)S(1)}, bf16[128,2048]{1,0:T(8,128)(2,1)}, u32[]{:S(2)}, u32[]{:S(2)}) collective-permute-start(bf16[128,2048]{1,0:T(8,128)(2,1)S(1)} %get-tuple-element.151), channel_id=1, source_target_pairs={{0,8},{8,0},{16,24},{24,16},{1,9},{9,1},{17,25},{25,17},{2,10},{10... | collective-permute-start | bytes 1572872 | tf_op jit(solution)/shard_map/ppermute | solution.py:875
  294.9 203.8 %reduce-scatter.11.cloned.1.call-start = ((), (), s32[]{:S(2)}) async-start(), calls=%async_computation.9 | async-start | bytes 3932160 | tf_op jit(solution)/shard_map/reduce_scatter | solution.py:1711
  379.7 31.2 %collective-permute-start.8 = (bf16[176,2048]{1,0:T(8,128)(2,1)}, bf16[176,2048]{1,0:T(8,128)(2,1)S(1)}, u32[]{:S(2)}, u32[]{:S(2)}) collective-permute-start(bf16[176,2048]{1,0:T(8,128)(2,1)} %reduce-scatter.5.cloned.1.call-done.own), channel_id=1, source_target_pairs={{0,8},{8,0},{16,24},{24,16},{1,9},{9,1},{17,25},{25,17},{2,10},{10... | collective-permute-start | bytes 2162696 | tf_op jit(solution)/shard_map/ppermute | solution.py:875
  380.3 32.0 %collective-permute-start.9 = (bf16[176,2048]{1,0:T(8,128)(2,1)}, bf16[176,2048]{1,0:T(8,128)(2,1)S(1)}, u32[]{:S(2)}, u32[]{:S(2)}) collective-permute-start(bf16[176,2048]{1,0:T(8,128)(2,1)} %reduce-scatter.5.cloned.1.call-done.own), channel_id=1, source_target_pairs={{0,16},{8,24},{16,0},{24,8},{1,17},{9,25},{17,1},{25,9},{2,18},{10... | collective-permute-start | bytes 2162696 | tf_op jit(solution)/shard_map/ppermute | solution.py:875
  381.7 32.8 %collective-permute-start.12 = (bf16[256,1408]{1,0:T(8,128)(2,1)}, bf16[256,1408]{1,0:T(8,128)(2,1)S(1)}, u32[]{:S(2)}, u32[]{:S(2)}) collective-permute-start(bf16[256,1408]{1,0:T(8,128)(2,1)} %reduce-scatter.7.cloned.1.call-done.refs_0_), channel_id=1, source_target_pairs={{0,8},{8,0},{16,24},{24,16},{1,9},{9,1},{17,25},{25,17},{2,10},{10... | collective-permute-start | bytes 2162696 | tf_op jit(solution)/shard_map/ppermute | solution.py:875
  382.3 33.6 %collective-permute-start.13 = (bf16[256,1408]{1,0:T(8,128)(2,1)}, bf16[256,1408]{1,0:T(8,128)(2,1)S(1)}, u32[]{:S(2)}, u32[]{:S(2)}) collective-permute-start(bf16[256,1408]{1,0:T(8,128)(2,1)} %reduce-scatter.7.cloned.1.call-done.refs_0_), channel_id=1, source_target_pairs={{0,16},{8,24},{16,0},{24,8},{1,17},{9,25},{17,1},{25,9},{2,18},{10... | collective-permute-start | bytes 2162696 | tf_op jit(solution)/shard_map/ppermute | solution.py:875
  411.7 22.6 %collective-permute-start.10 = (bf16[88,2048]{1,0:T(8,128)(2,1)}, bf16[88,2048]{1,0:T(8,128)(2,1)}, u32[]{:S(2)}, u32[]{:S(2)}) collective-permute-start(bf16[88,2048]{1,0:T(8,128)(2,1)} %slice.56), channel_id=1, source_target_pairs={{0,16},{8,24},{16,0},{24,8},{1,17},{9,25},{17,1},{25,9},{2,18},{10... | collective-permute-start | bytes 1081352 | tf_op jit(solution)/shard_map/ppermute | solution.py:875
  413.1 21.2 %collective-permute-start.11 = (bf16[88,2048]{1,0:T(8,128)(2,1)}, bf16[88,2048]{1,0:T(8,128)(2,1)}, u32[]{:S(2)}, u32[]{:S(2)}) collective-permute-start(bf16[88,2048]{1,0:T(8,128)(2,1)} %slice.57), channel_id=1, source_target_pairs={{0,8},{8,0},{16,24},{24,16},{1,9},{9,1},{17,25},{25,17},{2,10},{10... | collective-permute-start | bytes 1081352 | tf_op jit(solution)/shard_map/ppermute | solution.py:875
  415.4 19.0 %collective-permute-start.14 = (bf16[128,1408]{1,0:T(8,128)(2,1)}, bf16[128,1408]{1,0:T(8,128)(2,1)}, u32[]{:S(2)}, u32[]{:S(2)}) collective-permute-start(bf16[128,1408]{1,0:T(8,128)(2,1)} %slice.58), channel_id=1, source_target_pairs={{0,16},{8,24},{16,0},{24,8},{1,17},{9,25},{17,1},{25,9},{2,18},{10... | collective-permute-start | bytes 1081352 | tf_op jit(solution)/shard_map/ppermute | solution.py:875
  416.8 17.6 %collective-permute-start.15 = (bf16[128,1408]{1,0:T(8,128)(2,1)}, bf16[128,1408]{1,0:T(8,128)(2,1)}, u32[]{:S(2)}, u32[]{:S(2)}) collective-permute-start(bf16[128,1408]{1,0:T(8,128)(2,1)} %slice.59), channel_id=1, source_target_pairs={{0,8},{8,0},{16,24},{24,16},{1,9},{9,1},{17,25},{25,17},{2,10},{10... | collective-permute-start | bytes 1081352 | tf_op jit(solution)/shard_map/ppermute | solution.py:875
  498.7 19.2 %collective-permute-start.16 = (bf16[256,1536]{1,0:T(8,128)(2,1)}, bf16[256,1536]{1,0:T(8,128)(2,1)S(1)}, u32[]{:S(2)}, u32[]{:S(2)}) collective-permute-start(bf16[256,1536]{1,0:T(8,128)(2,1)} %reduce-scatter.11.cloned.1.call-done.own), channel_id=1, source_target_pairs={{0,8},{8,0},{16,24},{24,16},{1,9},{9,1},{17,25},{25,17},{2,10},{10... | collective-permute-start | bytes 2359304 | tf_op jit(solution)/shard_map/ppermute | solution.py:875
  499.4 20.3 %collective-permute-start.17 = (bf16[256,1536]{1,0:T(8,128)(2,1)}, bf16[256,1536]{1,0:T(8,128)(2,1)}, u32[]{:S(2)}, u32[]{:S(2)}) collective-permute-start(bf16[256,1536]{1,0:T(8,128)(2,1)} %reduce-scatter.11.cloned.1.call-done.own), channel_id=1, source_target_pairs={{0,16},{8,24},{16,0},{24,8},{1,17},{9,25},{17,1},{25,9},{2,18},{10... | collective-permute-start | bytes 2359304 | tf_op jit(solution)/shard_map/ppermute | solution.py:875
  518.7 21.7 %collective-permute-start.18 = (bf16[128,1536]{1,0:T(8,128)(2,1)}, bf16[128,1536]{1,0:T(8,128)(2,1)}, u32[]{:S(2)}, u32[]{:S(2)}) collective-permute-start(bf16[128,1536]{1,0:T(8,128)(2,1)} %slice.60), channel_id=1, source_target_pairs={{0,16},{8,24},{16,0},{24,8},{1,17},{9,25},{17,1},{25,9},{2,18},{10... | collective-permute-start | bytes 1179656 | tf_op jit(solution)/shard_map/ppermute | solution.py:875
  521.5 18.8 %collective-permute-start.19 = (bf16[128,1536]{1,0:T(8,128)(2,1)}, bf16[128,1536]{1,0:T(8,128)(2,1)}, u32[]{:S(2)}, u32[]{:S(2)}) collective-permute-start(bf16[128,1536]{1,0:T(8,128)(2,1)} %slice.61), channel_id=1, source_target_pairs={{0,8},{8,0},{16,24},{24,16},{1,9},{9,1},{17,25},{25,17},{2,10},{10... | collective-permute-start | bytes 1179656 | tf_op jit(solution)/shard_map/ppermute | solution.py:875
  (17 other events, 256.3 us)
Sparse Core Ops, SparseCore 0:
  73.3 107.1 all-gather.2
  182.2 58.7 all-gather.4
  243.2 54.8 reduce-scatter.4
  300.3 56.0 reduce-scatter.6
  358.5 56.0 reduce-scatter.8
  434.5 58.1 reduce-scatter.10

commit v5 on v4

--- a/solution.py
+++ b/solution.py
@@ -238,15 +238,12 @@
         target = self.out.at[pl.ds(pl.multiple_of(self.me * rows, rows), rows)]
         return pltpu.make_async_copy(self.own, target, self.local_sem)
 
-    def start(self):
-        for chunk in range(CHUNKS):
-            for way in (0, 1):
-                pl.when(self.can_send(way))(
-                    lambda way=way, chunk=chunk: self.hop(way, 0, chunk).start()
-                )
-        for chunk in range(CHUNKS):
-            self.cross(0, 0, chunk).start()
-        self.local().start()
+    def start(self, chunk):
+        for way in (0, 1):
+            pl.when(self.can_send(way))(lambda way=way: self.hop(way, 0, chunk).start())
+        self.cross(0, 0, chunk).start()
+        if chunk == 0:
+            self.local().start()
 
     def step(self, distance, chunk):
         for way in (0, 1):
@@ -350,11 +347,13 @@
     def store_own(self, columns, value):
         self.total[:, columns] = value
 
-    def run(self):
+    def run(self, others=()):
         if self.count == 4:
-            self.run_relayed()
+            self.run_relayed(list(others))
         else:
             self.run_direct()
+            for other in others:
+                other()
 
     def run_direct(self):
         for tile in range(self.tiles):
@@ -371,7 +370,7 @@
         self.block(self.count - 1, self.store_own)
         self.relays, self.copies = ([], copies)
 
-    def run_relayed(self):
+    def run_relayed(self, others):
         corner, across, along, me = self.owners()
         send_buf, kept, tiles = (self.send_buf, self.kept, self.tiles)
         half = self.rows // 2
@@ -403,9 +402,13 @@
         self.block(2, store_along)
         copies.append(self.send(1, high, whole, 4 * tiles + 1, along))
         self.block(3, self.store_own)
+        for _ in range(len(others) - tiles - 1):
+            others.pop(0)()
         for tile in range(tiles):
             columns = pl.ds(tile * TILE, TILE)
             for side, peer in ((0, along), (1, across)):
+                if others and side == 0:
+                    others.pop(0)()
                 relays[tile][side].wait_recv()
                 part = (low, high)[side]
 
@@ -419,6 +422,8 @@
                 sem = (2 + side) * tiles + tile
                 copies.append(self.send(2, part, columns, sem, peer))
         self.relays, self.copies = (relays, copies)
+        for other in others:
+            other()
 
     def finish(self):
         for pair in self.relays:
@@ -556,22 +561,20 @@
     if count == 4:
         weights_all, packed_hidden, *refs = refs
     gains, gains_all, gain_send, gain_recv, *refs = refs
-    meet(count, shards)
     first = RowGather(count, tokens, tokens_all, refs[:3])
     half = PIECES // 2
-    first.send(0)
-    first.send(half)
     if count == 4:
         packed, gate, up, load_sem, *line_refs = refs[3:]
         loads = [
-            pltpu.make_async_copy(weights[4 + i], target, load_sem.at[i])
-            for i, target in enumerate((gate, up))
+            begin(weights[4 + i], target, load_sem.at[i]) for i, target in enumerate((gate, up))
         ]
-        for load in loads:
-            load.start()
+        line = LineGather(shards, packed, weights_all, line_refs)
         pack_attention(shards, *weights[:4], packed)
-        line = LineGather(shards, packed, weights_all, line_refs)
-        line.start()
+    meet(count, shards)
+    if count == 4:
+        line.start(0)
+    first.send(0)
+    first.send(half)
     me = lax.axis_index("fsdp")
     gains[0:1, :] = first_gain[...]
     gains[1:2, :] = second_gain[...]
@@ -594,11 +597,13 @@
         first.finish()
     else:
         steps = [(d, c) for d in range(1, line.hops + 1) for c in range(CHUNKS)]
+        write_tables(cosine, sine)
+        for chunk in range(1, CHUNKS):
+            line.start(chunk)
         line.step(*steps[0])
         first.relay((0, half))
         first.send(1)
         first.send(half + 1)
-        write_tables(cosine, sine)
         for step in steps[1:3]:
             line.step(*step)
         for load in loads:
@@ -889,51 +894,6 @@
     return plane_far(plane_near(array))
 
 
-def take_half(partial, owner, side):
-    rows = partial.shape[0] // lax.axis_size("ctx")
-    half = rows // 2
-    return lax.dynamic_slice_in_dim(partial, owner * rows + side * half, half, 0)
-
-
-def plane_relay(partial):
-    if lax.axis_size("ctx") != 4:
-        return (partial,)
-    me, across, along, corner = plane_places()
-    take = functools.partial(take_half, partial)
-    low = swap(jnp.stack([take(corner, 0), take(across, 0)]), False)
-    high = swap(jnp.stack([take(corner, 1), take(along, 1)]), True)
-    return (low, high)
-
-
-def add_parts(first, second):
-    return first.astype(jnp.float32) + second.astype(jnp.float32)
-
-
-def plane_last(partial, relayed):
-    if lax.axis_size("ctx") != 4:
-        return (lax.psum_scatter(relayed[0], "ctx", scatter_dimension=0, tiled=True),)
-    me, across, along, corner = plane_places()
-    take = functools.partial(take_half, partial)
-    low, high = relayed
-    last_low = swap(add_parts(take(along, 0), low[0]).astype(jnp.bfloat16), True)
-    last_high = swap(add_parts(take(across, 1), high[0]).astype(jnp.bfloat16), False)
-    return (last_low, last_high)
-
-
-def plane_scatter(partial, relayed, last):
-    if lax.axis_size("ctx") != 4:
-        return last[0].astype(jnp.float32)
-    me = lax.axis_index("ctx")
-    return jnp.concatenate(
-        [
-            add_parts(take_half(partial, me, side), relayed[side][1])
-            + last[side].astype(jnp.float32)
-            for side in (0, 1)
-        ],
-        axis=0,
-    )
-
-
 def hidden_body(rows, gate_weight, up_weight, gate_up, hidden, rows_across, hidden_across):
     width = hidden.shape[1]
     rows_across[...] = rows[...].T
@@ -974,9 +934,8 @@
     )(second_all, gate_weight, up_weight)
 
 
-def hidden_back_body(grad_rows, down_weight, gate_up, hidden, grad_gate_up, partial):
+def hidden_back_body(grad_rows, down_weight, gate_up, grad_gate_up):
     width = down_weight.shape[0]
-    partial[...] = product(hidden[...], down_weight[...]).astype(jnp.bfloat16)
     grad_hidden = times_transposed(grad_rows[...], down_weight[...])
     gate, upward = (gate_up[:, :width], gate_up[:, width:])
     sigmoid_gate = jax.nn.sigmoid(gate)
@@ -986,36 +945,36 @@
     grad_gate_up[:, width:] = (grad_hidden * silu_gate).astype(jnp.bfloat16)
 
 
-def hidden_backward(grad_out_all, down_weight, gate_up, hidden):
+def hidden_backward(grad_out_all, down_weight, gate_up):
     length, depth = grad_out_all.shape
     width = down_weight.shape[0]
     step = QUERY_ROWS
     return pl.pallas_call(
         hidden_back_body,
         grid=(length // step,),
-        out_shape=(shape((length, 2 * width)), shape((length, depth))),
+        out_shape=shape((length, 2 * width)),
         in_specs=[
             pl.BlockSpec((step, depth), lambda i: (i, 0)),
             pl.BlockSpec((width, depth), lambda i: (0, 0)),
             pl.BlockSpec((step, 2 * width), lambda i: (i, 0)),
-            pl.BlockSpec((step, width), lambda i: (i, 0)),
         ],
-        out_specs=(
-            pl.BlockSpec((step, 2 * width), lambda i: (i, 0)),
-            pl.BlockSpec((step, depth), lambda i: (i, 0)),
-        ),
+        out_specs=pl.BlockSpec((step, 2 * width), lambda i: (i, 0)),
         compiler_params=pltpu.CompilerParams(vmem_limit_bytes=VMEM_MEGABYTES << 20),
         cost_estimate=pl.CostEstimate(
             flops=4 * length * depth * width, bytes_accessed=3 * 10**7, transcendentals=10**6
         ),
-    )(grad_out_all, down_weight, gate_up, hidden)
-
-
-def meet_twin():
+    )(grad_out_all, down_weight, gate_up)
+
+
+def meet_twin(neighbours=False):
     me = lax.axis_index("fsdp")
     barrier = pltpu.get_barrier_semaphore()
     signal(barrier, fsdp=me + 1 - 2 * lax.rem(me, 2))
-    pl.semaphore_wait(barrier, 1)
+    if neighbours:
+        _, across, along, _ = plane_places()
+        signal(barrier, ctx=across)
+        signal(barrier, ctx=along)
+    pl.semaphore_wait(barrier, 3 if neighbours else 1)
 
 
 def shard_rows(array, shards, core):
@@ -1049,8 +1008,7 @@
     return pl.ds(pl.multiple_of(tile * GRAD_TILE, GRAD_TILE), GRAD_TILE)
 
 
-def core_grads_body(shards, across, gradient, *refs):
-    *outs, half, send_buf, recv_buf, send_sem, recv_sem = refs
+def core_grads_body(shards, across, gradient, out, half, send_buf, recv_buf, send_sem, recv_sem):
     core = lax.rem(lax.axis_index("fsdp"), 2)
     tiles = gradient.shape[1] // GRAD_TILE
     sums = CoreSum(send_buf, recv_buf, send_sem, recv_sem)
@@ -1066,44 +1024,25 @@
     lax.fori_loop(0, tiles, send, 0)
     half[...] = shard_rows(across, shards, core)
 
-    def total(tile):
+    def keep(tile, carry):
         columns = column_tile(tile)
         value = product(half[...], gradient[:, columns])
         sums.copy(tile).wait()
-        return (value + recv_buf[:, columns].astype(jnp.float32)).astype(jnp.bfloat16)
-
-    done = 0
-    first = 0
-    for out in outs:
-        width = out.shape[1]
-        whole = (first + width) // GRAD_TILE
-
-        def keep(tile, carry, out=out, first=first):
-            start = pl.multiple_of(tile * GRAD_TILE - first, LANES)
-            out[:, pl.ds(start, GRAD_TILE)] = total(tile)
-            return carry
-
-        lax.fori_loop(done // GRAD_TILE, whole, keep, 0)
-        done = whole * GRAD_TILE
-        rest = first + width - done
-        if rest and out is not outs[-1]:
-            value = total(whole)
-            out[:, width - rest :] = value[:, :rest]
-            following = outs[outs.index(out) + 1]
-            following[:, : GRAD_TILE - rest] = value[:, rest:]
-            done += GRAD_TILE
-        first += width
-
-
-def core_grads(shards, ident, source, gradient, parts=1):
+        out[:, columns] = (value + recv_buf[:, columns].astype(jnp.float32)).astype(jnp.bfloat16)
+        return carry
+
+    lax.fori_loop(0, tiles, keep, 0)
+
+
+def core_grads(shards, ident, source, gradient):
     depth, length = source.shape
     width = gradient.shape[1]
     tiles = width // GRAD_TILE
     return call_plane(
         functools.partial(core_grads_body, shards),
         ident,
-        (shape((depth // 2, width // parts)),) * parts,
-        (VMEM,) * parts,
+        shape((depth // 2, width)),
+        VMEM,
         [VMEM] * 2,
         [
             pltpu.VMEM((depth // 2, length), jnp.bfloat16),
@@ -1118,9 +1057,99 @@
     )
 
 
+def hidden_grads_body(
+    count, shards, across, gradient, hidden, down_weight, gate_out, up_out, output, half, gradient_buf,
+    send_buf, recv_buf, send_sem, recv_sem, load_sem, *refs
+):
+    core = lax.rem(lax.axis_index("fsdp"), 2)
+    scatter = Scatter(count, hidden, down_weight, False, refs[:SCATTER_REFS])
+    span = half.shape[1] // (shards // 2)
+    grad_loads = []
+    for which in range(2):
+        owner = (1 - core, core)[which]
+        for chip in range(shards // 2):
+            start = pl.multiple_of((2 * chip + owner) * span, 16)
+            target = half.at[which, pl.ds(chip * span, span)]
+            sem = load_sem.at[which, chip]
+            grad_loads.append(begin(across.at[pl.ds(start, span)], target, sem))
+    grad_loads.append(begin(gradient, gradient_buf, load_sem.at[2, 0]))
+    meet(count, shards)
+    sums = CoreSum(send_buf, recv_buf, send_sem, recv_sem)
+    tiles = gradient_buf.shape[1] // GRAD_TILE
+    width = gate_out.shape[1]
+
+    def send(tile, carry):
+        columns = column_tile(tile)
+        value = product(half[0], gradient_buf[:, columns])
+        send_buf[:, columns] = value.astype(jnp.bfloat16)
+        sums.copy(tile).start()
+        return carry
+
+    def keep(tile, carry):
+        columns = column_tile(tile)
+        value = product(half[1], gradient_buf[:, columns])
+        sums.copy(tile).wait()
+        value = (value + recv_buf[:, columns].astype(jnp.float32)).astype(jnp.bfloat16)
+        send_buf[:, columns] = value
+        return carry
+
+    def wait_loads():
+        for load in grad_loads:
+            load.wait()
+
+    bounds = [0, 3, 6, 9, tiles]
+    others = [wait_loads]
+    for body in (send, keep):
+        for first, last in zip(bounds, bounds[1:]):
+            others.append(lambda body=body, a=first, b=last: lax.fori_loop(a, b, body, 0))
+    scatter.run(others)
+    stores = [
+        begin(send_buf.at[:, pl.ds(i * width, width)], out, load_sem.at[2, 1 + i])
+        for i, out in enumerate((gate_out, up_out))
+    ]
+    scatter.finish()
+
+    def strip(where):
+        output[where, :] = received(count, scatter.recv_buf, scatter.total, where)
+
+    for_strips(0, output.shape[0], strip)
+    for store in stores:
+        store.wait()
+
+
+def hidden_grads(count, shards, ident, across, gradient, hidden, down_weight):
+    depth, length = across.shape
+    width = gradient.shape[1]
+    tiles = width // GRAD_TILE
+    rows = length // count
+    half = shape((depth // 2, width // 2))
+    return call_plane(
+        functools.partial(hidden_grads_body, count, shards),
+        ident,
+        (half, half, shape((rows, depth), jnp.float32)),
+        (HBM, HBM, VMEM),
+        [HBM] * 4,
+        [
+            pltpu.VMEM((2, depth // 2, length), jnp.bfloat16),
+            pltpu.VMEM((length, width), jnp.bfloat16),
+            pltpu.VMEM((depth // 2, width), jnp.bfloat16),
+            pltpu.VMEM((depth // 2, width), jnp.bfloat16),
+            pltpu.SemaphoreType.DMA((tiles,)),
+            pltpu.SemaphoreType.DMA((tiles,)),
+            pltpu.SemaphoreType.DMA((3, shards // 2)),
+        ]
+        + scatter_scratch(count, rows, depth, hidden, down_weight, False, hidden.shape[1]),
+        6 * 10**10,
+        VMEM_MEGABYTES,
+        (across, gradient, hidden, down_weight),
+    )
+
+
 def attention_grads_body(
-    shards, across, gradient, heads, branch_all, out, half, outs, send_buf, recv_buf, send_sem, recv_sem
+    shards, across, gradient, heads, branch_all, *refs
 ):
+    near, out, far, refs = (refs[:4], refs[4], refs[5:9], refs[9:])
+    half, outs, send_buf, recv_buf, send_sem, recv_sem, far_send, far_recv = refs
     core = lax.rem(lax.axis_index("fsdp"), 2)
     width = gradient.shape[1]
     tiles = width // GRAD_TILE
@@ -1129,7 +1158,17 @@
     span = out.shape[0] // (shards // 2)
     height = HEAD_DIM
     sums = CoreSum(send_buf, recv_buf, send_sem, recv_sem)
-    meet_twin()
+    meet_twin(True)
+    copies = []
+    _, to_across, to_along, _ = plane_places()
+    for index, target in enumerate(far):
+        source = near[index]
+        rows = source.shape[0] // 2
+        half_rows = pl.ds(rows * (index % 2), rows)
+        peer = (to_along, to_across)[index % 2]
+        copies.append(
+            remote(source.at[half_rows], target, far_send.at[index], far_recv.at[index], ctx=peer)
+        )
 
     def heads_product(index, carry):
         columns = pl.ds(pl.multiple_of(index * 512, 512), 512)
@@ -1173,9 +1212,11 @@
     for rows, value in pieces(core):
         value = value + recv_buf[rows, width:].astype(jnp.float32)
         out[rows, width:] = value.astype(jnp.bfloat16)
-
-
-def attention_grads(shards, ident, first_across, grad_packed, heads_across, branch_all):
+    for copy in copies:
+        copy.wait()
+
+
+def attention_grads(shards, ident, first_across, grad_packed, heads_across, branch_all, *near):
     depth, length = first_across.shape
     heads = heads_across.shape[0]
     width = grad_packed.shape[1] + heads
@@ -1183,9 +1224,9 @@
     return call_plane(
         functools.partial(attention_grads_body, shards),
         ident,
-        shape((depth // 2, width)),
-        VMEM,
-        [VMEM] * 4,
+        (shape((depth // 2, width)), *[shape((n.shape[0] // 2, n.shape[1])) for n in near]),
+        (VMEM,) + (HBM,) * 4,
+        [VMEM] * 4 + [HBM] * 4,
         [
             pltpu.VMEM((depth // 2, length), jnp.bfloat16),
             pltpu.VMEM((heads, branch_all.shape[1]), jnp.float32),
@@ -1193,10 +1234,12 @@
             pltpu.VMEM((depth // 2, width), jnp.bfloat16),
             pltpu.SemaphoreType.DMA((tiles,)),
             pltpu.SemaphoreType.DMA((tiles,)),
+            pltpu.SemaphoreType.DMA((4,)),
+            pltpu.SemaphoreType.DMA((4,)),
         ],
         2 * length * depth * width,
         VMEM_MEGABYTES,
-        (first_across, grad_packed, heads_across, branch_all),
+        (first_across, grad_packed, heads_across, branch_all, *near),
     )
 
 
@@ -1789,33 +1832,32 @@
     if dealt_heads:
         hidden_across, *near = tie((hidden_across, *near))
         grad_out_all = place_rows(plane_far(near), jnp.bfloat16)
-        (down_term,) = core_grads(shard_count, 5, hidden_across, grad_out_all)
+        down_term = core_grads(shard_count, 5, hidden_across, grad_out_all)
     else:
         down_term = column_term(hidden, grad_out_all)
     down_part, down_term = tie((down_part, down_term))
     down_piece = scatter_shards(down_term, dealt_heads)
-    grad_gate_up, output_partial = hidden_backward(grad_out_all, down_part, gate_up, hidden)
-    relayed = plane_relay(output_partial)
+    grad_gate_up = hidden_backward(grad_out_all, down_part, gate_up)
     if dealt_heads:
-        terms = core_grads(shard_count, 6, second_across, grad_gate_up, 2)
+        *terms, output_sum = hidden_grads(
+            part_count, shard_count, 6, second_across, grad_gate_up, hidden, down_part
+        )
     else:
         gate_up_term = column_term(second_all, grad_gate_up).astype(jnp.bfloat16)
         terms = (gate_up_term[:, : FF // part_count], gate_up_term[:, FF // part_count :])
-    grad_gate_up, *tied = tie((grad_gate_up, *terms, *relayed))
-    terms, relayed = (tied[:2], tied[2:])
+        output_partial = product(hidden, down_part).astype(jnp.bfloat16)
+        output_sum = lax.psum_scatter(output_partial, "ctx", scatter_dimension=0, tiled=True)
+    block_output = (residual_mid + output_sum.astype(jnp.float32)).astype(jnp.bfloat16)
+    grad_gate_up, down_piece, *terms = tie((grad_gate_up, down_piece, *terms))
     gate_piece = scatter_shards(terms[0], dealt_heads)
     up_piece = scatter_shards(terms[1], dealt_heads)
-    last = plane_last(output_partial, relayed)
     grad_mid, second_gain_part, branch_all = middle_back(
         part_count, 3, grad_gate_up, gate_up_part, residual_mid, gain_second, cotangent[0]
     )
-    branch_all, down_piece, gate_piece, *last = tie((branch_all, down_piece, gate_piece, *last))
-    block_output = (residual_mid + plane_scatter(output_partial, relayed, last)).astype(
-        jnp.bfloat16
-    )
+    branch_all, gate_piece, down_piece = tie((branch_all, gate_piece, down_piece))
     if dealt_heads:
-        down_parts = plane_gather(down_piece)
-        gate_parts = plane_gather(gate_piece)
+        down_near = plane_near(down_piece)
+        gate_near = plane_near(gate_piece)
 
     grad_packed = attend_backward(
         block_rows,
@@ -1830,11 +1872,18 @@
         tables,
     )
     if dealt_heads:
-        packed_term = attention_grads(
-            shard_count, 7, first_across, grad_packed, heads_across, branch_all
+        packed_term, *far = attention_grads(
+            shard_count,
+            7,
+            first_across,
+            grad_packed,
+            heads_across,
+            branch_all,
+            *down_near[1:],
+            *gate_near[1:],
         )
-        grad_packed, packed_term, *parts = tie((grad_packed, packed_term, *down_parts, *gate_parts))
-        down_parts, gate_parts = (parts[:5], parts[5:])
+        down_parts, gate_parts = ((*down_near, *far[:2]), (*gate_near, *far[2:]))
+        grad_packed, packed_term = tie((grad_packed, packed_term))
         packed_piece = scatter_shards(packed_term, True)
     grad_input, gain_shard, up_all = input_back(
         part_count,
@@ -1850,11 +1899,13 @@
     )
     if dealt_heads:
         grad_input, packed_piece = tie((grad_input, packed_piece))
+        packed_near = plane_near(packed_piece)
         gate_shard = place_hidden(shard_count, gate_parts)
         up_shard = place_sorted(shard_count, up_all)
         down_shard = place_rows(down_parts, jnp.float32)
+        gate_shard, up_shard, *packed_near = tie((gate_shard, up_shard, *packed_near))
         query_shard, key_shard, value_shard, output_shard = place_attention(
-            shard_count, plane_gather(packed_piece)
+            shard_count, plane_far(packed_near)
         )
     else:
 

time: 556 us -> 550 us (0.989)
  Pallas kernels: 465 us -> 479 us
  starting transfers between devices: 22.6 us -> 13.1 us
    pallas_call x7, Pallas kernels: 344 us -> 365 us  [call_plane(): pl.pallas_call(body, out_shape=outs, in_specs=in_specs, out_specs=out_spe...]
    ppermute x20 -> x12, starting transfers between devices: 21.6 us -> 12.5 us  [swap(): return lax.ppermute(array, 'ctx', pairs)]
    pallas_call x1, Pallas kernels: 20.8 us -> 14.1 us  [hidden_backward(): pl.pallas_call(hidden_back_body, grid=(length // step,), out_shape=shape(...]
    ppermute x20 -> x12, waiting for transfers between devices: 28 us -> 21.5 us  [swap(): return lax.ppermute(array, 'ctx', pairs)]
  transfers between devices with their start and end apart: 26 -> 18, of which waited for: 7 -> 11; matrix products, arithmetic and copies ran while one was open for 3% -> 1% of each run, Pallas kernels for 72% -> 75%
where the time goes in v5:
time: 550 us; the launch traced here: 547 us
  Pallas kernels  479 us (87%)
  waiting for transfers between devices  27.8 us (5%)
  between operations  14.5 us (3%)
  starting transfers between devices  13.1 us (2%)
  local copies, waits for them, and re-layouts  10.2 us (2%)
    pallas_call x7, Pallas kernels, call_plane(): pl.pallas_call(body, out_shape=outs, in_specs=in_specs, out_specs=out_spe...  365 us
    pallas_call x1, Pallas kernels, attend_backward(): pl.pallas_call(functools.partial(attend_back_body, block_rows), out_shape...  27.1 us
    pallas_call x1, Pallas kernels, attend_forward(): pl.pallas_call(functools.partial(attend_body, block_rows), out_shape=(sha...  26.4 us
    ppermute x12, waiting for transfers between devices, swap(): return lax.ppermute(array, 'ctx', pairs)  21.5 us
    pallas_call x1, Pallas kernels, hidden_forward(): pl.pallas_call(hidden_body, grid=(length // step,), out_shape=(shape((len...  21.1 us
    pallas_call x1, Pallas kernels, hidden_backward(): pl.pallas_call(hidden_back_body, grid=(length // step,), out_shape=shape(...  14.1 us
    ppermute x12, starting transfers between devices, swap(): return lax.ppermute(array, 'ctx', pairs)  12.5 us
  transfers between devices with their start and end apart: 18, of which 11 were waited for; matrix products, arithmetic and copies ran while one was open for 1% of the time, Pallas kernels for 75%

profile of v5, /device:TPU:0, one launch (start us, length us, event | category | flops | bytes accessed | tf_op | source)
XLA Modules:
  0.0 547.2 jit_solution(12982307146886308034)
XLA Ops:
  9.8 63.3 %shard_map.203 = (bf16[1024,2048]{1,0:T(8,128)(2,1)}, f32[1,2048]{1,0:T(1,128)}, f32[1,2048]{1,0:T(1,128)}, f32[1024,128]{1,0:T(8,128)}, f32[1024,128]{1,0:T(8,1...) custom-call(bf16[256,2048]{1,0:T(8,128)(2,1)} %bitcast.14, bf16[1,256]{1,0:T(2,128)(2,1)} %broadcast_in_dim.12.first_gain, ...), custom_call_target="tpu_custom_call" | custom-call | flops 49999998976 | bytes 166666672 | tf_op jit(solution)/shard_map/pallas_call | solution.py:482
  74.4 26.4 %shard_map.204 = (bf16[1024,512]{1,0:T(8,128)(2,1)}, bf16[1024,512]{1,0:T(8,128)(2,1)}, bf16[4,1024,128]{2,1,0:T(8,128)(2,1)}, bf16[4,1024,128]{2,1,0:T(8,128)(2...) custom-call(s32[1,8]{1,0:T(1,128)} %dealing.3, ...), custom_call_target="tpu_custom_call" | custom-call | flops 30000001024 | bytes 10000000 | tf_op jit(solution)/shard_map/pallas_call | solution.py:1558
  100.9 77.1 %shard_map.205 = (f32[256,2048]{1,0:T(8,128)}, bf16[1024,2048]{1,0:T(8,128)(2,1)}) custom-call(bf16[1024,512]{1,0:T(8,128)(2,1)} %get-tuple-element.83.attended, bf16[512,2048]{1,0:T(8,128)(2,1)} %get-tuple-element.84.weight.output_weight, bf16[256,2048]{1,0:T(8,128)(2,1)} %bitcast.15, f32[1,2048]{1,0:T(1,128)} %get-tuple-element.85.gain), custom_call_target="tpu_custom_call" | custom-call | flops 60000002048 | bytes 200000000 | tf_op jit(solution)/shard_map/pallas_call | solution.py:482
  178.4 1.7 collective-permute-start
  180.6 21.1 %shard_map.206 = (f32[1024,2816]{1,0:T(8,128)}, bf16[1024,1408]{1,0:T(8,128)(2,1)}, bf16[2048,1024]{1,0:T(8,128)(2,1)}, bf16[1408,1024]{1,0:T(8,128)(2,1)}) custom-call(bf16[1024,2048]{1,0:T(8,128)(2,1)} %get-tuple-element.88.rows, bf16[2048,2816]{1,0:T(8,128)(2,1)} %all-gather.3.cloned.1.call-done.gate_weight.up_weight.gate_up_weight, ...), custom_call_target="tpu_custom_call" | custom-call | flops 11811160064 | bytes 30000000 | tf_op jit(solution)/shard_map/pallas_call | solution.py:914
  202.7 1.7 collective-permute-start.3
  204.8 11.1 %collective-permute-done.3.high = bf16[128,2048]{1,0:T(8,128)(2,1)S(1)} collective-permute-done((bf16[128,2048]{1,0:T(8,128)(2,1)S(1)}, bf16[128,2048]{1,0:T(8,128)(2,1)S(1)}, u32[]{:S(2)}, u32[]{:S(2)}) %collective-permute-start.3) | collective-permute-done | bytes 524320 | tf_op jit(solution)/shard_map/ppermute | solution.py:880
  218.0 4.4 shard_map.207.gradient.grad_rows
  222.4 15.0 %shard_map.208 = bf16[704,2048]{1,0:T(8,128)(2,1)} custom-call(bf16[1408,1024]{1,0:T(8,128)(2,1)} %get-tuple-element.96.across, bf16[1024,2048]{1,0:T(8,128)(2,1)} %shard_map.207.gradient.grad_rows), custom_call_target="tpu_custom_call" | custom-call | flops 5905580032 | bytes 19685266 | tf_op jit(solution)/shard_map/pallas_call | solution.py:482
  237.4 3.6 all-gather.5.cloned.1.call-done.down_weight
  241.3 14.1 %shard_map.209.gradient.grad_gate_up = bf16[1024,2816]{1,0:T(8,128)(2,1)} custom-call(bf16[1024,2048]{1,0:T(8,128)(2,1)} %shard_map.207.gradient.grad_rows, bf16[1408,2048]{1,0:T(8,128)(2,1)} %all-gather.5.cloned.1.call-done.down_weight, f32[1024,2816]{1,0:T(8,128)} %get-tuple-element.98.gate_up), custom_call_target="tpu_custom_call" | custom-call | flops 11811160064 | bytes 30000000 | tf_op jit(solution)/shard_map/pallas_call | solution.py:952
  255.3 41.3 %shard_map.210 = (bf16[1024,1408]{1,0:T(8,128)(2,1)}, bf16[1024,1408]{1,0:T(8,128)(2,1)}, f32[256,2048]{1,0:T(8,128)}) custom-call(bf16[2048,1024]{1,0:T(8,128)(2,1)} %get-tuple-element.90.across, bf16[1024,2816]{1,0:T(8,128)(2,1)} %shard_map.209.gradient.grad_gate_up, bf16[1024,1408]{1,0:T(8,128)(2,1)} %get-tuple-element.99.hidden, ...), custom_call_target="tpu_custom_call" | custom-call | flops 60000002048 | bytes 200000000 | tf_op jit(solution)/shard_map/pallas_call | solution.py:482
  296.6 1.6 reduce-scatter.5.cloned.1.call-done.own
  298.8 78.6 %shard_map.211 = (f32[256,2048]{1,0:T(8,128)}, f32[1,2048]{1,0:T(1,128)}, bf16[1024,2048]{1,0:T(8,128)(2,1)}) custom-call(bf16[1024,2816]{1,0:T(8,128)(2,1)} %shard_map.209.gradient.grad_gate_up, bf16[2048,2816]{1,0:T(8,128)(2,1)} %all-gather.3.cloned.1.call-done.gate_weight.up_weight.gate_up_weight, f32[256,2048]{1,0:T(8,128)} %get-tuple-element.86.residual, ...), custom_call_target="tpu_custom_call" | custom-call | flops 60000002048 | bytes 200000000 | tf_op jit(solution)/shard_map/pallas_call | solution.py:482
  381.6 27.1 %shard_map.212.gradient.grad_packed = bf16[1024,1024]{1,0:T(8,128)(2,1)} custom-call(s32[1,8]{1,0:T(1,128)} %dealing.3, bf16[1024,2048]{1,0:T(8,128)(2,1)} %get-tuple-element.108.branch_all, bf16[512,2048]{1,0:T(8,128)(2,1)} %get-tuple-element.84.weight.output_weight, bf16[1024,512]{1,0:T(8,128)(2,1)} %get-tuple-element.109.queries, ...), custom_call_target="tpu_custom_call" | custom-call | flops 60000002048 | bytes 10000000 | tf_op jit(solution)/shard_map/pallas_call | solution.py:1697
  411.0 24.4 %shard_map.213 = (bf16[1024,1536]{1,0:T(8,128)(2,1)}, bf16[88,2048]{1,0:T(8,128)(2,1)}, bf16[88,2048]{1,0:T(8,128)(2,1)}, bf16[128,1408]{1,0:T(8,128)(2,1)}, bf16[128,1408]{1,0:T(8,128)(2,1)}) custom-call(bf16[2048,1024]{1,0:T(8,128)(2,1)} %get-tuple-element.113.across, bf16[1024,1024]{1,0:T(8,128)(2,1)} %shard_map.212.gradient.grad_packed, ...), custom_call_target="tpu_custom_call" | custom-call | flops 6442450944 | bytes 21474836 | tf_op jit(solution)/shard_map/pallas_call | solution.py:482
  435.4 65.3 %shard_map.214 = (bf16[256,2048]{1,0:T(8,128)(2,1)}, f32[2,256]{1,0:T(2,128)}, bf16[1024,1408]{1,0:T(8,128)(2,1)}) custom-call(bf16[1024,1024]{1,0:T(8,128)(2,1)} %shard_map.212.gradient.grad_packed, bf16[2048,1536]{1,0:T(8,128)(2,1)} %get-tuple-element.80.weight, bf16[256,2048]{1,0:T(8,128)(2,1)} %bitcast.16, f32[256,2048]{1,0:T(8,128)} %get-tuple-element.119.grad_mid, ...), custom_call_target="tpu_custom_call" | custom-call | flops 49999998976 | bytes 166666672 | tf_op jit(solution)/shard_map/pallas_call | solution.py:482
  502.9 5.5 %shard_map.216 = f32[256,5632]{1,0:T(8,128)} custom-call(bf16[1024,1408]{1,0:T(8,128)(2,1)} %get-tuple-element.128.refs_0_.refs_1_.refs_2_.refs_3_, bf16[1024,1408]{1,0:T(8,128)(2,1)} %get-tuple-element.128.refs_0_.refs_1_.refs_2_.refs_3_, bf16[1024,1408]{1,0:T(8,128)(2,1)} %get-tuple-element.128.refs_0_.refs_1_.refs_2_.refs_3_, ...), custom_call_target="tpu_custom_call" | custom-call | bytes 10000000 | tf_op jit(solution)/shard_map/pallas_call | solution.py:1278
  508.4 5.7 %shard_map.215 = f32[256,5632]{1,0:T(8,128)} custom-call(bf16[256,1408]{1,0:T(8,128)(2,1)} %reduce-scatter.7.cloned.1.call-done.refs_0_, bf16[256,1408]{1,0:T(8,128)(2,1)} %collective-permute-done.6.refs_2_.refs_1_, bf16[256,1408]{1,0:T(8,128)(2,1)} %copy-done.11, bf16[128,1408]{1,0:T(8,128)(2,1)} %get-tuple-element.126.refs_3_, ...), custom_call_target="tpu_custom_call" | custom-call | bytes 10000000 | tf_op jit(solution)/shard_map/pallas_call | solution.py:1307
  514.1 5.7 %collective-permute-done.9.from_along = bf16[256,1536]{1,0:T(8,128)(2,1)S(1)} collective-permute-done((bf16[256,1536]{1,0:T(8,128)(2,1)}, bf16[256,1536]{1,0:T(8,128)(2,1)S(1)}, u32[]{:S(2)}, u32[]{:S(2)}) %collective-permute-start.9) | collective-permute-done | bytes 786464 | tf_op jit(solution)/shard_map/ppermute | solution.py:880
  524.2 2.8 fusion
  527.1 4.8 shard_map.218
  533.2 4.7 shard_map.217
  537.9 2.3 copy.24
  (76 shorter events, 23.3 us)
Async XLA Ops:
  7.2 66.1 %copy-start = (bf16[704,2048]{1,0:T(8,128)(2,1)S(1)}, bf16[704,2048]{1,0:T(8,128)(2,1)}, u32[]{:S(2)}) copy-start(bf16[704,2048]{1,0:T(8,128)(2,1)} %param.22) | copy-start | bytes 8650756
  7.2 173.4 %all-gather.3.cloned.1.call-start = ((), (), s32[]{:S(2)}) async-start(), calls=%async_computation.4 | async-start | bytes 12976128 | tf_op jit(solution)/shard_map/all_gather | solution.py:1748
  73.2 167.8 %all-gather.5.cloned.1.call-start = ((), (), s32[]{:S(2)}) async-start(), calls=%async_computation.5 | async-start | bytes 6488064 | tf_op jit(solution)/shard_map/all_gather | solution.py:1748
  74.2 223.9 %reduce-scatter.5.cloned.1.call-start = ((), (), s32[]{:S(2)}) async-start(), calls=%async_computation.6 | async-start | bytes 3604480 | tf_op jit(solution)/shard_map/reduce_scatter | solution.py:1754
  100.9 77.1 %copy-start.7 = (bf16[1,256,2048]{2,1,0:T(8,128)(2,1)S(1)}, bf16[1,256,2048]{2,1,0:T(8,128)(2,1)}, u32[]{:S(2)}) copy-start(bf16[1,256,2048]{2,1,0:T(8,128)(2,1)} %param.23) | copy-start | bytes 3145732
  178.0 24.5 %collective-permute-start.1 = (bf16[256,2048]{1,0:T(8,128)(2,1)S(1)}, bf16[256,2048]{1,0:T(8,128)(2,1)S(1)}, u32[]{:S(2)}, u32[]{:S(2)}) collective-permute-start(bf16[256,2048]{1,0:T(8,128)(2,1)S(1)} %bitcast.10), channel_id=1, source_target_pairs={{0,16},{8,24},{16,0},{24,8},{1,17},{9,25},{17,1},{25,9},{2,18},{10... | collective-permute-start | bytes 3145736 | tf_op jit(solution)/shard_map/ppermute | solution.py:880
  178.4 24.2 %collective-permute-start = (bf16[256,2048]{1,0:T(8,128)(2,1)S(1)}, bf16[256,2048]{1,0:T(8,128)(2,1)S(1)}, u32[]{:S(2)}, u32[]{:S(2)}) collective-permute-start(bf16[256,2048]{1,0:T(8,128)(2,1)S(1)} %bitcast.11), channel_id=1, source_target_pairs={{0,8},{8,0},{16,24},{24,16},{1,9},{9,1},{17,25},{25,17},{2,10},{10... | collective-permute-start | bytes 3145736 | tf_op jit(solution)/shard_map/ppermute | solution.py:880
  202.5 14.6 %copy-start.2 = (bf16[256,2048]{1,0:T(8,128)(2,1)}, bf16[256,2048]{1,0:T(8,128)(2,1)S(1)}, u32[]{:S(2)}) copy-start(bf16[256,2048]{1,0:T(8,128)(2,1)S(1)} %collective-permute-done.1.from_along) | copy-start | bytes 3145732
  202.6 14.6 %copy-start.3 = (bf16[256,2048]{1,0:T(8,128)(2,1)}, bf16[256,2048]{1,0:T(8,128)(2,1)S(1)}, u32[]{:S(2)}) copy-start(bf16[256,2048]{1,0:T(8,128)(2,1)S(1)} %collective-permute-done.from_across) | copy-start | bytes 3145732
  202.7 13.3 %collective-permute-start.3 = (bf16[128,2048]{1,0:T(8,128)(2,1)S(1)}, bf16[128,2048]{1,0:T(8,128)(2,1)S(1)}, u32[]{:S(2)}, u32[]{:S(2)}) collective-permute-start(bf16[128,2048]{1,0:T(8,128)(2,1)S(1)} %slice.19), channel_id=1, source_target_pairs={{0,8},{8,0},{16,24},{24,16},{1,9},{9,1},{17,25},{25,17},{2,10},{10... | collective-permute-start | bytes 1572872 | tf_op jit(solution)/shard_map/ppermute | solution.py:880
  204.4 12.7 %collective-permute-start.2 = (bf16[128,2048]{1,0:T(8,128)(2,1)S(1)}, bf16[128,2048]{1,0:T(8,128)(2,1)S(1)}, u32[]{:S(2)}, u32[]{:S(2)}) collective-permute-start(bf16[128,2048]{1,0:T(8,128)(2,1)S(1)} %slice.18), channel_id=1, source_target_pairs={{0,16},{8,24},{16,0},{24,8},{1,17},{9,25},{17,1},{25,9},{2,18},{10... | collective-permute-start | bytes 1572872 | tf_op jit(solution)/shard_map/ppermute | solution.py:880
  241.0 136.5 %reduce-scatter.7.cloned.1.call-start = ((), (), s32[]{:S(2)}) async-start(), calls=%async_computation.7 | async-start | bytes 3604480 | tf_op jit(solution)/shard_map/reduce_scatter | solution.py:1754
  298.2 137.2 %reduce-scatter.9.cloned.1.call-start = ((), (), s32[]{:S(2)}) async-start(), calls=%async_computation.8 | async-start | bytes 3604480 | tf_op jit(solution)/shard_map/reduce_scatter | solution.py:1754
  298.8 202.0 %reduce-scatter.11.cloned.1.call-start = ((), (), s32[]{:S(2)}) async-start(), calls=%async_computation.9 | async-start | bytes 3932160 | tf_op jit(solution)/shard_map/reduce_scatter | solution.py:1754
  298.8 78.7 %copy-start.8 = (bf16[176,2048]{1,0:T(8,128)(2,1)S(1)}, bf16[176,2048]{1,0:T(8,128)(2,1)}, u32[]{:S(2)}) copy-start(bf16[176,2048]{1,0:T(8,128)(2,1)} %reduce-scatter.5.cloned.1.call-done.own) | copy-start | bytes 2162692
  377.5 31.2 %collective-permute-start.5 = (bf16[176,2048]{1,0:T(8,128)(2,1)S(1)}, bf16[176,2048]{1,0:T(8,128)(2,1)S(1)}, u32[]{:S(2)}, u32[]{:S(2)}) collective-permute-start(bf16[176,2048]{1,0:T(8,128)(2,1)S(1)} %copy-done.8), channel_id=1, source_target_pairs={{0,16},{8,24},{16,0},{24,8},{1,17},{9,25},{17,1},{25,9},{2,18},{10... | collective-permute-start | bytes 2162696 | tf_op jit(solution)/shard_map/ppermute | solution.py:880
  378.1 30.6 %collective-permute-start.4 = (bf16[176,2048]{1,0:T(8,128)(2,1)S(1)}, bf16[176,2048]{1,0:T(8,128)(2,1)S(1)}, u32[]{:S(2)}, u32[]{:S(2)}) collective-permute-start(bf16[176,2048]{1,0:T(8,128)(2,1)S(1)} %copy-done.8), channel_id=1, source_target_pairs={{0,8},{8,0},{16,24},{24,16},{1,9},{9,1},{17,25},{25,17},{2,10},{10... | collective-permute-start | bytes 2162696 | tf_op jit(solution)/shard_map/ppermute | solution.py:880
  379.6 30.5 %collective-permute-start.7 = (bf16[256,1408]{1,0:T(8,128)(2,1)}, bf16[256,1408]{1,0:T(8,128)(2,1)S(1)}, u32[]{:S(2)}, u32[]{:S(2)}) collective-permute-start(bf16[256,1408]{1,0:T(8,128)(2,1)} %reduce-scatter.7.cloned.1.call-done.refs_0_), channel_id=1, source_target_pairs={{0,16},{8,24},{16,0},{24,8},{1,17},{9,25},{17,1},{25,9},{2,18},{10... | collective-permute-start | bytes 2162696 | tf_op jit(solution)/shard_map/ppermute | solution.py:880
  380.2 30.4 %collective-permute-start.6 = (bf16[256,1408]{1,0:T(8,128)(2,1)}, bf16[256,1408]{1,0:T(8,128)(2,1)}, u32[]{:S(2)}, u32[]{:S(2)}) collective-permute-start(bf16[256,1408]{1,0:T(8,128)(2,1)} %reduce-scatter.7.cloned.1.call-done.refs_0_), channel_id=1, source_target_pairs={{0,8},{8,0},{16,24},{24,16},{1,9},{9,1},{17,25},{25,17},{2,10},{10... | collective-permute-start | bytes 2162696 | tf_op jit(solution)/shard_map/ppermute | solution.py:880
  500.8 19.0 %collective-permute-start.9 = (bf16[256,1536]{1,0:T(8,128)(2,1)}, bf16[256,1536]{1,0:T(8,128)(2,1)S(1)}, u32[]{:S(2)}, u32[]{:S(2)}) collective-permute-start(bf16[256,1536]{1,0:T(8,128)(2,1)} %reduce-scatter.11.cloned.1.call-done.own), channel_id=1, source_target_pairs={{0,16},{8,24},{16,0},{24,8},{1,17},{9,25},{17,1},{25,9},{2,18},{10... | collective-permute-start | bytes 2359304 | tf_op jit(solution)/shard_map/ppermute | solution.py:880
  501.8 18.7 %collective-permute-start.8 = (bf16[256,1536]{1,0:T(8,128)(2,1)}, bf16[256,1536]{1,0:T(8,128)(2,1)S(1)}, u32[]{:S(2)}, u32[]{:S(2)}) collective-permute-start(bf16[256,1536]{1,0:T(8,128)(2,1)} %reduce-scatter.11.cloned.1.call-done.own), channel_id=1, source_target_pairs={{0,8},{8,0},{16,24},{24,16},{1,9},{9,1},{17,25},{25,17},{2,10},{10... | collective-permute-start | bytes 2359304 | tf_op jit(solution)/shard_map/ppermute | solution.py:880
  508.4 15.9 %copy-start.4 = (f32[256,2048]{1,0:T(8,128)S(1)}, f32[256,2048]{1,0:T(8,128)}, u32[]{:S(2)}) copy-start(f32[256,2048]{1,0:T(8,128)} %get-tuple-element.86.residual) | copy-start | bytes 6291460
  522.2 10.3 %collective-permute-start.11 = (bf16[128,1536]{1,0:T(8,128)(2,1)}, bf16[128,1536]{1,0:T(8,128)(2,1)S(1)}, u32[]{:S(2)}, u32[]{:S(2)}) collective-permute-start(bf16[128,1536]{1,0:T(8,128)(2,1)} %slice.22), channel_id=1, source_target_pairs={{0,8},{8,0},{16,24},{24,16},{1,9},{9,1},{17,25},{25,17},{2,10},{10... | collective-permute-start | bytes 1179656 | tf_op jit(solution)/shard_map/ppermute | solution.py:880
  523.2 9.2 %collective-permute-start.10 = (bf16[128,1536]{1,0:T(8,128)(2,1)}, bf16[128,1536]{1,0:T(8,128)(2,1)}, u32[]{:S(2)}, u32[]{:S(2)}) collective-permute-start(bf16[128,1536]{1,0:T(8,128)(2,1)} %slice.21), channel_id=1, source_target_pairs={{0,16},{8,24},{16,0},{24,8},{1,17},{9,25},{17,1},{25,9},{2,18},{10... | collective-permute-start | bytes 1179656 | tf_op jit(solution)/shard_map/ppermute | solution.py:880
  (10 other events, 39.1 us)
Sparse Core Ops, SparseCore 0:
  73.3 107.2 all-gather.2
  182.2 58.7 all-gather.4
  243.3 54.8 reduce-scatter.4
  300.3 56.0 reduce-scatter.6
  358.6 56.0 reduce-scatter.8
  435.5 59.9 reduce-scatter.10

commit v6 on v5

--- a/solution.py
+++ b/solution.py
@@ -771,14 +771,14 @@
 
 
 def input_back_body(
-    count, shards, grad_packed, weight, tokens, grad_mid, piece, gain, second_part, grad_input, gain_sums,
+    count, shards, grad_packed, weight, tokens, piece, gain, second_part, grad_input, gain_sums,
     piece_all, gain_part, parts, part_recv, sums, sums_recv, part_send_sem, part_recv_sem, sums_send_sem,
     sums_recv_sem, *refs
 ):
     scatter = Scatter(count, grad_packed, weight, True, refs[:SCATTER_REFS])
-    side = refs[SCATTER_REFS : SCATTER_REFS + 3]
-    loads = side_loads([tokens, grad_mid], side)
-    gather = RowGather(count, piece, piece_all, refs[SCATTER_REFS + 3 :])
+    side = refs[SCATTER_REFS : SCATTER_REFS + 2]
+    loads = side_loads([tokens], side)
+    gather = RowGather(count, piece, piece_all, refs[SCATTER_REFS + 2 :])
     meet(count, shards)
     scatter.run()
     for part in range(PIECES):
@@ -792,8 +792,7 @@
         gradient = received(count, scatter.recv_buf, scatter.total, where)
         normed, inverse = norm_parts(side[0][where, :].astype(jnp.float32))
         gain_part[...] += jnp.sum(gradient * normed, axis=0, keepdims=True)
-        values = side[1][where, :] + norm_back(gradient * gain[...], normed, inverse)
-        grad_input[where, :] = values.astype(jnp.bfloat16)
+        grad_input[where, :] = norm_back(gradient * gain[...], normed, inverse)
 
     for_strips(0, grad_input.shape[0], strip)
     gather.relay()
@@ -841,7 +840,7 @@
 
 
 def input_back(
-    count, shards, ident, grad_packed, weight, tokens, gain, grad_mid, second_part, piece
+    count, shards, ident, grad_packed, weight, tokens, gain, second_part, piece
 ):
     rows, width = tokens.shape
     span = width // shards
@@ -849,12 +848,12 @@
         functools.partial(input_back_body, count, shards),
         ident,
         (
-            shape((rows, width)),
+            shape((rows, width), jnp.float32),
             shape((2, span), jnp.float32),
             shape((count * piece.shape[0], piece.shape[1])),
         ),
         (VMEM, VMEM, HBM),
-        [HBM] * 5 + [VMEM] * 2,
+        [HBM] * 4 + [VMEM] * 2,
         [
             pltpu.VMEM((1, width), jnp.float32),
             pltpu.VMEM((shards, 2, span), jnp.float32),
@@ -867,11 +866,11 @@
             pltpu.SemaphoreType.DMA((count - 1,)),
         ]
         + scatter_scratch(count, rows, width, grad_packed, weight, True, grad_packed.shape[1])
-        + side_scratch(tokens, grad_mid)
+        + side_scratch(tokens)
         + gather_sems(count),
         5 * 10**10,
         VMEM_MEGABYTES,
-        (grad_packed, weight, tokens, grad_mid, piece, gain, second_part),
+        (grad_packed, weight, tokens, piece, gain, second_part),
     )
 
 
@@ -1058,55 +1057,86 @@
 
 
 def hidden_grads_body(
-    count, shards, across, gradient, hidden, down_weight, gate_out, up_out, output, half, gradient_buf,
-    send_buf, recv_buf, send_sem, recv_sem, load_sem, *refs
+    count, shards, across, grad_rows, gate_up, hidden, down_weight, gate_out, up_out, output,
+    gradient_out, half, gradient, rows_buf, gate_up_buf, send_buf, recv_buf, send_sem, recv_sem,
+    half_sem, block_sem, store_sem, *refs
 ):
     core = lax.rem(lax.axis_index("fsdp"), 2)
-    scatter = Scatter(count, hidden, down_weight, False, refs[:SCATTER_REFS])
+    scatter = Scatter(count, hidden, down_weight, False, refs)
+    width = gate_out.shape[1]
+    step = rows_buf.shape[1]
+    blocks = gradient.shape[0] // step
+    block_loads = {}
+    stores = []
+
+    def load_block(index):
+        rows = pl.ds(index * step, step)
+        pairs = ((grad_rows, rows_buf), (gate_up, gate_up_buf))
+        block_loads[index] = [
+            begin(source.at[rows], target.at[index % 2], block_sem.at[which, index])
+            for which, (source, target) in enumerate(pairs)
+        ]
+
+    load_block(0)
+    load_block(1)
     span = half.shape[1] // (shards // 2)
-    grad_loads = []
+    half_loads = []
     for which in range(2):
         owner = (1 - core, core)[which]
         for chip in range(shards // 2):
             start = pl.multiple_of((2 * chip + owner) * span, 16)
             target = half.at[which, pl.ds(chip * span, span)]
-            sem = load_sem.at[which, chip]
-            grad_loads.append(begin(across.at[pl.ds(start, span)], target, sem))
-    grad_loads.append(begin(gradient, gradient_buf, load_sem.at[2, 0]))
+            sem = half_sem.at[which, chip]
+            half_loads.append(begin(across.at[pl.ds(start, span)], target, sem))
     meet(count, shards)
     sums = CoreSum(send_buf, recv_buf, send_sem, recv_sem)
-    tiles = gradient_buf.shape[1] // GRAD_TILE
-    width = gate_out.shape[1]
+    tiles = gradient.shape[1] // GRAD_TILE
+
+    def back(index):
+        for load in block_loads[index]:
+            load.wait()
+        rows = pl.ds(index * step, step)
+        grad_hidden = times_transposed(rows_buf[index % 2], scatter.right_buf[...])
+        gate = gate_up_buf[index % 2, :, :width]
+        upward = gate_up_buf[index % 2, :, width:]
+        sigmoid_gate = jax.nn.sigmoid(gate)
+        silu_gate = gate * sigmoid_gate
+        grad_gate = grad_hidden * upward * sigmoid_gate * (1.0 + gate * (1.0 - sigmoid_gate))
+        gradient[rows, :width] = grad_gate.astype(jnp.bfloat16)
+        gradient[rows, width:] = (grad_hidden * silu_gate).astype(jnp.bfloat16)
+        stores.append(begin(gradient.at[rows], gradient_out.at[rows], store_sem.at[index]))
+        if index + 2 < blocks:
+            load_block(index + 2)
 
     def send(tile, carry):
         columns = column_tile(tile)
-        value = product(half[0], gradient_buf[:, columns])
+        value = product(half[0], gradient[:, columns])
         send_buf[:, columns] = value.astype(jnp.bfloat16)
         sums.copy(tile).start()
         return carry
 
     def keep(tile, carry):
         columns = column_tile(tile)
-        value = product(half[1], gradient_buf[:, columns])
+        value = product(half[1], gradient[:, columns])
         sums.copy(tile).wait()
         value = (value + recv_buf[:, columns].astype(jnp.float32)).astype(jnp.bfloat16)
         send_buf[:, columns] = value
         return carry
 
-    def wait_loads():
-        for load in grad_loads:
+    def last_back():
+        back(blocks - 1)
+        for load in half_loads:
             load.wait()
 
+    others = [functools.partial(back, index) for index in range(blocks - 1)] + [last_back]
     bounds = [0, 3, 6, 9, tiles]
-    others = [wait_loads]
     for body in (send, keep):
         for first, last in zip(bounds, bounds[1:]):
             others.append(lambda body=body, a=first, b=last: lax.fori_loop(a, b, body, 0))
     scatter.run(others)
-    stores = [
-        begin(send_buf.at[:, pl.ds(i * width, width)], out, load_sem.at[2, 1 + i])
-        for i, out in enumerate((gate_out, up_out))
-    ]
+    for index, out in enumerate((gate_out, up_out)):
+        source = send_buf.at[:, pl.ds(index * width, width)]
+        stores.append(begin(source, out, store_sem.at[blocks + index]))
     scatter.finish()
 
     def strip(where):
@@ -1117,31 +1147,36 @@
         store.wait()
 
 
-def hidden_grads(count, shards, ident, across, gradient, hidden, down_weight):
+def hidden_grads(count, shards, ident, across, grad_rows, gate_up, hidden, down_weight):
     depth, length = across.shape
-    width = gradient.shape[1]
+    width = gate_up.shape[1]
     tiles = width // GRAD_TILE
     rows = length // count
+    step = QUERY_ROWS
     half = shape((depth // 2, width // 2))
     return call_plane(
         functools.partial(hidden_grads_body, count, shards),
         ident,
-        (half, half, shape((rows, depth), jnp.float32)),
-        (HBM, HBM, VMEM),
-        [HBM] * 4,
+        (half, half, shape((rows, depth), jnp.float32), shape((length, width))),
+        (HBM, HBM, VMEM, HBM),
+        [HBM] * 5,
         [
             pltpu.VMEM((2, depth // 2, length), jnp.bfloat16),
             pltpu.VMEM((length, width), jnp.bfloat16),
+            pltpu.VMEM((2, step, depth), jnp.bfloat16),
+            pltpu.VMEM((2, step, width), jnp.float32),
             pltpu.VMEM((depth // 2, width), jnp.bfloat16),
             pltpu.VMEM((depth // 2, width), jnp.bfloat16),
             pltpu.SemaphoreType.DMA((tiles,)),
             pltpu.SemaphoreType.DMA((tiles,)),
-            pltpu.SemaphoreType.DMA((3, shards // 2)),
+            pltpu.SemaphoreType.DMA((2, shards // 2)),
+            pltpu.SemaphoreType.DMA((2, length // step)),
+            pltpu.SemaphoreType.DMA((length // step + 2,)),
         ]
         + scatter_scratch(count, rows, depth, hidden, down_weight, False, hidden.shape[1]),
-        6 * 10**10,
+        8 * 10**10,
         VMEM_MEGABYTES,
-        (across, gradient, hidden, down_weight),
+        (across, grad_rows, gate_up, hidden, down_weight),
     )
 
 
@@ -1285,7 +1320,7 @@
         ],
         out_specs=pl.BlockSpec((step, 4 * width), lambda i: (i, 0)),
         cost_estimate=pl.CostEstimate(flops=0, bytes_accessed=10**7, transcendentals=0),
-        compiler_params=pltpu.CompilerParams(vmem_limit_bytes=VMEM_MEGABYTES << 20),
+        compiler_params=pltpu.CompilerParams(vmem_limit_bytes=24 << 20),
     )(array, array, array, array)
 
 
@@ -1312,7 +1347,7 @@
         out_specs=pl.BlockSpec((step, 4 * width), lambda i: (i, 0)),
         scratch_shapes=[pltpu.VMEM((4, step, width), jnp.bfloat16)],
         cost_estimate=pl.CostEstimate(flops=0, bytes_accessed=10**7, transcendentals=0),
-        compiler_params=pltpu.CompilerParams(vmem_limit_bytes=VMEM_MEGABYTES << 20),
+        compiler_params=pltpu.CompilerParams(vmem_limit_bytes=24 << 20),
     )(*parts)
 
 
@@ -1340,7 +1375,7 @@
         in_specs=[VMEM] * 5,
         out_specs=VMEM,
         cost_estimate=pl.CostEstimate(flops=0, bytes_accessed=10**7, transcendentals=0),
-        compiler_params=pltpu.CompilerParams(vmem_limit_bytes=VMEM_MEGABYTES << 20),
+        compiler_params=pltpu.CompilerParams(vmem_limit_bytes=24 << 20),
     )(*parts)
 
 
@@ -1390,7 +1425,7 @@
         out_specs=(VMEM,) * 4,
         scratch_shapes=[pltpu.VMEM((4, rows, width), jnp.bfloat16)],
         cost_estimate=pl.CostEstimate(flops=0, bytes_accessed=10**7, transcendentals=0),
-        compiler_params=pltpu.CompilerParams(vmem_limit_bytes=VMEM_MEGABYTES << 20),
+        compiler_params=pltpu.CompilerParams(vmem_limit_bytes=24 << 20),
     )(*parts)
 
 
@@ -1837,24 +1872,25 @@
         down_term = column_term(hidden, grad_out_all)
     down_part, down_term = tie((down_part, down_term))
     down_piece = scatter_shards(down_term, dealt_heads)
-    grad_gate_up = hidden_backward(grad_out_all, down_part, gate_up)
     if dealt_heads:
-        *terms, output_sum = hidden_grads(
-            part_count, shard_count, 6, second_across, grad_gate_up, hidden, down_part
+        *terms, output_sum, grad_gate_up = hidden_grads(
+            part_count, shard_count, 6, second_across, grad_out_all, gate_up, hidden, down_part
         )
     else:
+        grad_gate_up = hidden_backward(grad_out_all, down_part, gate_up)
         gate_up_term = column_term(second_all, grad_gate_up).astype(jnp.bfloat16)
         terms = (gate_up_term[:, : FF // part_count], gate_up_term[:, FF // part_count :])
         output_partial = product(hidden, down_part).astype(jnp.bfloat16)
         output_sum = lax.psum_scatter(output_partial, "ctx", scatter_dimension=0, tiled=True)
     block_output = (residual_mid + output_sum.astype(jnp.float32)).astype(jnp.bfloat16)
-    grad_gate_up, down_piece, *terms = tie((grad_gate_up, down_piece, *terms))
+    grad_gate_up, *terms = tie((grad_gate_up, *terms))
     gate_piece = scatter_shards(terms[0], dealt_heads)
     up_piece = scatter_shards(terms[1], dealt_heads)
     grad_mid, second_gain_part, branch_all = middle_back(
         part_count, 3, grad_gate_up, gate_up_part, residual_mid, gain_second, cotangent[0]
     )
-    branch_all, gate_piece, down_piece = tie((branch_all, gate_piece, down_piece))
+    branch_all, down_piece = tie((branch_all, down_piece))
+    branch_all, gate_piece = tie((branch_all, gate_piece))
     if dealt_heads:
         down_near = plane_near(down_piece)
         gate_near = plane_near(gate_piece)
@@ -1885,7 +1921,7 @@
         down_parts, gate_parts = ((*down_near, *far[:2]), (*gate_near, *far[2:]))
         grad_packed, packed_term = tie((grad_packed, packed_term))
         packed_piece = scatter_shards(packed_term, True)
-    grad_input, gain_shard, up_all = input_back(
+    grad_norm, gain_shard, up_all = input_back(
         part_count,
         shard_count,
         4,
@@ -1893,12 +1929,11 @@
         packed,
         tokens[0],
         gain_first,
-        grad_mid,
         second_gain_part,
         up_piece,
     )
     if dealt_heads:
-        grad_input, packed_piece = tie((grad_input, packed_piece))
+        grad_norm, packed_piece = tie((grad_norm, packed_piece))
         packed_near = plane_near(packed_piece)
         gate_shard = place_hidden(shard_count, gate_parts)
         up_shard = place_sorted(shard_count, up_all)
@@ -1935,7 +1970,7 @@
         key_shard, value_shard = (key_value_shard[:, :KV_WIDTH], key_value_shard[:, KV_WIDTH:])
     return (
         block_output[None],
-        grad_input[None],
+        (grad_mid + grad_norm).astype(jnp.bfloat16)[None],
         gain_shard[0],
         query_shard,
         key_shard,

time: 550 us -> 531 us (0.965)
  Pallas kernels: 479 us -> 455 us
  waiting for transfers between devices: 27.8 us -> 34.4 us
    pallas_call x1 -> x0, Pallas kernels: 14.1 us -> none  [hidden_backward(): pl.pallas_call(hidden_back_body, grid=(length // step,), out_shape=shape(...]
    pallas_call x2, Pallas kernels: 9.2 us -> 3.61 us  [place_rows(): pl.pallas_call(place_rows_body, out_shape=shape((4 * rows, width), kind),...]
  transfers between devices with their start and end apart: 18 -> 18, of which waited for: 11 -> 12; matrix products, arithmetic and copies ran while one was open for 1% -> 1% of each run, Pallas kernels for 75% -> 73%
where the time goes in v6:
time: 531 us; the launch traced here: 529 us
  Pallas kernels  455 us (86%)
  waiting for transfers between devices  34.4 us (6%)
  between operations  14.7 us (3%)
  starting transfers between devices  13.1 us (2%)
  local copies, waits for them, and re-layouts  7.15 us (1%)
    pallas_call x7, Pallas kernels, call_plane(): pl.pallas_call(body, out_shape=outs, in_specs=in_specs, out_specs=out_spe...  367 us
    pallas_call x1, Pallas kernels, attend_backward(): pl.pallas_call(functools.partial(attend_back_body, block_rows), out_shape...  27 us
    pallas_call x1, Pallas kernels, attend_forward(): pl.pallas_call(functools.partial(attend_body, block_rows), out_shape=(sha...  26.5 us
    ppermute x12, waiting for transfers between devices, swap(): return lax.ppermute(array, 'ctx', pairs)  26.4 us
    pallas_call x1, Pallas kernels, hidden_forward(): pl.pallas_call(hidden_body, grid=(length // step,), out_shape=(shape((len...  21.2 us
    ppermute x12, starting transfers between devices, swap(): return lax.ppermute(array, 'ctx', pairs)  12.6 us
  transfers between devices with their start and end apart: 18, of which 12 were waited for; matrix products, arithmetic and copies ran while one was open for 1% of the time, Pallas kernels for 73%

profile of v6, /device:TPU:0, one launch (start us, length us, event | category | flops | bytes accessed | tf_op | source)
XLA Modules:
  0.0 528.5 jit_solution(7549159196287723470)
XLA Ops:
  9.8 63.3 %shard_map.203 = (bf16[1024,2048]{1,0:T(8,128)(2,1)}, f32[1,2048]{1,0:T(1,128)}, f32[1,2048]{1,0:T(1,128)}, f32[1024,128]{1,0:T(8,128)}, f32[1024,128]{1,0:T(8,1...) custom-call(bf16[256,2048]{1,0:T(8,128)(2,1)} %bitcast.14, bf16[1,256]{1,0:T(2,128)(2,1)} %broadcast_in_dim.12.first_gain, ...), custom_call_target="tpu_custom_call" | custom-call | flops 49999998976 | bytes 166666672 | tf_op jit(solution)/shard_map/pallas_call | solution.py:482
  74.4 26.5 %shard_map.204 = (bf16[1024,512]{1,0:T(8,128)(2,1)}, bf16[1024,512]{1,0:T(8,128)(2,1)}, bf16[4,1024,128]{2,1,0:T(8,128)(2,1)}, bf16[4,1024,128]{2,1,0:T(8,128)(2...) custom-call(s32[1,8]{1,0:T(1,128)} %dealing.3, ...), custom_call_target="tpu_custom_call" | custom-call | flops 30000001024 | bytes 10000000 | tf_op jit(solution)/shard_map/pallas_call | solution.py:1593
  100.9 77.1 %shard_map.205 = (f32[256,2048]{1,0:T(8,128)}, bf16[1024,2048]{1,0:T(8,128)(2,1)}) custom-call(bf16[1024,512]{1,0:T(8,128)(2,1)} %get-tuple-element.84.attended, bf16[512,2048]{1,0:T(8,128)(2,1)} %get-tuple-element.85.weight.output_weight, bf16[256,2048]{1,0:T(8,128)(2,1)} %bitcast.15, f32[1,2048]{1,0:T(1,128)} %get-tuple-element.86.gain), custom_call_target="tpu_custom_call" | custom-call | flops 60000002048 | bytes 200000000 | tf_op jit(solution)/shard_map/pallas_call | solution.py:482
  178.4 1.7 collective-permute-start
  180.6 21.2 %shard_map.206 = (f32[1024,2816]{1,0:T(8,128)}, bf16[1024,1408]{1,0:T(8,128)(2,1)}, bf16[2048,1024]{1,0:T(8,128)(2,1)}, bf16[1408,1024]{1,0:T(8,128)(2,1)}) custom-call(bf16[1024,2048]{1,0:T(8,128)(2,1)} %get-tuple-element.89.rows, bf16[2048,2816]{1,0:T(8,128)(2,1)} %all-gather.3.cloned.1.call-done.gate_weight.up_weight.gate_up_weight, ...), custom_call_target="tpu_custom_call" | custom-call | flops 11811160064 | bytes 30000000 | tf_op jit(solution)/shard_map/pallas_call | solution.py:913
  202.7 1.7 collective-permute-start.3
  204.9 11.1 %collective-permute-done.3.high = bf16[128,2048]{1,0:T(8,128)(2,1)S(1)} collective-permute-done((bf16[128,2048]{1,0:T(8,128)(2,1)S(1)}, bf16[128,2048]{1,0:T(8,128)(2,1)S(1)}, u32[]{:S(2)}, u32[]{:S(2)}) %collective-permute-start.3) | collective-permute-done | bytes 524320 | tf_op jit(solution)/shard_map/ppermute | solution.py:879
  217.5 2.0 copy-done.3
  219.5 15.2 %shard_map.208 = bf16[704,2048]{1,0:T(8,128)(2,1)} custom-call(bf16[1408,1024]{1,0:T(8,128)(2,1)} %get-tuple-element.99.across, bf16[1024,2048]{1,0:T(8,128)(2,1)} %copy-done.3), custom_call_target="tpu_custom_call" | custom-call | flops 5905580032 | bytes 19685266 | tf_op jit(solution)/shard_map/pallas_call | solution.py:482
  234.7 6.8 %all-gather.5.cloned.1.call-done.down_weight = bf16[1408,2048]{1,0:T(8,128)(2,1)} async-done(((bf16[176,2048]{1,0:T(8,128)(2,1)}), bf16[1408,2048]{1,0:T(8,128)(2,1)}) %all-gather.5.cloned.1.call-update) | async-done | bytes 5767184 | tf_op jit(solution)/shard_map/all_gather | solution.py:1783
  241.6 44.4 %shard_map.209 = (bf16[1024,1408]{1,0:T(8,128)(2,1)}, bf16[1024,1408]{1,0:T(8,128)(2,1)}, f32[256,2048]{1,0:T(8,128)}, bf16[1024,2816]{1,0:T(8,128)(2,1)}) custom-call(bf16[2048,1024]{1,0:T(8,128)(2,1)} %get-tuple-element.91.across, bf16[1024,2048]{1,0:T(8,128)(2,1)} %copy-done.3, f32[1024,2816]{1,0:T(8,128)} %get-tuple-element.97.gate_up, ...), custom_call_target="tpu_custom_call" | custom-call | flops 80000000000 | bytes 266666672 | tf_op jit(solution)/shard_map/pallas_call | solution.py:482
  286.7 77.8 %shard_map.210 = (f32[256,2048]{1,0:T(8,128)}, f32[1,2048]{1,0:T(1,128)}, bf16[1024,2048]{1,0:T(8,128)(2,1)}) custom-call(bf16[1024,2816]{1,0:T(8,128)(2,1)} %get-tuple-element.105.grad_gate_up, bf16[2048,2816]{1,0:T(8,128)(2,1)} %all-gather.3.cloned.1.call-done.gate_weight.up_weight.gate_up_weight, f32[256,2048]{1,0:T(8,128)} %get-tuple-element.87.residual, ...), custom_call_target="tpu_custom_call" | custom-call | flops 60000002048 | bytes 200000000 | tf_op jit(solution)/shard_map/pallas_call | solution.py:482
  364.6 1.6 collective-permute-start.7
  368.7 27.0 %shard_map.211.gradient.grad_packed = bf16[1024,1024]{1,0:T(8,128)(2,1)} custom-call(s32[1,8]{1,0:T(1,128)} %dealing.3, bf16[1024,2048]{1,0:T(8,128)(2,1)} %get-tuple-element.111.branch_all, bf16[512,2048]{1,0:T(8,128)(2,1)} %get-tuple-element.85.weight.output_weight, bf16[1024,512]{1,0:T(8,128)(2,1)} %get-tuple-element.112.queries, ...), custom_call_target="tpu_custom_call" | custom-call | flops 60000002048 | bytes 10000000 | tf_op jit(solution)/shard_map/pallas_call | solution.py:1732
  395.8 1.5 collective-permute-done.5.refs_1_.from_along
  399.4 23.8 %shard_map.212 = (bf16[1024,1536]{1,0:T(8,128)(2,1)}, bf16[88,2048]{1,0:T(8,128)(2,1)}, bf16[88,2048]{1,0:T(8,128)(2,1)}, bf16[128,1408]{1,0:T(8,128)(2,1)}, bf16[128,1408]{1,0:T(8,128)(2,1)}) custom-call(bf16[2048,1024]{1,0:T(8,128)(2,1)} %get-tuple-element.116.across, bf16[1024,1024]{1,0:T(8,128)(2,1)} %shard_map.211.gradient.grad_packed, ...), custom_call_target="tpu_custom_call" | custom-call | flops 6442450944 | bytes 21474836 | tf_op jit(solution)/shard_map/pallas_call | solution.py:482
  423.2 64.9 %shard_map.213 = (f32[256,2048]{1,0:T(8,128)}, f32[2,256]{1,0:T(2,128)}, bf16[1024,1408]{1,0:T(8,128)(2,1)}) custom-call(bf16[1024,1024]{1,0:T(8,128)(2,1)} %shard_map.211.gradient.grad_packed, bf16[2048,1536]{1,0:T(8,128)(2,1)} %get-tuple-element.81.weight, bf16[256,2048]{1,0:T(8,128)(2,1)} %bitcast.16, ...), custom_call_target="tpu_custom_call" | custom-call | flops 49999998976 | bytes 166666672 | tf_op jit(solution)/shard_map/pallas_call | solution.py:482
  490.3 3.5 fusion
  493.8 3.4 shard_map.215
  497.2 3.5 shard_map.214
  500.8 3.3 shard_map.217
  504.7 2.9 collective-permute-done.9.from_along
  511.7 5.8 %collective-permute-done.11.high = bf16[128,1536]{1,0:T(8,128)(2,1)S(1)} collective-permute-done((bf16[128,1536]{1,0:T(8,128)(2,1)S(1)}, bf16[128,1536]{1,0:T(8,128)(2,1)S(1)}, u32[]{:S(2)}, u32[]{:S(2)}) %collective-permute-start.11) | collective-permute-done | bytes 393248 | tf_op jit(solution)/shard_map/ppermute | solution.py:879
  518.6 2.8 shard_map.216
  (89 shorter events, 20.9 us)
Async XLA Ops:
  7.2 66.1 %copy-start = (bf16[704,2048]{1,0:T(8,128)(2,1)S(1)}, bf16[704,2048]{1,0:T(8,128)(2,1)}, u32[]{:S(2)}) copy-start(bf16[704,2048]{1,0:T(8,128)(2,1)} %param.22) | copy-start | bytes 8650756
  7.2 173.4 %all-gather.3.cloned.1.call-start = ((), (), s32[]{:S(2)}) async-start(), calls=%async_computation.4 | async-start | bytes 12976128 | tf_op jit(solution)/shard_map/all_gather | solution.py:1783
  73.2 168.4 %all-gather.5.cloned.1.call-start = ((), (), s32[]{:S(2)}) async-start(), calls=%async_computation.5 | async-start | bytes 6488064 | tf_op jit(solution)/shard_map/all_gather | solution.py:1783
  74.2 290.4 %reduce-scatter.5.cloned.1.call-start = ((), (), s32[]{:S(2)}) async-start(), calls=%async_computation.6 | async-start | bytes 3604480 | tf_op jit(solution)/shard_map/reduce_scatter | solution.py:1789
  100.9 77.1 %copy-start.4 = (bf16[1,256,2048]{2,1,0:T(8,128)(2,1)S(1)}, bf16[1,256,2048]{2,1,0:T(8,128)(2,1)}, u32[]{:S(2)}) copy-start(bf16[1,256,2048]{2,1,0:T(8,128)(2,1)} %param.23) | copy-start | bytes 3145732
  178.0 24.5 %collective-permute-start.1 = (bf16[256,2048]{1,0:T(8,128)(2,1)S(1)}, bf16[256,2048]{1,0:T(8,128)(2,1)S(1)}, u32[]{:S(2)}, u32[]{:S(2)}) collective-permute-start(bf16[256,2048]{1,0:T(8,128)(2,1)S(1)} %bitcast.9), channel_id=1, source_target_pairs={{0,16},{8,24},{16,0},{24,8},{1,17},{9,25},{17,1},{25,9},{2,18},{10... | collective-permute-start | bytes 3145736 | tf_op jit(solution)/shard_map/ppermute | solution.py:879
  178.4 24.2 %collective-permute-start = (bf16[256,2048]{1,0:T(8,128)(2,1)S(1)}, bf16[256,2048]{1,0:T(8,128)(2,1)S(1)}, u32[]{:S(2)}, u32[]{:S(2)}) collective-permute-start(bf16[256,2048]{1,0:T(8,128)(2,1)S(1)} %bitcast.10), channel_id=1, source_target_pairs={{0,8},{8,0},{16,24},{24,16},{1,9},{9,1},{17,25},{25,17},{2,10},{10... | collective-permute-start | bytes 3145736 | tf_op jit(solution)/shard_map/ppermute | solution.py:879
  202.7 13.3 %collective-permute-start.3 = (bf16[128,2048]{1,0:T(8,128)(2,1)S(1)}, bf16[128,2048]{1,0:T(8,128)(2,1)S(1)}, u32[]{:S(2)}, u32[]{:S(2)}) collective-permute-start(bf16[128,2048]{1,0:T(8,128)(2,1)S(1)} %slice.19), channel_id=1, source_target_pairs={{0,8},{8,0},{16,24},{24,16},{1,9},{9,1},{17,25},{25,17},{2,10},{10... | collective-permute-start | bytes 1572872 | tf_op jit(solution)/shard_map/ppermute | solution.py:879
  204.4 12.8 %collective-permute-start.2 = (bf16[128,2048]{1,0:T(8,128)(2,1)S(1)}, bf16[128,2048]{1,0:T(8,128)(2,1)S(1)}, u32[]{:S(2)}, u32[]{:S(2)}) collective-permute-start(bf16[128,2048]{1,0:T(8,128)(2,1)S(1)} %slice.18), channel_id=1, source_target_pairs={{0,16},{8,24},{16,0},{24,8},{1,17},{9,25},{17,1},{25,9},{2,18},{10... | collective-permute-start | bytes 1572872 | tf_op jit(solution)/shard_map/ppermute | solution.py:879
  241.6 123.0 %reduce-scatter.7.cloned.1.call-start = ((), (), s32[]{:S(2)}) async-start(), calls=%async_computation.7 | async-start | bytes 3604480 | tf_op jit(solution)/shard_map/reduce_scatter | solution.py:1789
  286.1 137.2 %reduce-scatter.9.cloned.1.call-start = ((), (), s32[]{:S(2)}) async-start(), calls=%async_computation.8 | async-start | bytes 3604480 | tf_op jit(solution)/shard_map/reduce_scatter | solution.py:1789
  286.7 201.5 %reduce-scatter.11.cloned.1.call-start = ((), (), s32[]{:S(2)}) async-start(), calls=%async_computation.9 | async-start | bytes 3932160 | tf_op jit(solution)/shard_map/reduce_scatter | solution.py:1789
  364.6 31.2 %collective-permute-start.7 = (bf16[256,1408]{1,0:T(8,128)(2,1)}, bf16[256,1408]{1,0:T(8,128)(2,1)S(1)}, u32[]{:S(2)}, u32[]{:S(2)}) collective-permute-start(bf16[256,1408]{1,0:T(8,128)(2,1)} %reduce-scatter.7.cloned.1.call-done.refs_0_), channel_id=1, source_target_pairs={{0,16},{8,24},{16,0},{24,8},{1,17},{9,25},{17,1},{25,9},{2,18},{10... | collective-permute-start | bytes 2162696 | tf_op jit(solution)/shard_map/ppermute | solution.py:879
  366.1 29.6 %collective-permute-start.6 = (bf16[256,1408]{1,0:T(8,128)(2,1)}, bf16[256,1408]{1,0:T(8,128)(2,1)S(1)}, u32[]{:S(2)}, u32[]{:S(2)}) collective-permute-start(bf16[256,1408]{1,0:T(8,128)(2,1)} %reduce-scatter.7.cloned.1.call-done.refs_0_), channel_id=1, source_target_pairs={{0,8},{8,0},{16,24},{24,16},{1,9},{9,1},{17,25},{25,17},{2,10},{10... | collective-permute-start | bytes 2162696 | tf_op jit(solution)/shard_map/ppermute | solution.py:879
  366.7 30.6 %collective-permute-start.5 = (bf16[176,2048]{1,0:T(8,128)(2,1)}, bf16[176,2048]{1,0:T(8,128)(2,1)S(1)}, u32[]{:S(2)}, u32[]{:S(2)}) collective-permute-start(bf16[176,2048]{1,0:T(8,128)(2,1)} %reduce-scatter.5.cloned.1.call-done.own), channel_id=1, source_target_pairs={{0,16},{8,24},{16,0},{24,8},{1,17},{9,25},{17,1},{25,9},{2,18},{10... | collective-permute-start | bytes 2162696 | tf_op jit(solution)/shard_map/ppermute | solution.py:879
  368.2 30.4 %collective-permute-start.4 = (bf16[176,2048]{1,0:T(8,128)(2,1)}, bf16[176,2048]{1,0:T(8,128)(2,1)S(1)}, u32[]{:S(2)}, u32[]{:S(2)}) collective-permute-start(bf16[176,2048]{1,0:T(8,128)(2,1)} %reduce-scatter.5.cloned.1.call-done.own), channel_id=1, source_target_pairs={{0,8},{8,0},{16,24},{24,16},{1,9},{9,1},{17,25},{25,17},{2,10},{10... | collective-permute-start | bytes 2162696 | tf_op jit(solution)/shard_map/ppermute | solution.py:879
  488.2 19.4 %collective-permute-start.9 = (bf16[256,1536]{1,0:T(8,128)(2,1)}, bf16[256,1536]{1,0:T(8,128)(2,1)S(1)}, u32[]{:S(2)}, u32[]{:S(2)}) collective-permute-start(bf16[256,1536]{1,0:T(8,128)(2,1)} %reduce-scatter.11.cloned.1.call-done.own), channel_id=1, source_target_pairs={{0,16},{8,24},{16,0},{24,8},{1,17},{9,25},{17,1},{25,9},{2,18},{10... | collective-permute-start | bytes 2359304 | tf_op jit(solution)/shard_map/ppermute | solution.py:879
  489.6 18.7 %collective-permute-start.8 = (bf16[256,1536]{1,0:T(8,128)(2,1)}, bf16[256,1536]{1,0:T(8,128)(2,1)S(1)}, u32[]{:S(2)}, u32[]{:S(2)}) collective-permute-start(bf16[256,1536]{1,0:T(8,128)(2,1)} %reduce-scatter.11.cloned.1.call-done.own), channel_id=1, source_target_pairs={{0,8},{8,0},{16,24},{24,16},{1,9},{9,1},{17,25},{25,17},{2,10},{10... | collective-permute-start | bytes 2359304 | tf_op jit(solution)/shard_map/ppermute | solution.py:879
  500.8 9.7 %copy-start.20 = (f32[256,2048]{1,0:T(8,128)S(1)}, f32[256,2048]{1,0:T(8,128)}, u32[]{:S(2)}) copy-start(f32[256,2048]{1,0:T(8,128)} %get-tuple-element.106) | copy-start | bytes 6291460
  500.8 9.7 %copy-start.21 = (f32[256,2048]{1,0:T(8,128)S(1)}, f32[256,2048]{1,0:T(8,128)}, u32[]{:S(2)}) copy-start(f32[256,2048]{1,0:T(8,128)} %get-tuple-element.126) | copy-start | bytes 6291460
  508.3 10.3 %copy-start.5 = (bf16[256,1536]{1,0:T(8,128)(2,1)S(1)}, bf16[256,1536]{1,0:T(8,128)(2,1)}, u32[]{:S(2)}) copy-start(bf16[256,1536]{1,0:T(8,128)(2,1)} %reduce-scatter.11.cloned.1.call-done.own) | copy-start | bytes 2359300
  508.4 9.2 %collective-permute-start.11 = (bf16[128,1536]{1,0:T(8,128)(2,1)S(1)}, bf16[128,1536]{1,0:T(8,128)(2,1)S(1)}, u32[]{:S(2)}, u32[]{:S(2)}) collective-permute-start(bf16[128,1536]{1,0:T(8,128)(2,1)S(1)} %slice.22), channel_id=1, source_target_pairs={{0,8},{8,0},{16,24},{24,16},{1,9},{9,1},{17,25},{25,17},{2,10},{10... | collective-permute-start | bytes 1179656 | tf_op jit(solution)/shard_map/ppermute | solution.py:879
  509.4 9.2 %collective-permute-start.10 = (bf16[128,1536]{1,0:T(8,128)(2,1)S(1)}, bf16[128,1536]{1,0:T(8,128)(2,1)S(1)}, u32[]{:S(2)}, u32[]{:S(2)}) collective-permute-start(bf16[128,1536]{1,0:T(8,128)(2,1)S(1)} %slice.21), channel_id=1, source_target_pairs={{0,16},{8,24},{16,0},{24,8},{1,17},{9,25},{17,1},{25,9},{2,18},{10... | collective-permute-start | bytes 1179656 | tf_op jit(solution)/shard_map/ppermute | solution.py:879
  510.5 11.0 %copy-start.1 = (bf16[704,2048]{1,0:T(8,128)(2,1)S(1)}, bf16[704,2048]{1,0:T(8,128)(2,1)}, u32[]{:S(2)}) copy-start(bf16[704,2048]{1,0:T(8,128)(2,1)} %param.22) | copy-start | bytes 8650756
  (17 other events, 53.4 us)
Sparse Core Ops, SparseCore 0:
  73.3 107.2 all-gather.2
  182.8 58.7 all-gather.4
  243.8 54.9 reduce-scatter.4
  301.0 56.0 reduce-scatter.6
  359.2 56.0 reduce-scatter.8
  423.3 58.9 reduce-scatter.10

commit v7 on v6

--- a/solution.py
+++ b/solution.py
@@ -59,7 +59,8 @@
 
 
 STRIP = 32
-PIECES = 4
+PIECES = 8
+ORDER = [half * PIECES // 2 + i for i in range(PIECES // 2) for half in range(2)]
 
 
 def plane_places():
@@ -71,14 +72,22 @@
     pl.semaphore_signal(barrier, inc=1, device_id=place, device_id_type=MESH)
 
 
-def meet(count, shards=1):
+def greet(count, shards=1):
     me = lax.axis_index("ctx")
     barrier = pltpu.get_barrier_semaphore()
     for step in range(1, count):
         signal(barrier, ctx=lax.rem(me + step, count))
     for step in range(1, shards):
         signal(barrier, fsdp=lax.rem(lax.axis_index("fsdp") + step, shards))
-    pl.semaphore_wait(barrier, count - 1 + shards - 1)
+
+
+def met(count, shards=1):
+    pl.semaphore_wait(pltpu.get_barrier_semaphore(), count - 1 + shards - 1)
+
+
+def meet(count, shards=1):
+    greet(count, shards)
+    met(count, shards)
 
 
 def remote(source, target, send_sem, recv_sem, **place):
@@ -142,7 +151,7 @@
         self.relay()
         self.drain()
 
-    def relay(self, pieces=(0, PIECES // 2, 1, PIECES // 2 + 1)):
+    def relay(self, pieces=tuple(ORDER)):
         relays = self.relays
         if self.count != 4:
             return
@@ -347,10 +356,11 @@
     def store_own(self, columns, value):
         self.total[:, columns] = value
 
-    def run(self, others=()):
+    def run(self, shards=1, others=()):
         if self.count == 4:
-            self.run_relayed(list(others))
+            self.run_relayed(shards, list(others))
         else:
+            met(self.count, shards)
             self.run_direct()
             for other in others:
                 other()
@@ -370,7 +380,7 @@
         self.block(self.count - 1, self.store_own)
         self.relays, self.copies = ([], copies)
 
-    def run_relayed(self, others):
+    def run_relayed(self, shards, others):
         corner, across, along, me = self.owners()
         send_buf, kept, tiles = (self.send_buf, self.kept, self.tiles)
         half = self.rows // 2
@@ -382,6 +392,8 @@
             columns = pl.ds(tile * TILE, TILE)
             self.loads["tile", tile].wait()
             send_buf[0, :, columns] = self.tile(corner, columns).astype(send_buf.dtype)
+            if tile == 0:
+                met(self.count, shards)
             relays.append(
                 (
                     self.send(0, low, columns, tile, across),
@@ -562,7 +574,6 @@
         weights_all, packed_hidden, *refs = refs
     gains, gains_all, gain_send, gain_recv, *refs = refs
     first = RowGather(count, tokens, tokens_all, refs[:3])
-    half = PIECES // 2
     if count == 4:
         packed, gate, up, load_sem, *line_refs = refs[3:]
         loads = [
@@ -573,11 +584,13 @@
     meet(count, shards)
     if count == 4:
         line.start(0)
-    first.send(0)
-    first.send(half)
+    early, late = (ORDER[: PIECES // 2], ORDER[PIECES // 2 :])
+    for piece in early:
+        first.send(piece)
     me = lax.axis_index("fsdp")
-    gains[0:1, :] = first_gain[...]
-    gains[1:2, :] = second_gain[...]
+    for index, gain in enumerate((first_gain, second_gain)):
+        row = gain[...].astype(jnp.float32)[None, :]
+        gains[index : index + 1, :] = row.astype(jnp.bfloat16)
     gains_all[me] = gains[...]
     copies = []
     for step in range(1, shards):
@@ -592,8 +605,8 @@
         )
     if count != 4:
         write_tables(cosine, sine)
-        first.send(1)
-        first.send(half + 1)
+        for piece in late:
+            first.send(piece)
         first.finish()
     else:
         steps = [(d, c) for d in range(1, line.hops + 1) for c in range(CHUNKS)]
@@ -601,15 +614,15 @@
         for chunk in range(1, CHUNKS):
             line.start(chunk)
         line.step(*steps[0])
-        first.relay((0, half))
-        first.send(1)
-        first.send(half + 1)
+        first.relay(early)
+        for piece in late:
+            first.send(piece)
         for step in steps[1:3]:
             line.step(*step)
         for load in loads:
             load.wait()
         pack_hidden(shards, gate, up, packed_hidden)
-        first.relay((1, half + 1))
+        first.relay(late)
         for step in steps[3:-1]:
             line.step(*step)
         first.drain()
@@ -627,7 +640,7 @@
 
 def start_gather(count, shards, ident, tokens, first_gain, second_gain, *weights):
     rows, width = tokens.shape
-    span = first_gain.shape[1]
+    span = first_gain.shape[0]
     wide = shape((1, width), jnp.float32)
     table = shape((count * rows, LANES), jnp.float32)
     outs = [shape((count * rows, width)), wide, wide, table, table]
@@ -666,17 +679,17 @@
 
 def strips_and_send(gather, strip):
     size = gather.size
-    for piece in range(PIECES):
+    for piece in ORDER:
         for_strips(piece * size, size, strip)
         gather.send(piece)
     gather.finish()
 
 
 def middle_body(count, attended, weight, tokens, gain, residual, second_all, own, *refs):
+    greet(count)
     scatter = Scatter(count, attended, weight, False, refs[:SCATTER_REFS])
     side = refs[SCATTER_REFS : SCATTER_REFS + 2]
     loads = side_loads([tokens], side)
-    meet(count)
     scatter.run()
     scatter.finish()
     for load in loads:
@@ -715,10 +728,10 @@
     count, grad_gate_up, gate_up_weight, residual, grad_out, gain, grad_mid, gain_part, branch_all, own,
     *refs
 ):
+    greet(count)
     scatter = Scatter(count, grad_gate_up, gate_up_weight, True, refs[:SCATTER_REFS])
     side = refs[SCATTER_REFS : SCATTER_REFS + 3]
     loads = side_loads([residual, grad_out], side)
-    meet(count)
     scatter.run()
     scatter.finish()
     gain_part[...] = jnp.zeros_like(gain_part)
@@ -775,13 +788,13 @@
     piece_all, gain_part, parts, part_recv, sums, sums_recv, part_send_sem, part_recv_sem, sums_send_sem,
     sums_recv_sem, *refs
 ):
+    greet(count, shards)
     scatter = Scatter(count, grad_packed, weight, True, refs[:SCATTER_REFS])
     side = refs[SCATTER_REFS : SCATTER_REFS + 2]
     loads = side_loads([tokens], side)
     gather = RowGather(count, piece, piece_all, refs[SCATTER_REFS + 2 :])
-    meet(count, shards)
-    scatter.run()
-    for part in range(PIECES):
+    scatter.run(shards)
+    for part in ORDER:
         gather.send(part)
     scatter.finish()
     gain_part[...] = jnp.zeros_like(gain_part)
@@ -1062,6 +1075,7 @@
     half_sem, block_sem, store_sem, *refs
 ):
     core = lax.rem(lax.axis_index("fsdp"), 2)
+    greet(count, shards)
     scatter = Scatter(count, hidden, down_weight, False, refs)
     width = gate_out.shape[1]
     step = rows_buf.shape[1]
@@ -1088,7 +1102,6 @@
             target = half.at[which, pl.ds(chip * span, span)]
             sem = half_sem.at[which, chip]
             half_loads.append(begin(across.at[pl.ds(start, span)], target, sem))
-    meet(count, shards)
     sums = CoreSum(send_buf, recv_buf, send_sem, recv_sem)
     tiles = gradient.shape[1] // GRAD_TILE
 
@@ -1133,7 +1146,7 @@
     for body in (send, keep):
         for first, last in zip(bounds, bounds[1:]):
             others.append(lambda body=body, a=first, b=last: lax.fori_loop(a, b, body, 0))
-    scatter.run(others)
+    scatter.run(shards, others)
     for index, out in enumerate((gate_out, up_out)):
         source = send_buf.at[:, pl.ds(index * width, width)]
         stores.append(begin(source, out, store_sem.at[blocks + index]))
@@ -1821,7 +1834,7 @@
     kv_first = 0 if dealt_heads else ctx_index * KV_HEADS // part_count
     tie = lax.optimization_barrier
     start = functools.partial(
-        start_gather, part_count, shard_count, 1, tokens[0], first_gain[None], second_gain[None]
+        start_gather, part_count, shard_count, 1, tokens[0], first_gain, second_gain
     )
     if dealt_heads:
         tokens_all, gain_first, gain_second, cosine, sine, packed, packed_hidden = start(

time: 531 us -> 528 us (level)
  transfers between devices with their start and end apart: 18 -> 18, of which waited for: 12 -> 12; matrix products, arithmetic and copies ran while one was open for 1% -> 1% of each run, Pallas kernels for 73% -> 74%
where the time goes in v7:
time: 528 us; the launch traced here: 525 us
  Pallas kernels  455 us (86%)
  waiting for transfers between devices  33.7 us (6%)
  between operations  14.7 us (3%)
  starting transfers between devices  12.9 us (2%)
    pallas_call x7, Pallas kernels, call_plane(): pl.pallas_call(body, out_shape=outs, in_specs=in_specs, out_specs=out_spe...  367 us
    pallas_call x1, Pallas kernels, attend_backward(): pl.pallas_call(functools.partial(attend_back_body, block_rows), out_shape...  27.1 us
    pallas_call x1, Pallas kernels, attend_forward(): pl.pallas_call(functools.partial(attend_body, block_rows), out_shape=(sha...  26.4 us
    ppermute x12, waiting for transfers between devices, swap(): return lax.ppermute(array, 'ctx', pairs)  25.8 us
    pallas_call x1, Pallas kernels, hidden_forward(): pl.pallas_call(hidden_body, grid=(length // step,), out_shape=(shape((len...  21.2 us
    ppermute x12, starting transfers between devices, swap(): return lax.ppermute(array, 'ctx', pairs)  12.5 us
  transfers between devices with their start and end apart: 18, of which 12 were waited for; matrix products, arithmetic and copies ran while one was open for 1% of the time, Pallas kernels for 74%

profile of v7, /device:TPU:0, one launch (start us, length us, event | category | flops | bytes accessed | tf_op | source)
XLA Modules:
  0.0 525.3 jit_solution(11361794249933078322)
XLA Ops:
  7.2 63.7 %shard_map.203 = (bf16[1024,2048]{1,0:T(8,128)(2,1)}, f32[1,2048]{1,0:T(1,128)}, f32[1,2048]{1,0:T(1,128)}, f32[1024,128]{1,0:T(8,128)}, f32[1024,128]{1,0:T(8,1...) custom-call(bf16[256,2048]{1,0:T(8,128)(2,1)} %bitcast.14, bf16[256]{0:T(256)(128)(2,1)} %first_gain.1, ...), custom_call_target="tpu_custom_call" | custom-call | flops 49999998976 | bytes 166666672 | tf_op jit(solution)/shard_map/pallas_call | solution.py:494
  72.2 26.4 %shard_map.204 = (bf16[1024,512]{1,0:T(8,128)(2,1)}, bf16[1024,512]{1,0:T(8,128)(2,1)}, bf16[4,1024,128]{2,1,0:T(8,128)(2,1)}, bf16[4,1024,128]{2,1,0:T(8,128)(2...) custom-call(s32[1,8]{1,0:T(1,128)} %dealing.3, ...), custom_call_target="tpu_custom_call" | custom-call | flops 30000001024 | bytes 10000000 | tf_op jit(solution)/shard_map/pallas_call | solution.py:1606
  98.7 77.2 %shard_map.205 = (f32[256,2048]{1,0:T(8,128)}, bf16[1024,2048]{1,0:T(8,128)(2,1)}) custom-call(bf16[1024,512]{1,0:T(8,128)(2,1)} %get-tuple-element.84.attended, bf16[512,2048]{1,0:T(8,128)(2,1)} %get-tuple-element.85.weight.output_weight, bf16[256,2048]{1,0:T(8,128)(2,1)} %bitcast.15, f32[1,2048]{1,0:T(1,128)} %get-tuple-element.86.gain), custom_call_target="tpu_custom_call" | custom-call | flops 60000002048 | bytes 200000000 | tf_op jit(solution)/shard_map/pallas_call | solution.py:494
  176.5 1.4 collective-permute-start
  178.4 21.2 %shard_map.206 = (f32[1024,2816]{1,0:T(8,128)}, bf16[1024,1408]{1,0:T(8,128)(2,1)}, bf16[2048,1024]{1,0:T(8,128)(2,1)}, bf16[1408,1024]{1,0:T(8,128)(2,1)}) custom-call(bf16[1024,2048]{1,0:T(8,128)(2,1)} %get-tuple-element.89.rows, bf16[2048,2816]{1,0:T(8,128)(2,1)} %all-gather.3.cloned.1.call-done.gate_weight.up_weight.gate_up_weight, ...), custom_call_target="tpu_custom_call" | custom-call | flops 11811160064 | bytes 30000000 | tf_op jit(solution)/shard_map/pallas_call | solution.py:926
  200.8 1.4 collective-permute-start.3
  202.9 10.9 %collective-permute-done.3.high = bf16[128,2048]{1,0:T(8,128)(2,1)S(1)} collective-permute-done((bf16[128,2048]{1,0:T(8,128)(2,1)S(1)}, bf16[128,2048]{1,0:T(8,128)(2,1)S(1)}, u32[]{:S(2)}, u32[]{:S(2)}) %collective-permute-start.3) | collective-permute-done | bytes 524320 | tf_op jit(solution)/shard_map/ppermute | solution.py:892
  215.3 2.0 copy-done.3
  217.3 15.2 %shard_map.208 = bf16[704,2048]{1,0:T(8,128)(2,1)} custom-call(bf16[1408,1024]{1,0:T(8,128)(2,1)} %get-tuple-element.99.across, bf16[1024,2048]{1,0:T(8,128)(2,1)} %copy-done.3), custom_call_target="tpu_custom_call" | custom-call | flops 5905580032 | bytes 19685266 | tf_op jit(solution)/shard_map/pallas_call | solution.py:494
  232.6 6.8 %all-gather.5.cloned.1.call-done.down_weight = bf16[1408,2048]{1,0:T(8,128)(2,1)} async-done(((bf16[176,2048]{1,0:T(8,128)(2,1)}), bf16[1408,2048]{1,0:T(8,128)(2,1)}) %all-gather.5.cloned.1.call-update) | async-done | bytes 5767184 | tf_op jit(solution)/shard_map/all_gather | solution.py:1796
  239.4 45.3 %shard_map.209 = (bf16[1024,1408]{1,0:T(8,128)(2,1)}, bf16[1024,1408]{1,0:T(8,128)(2,1)}, f32[256,2048]{1,0:T(8,128)}, bf16[1024,2816]{1,0:T(8,128)(2,1)}) custom-call(bf16[2048,1024]{1,0:T(8,128)(2,1)} %get-tuple-element.91.across, bf16[1024,2048]{1,0:T(8,128)(2,1)} %copy-done.3, f32[1024,2816]{1,0:T(8,128)} %get-tuple-element.97.gate_up, ...), custom_call_target="tpu_custom_call" | custom-call | flops 80000000000 | bytes 266666672 | tf_op jit(solution)/shard_map/pallas_call | solution.py:494
  285.5 77.3 %shard_map.210 = (f32[256,2048]{1,0:T(8,128)}, f32[1,2048]{1,0:T(1,128)}, bf16[1024,2048]{1,0:T(8,128)(2,1)}) custom-call(bf16[1024,2816]{1,0:T(8,128)(2,1)} %get-tuple-element.105.grad_gate_up, bf16[2048,2816]{1,0:T(8,128)(2,1)} %all-gather.3.cloned.1.call-done.gate_weight.up_weight.gate_up_weight, f32[256,2048]{1,0:T(8,128)} %get-tuple-element.87.residual, ...), custom_call_target="tpu_custom_call" | custom-call | flops 60000002048 | bytes 200000000 | tf_op jit(solution)/shard_map/pallas_call | solution.py:494
  362.8 1.4 collective-permute-start.7
  366.9 27.1 %shard_map.211.gradient.grad_packed = bf16[1024,1024]{1,0:T(8,128)(2,1)} custom-call(s32[1,8]{1,0:T(1,128)} %dealing.3, bf16[1024,2048]{1,0:T(8,128)(2,1)} %get-tuple-element.111.branch_all, bf16[512,2048]{1,0:T(8,128)(2,1)} %get-tuple-element.85.weight.output_weight, bf16[1024,512]{1,0:T(8,128)(2,1)} %get-tuple-element.112.queries, ...), custom_call_target="tpu_custom_call" | custom-call | flops 60000002048 | bytes 10000000 | tf_op jit(solution)/shard_map/pallas_call | solution.py:1745
  394.0 1.5 collective-permute-done.5.refs_1_.from_along
  397.4 24.0 %shard_map.212 = (bf16[1024,1536]{1,0:T(8,128)(2,1)}, bf16[88,2048]{1,0:T(8,128)(2,1)}, bf16[88,2048]{1,0:T(8,128)(2,1)}, bf16[128,1408]{1,0:T(8,128)(2,1)}, bf16[128,1408]{1,0:T(8,128)(2,1)}) custom-call(bf16[2048,1024]{1,0:T(8,128)(2,1)} %get-tuple-element.116.across, bf16[1024,1024]{1,0:T(8,128)(2,1)} %shard_map.211.gradient.grad_packed, ...), custom_call_target="tpu_custom_call" | custom-call | flops 6442450944 | bytes 21474836 | tf_op jit(solution)/shard_map/pallas_call | solution.py:494
  421.4 64.0 %shard_map.213 = (f32[256,2048]{1,0:T(8,128)}, f32[2,256]{1,0:T(2,128)}, bf16[1024,1408]{1,0:T(8,128)(2,1)}) custom-call(bf16[1024,1024]{1,0:T(8,128)(2,1)} %shard_map.211.gradient.grad_packed, bf16[2048,1536]{1,0:T(8,128)(2,1)} %get-tuple-element.81.weight, bf16[256,2048]{1,0:T(8,128)(2,1)} %bitcast.16, ...), custom_call_target="tpu_custom_call" | custom-call | flops 49999998976 | bytes 166666672 | tf_op jit(solution)/shard_map/pallas_call | solution.py:494
  487.6 3.5 fusion
  491.1 3.4 shard_map.215
  494.6 3.5 shard_map.214
  498.1 3.3 shard_map.217
  502.0 2.5 collective-permute-done.9.from_along
  508.6 5.8 %collective-permute-done.11.high = bf16[128,1536]{1,0:T(8,128)(2,1)S(1)} collective-permute-done((bf16[128,1536]{1,0:T(8,128)(2,1)S(1)}, bf16[128,1536]{1,0:T(8,128)(2,1)S(1)}, u32[]{:S(2)}, u32[]{:S(2)}) %collective-permute-start.11) | collective-permute-done | bytes 393248 | tf_op jit(solution)/shard_map/ppermute | solution.py:892
  515.4 2.8 shard_map.216
  (87 shorter events, 18.8 us)
Async XLA Ops:
  7.2 63.9 %copy-start = (bf16[704,2048]{1,0:T(8,128)(2,1)S(1)}, bf16[704,2048]{1,0:T(8,128)(2,1)}, u32[]{:S(2)}) copy-start(bf16[704,2048]{1,0:T(8,128)(2,1)} %param.22) | copy-start | bytes 8650756
  7.2 171.2 %all-gather.3.cloned.1.call-start = ((), (), s32[]{:S(2)}) async-start(), calls=%async_computation.4 | async-start | bytes 12976128 | tf_op jit(solution)/shard_map/all_gather | solution.py:1796
  71.0 168.4 %all-gather.5.cloned.1.call-start = ((), (), s32[]{:S(2)}) async-start(), calls=%async_computation.5 | async-start | bytes 6488064 | tf_op jit(solution)/shard_map/all_gather | solution.py:1796
  72.0 290.7 %reduce-scatter.5.cloned.1.call-start = ((), (), s32[]{:S(2)}) async-start(), calls=%async_computation.6 | async-start | bytes 3604480 | tf_op jit(solution)/shard_map/reduce_scatter | solution.py:1802
  98.7 77.2 %copy-start.4 = (bf16[1,256,2048]{2,1,0:T(8,128)(2,1)S(1)}, bf16[1,256,2048]{2,1,0:T(8,128)(2,1)}, u32[]{:S(2)}) copy-start(bf16[1,256,2048]{2,1,0:T(8,128)(2,1)} %param.23) | copy-start | bytes 3145732
  175.9 24.5 %collective-permute-start.1 = (bf16[256,2048]{1,0:T(8,128)(2,1)S(1)}, bf16[256,2048]{1,0:T(8,128)(2,1)S(1)}, u32[]{:S(2)}, u32[]{:S(2)}) collective-permute-start(bf16[256,2048]{1,0:T(8,128)(2,1)S(1)} %bitcast.9), channel_id=1, source_target_pairs={{0,16},{8,24},{16,0},{24,8},{1,17},{9,25},{17,1},{25,9},{2,18},{10... | collective-permute-start | bytes 3145736 | tf_op jit(solution)/shard_map/ppermute | solution.py:892
  176.5 24.2 %collective-permute-start = (bf16[256,2048]{1,0:T(8,128)(2,1)S(1)}, bf16[256,2048]{1,0:T(8,128)(2,1)S(1)}, u32[]{:S(2)}, u32[]{:S(2)}) collective-permute-start(bf16[256,2048]{1,0:T(8,128)(2,1)S(1)} %bitcast.10), channel_id=1, source_target_pairs={{0,8},{8,0},{16,24},{24,16},{1,9},{9,1},{17,25},{25,17},{2,10},{10... | collective-permute-start | bytes 3145736 | tf_op jit(solution)/shard_map/ppermute | solution.py:892
  200.8 13.0 %collective-permute-start.3 = (bf16[128,2048]{1,0:T(8,128)(2,1)S(1)}, bf16[128,2048]{1,0:T(8,128)(2,1)S(1)}, u32[]{:S(2)}, u32[]{:S(2)}) collective-permute-start(bf16[128,2048]{1,0:T(8,128)(2,1)S(1)} %slice.19), channel_id=1, source_target_pairs={{0,8},{8,0},{16,24},{24,16},{1,9},{9,1},{17,25},{25,17},{2,10},{10... | collective-permute-start | bytes 1572872 | tf_op jit(solution)/shard_map/ppermute | solution.py:892
  202.2 12.8 %collective-permute-start.2 = (bf16[128,2048]{1,0:T(8,128)(2,1)S(1)}, bf16[128,2048]{1,0:T(8,128)(2,1)S(1)}, u32[]{:S(2)}, u32[]{:S(2)}) collective-permute-start(bf16[128,2048]{1,0:T(8,128)(2,1)S(1)} %slice.18), channel_id=1, source_target_pairs={{0,16},{8,24},{16,0},{24,8},{1,17},{9,25},{17,1},{25,9},{2,18},{10... | collective-permute-start | bytes 1572872 | tf_op jit(solution)/shard_map/ppermute | solution.py:892
  239.4 123.4 %reduce-scatter.7.cloned.1.call-start = ((), (), s32[]{:S(2)}) async-start(), calls=%async_computation.7 | async-start | bytes 3604480 | tf_op jit(solution)/shard_map/reduce_scatter | solution.py:1802
  284.8 136.6 %reduce-scatter.9.cloned.1.call-start = ((), (), s32[]{:S(2)}) async-start(), calls=%async_computation.8 | async-start | bytes 3604480 | tf_op jit(solution)/shard_map/reduce_scatter | solution.py:1802
  285.4 200.1 %reduce-scatter.11.cloned.1.call-start = ((), (), s32[]{:S(2)}) async-start(), calls=%async_computation.9 | async-start | bytes 3932160 | tf_op jit(solution)/shard_map/reduce_scatter | solution.py:1802
  362.8 31.2 %collective-permute-start.7 = (bf16[256,1408]{1,0:T(8,128)(2,1)}, bf16[256,1408]{1,0:T(8,128)(2,1)S(1)}, u32[]{:S(2)}, u32[]{:S(2)}) collective-permute-start(bf16[256,1408]{1,0:T(8,128)(2,1)} %reduce-scatter.7.cloned.1.call-done.refs_0_), channel_id=1, source_target_pairs={{0,16},{8,24},{16,0},{24,8},{1,17},{9,25},{17,1},{25,9},{2,18},{10... | collective-permute-start | bytes 2162696 | tf_op jit(solution)/shard_map/ppermute | solution.py:892
  364.2 29.8 %collective-permute-start.6 = (bf16[256,1408]{1,0:T(8,128)(2,1)}, bf16[256,1408]{1,0:T(8,128)(2,1)S(1)}, u32[]{:S(2)}, u32[]{:S(2)}) collective-permute-start(bf16[256,1408]{1,0:T(8,128)(2,1)} %reduce-scatter.7.cloned.1.call-done.refs_0_), channel_id=1, source_target_pairs={{0,8},{8,0},{16,24},{24,16},{1,9},{9,1},{17,25},{25,17},{2,10},{10... | collective-permute-start | bytes 2162696 | tf_op jit(solution)/shard_map/ppermute | solution.py:892
  364.9 30.6 %collective-permute-start.5 = (bf16[176,2048]{1,0:T(8,128)(2,1)}, bf16[176,2048]{1,0:T(8,128)(2,1)S(1)}, u32[]{:S(2)}, u32[]{:S(2)}) collective-permute-start(bf16[176,2048]{1,0:T(8,128)(2,1)} %reduce-scatter.5.cloned.1.call-done.own), channel_id=1, source_target_pairs={{0,16},{8,24},{16,0},{24,8},{1,17},{9,25},{17,1},{25,9},{2,18},{10... | collective-permute-start | bytes 2162696 | tf_op jit(solution)/shard_map/ppermute | solution.py:892
  366.2 30.3 %collective-permute-start.4 = (bf16[176,2048]{1,0:T(8,128)(2,1)}, bf16[176,2048]{1,0:T(8,128)(2,1)S(1)}, u32[]{:S(2)}, u32[]{:S(2)}) collective-permute-start(bf16[176,2048]{1,0:T(8,128)(2,1)} %reduce-scatter.5.cloned.1.call-done.own), channel_id=1, source_target_pairs={{0,8},{8,0},{16,24},{24,16},{1,9},{9,1},{17,25},{25,17},{2,10},{10... | collective-permute-start | bytes 2162696 | tf_op jit(solution)/shard_map/ppermute | solution.py:892
  485.5 19.1 %collective-permute-start.9 = (bf16[256,1536]{1,0:T(8,128)(2,1)}, bf16[256,1536]{1,0:T(8,128)(2,1)S(1)}, u32[]{:S(2)}, u32[]{:S(2)}) collective-permute-start(bf16[256,1536]{1,0:T(8,128)(2,1)} %reduce-scatter.11.cloned.1.call-done.own), channel_id=1, source_target_pairs={{0,16},{8,24},{16,0},{24,8},{1,17},{9,25},{17,1},{25,9},{2,18},{10... | collective-permute-start | bytes 2359304 | tf_op jit(solution)/shard_map/ppermute | solution.py:892
  486.6 18.6 %collective-permute-start.8 = (bf16[256,1536]{1,0:T(8,128)(2,1)}, bf16[256,1536]{1,0:T(8,128)(2,1)S(1)}, u32[]{:S(2)}, u32[]{:S(2)}) collective-permute-start(bf16[256,1536]{1,0:T(8,128)(2,1)} %reduce-scatter.11.cloned.1.call-done.own), channel_id=1, source_target_pairs={{0,8},{8,0},{16,24},{24,16},{1,9},{9,1},{17,25},{25,17},{2,10},{10... | collective-permute-start | bytes 2359304 | tf_op jit(solution)/shard_map/ppermute | solution.py:892
  498.1 9.3 %copy-start.20 = (f32[256,2048]{1,0:T(8,128)S(1)}, f32[256,2048]{1,0:T(8,128)}, u32[]{:S(2)}) copy-start(f32[256,2048]{1,0:T(8,128)} %get-tuple-element.106) | copy-start | bytes 6291460
  498.1 9.3 %copy-start.21 = (f32[256,2048]{1,0:T(8,128)S(1)}, f32[256,2048]{1,0:T(8,128)}, u32[]{:S(2)}) copy-start(f32[256,2048]{1,0:T(8,128)} %get-tuple-element.126) | copy-start | bytes 6291460
  505.3 10.1 %copy-start.5 = (bf16[256,1536]{1,0:T(8,128)(2,1)S(1)}, bf16[256,1536]{1,0:T(8,128)(2,1)}, u32[]{:S(2)}) copy-start(bf16[256,1536]{1,0:T(8,128)(2,1)} %reduce-scatter.11.cloned.1.call-done.own) | copy-start | bytes 2359300
  505.3 9.1 %collective-permute-start.11 = (bf16[128,1536]{1,0:T(8,128)(2,1)S(1)}, bf16[128,1536]{1,0:T(8,128)(2,1)S(1)}, u32[]{:S(2)}, u32[]{:S(2)}) collective-permute-start(bf16[128,1536]{1,0:T(8,128)(2,1)S(1)} %slice.22), channel_id=1, source_target_pairs={{0,8},{8,0},{16,24},{24,16},{1,9},{9,1},{17,25},{25,17},{2,10},{10... | collective-permute-start | bytes 1179656 | tf_op jit(solution)/shard_map/ppermute | solution.py:892
  506.5 8.9 %collective-permute-start.10 = (bf16[128,1536]{1,0:T(8,128)(2,1)S(1)}, bf16[128,1536]{1,0:T(8,128)(2,1)S(1)}, u32[]{:S(2)}, u32[]{:S(2)}) collective-permute-start(bf16[128,1536]{1,0:T(8,128)(2,1)S(1)} %slice.21), channel_id=1, source_target_pairs={{0,16},{8,24},{16,0},{24,8},{1,17},{9,25},{17,1},{25,9},{2,18},{10... | collective-permute-start | bytes 1179656 | tf_op jit(solution)/shard_map/ppermute | solution.py:892
  507.4 10.8 %copy-start.1 = (bf16[704,2048]{1,0:T(8,128)(2,1)S(1)}, bf16[704,2048]{1,0:T(8,128)(2,1)}, u32[]{:S(2)}) copy-start(bf16[704,2048]{1,0:T(8,128)(2,1)} %param.22) | copy-start | bytes 8650756
  (17 other events, 52.9 us)
Sparse Core Ops, SparseCore 0:
  71.1 107.2 all-gather.2
  180.6 58.7 all-gather.4
  241.7 54.8 reduce-scatter.4
  298.8 56.0 reduce-scatter.6
  357.0 56.0 reduce-scatter.8
  421.5 58.0 reduce-scatter.10
